TPU v7x, 32 devices: a whole 2x2x4 slice. The times are simulated.
32 devices in a mesh: groups: 2 (over y), seq: 4 (over z), chan: 4 (over x, core).
Axes of the slice: x: 2, y: 2, z: 4, core: 2. Of those that a mesh axis runs over, the one named last changes fastest.
Arguments:
- tokens: int32 [6144], P(('groups', 'seq')), parts along dimension 0, may hold values from 0 to 3
- cotangent: bfloat16 [6144, 768], P(('groups', 'seq'), 'chan'), parts along dimension 0, may hold values from -6 to 6
- embed: bfloat16 [4, 768], P(None, 'chan'), may hold values from -6 to 6
- taps: bfloat16 [2, 5, 768], P(None, None, 'chan'), may hold values from -2.5 to 2.5
- mix: bfloat16 [2, 768, 768], P(None, None, 'chan'), may hold values from -0.21875 to 0.21875
- dilations: int32 [2], replicated, may hold values from 1 to 8, as said below
Outputs:
- output: bfloat16 [6144, 768], P(('groups', 'seq'), 'chan'), parts along dimension 0
- grad_mix: float32 [4, 768, 768], P('groups', None, 'chan'), parts along dimension 0
- grad_taps: float32 [4, 5, 768], P('groups', None, 'chan'), parts along dimension 0
- grad_embed: float32 [8, 768], P('groups', 'chan'), parts along dimension 0
There are 2 independent parts, one for each index of `groups`. A program takes and returns all parts, laid end to end along the dimension named above; an argument that names none is the same for every part. Nothing has to cross between parts.
Inputs may be any that keep to these rules, and one draw needn't show every extreme that they name: `dilations`: each block's dilation lies in 1 to 8, and at least one block has exactly 8.
All inputs are finite; a program needn't handle non-finite values.
Results may differ from a plain program's by a relative error of at most 0.025.
Values may be sent and summed in bfloat16 or wider, within the bound.
No kernel may reach another device: no remote copies, remote signals or barrier semaphores. Data moves between devices by JAX's collectives and lax.ppermute only.
A program may use at most 64 MiB of HBM per device.

v0:
```python
import math

import jax
import jax.numpy as jnp
from jax import lax
from jax.sharding import PartitionSpec as P

TAPS = 5
BASES = 4
BLOCKS = 2
DMAX = 8


gelu_scale = math.sqrt(2.0 / math.pi)
cubic_term = 0.044715


def with_halo(cells, sides, width):
    for axis, dim in sides:
        count = lax.axis_size(axis)
        ends = count - 1
        head = lax.slice_in_dim(cells, 0, width, axis=dim)
        tail = lax.slice_in_dim(cells, cells.shape[dim] - width, cells.shape[dim], axis=dim)
        cells = jnp.concatenate(
            [
                lax.ppermute(tail, axis, [(i, (i + 1) % count) for i in range(ends)]),
                cells,
                lax.ppermute(head, axis, [((i + 1) % count, i) for i in range(ends)]),
            ],
            axis=dim,
        )
    return cells


def partner_2(shard, axis, stride):
    return lax.ppermute(shard, axis, [(i, i ^ 1 << stride) for i in range(lax.axis_size(axis))])


def gelu_value(inputs):
    inner = gelu_scale * (inputs + cubic_term * inputs * inputs * inputs)
    return 0.5 * inputs * (1.0 + jnp.tanh(inner))


def gelu_slope(inputs):
    tangent = jnp.tanh(gelu_scale * (inputs + cubic_term * inputs * inputs * inputs))
    return 0.5 * (1.0 + tangent) + 0.5 * inputs * (1.0 - tangent * tangent) * gelu_scale * (
        1.0 + 3.0 * cubic_term * inputs * inputs
    )


def taps_apply(padded, taps_block, dilation, rows_out, orient):
    reach = TAPS // 2 * DMAX
    result = jnp.zeros((rows_out, padded.shape[1]), jnp.float32)
    for offset in range(TAPS):
        first = reach + orient * (offset - TAPS // 2) * dilation
        window = lax.dynamic_slice_in_dim(padded, first, rows_out, 0).astype(jnp.float32)
        result = result + taps_block[offset].astype(jnp.float32)[None, :] * window
    return result


def extend_rows(values):
    return with_halo(values, (("seq", 0),), TAPS // 2 * DMAX)


def mirrored(values):
    seq_count = lax.axis_size("seq")
    chan_count = lax.axis_size("chan")
    moved = values
    for bit_index in range(seq_count.bit_length() - 1):
        moved = partner_2(moved, "seq", bit_index)
    for bit_index in range(chan_count.bit_length() - 1):
        moved = partner_2(moved, "chan", bit_index)
    result = moved[::-1, ::-1]
    return result


def body(tokens, cotangent, embed, taps, mix, dilations):
    reach = TAPS // 2 * DMAX
    rows_local = tokens.shape[0]
    lanes_local = embed.shape[1]
    length_all = rows_local * lax.axis_size("seq")
    current = jnp.zeros((rows_local, lanes_local), jnp.float32)
    for letter in range(BASES):
        current = current + jnp.where(
            tokens[:, None] == letter, embed[letter].astype(jnp.float32)[None, :], 0.0
        )
    current = current.astype(jnp.bfloat16)
    saved = []
    for layer_index in range(BLOCKS):
        dilation = dilations[layer_index]
        weights = mix[layer_index]
        padded = extend_rows(current)
        conv_out = taps_apply(padded, taps[layer_index], dilation, rows_local, 1).astype(
            jnp.bfloat16
        )
        partner = mirrored(conv_out)
        mixed_local = (conv_out.astype(jnp.float32) + partner.astype(jnp.float32)).astype(
            jnp.bfloat16
        )
        kept = mixed_local

        def accumulate(carry, piece, first, weights=weights):
            return jnp.dot(piece, weights, preferred_element_type=jnp.float32)

        empty = jnp.zeros((rows_local, weights.shape[1]), jnp.float32)
        preact = accumulate(
            empty, lax.all_gather(mixed_local, "chan", axis=1, tiled=True), jnp.int32(0)
        )
        saved.append((padded, kept, preact, dilation))
        current = (current.astype(jnp.float32) + gelu_value(preact)).astype(jnp.bfloat16)
    upstream = cotangent.astype(jnp.float32) * (1.0 / math.sqrt(length_all))
    mix_grads = []
    taps_grads = []
    for layer_index in reversed(range(BLOCKS)):
        padded, kept, preact, dilation = saved[layer_index]
        weights = mix[layer_index]
        slope_in = (upstream * gelu_slope(preact)).astype(jnp.bfloat16)

        def outer_rows(piece, first, slope_in=slope_in):
            return lax.dot_general(
                piece, slope_in, (((0,), (0,)), ((), ())), preferred_element_type=jnp.float32
            )

        mix_grad = outer_rows(lax.all_gather(kept, "chan", axis=1, tiled=True), jnp.int32(0))
        mix_grads.insert(0, mix_grad)
        partials = lax.dot_general(
            slope_in, weights, (((1,), (1,)), ((), ())), preferred_element_type=jnp.float32
        )
        mix_back = lax.psum_scatter(
            partials.astype(jnp.bfloat16), "chan", scatter_dimension=1, tiled=True
        )
        folded = mix_back.astype(jnp.float32) + mirrored(mix_back).astype(jnp.float32)
        grad_padded = with_halo(folded.astype(jnp.bfloat16), (("seq", 0),), reach).astype(
            folded.dtype
        )
        rows_taps = []
        for offset in range(TAPS):
            first = reach + (offset - TAPS // 2) * dilation
            window = lax.dynamic_slice_in_dim(padded, first, rows_local, 0).astype(jnp.float32)
            rows_taps.append(jnp.sum(folded * window, axis=0))
        taps_grads.insert(0, jnp.stack(rows_taps))
        upstream = upstream + taps_apply(grad_padded, taps[layer_index], dilation, rows_local, -1)
    masks = (jnp.arange(BASES, dtype=jnp.int32)[:, None] == tokens[None, :]).astype(jnp.float32)
    embed_grad = jnp.dot(masks, upstream, precision=lax.Precision.HIGHEST)
    grad_mix, grad_taps, grad_embed = lax.psum(
        (jnp.stack(mix_grads), jnp.stack(taps_grads), embed_grad), "seq"
    )
    return (current, grad_mix, grad_taps, grad_embed)


def solution(mesh):
    in_specs = (
        P(("groups", "seq")),
        P(("groups", "seq"), "chan"),
        P(None, "chan"),
        P(None, None, "chan"),
        P(None, None, "chan"),
        P(),
    )
    out_specs = (
        P(("groups", "seq"), "chan"),
        P("groups", None, "chan"),
        P("groups", None, "chan"),
        P("groups", "chan"),
    )
    return jax.shard_map(body, mesh=mesh, in_specs=in_specs, out_specs=out_specs, check_vma=False)
```

profile of v0, /device:TPU:0, one launch (start us, length us, event | category | flops | bytes accessed | tf_op | source)
XLA Modules:
  0.0 351.9 jit_solution(9423095986557139028)
XLA Ops:
  9.1 4.9 %collective-permute-start = (bf16[16,192]{0,1:T(8,128)(2,1)S(1)}, bf16[16,192]{0,1:T(8,128)(2,1)S(1)}, u32[]{:S(2)}, u32[]{:S(2)}) collective-permute-start(bf16[16,192]{0,1:T(8,128)(2,1)S(1)} %get-tuple-element.31), channel_id=1, source_target_pairs={{0,4},{4,8},{8,12},{1,5},{5,9},{9,13},{2,6},{6,10},{10,14},{3,7},{... | collective-permute-start | bytes 18440 | tf_op jit(solution)/shard_map/ppermute | solution.py:26
  22.1 2.7 collective-permute-start.2
  24.8 6.4 %collective-permute-done.2 = bf16[768,192]{0,1:T(8,128)(2,1)S(1)} collective-permute-done((bf16[768,192]{0,1:T(8,128)(2,1)S(1)}, bf16[768,192]{0,1:T(8,128)(2,1)S(1)}, u32[]{:S(2)}, u32[]{:S(2)}) %collective-permute-start.2) | collective-permute-done | bytes 294944 | tf_op jit(solution)/shard_map/ppermute | solution.py:36
  31.2 2.8 collective-permute-start.3
  34.0 12.0 %collective-permute-done.3 = bf16[768,192]{0,1:T(8,128)(2,1)S(1)} collective-permute-done((bf16[768,192]{0,1:T(8,128)(2,1)S(1)}, bf16[768,192]{0,1:T(8,128)(2,1)S(1)}, u32[]{:S(2)}, u32[]{:S(2)}) %collective-permute-start.3) | collective-permute-done | bytes 294944 | tf_op jit(solution)/shard_map/ppermute | solution.py:36
  49.1 7.6 %collective-permute-done.5 = bf16[768,192]{0,1:T(8,128)(2,1)S(1)} collective-permute-done((bf16[768,192]{0,1:T(8,128)(2,1)S(1)}, bf16[768,192]{0,1:T(8,128)(2,1)S(1)}, u32[]{:S(2)}, u32[]{:S(2)}) %collective-permute-start.5) | collective-permute-done | bytes 294944 | tf_op jit(solution)/shard_map/ppermute | solution.py:36
  60.6 18.6 %all-gather.3.cloned.1.call-done = bf16[768,768]{0,1:T(8,128)(2,1)} async-done(((bf16[768,192]{0,1:T(8,128)(2,1)}), bf16[768,768]{0,1:T(8,128)(2,1)}) %all-gather.3.cloned.1.call-update) | async-done | bytes 1179664 | tf_op jit(solution)/shard_map/all_gather | solution.py:107
  81.1 3.4 collective-permute-start.6
  93.2 6.6 %collective-permute-done.8 = bf16[768,192]{0,1:T(8,128)(2,1)S(1)} collective-permute-done((bf16[768,192]{0,1:T(8,128)(2,1)S(1)}, bf16[768,192]{0,1:T(8,128)(2,1)S(1)}, u32[]{:S(2)}, u32[]{:S(2)}) %collective-permute-start.8) | collective-permute-done | bytes 294944 | tf_op jit(solution)/shard_map/ppermute | solution.py:36
  99.8 2.7 collective-permute-start.9
  102.5 12.0 %collective-permute-done.9 = bf16[768,192]{0,1:T(8,128)(2,1)S(1)} collective-permute-done((bf16[768,192]{0,1:T(8,128)(2,1)S(1)}, bf16[768,192]{0,1:T(8,128)(2,1)S(1)}, u32[]{:S(2)}, u32[]{:S(2)}) %collective-permute-start.9) | collective-permute-done | bytes 294944 | tf_op jit(solution)/shard_map/ppermute | solution.py:36
  116.6 8.5 %collective-permute-done.11 = bf16[768,192]{0,1:T(8,128)(2,1)S(1)} collective-permute-done((bf16[768,192]{0,1:T(8,128)(2,1)S(1)}, bf16[768,192]{0,1:T(8,128)(2,1)S(1)}, u32[]{:S(2)}, u32[]{:S(2)}) %collective-permute-start.11) | collective-permute-done | bytes 294944 | tf_op jit(solution)/shard_map/ppermute | solution.py:36
  127.9 17.8 %all-gather.5.cloned.1.call-done = bf16[768,768]{0,1:T(8,128)(2,1)} async-done(((bf16[768,192]{0,1:T(8,128)(2,1)}), bf16[768,768]{0,1:T(8,128)(2,1)}) %all-gather.5.cloned.1.call-update) | async-done | bytes 1179664 | tf_op jit(solution)/shard_map/all_gather | solution.py:107
  149.3 25.8 %reduce-scatter.3.cloned.1.call-done = bf16[768,192]{0,1:T(8,128)(2,1)} async-done(((bf16[768,768]{0,1:T(8,128)(2,1)}), bf16[768,192]{0,1:T(8,128)(2,1)}) %reduce-scatter.3.cloned.1.call-update) | async-done | bytes 294928 | tf_op jit(solution)/shard_map/reduce_scatter | solution.py:129
  176.6 7.5 %collective-permute-done.12 = bf16[768,192]{0,1:T(8,128)(2,1)S(1)} collective-permute-done((bf16[768,192]{0,1:T(8,128)(2,1)}, bf16[768,192]{0,1:T(8,128)(2,1)S(1)}, u32[]{:S(2)}, u32[]{:S(2)}) %collective-permute-start.12) | collective-permute-done | bytes 294944 | tf_op jit(solution)/shard_map/ppermute | solution.py:36
  184.1 2.4 collective-permute-start.13
  186.5 12.7 %collective-permute-done.13 = bf16[768,192]{0,1:T(8,128)(2,1)S(1)} collective-permute-done((bf16[768,192]{0,1:T(8,128)(2,1)S(1)}, bf16[768,192]{0,1:T(8,128)(2,1)S(1)}, u32[]{:S(2)}, u32[]{:S(2)}) %collective-permute-start.13) | collective-permute-done | bytes 294944 | tf_op jit(solution)/shard_map/ppermute | solution.py:36
  201.4 8.5 %collective-permute-done.15 = bf16[768,192]{0,1:T(8,128)(2,1)} collective-permute-done((bf16[768,192]{0,1:T(8,128)(2,1)S(1)}, bf16[768,192]{0,1:T(8,128)(2,1)}, u32[]{:S(2)}, u32[]{:S(2)}) %collective-permute-start.15) | collective-permute-done | bytes 294944 | tf_op jit(solution)/shard_map/ppermute | solution.py:36
  209.9 5.3 %rev.14 = bf16[768,192]{0,1:T(8,128)(2,1)S(1)} reverse(bf16[768,192]{0,1:T(8,128)(2,1)} %collective-permute-done.15), dimensions={0,1} | reverse | bytes 589824 | tf_op jit(solution)/shard_map/rev | solution.py:73
  215.3 2.9 fusion.17
  218.2 2.4 collective-permute-start.16
  222.3 4.3 %collective-permute-done.17 = bf16[16,192]{0,1:T(8,128)(2,1)S(1)} collective-permute-done((bf16[16,192]{0,1:T(8,128)(2,1)S(1)}, bf16[16,192]{0,1:T(8,128)(2,1)S(1)}, u32[]{:S(2)}, u32[]{:S(2)}) %collective-permute-start.17) | collective-permute-done | bytes 6176 | tf_op jit(solution)/shard_map/ppermute | solution.py:28
  230.5 25.7 %reduce-scatter.5.cloned.1.call-done = bf16[768,192]{0,1:T(8,128)(2,1)} async-done(((bf16[768,768]{0,1:T(8,128)(2,1)}), bf16[768,192]{0,1:T(8,128)(2,1)}) %reduce-scatter.5.cloned.1.call-update) | async-done | bytes 294928 | tf_op jit(solution)/shard_map/reduce_scatter | solution.py:129
  257.7 7.5 %collective-permute-done.18 = bf16[768,192]{0,1:T(8,128)(2,1)S(1)} collective-permute-done((bf16[768,192]{0,1:T(8,128)(2,1)}, bf16[768,192]{0,1:T(8,128)(2,1)S(1)}, u32[]{:S(2)}, u32[]{:S(2)}) %collective-permute-start.18) | collective-permute-done | bytes 294944 | tf_op jit(solution)/shard_map/ppermute | solution.py:36
  265.2 2.4 collective-permute-start.19
  267.6 12.7 %collective-permute-done.19 = bf16[768,192]{0,1:T(8,128)(2,1)S(1)} collective-permute-done((bf16[768,192]{0,1:T(8,128)(2,1)S(1)}, bf16[768,192]{0,1:T(8,128)(2,1)S(1)}, u32[]{:S(2)}, u32[]{:S(2)}) %collective-permute-start.19) | collective-permute-done | bytes 294944 | tf_op jit(solution)/shard_map/ppermute | solution.py:36
  284.8 7.6 %collective-permute-done.21 = bf16[768,192]{0,1:T(8,128)(2,1)S(1)} collective-permute-done((bf16[768,192]{0,1:T(8,128)(2,1)S(1)}, bf16[768,192]{0,1:T(8,128)(2,1)S(1)}, u32[]{:S(2)}, u32[]{:S(2)}) %collective-permute-start.21) | collective-permute-done | bytes 294944 | tf_op jit(solution)/shard_map/ppermute | solution.py:36
  295.7 2.5 collective-permute-start.22
  301.1 5.7 %collective-permute-done.23 = bf16[16,192]{0,1:T(8,128)(2,1)S(1)} collective-permute-done((bf16[16,192]{0,1:T(8,128)(2,1)S(1)}, bf16[16,192]{0,1:T(8,128)(2,1)S(1)}, u32[]{:S(2)}, u32[]{:S(2)}) %collective-permute-start.23) | collective-permute-done | bytes 6176 | tf_op jit(solution)/shard_map/ppermute | solution.py:28
  308.2 18.0 %all-reduce = (f32[2,5,192]{2,1,0:T(8,128)S(1)}, f32[4,192]{1,0:T(4,128)}) all-reduce(f32[2,5,192]{2,1,0:T(8,128)S(1)} %pad_maximum_fusion.3, f32[4,192]{1,0:T(4,128)S(1)} %fusion.40), channel_id=1, replica_groups=mesh['groups'=2,'seq'=4,'chan'=4] {'seq'}, use_global_device_ids=true, to_apply=%region_13.14 | all-reduce | flops 2688 | bytes 21504 | tf_op jit(solution)/shard_map/psum | solution.py:145
  326.8 16.2 %all-reduce.3.cloned.1.call-done = f32[2,768,192]{1,2,0:T(8,128)} async-done(((f32[2,768,192]{1,2,0:T(8,128)}), f32[2,768,192]{1,2,0:T(8,128)}) %all-reduce.3.cloned.1.call-update) | async-done | bytes 1179664 | tf_op jit(solution)/shard_map/psum | solution.py:145
  343.0 2.4 copy.12
  (81 shorter events, 53.0 us)
Async XLA Ops:
  7.2 72.0 %all-gather.3.cloned.1.call-start = ((), (), s32[]{:S(2)}) async-start(), calls=%async_computation.2 | async-start | bytes 1474560 | tf_op jit(solution)/shard_map/all_gather | solution.py:107
  9.1 11.6 %collective-permute-start = (bf16[16,192]{0,1:T(8,128)(2,1)S(1)}, bf16[16,192]{0,1:T(8,128)(2,1)S(1)}, u32[]{:S(2)}, u32[]{:S(2)}) collective-permute-start(bf16[16,192]{0,1:T(8,128)(2,1)S(1)} %get-tuple-element.31), channel_id=1, source_target_pairs={{0,4},{4,8},{8,12},{1,5},{5,9},{9,13},{2,6},{6,10},{10,14},{3,7},{... | collective-permute-start | bytes 18440 | tf_op jit(solution)/shard_map/ppermute | solution.py:26
  14.0 6.7 %collective-permute-start.1 = (bf16[16,192]{0,1:T(8,128)(2,1)S(1)}, bf16[16,192]{0,1:T(8,128)(2,1)S(1)}, u32[]{:S(2)}, u32[]{:S(2)}) collective-permute-start(bf16[16,192]{0,1:T(8,128)(2,1)S(1)} %get-tuple-element.32), channel_id=1, source_target_pairs={{4,0},{8,4},{12,8},{5,1},{9,5},{13,9},{6,2},{10,6},{14,10},{7,3},{... | collective-permute-start | bytes 18440 | tf_op jit(solution)/shard_map/ppermute | solution.py:28
  22.1 9.2 %collective-permute-start.2 = (bf16[768,192]{0,1:T(8,128)(2,1)S(1)}, bf16[768,192]{0,1:T(8,128)(2,1)S(1)}, u32[]{:S(2)}, u32[]{:S(2)}) collective-permute-start(bf16[768,192]{0,1:T(8,128)(2,1)S(1)} %fusion.4), channel_id=1, source_target_pairs={{0,4},{4,0},{8,12},{12,8},{1,5},{5,1},{9,13},{13,9},{2,6},{6,2},{1... | collective-permute-start | bytes 884744 | tf_op jit(solution)/shard_map/ppermute | solution.py:36
  31.2 14.8 %collective-permute-start.3 = (bf16[768,192]{0,1:T(8,128)(2,1)S(1)}, bf16[768,192]{0,1:T(8,128)(2,1)S(1)}, u32[]{:S(2)}, u32[]{:S(2)}) collective-permute-start(bf16[768,192]{0,1:T(8,128)(2,1)S(1)} %collective-permute-done.2), channel_id=1, source_target_pairs={{0,8},{4,12},{8,0},{12,4},{1,9},{5,13},{9,1},{13,5},{2,10},{6,14},... | collective-permute-start | bytes 884744 | tf_op jit(solution)/shard_map/ppermute | solution.py:36
  46.0 1.6 collective-permute-start.4
  47.6 9.1 %collective-permute-start.5 = (bf16[768,192]{0,1:T(8,128)(2,1)S(1)}, bf16[768,192]{0,1:T(8,128)(2,1)S(1)}, u32[]{:S(2)}, u32[]{:S(2)}) collective-permute-start(bf16[768,192]{0,1:T(8,128)(2,1)S(1)} %collective-permute-done.4), channel_id=1, source_target_pairs={{0,2},{1,3},{2,0},{3,1},{4,6},{5,7},{6,4},{7,5},{8,10},{9,11},{10,... | collective-permute-start | bytes 884744 | tf_op jit(solution)/shard_map/ppermute | solution.py:36
  58.6 20.6 %copy-start.1 = (bf16[2,768,192]{1,2,0:T(8,128)(2,1)S(1)}, bf16[2,768,192]{1,2,0:T(8,128)(2,1)}, u32[]{:S(2)}) copy-start(bf16[2,768,192]{1,2,0:T(8,128)(2,1)} %param.10) | copy-start | bytes 1769476
  60.6 85.1 %all-gather.5.cloned.1.call-start = ((), (), s32[]{:S(2)}) async-start(), calls=%async_computation.3 | async-start | bytes 1474560 | tf_op jit(solution)/shard_map/all_gather | solution.py:107
  81.1 8.0 %collective-permute-start.6 = (bf16[16,192]{0,1:T(8,128)(2,1)S(1)}, bf16[16,192]{0,1:T(8,128)(2,1)S(1)}, u32[]{:S(2)}, u32[]{:S(2)}) collective-permute-start(bf16[16,192]{0,1:T(8,128)(2,1)S(1)} %get-tuple-element.29), channel_id=1, source_target_pairs={{0,4},{4,8},{8,12},{1,5},{5,9},{9,13},{2,6},{6,10},{10,14},{3,7},{... | collective-permute-start | bytes 18440 | tf_op jit(solution)/shard_map/ppermute | solution.py:26
  84.5 6.0 %collective-permute-start.7 = (bf16[16,192]{0,1:T(8,128)(2,1)S(1)}, bf16[16,192]{0,1:T(8,128)(2,1)S(1)}, u32[]{:S(2)}, u32[]{:S(2)}) collective-permute-start(bf16[16,192]{0,1:T(8,128)(2,1)S(1)} %get-tuple-element.30), channel_id=1, source_target_pairs={{4,0},{8,4},{12,8},{5,1},{9,5},{13,9},{6,2},{10,6},{14,10},{7,3},{... | collective-permute-start | bytes 18440 | tf_op jit(solution)/shard_map/ppermute | solution.py:28
  91.7 8.1 %collective-permute-start.8 = (bf16[768,192]{0,1:T(8,128)(2,1)S(1)}, bf16[768,192]{0,1:T(8,128)(2,1)S(1)}, u32[]{:S(2)}, u32[]{:S(2)}) collective-permute-start(bf16[768,192]{0,1:T(8,128)(2,1)S(1)} %fusion.13), channel_id=1, source_target_pairs={{0,4},{4,0},{8,12},{12,8},{1,5},{5,1},{9,13},{13,9},{2,6},{6,2},{1... | collective-permute-start | bytes 884744 | tf_op jit(solution)/shard_map/ppermute | solution.py:36
  99.8 14.6 %collective-permute-start.9 = (bf16[768,192]{0,1:T(8,128)(2,1)S(1)}, bf16[768,192]{0,1:T(8,128)(2,1)S(1)}, u32[]{:S(2)}, u32[]{:S(2)}) collective-permute-start(bf16[768,192]{0,1:T(8,128)(2,1)S(1)} %collective-permute-done.8), channel_id=1, source_target_pairs={{0,8},{4,12},{8,0},{12,4},{1,9},{5,13},{9,1},{13,5},{2,10},{6,14},... | collective-permute-start | bytes 884744 | tf_op jit(solution)/shard_map/ppermute | solution.py:36
  114.4 1.6 collective-permute-start.10
  116.0 9.1 %collective-permute-start.11 = (bf16[768,192]{0,1:T(8,128)(2,1)S(1)}, bf16[768,192]{0,1:T(8,128)(2,1)S(1)}, u32[]{:S(2)}, u32[]{:S(2)}) collective-permute-start(bf16[768,192]{0,1:T(8,128)(2,1)S(1)} %collective-permute-done.10), channel_id=1, source_target_pairs={{0,2},{1,3},{2,0},{3,1},{4,6},{5,7},{6,4},{7,5},{8,10},{9,11},{10,... | collective-permute-start | bytes 884744 | tf_op jit(solution)/shard_map/ppermute | solution.py:36
  127.8 19.5 %copy-start.3 = (bf16[768,192]{0,1:T(8,128)(2,1)S(1)}, bf16[768,192]{0,1:T(8,128)(2,1)}, u32[]{:S(2)}) copy-start(bf16[768,192]{0,1:T(8,128)(2,1)} %param.7) | copy-start | bytes 884740
  127.9 47.2 %reduce-scatter.3.cloned.1.call-start = ((), (), s32[]{:S(2)}) async-start(), calls=%async_computation.4 | async-start | bytes 1474560 | tf_op jit(solution)/shard_map/reduce_scatter | solution.py:129
  149.2 107.0 %reduce-scatter.5.cloned.1.call-start = ((), (), s32[]{:S(2)}) async-start(), calls=%async_computation.6 | async-start | bytes 1474560 | tf_op jit(solution)/shard_map/reduce_scatter | solution.py:129
  175.1 9.0 %collective-permute-start.12 = (bf16[768,192]{0,1:T(8,128)(2,1)}, bf16[768,192]{0,1:T(8,128)(2,1)S(1)}, u32[]{:S(2)}, u32[]{:S(2)}) collective-permute-start(bf16[768,192]{0,1:T(8,128)(2,1)} %reduce-scatter.3.cloned.1.call-done), channel_id=1, source_target_pairs={{0,4},{4,0},{8,12},{12,8},{1,5},{5,1},{9,13},{13,9},{2,6},{6,2},{1... | collective-permute-start | bytes 884744 | tf_op jit(solution)/shard_map/ppermute | solution.py:36
  184.1 15.1 %collective-permute-start.13 = (bf16[768,192]{0,1:T(8,128)(2,1)S(1)}, bf16[768,192]{0,1:T(8,128)(2,1)S(1)}, u32[]{:S(2)}, u32[]{:S(2)}) collective-permute-start(bf16[768,192]{0,1:T(8,128)(2,1)S(1)} %collective-permute-done.12), channel_id=1, source_target_pairs={{0,8},{4,12},{8,0},{12,4},{1,9},{5,13},{9,1},{13,5},{2,10},{6,14},... | collective-permute-start | bytes 884744 | tf_op jit(solution)/shard_map/ppermute | solution.py:36
  199.2 1.6 collective-permute-start.14
  200.7 9.2 %collective-permute-start.15 = (bf16[768,192]{0,1:T(8,128)(2,1)S(1)}, bf16[768,192]{0,1:T(8,128)(2,1)}, u32[]{:S(2)}, u32[]{:S(2)}) collective-permute-start(bf16[768,192]{0,1:T(8,128)(2,1)S(1)} %collective-permute-done.14), channel_id=1, source_target_pairs={{0,2},{1,3},{2,0},{3,1},{4,6},{5,7},{6,4},{7,5},{8,10},{9,11},{10,... | collective-permute-start | bytes 884744 | tf_op jit(solution)/shard_map/ppermute | solution.py:36
  218.2 4.1 %collective-permute-start.16 = (bf16[16,192]{0,1:T(8,128)(2,1)S(1)}, bf16[16,192]{0,1:T(8,128)(2,1)S(1)}, u32[]{:S(2)}, u32[]{:S(2)}) collective-permute-start(bf16[16,192]{0,1:T(8,128)(2,1)S(1)} %get-tuple-element.27), channel_id=1, source_target_pairs={{0,4},{4,8},{8,12},{1,5},{5,9},{9,13},{2,6},{6,10},{10,14},{3,7},{... | collective-permute-start | bytes 18440 | tf_op jit(solution)/shard_map/ppermute | solution.py:26
  220.6 6.0 %collective-permute-start.17 = (bf16[16,192]{0,1:T(8,128)(2,1)S(1)}, bf16[16,192]{0,1:T(8,128)(2,1)S(1)}, u32[]{:S(2)}, u32[]{:S(2)}) collective-permute-start(bf16[16,192]{0,1:T(8,128)(2,1)S(1)} %get-tuple-element.28), channel_id=1, source_target_pairs={{4,0},{8,4},{12,8},{5,1},{9,5},{13,9},{6,2},{10,6},{14,10},{7,3},{... | collective-permute-start | bytes 18440 | tf_op jit(solution)/shard_map/ppermute | solution.py:28
  230.3 52.0 %copy-start = (bf16[768,768]{0,1:T(8,128)(2,1)S(1)}, bf16[768,768]{0,1:T(8,128)(2,1)}, u32[]{:S(2)}) copy-start(bf16[768,768]{0,1:T(8,128)(2,1)} %all-gather.3.cloned.1.call-done) | copy-start | bytes 3538948
  230.3 112.7 %all-reduce.3.cloned.1.call-start = ((), (), s32[]{:S(2)}) async-start(), calls=%async_computation.5 | async-start | bytes 2359296 | tf_op jit(solution)/shard_map/psum | solution.py:145
  256.2 9.0 %collective-permute-start.18 = (bf16[768,192]{0,1:T(8,128)(2,1)}, bf16[768,192]{0,1:T(8,128)(2,1)S(1)}, u32[]{:S(2)}, u32[]{:S(2)}) collective-permute-start(bf16[768,192]{0,1:T(8,128)(2,1)} %reduce-scatter.5.cloned.1.call-done), channel_id=1, source_target_pairs={{0,4},{4,0},{8,12},{12,8},{1,5},{5,1},{9,13},{13,9},{2,6},{6,2},{1... | collective-permute-start | bytes 884744 | tf_op jit(solution)/shard_map/ppermute | solution.py:36
  265.2 15.1 %collective-permute-start.19 = (bf16[768,192]{0,1:T(8,128)(2,1)S(1)}, bf16[768,192]{0,1:T(8,128)(2,1)S(1)}, u32[]{:S(2)}, u32[]{:S(2)}) collective-permute-start(bf16[768,192]{0,1:T(8,128)(2,1)S(1)} %collective-permute-done.18), channel_id=1, source_target_pairs={{0,8},{4,12},{8,0},{12,4},{1,9},{5,13},{9,1},{13,5},{2,10},{6,14},... | collective-permute-start | bytes 884744 | tf_op jit(solution)/shard_map/ppermute | solution.py:36
  280.3 2.6 collective-permute-start.20
  282.9 9.5 %collective-permute-start.21 = (bf16[768,192]{0,1:T(8,128)(2,1)S(1)}, bf16[768,192]{0,1:T(8,128)(2,1)S(1)}, u32[]{:S(2)}, u32[]{:S(2)}) collective-permute-start(bf16[768,192]{0,1:T(8,128)(2,1)S(1)} %collective-permute-done.20), channel_id=1, source_target_pairs={{0,2},{1,3},{2,0},{3,1},{4,6},{5,7},{6,4},{7,5},{8,10},{9,11},{10,... | collective-permute-start | bytes 884744 | tf_op jit(solution)/shard_map/ppermute | solution.py:36
  295.7 5.4 %collective-permute-start.22 = (bf16[16,192]{0,1:T(8,128)(2,1)S(1)}, bf16[16,192]{0,1:T(8,128)(2,1)S(1)}, u32[]{:S(2)}, u32[]{:S(2)}) collective-permute-start(bf16[16,192]{0,1:T(8,128)(2,1)S(1)} %get-tuple-element.24), channel_id=1, source_target_pairs={{0,4},{4,8},{8,12},{1,5},{5,9},{9,13},{2,6},{6,10},{10,14},{3,7},{... | collective-permute-start | bytes 18440 | tf_op jit(solution)/shard_map/ppermute | solution.py:26
  298.2 8.5 %collective-permute-start.23 = (bf16[16,192]{0,1:T(8,128)(2,1)S(1)}, bf16[16,192]{0,1:T(8,128)(2,1)S(1)}, u32[]{:S(2)}, u32[]{:S(2)}) collective-permute-start(bf16[16,192]{0,1:T(8,128)(2,1)S(1)} %get-tuple-element.25), channel_id=1, source_target_pairs={{4,0},{8,4},{12,8},{5,1},{9,5},{13,9},{6,2},{10,6},{14,10},{7,3},{... | collective-permute-start | bytes 18440 | tf_op jit(solution)/shard_map/ppermute | solution.py:28
  (3 other events, 32.4 us)
Sparse Core Ops, SparseCore 0:
  60.7 18.4 all-gather.2
  128.0 17.6 all-gather.4
  149.4 25.7 reduce-scatter.2
  230.4 25.7 reduce-scatter.4
  284.9 58.0 all-reduce.2
where the time goes:
time: 353 us; the launch traced here: 352 us
  waiting for transfers between devices  232 us (66%)
  starting transfers between devices  39.7 us (11%)
  between operations  20.6 us (6%)
  blocking collectives  18 us (5%)
  local copies, waits for them, and re-layouts  15.9 us (5%)
  other arithmetic  15.3 us (4%)
  matrix products  10.7 us (3%)
    ppermute x16, waiting for transfers between devices, partner_2(): lax.ppermute(shard, axis, [(i, i ^ 1 << stride) for i in range(lax.axis_s...  114 us
    reduce_scatter x2, waiting for transfers between devices, body(): lax.psum_scatter(partials.astype(jnp.bfloat16), 'chan', scatter_dimension...  51.5 us
    all_gather x2, waiting for transfers between devices, body(): lax.all_gather(mixed_local, 'chan', axis=1, tiled=True)  36.4 us
    ppermute x16, starting transfers between devices, partner_2(): lax.ppermute(shard, axis, [(i, i ^ 1 << stride) for i in range(lax.axis_s...  20.9 us
    psum x1, blocking collectives, body(): lax.psum((jnp.stack(mix_grads), jnp.stack(taps_grads), embed_grad), 'seq')  18 us
    psum x1, waiting for transfers between devices, body(): lax.psum((jnp.stack(mix_grads), jnp.stack(taps_grads), embed_grad), 'seq')  16.2 us
    ppermute x4, starting transfers between devices, with_halo(): lax.ppermute(tail, axis, [(i, (i + 1) % count) for i in range(ends)])  13.2 us
    ppermute x4, waiting for transfers between devices, with_halo(): lax.ppermute(head, axis, [((i + 1) % count, i) for i in range(ends)])  11.4 us
  transfers between devices with their start and end apart: 29, of which 25 were waited for; matrix products, arithmetic and copies ran while one was open for 3% of the time, Pallas kernels for 0%

commit v1 on v0

v1 whole, which is shorter than its diff:
```python
import functools
import math

import jax
import jax.numpy as jnp
from jax import lax
from jax.experimental import pallas as pl
from jax.experimental.pallas import tpu as pltpu
from jax.sharding import PartitionSpec as P

TAPS = 5
BASES = 4
BLOCKS = 2
DMAX = 8
HALF = TAPS // 2
REACH = HALF * DMAX
LANE = 128
JB = 32
GELU_SCALE = math.sqrt(2.0 / math.pi)
CUBIC = 0.044715
BF = jnp.bfloat16
F32 = jnp.float32
ROW_EMBED, ROW_TAPS0, ROW_TAPS1, TABLE = 0, BASES, BASES + TAPS, 16
ROW_GT0, ROW_GT1, ROW_GE, SUMS = 2 * JB, 2 * JB + 8, 2 * JB + 16, 2 * JB + 24


def dot(a, b, **kw):
    return jnp.dot(a, b, preferred_element_type=F32, **kw)


def dot_t(a, b):
    return lax.dot_general(a, b, (((1,), (1,)), ((), ())), preferred_element_type=F32)


def t_dot(a, b):
    return lax.dot_general(a, b, (((0,), (0,)), ((), ())), preferred_element_type=F32)


def iotas(shape):
    return lax.broadcasted_iota(jnp.int32, shape, 0), lax.broadcasted_iota(jnp.int32, shape, 1)


def as_bf(mask):
    return mask.astype(F32).astype(BF)


def reversal(size):
    row, col = iotas((size, size))
    return as_bf(row + col == size - 1)


def split_bf(x):
    high = x.astype(BF)
    return high, (x - high.astype(F32)).astype(BF)


def flip_exact(x, rev):
    high, rest = split_bf(x)
    mid, low = split_bf(rest.astype(F32))
    rest2 = (x - high.astype(F32) - mid.astype(F32)).astype(BF)
    del rest, low
    return dot(high, rev) + dot(mid, rev) + dot(rest2, rev)


def gelu_parts(v):
    square = v * v
    tangent = jnp.tanh(v * (GELU_SCALE + (GELU_SCALE * CUBIC) * square))
    half = 0.5 + 0.5 * tangent
    value = v * half
    slope = half + (v * (1.0 - tangent * tangent)) * (
        0.5 * GELU_SCALE + (1.5 * GELU_SCALE * CUBIC) * square
    )
    return value, slope


def select_rows(kind, rows):
    row, col = iotas((rows, TABLE))
    local = row % JB
    used = local < TAPS * BASES
    tap, letter = local // BASES, local % BASES
    want = {"tap0": ROW_TAPS0 + tap, "tap1": ROW_TAPS1 + tap, "letter": ROW_EMBED + letter}[kind]
    return as_bf(used & (col == want))


def one_hot_t(tokens):
    n = tokens.shape[1]
    row = lax.broadcasted_iota(jnp.int32, (2 * JB, n), 0)
    local = row % JB
    group = jnp.where(local < TAPS * BASES, local // BASES + TAPS * (row // JB), -1)
    seen = jnp.zeros((2 * JB, n), jnp.int32)
    for g in range(2 * TAPS):
        seen = jnp.where(group == g, jnp.broadcast_to(tokens[g : g + 1, :], (2 * JB, n)), seen)
    return (seen == local % BASES + 1).astype(F32)


def pair_table(pks, rev_w):
    sel_t, sel_e = select_rows("tap0", JB), select_rows("letter", JB)
    tables = [pk[0:TABLE, :] for pk in pks]
    plain = [dot(sel_t, t) * dot(sel_e, t) for t in tables]
    n = len(pks)
    out = []
    for k in range(n):
        high, low = split_bf(plain[k])
        fhigh, flow = split_bf(plain[n - 1 - k])
        out.append((high, dot(fhigh, rev_w).astype(BF), low, dot(flow, rev_w).astype(BF)))
    return out


def forward_kernel(
    n_chan, rows, width, scale,
    scal, tok, *refs,
):
    pks = refs[:n_chan]
    mix_ref, cot_ref = refs[n_chan : n_chan + 2]
    x2_ref, gm_ref, s_ref, x1_ref, gp_ref = refs[n_chan + 2 : n_chan + 7]
    w_ref, e_ref, wt_ref, et_ref, a_ref, m_ref, mixl_ref = refs[n_chan + 7 :]
    tiles = n_chan * width // LANE
    ext = rows + 2 * REACH
    me, dil = scal[0], scal[2]
    rev, rev_w = reversal(LANE), reversal(width)

    hot = one_hot_t(tok[...])
    a_ref[...] = jnp.concatenate([hot, hot], axis=0).T.astype(BF)

    stacks = [jnp.concatenate(p, axis=0) for p in pair_table(pks, rev_w)]
    starts = [pl.multiple_of(lax.bitwise_xor(me, k) * width, width) for k in range(n_chan)]
    for k in range(n_chan):
        total = jnp.zeros((4 * JB, width), F32)
        for kk in range(n_chan):
            total = total + dot(stacks[kk], pks[k][pl.ds(TABLE + starts[kk], width), :])
        high, low = split_bf(total[: 2 * JB] + total[2 * JB :])
        w_ref[:, k * width : (k + 1) * width] = jnp.concatenate([high, low], axis=0)
        e_ref[:, k * width : (k + 1) * width] = pks[k][0:TABLE, :]
        mixl_ref[k * width : (k + 1) * width, :] = mix_ref[pl.ds(starts[k], width), :]

    for t in range(tiles):
        src = slice((tiles - 1 - t) * LANE, (tiles - t) * LANE)
        dst = slice(t * LANE, (t + 1) * LANE)
        flipped = dot(w_ref[:, src], rev).astype(BF)
        wt_ref[:, dst] = jnp.concatenate(
            [flipped[JB : 2 * JB], flipped[:JB], flipped[3 * JB :], flipped[2 * JB : 3 * JB]], axis=0
        )
        et_ref[:, dst] = dot(e_ref[:, src], rev).astype(BF)

    row, col = iotas((4 * JB, TABLE))
    centre = HALF * BASES
    pick_f = as_bf((row - centre == col) & (col < BASES))
    pick_r = as_bf((row - centre - JB == col) & (col < BASES))
    chunk = ext // 5
    for t in range(tiles):
        dst = slice(t * LANE, (t + 1) * LANE)
        for strand, (wr, er, pick) in enumerate(((w_ref, e_ref, pick_f), (wt_ref, et_ref, pick_r))):
            rhs = jnp.concatenate([wr[:, dst], dot(pick, er[:, dst]).astype(BF)], axis=1)

            @pl.loop(0, 5)
            def _(i, t=t, strand=strand, rhs=rhs):
                where = pl.ds(pl.multiple_of(i * chunk, 16), chunk)
                both = dot(a_ref[where, :], rhs)
                value, slope = gelu_parts(both[:, :LANE])
                x1 = (both[:, LANE:] + value).astype(BF).astype(F32)
                x1_ref[strand, t, where, :] = x1
                gp_ref[strand, t, where, :] = slope.astype(BF)

    mchunk = rows // 6
    for t in range(tiles):
        dst = slice(t * LANE, (t + 1) * LANE)
        taps_f = e_ref[:, dst].astype(F32)
        taps_r = et_ref[:, dst].astype(F32)

        @pl.loop(0, 6)
        def _(i, t=t, dst=dst, taps_f=taps_f, taps_r=taps_r):
            first = i * mchunk
            u = jnp.zeros((mchunk, LANE), F32)
            v = jnp.zeros((mchunk, LANE), F32)
            for j in range(TAPS):
                shift = (j - HALF) * dil
                u += taps_f[ROW_TAPS1 + j : ROW_TAPS1 + j + 1, :] * x1_ref[0, t, pl.ds(first + REACH + shift, mchunk), :]
                v += taps_r[ROW_TAPS1 + j : ROW_TAPS1 + j + 1, :] * x1_ref[1, t, pl.ds(first + REACH - shift, mchunk), :]
            total = u.astype(BF).astype(F32) + v.astype(BF).astype(F32)
            m_ref[pl.ds(pl.multiple_of(first, 16), mchunk), dst] = total.astype(BF)

    @pl.loop(0, 6)
    def _(i):
        where = pl.ds(pl.multiple_of(i * mchunk, 16), mchunk)
        value, slope = gelu_parts(dot(m_ref[where, :], mixl_ref[...]))
        inner = pl.ds(pl.multiple_of(REACH + i * mchunk, 16), mchunk)
        n_own = pl.cdiv(width, LANE)
        own = jnp.concatenate([x1_ref[0, t, inner, :] for t in range(n_own)], axis=1)[:, :width]
        x2_ref[where, :] = (own + value).astype(BF)
        s_ref[where, :] = ((cot_ref[where, :].astype(F32) * scale) * slope).astype(BF)

    for k in range(n_chan):
        part = t_dot(m_ref[:, k * width : (k + 1) * width], s_ref[...])
        gm_ref[pl.ds(starts[k], width), :] = part.astype(BF)


def backward_kernel(
    n_chan, rows, width, scale,
    scal, tok, tok1, *refs,
):
    pks = refs[:n_chan]
    mix_ref, cot_ref, s_ref, x1_ref, gp_ref = refs[n_chan : n_chan + 5]
    out_ref = refs[n_chan + 5]
    p_ref, g2_ref, s0_ref, e_ref, et_ref, mixl_ref, dw_ref, gt_ref, g1_ref, pb_ref = refs[n_chan + 6 :]
    chans = n_chan * width
    tiles = chans // LANE
    ext = rows + 2 * REACH
    padded = tok.shape[1]
    me, dil = scal[0], scal[2]
    rev, rev_w = reversal(LANE), reversal(width)
    starts = [pl.multiple_of(lax.bitwise_xor(me, k) * width, width) for k in range(n_chan)]
    for k in range(n_chan):
        e_ref[:, k * width : (k + 1) * width] = pks[k][0:TABLE, :]
        mixl_ref[k * width : (k + 1) * width, :] = mix_ref[pl.ds(starts[k], width), :]
    for t in range(tiles):
        src = slice((tiles - 1 - t) * LANE, (tiles - t) * LANE)
        et_ref[:, t * LANE : (t + 1) * LANE] = dot(e_ref[:, src], rev).astype(BF)

    edge = 2 * REACH
    n_own = pl.cdiv(width, LANE)
    g2 = cot_ref[...].astype(F32) * scale
    g2_ref[:, :REACH, :] = jnp.zeros((n_own, REACH, LANE), F32)
    g2_ref[:, rows + REACH :, :] = jnp.zeros((n_own, REACH, LANE), F32)
    g2 = jnp.concatenate([g2, jnp.zeros((rows, n_own * LANE - width), F32)], axis=1)
    for t in range(n_own):
        g2_ref[t, REACH : rows + REACH, :] = g2[:, t * LANE : (t + 1) * LANE]
    s0_ref[:, ext:, :] = jnp.zeros((2, padded - ext, chans), BF)
    for t in range(tiles):
        p_ref[t, :edge, :] = jnp.zeros((edge, LANE), F32)
        p_ref[t, rows + edge :, :] = jnp.zeros((edge, LANE), F32)
        part = dot_t(s_ref[...], mixl_ref[t * LANE : (t + 1) * LANE, :])
        p_ref[t, edge : rows + edge, :] = part
        pb_ref[:, t * LANE : (t + 1) * LANE] = part.astype(BF)

    mchunk, chunk = rows // 6, ext // 5
    for t in range(tiles):
        dst = slice(t * LANE, (t + 1) * LANE)
        taps_f = e_ref[:, dst].astype(F32)
        taps_r = et_ref[:, dst].astype(F32)

        @pl.loop(0, 5)
        def _(i, t=t, dst=dst, taps_f=taps_f, taps_r=taps_r):
            first = i * chunk
            where = pl.ds(pl.multiple_of(first, 16), chunk)
            f = jnp.zeros((chunk, LANE), F32)
            r = jnp.zeros((chunk, LANE), F32)
            for j in range(TAPS):
                shift = (j - HALF) * dil
                tap_f = taps_f[ROW_TAPS1 + j : ROW_TAPS1 + j + 1, :]
                tap_r = taps_r[ROW_TAPS1 + j : ROW_TAPS1 + j + 1, :]
                f += tap_f * p_ref[t, pl.ds(first + REACH - shift, chunk), :]
                r += tap_r * p_ref[t, pl.ds(first + REACH + shift, chunk), :]
            if t < n_own:
                f += g2_ref[t, where, :]
            s0_ref[0, where, dst] = (f * gp_ref[0, t, where, :].astype(F32)).astype(BF)
            s0_ref[1, where, dst] = (r * gp_ref[1, t, where, :].astype(F32)).astype(BF)

        def taps_step(i, carry, t=t):
            first = i * mchunk
            here = p_ref[t, pl.ds(pl.multiple_of(edge + first, 16), mchunk), :]
            out = []
            for strand in range(2):
                for j in range(TAPS):
                    shift = (j - HALF) * dil * (1 - 2 * strand)
                    prod = here * x1_ref[strand, t, pl.ds(first + REACH + shift, mchunk), :]
                    out.append(carry[strand * TAPS + j] + prod.reshape(mchunk // 8, 8, LANE).sum(0))
            return tuple(out)

        sums = lax.fori_loop(0, 6, taps_step, tuple(jnp.zeros((8, LANE), F32) for _ in range(2 * TAPS)))
        for strand in range(2):
            rows_t = [jnp.sum(sums[strand * TAPS + j], axis=0, keepdims=True) for j in range(TAPS)]
            gt_ref[strand, :, dst] = jnp.concatenate(rows_t + [jnp.zeros((8 - TAPS, LANE), F32)], axis=0)

    hot = one_hot_t(tok[...]).astype(BF)
    hot1 = one_hot_t(tok1[...]).astype(BF)
    dw_ref[...] = dot(hot, s0_ref[0])
    other = dot(hot, s0_ref[1])
    by_tap = dot(hot1, pb_ref[...])
    own_letters = dot(hot1[: 16, :], cot_ref[...]) * scale
    srow, scol = iotas((8, JB))
    sum_letter = as_bf((scol % BASES == srow) & (scol < TAPS * BASES))
    sum_tap = as_bf((scol // BASES == srow) & (scol < TAPS * BASES))

    def sums_of(sel, x):
        high, rest = split_bf(x)
        return dot(sel, high) + dot(sel, rest)

    sel1 = select_rows("tap1", JB)
    g1_other = []
    for t in range(tiles):
        dst = slice(t * LANE, (t + 1) * LANE)
        g1_ref[:, dst] = sums_of(sum_letter, by_tap[:JB, dst] * dot(sel1, e_ref[:, dst]))
        g1_other.append(sums_of(sum_letter, by_tap[JB:, dst] * dot(sel1, et_ref[:, dst])))
    for t in range(tiles):
        dst = slice(t * LANE, (t + 1) * LANE)
        src = slice((tiles - 1 - t) * LANE, (tiles - t) * LANE)
        flipped = flip_exact(other[:, src], rev)
        dw_ref[:, dst] += jnp.concatenate([flipped[JB:], flipped[:JB]], axis=0)
        g1_ref[:, dst] += flip_exact(g1_other[tiles - 1 - t], rev)
        gt_ref[0, :, dst] += flip_exact(gt_ref[1, :, src], rev)

    sel_t, sel_e = select_rows("tap0", JB), select_rows("letter", JB)
    grads = []
    for kk in range(n_chan):
        total = jnp.zeros((2 * JB, width), F32)
        for k in range(n_chan):
            part = dw_ref[:, k * width : (k + 1) * width].astype(BF)
            total = total + dot_t(part, pks[k][pl.ds(TABLE + starts[kk], width), :])
        grads.append(total)
    for kk in range(n_chan):
        both = grads[kk][:JB] + flip_exact(grads[n_chan - 1 - kk][JB:], rev_w)
        table = pks[kk][0:TABLE, :]
        lanes = slice(kk * width, (kk + 1) * width)
        out_ref[kk, : 2 * JB, :] = dw_ref[:, lanes]
        out_ref[kk, ROW_GT0 : ROW_GT0 + 8, :] = sums_of(sum_tap, both * dot(sel_e, table))
        out_ref[kk, ROW_GT1 : ROW_GT1 + 8, :] = gt_ref[0, :, lanes]
        letters = sums_of(sum_letter, both * dot(sel_t, table)) + g1_ref[:, lanes]
        if kk == 0:
            zeros = jnp.zeros((BASES, width), F32)
            own = own_letters[HALF * BASES : (HALF + 1) * BASES, :]
            letters = letters + jnp.concatenate([own, zeros], axis=0)
        out_ref[kk, ROW_GE : ROW_GE + 8, :] = letters


def finish_kernel(n_chan, width, scal, *refs):
    pks = refs[:n_chan]
    sa_ref, sb_ref, ga_ref, gb_ref = refs[n_chan : n_chan + 4]
    gm_ref, gt_ref, ge_ref = refs[n_chan + 4 :]
    me = scal[0]
    rev_w = reversal(width)
    sums = sa_ref[...] + sb_ref[...]
    dw = sums[: 2 * JB].astype(BF)
    for k, (high, fhigh, _, _) in enumerate(pair_table(pks, rev_w)):
        start = pl.multiple_of(lax.bitwise_xor(me, k) * width, width)
        gm_ref[0, pl.ds(start, width), :] = t_dot(jnp.concatenate([high, fhigh], axis=0), dw)
    gm_ref[1] = ga_ref[...].astype(F32) + gb_ref[...].astype(F32)
    gt_ref[0] = sums[ROW_GT0 : ROW_GT0 + TAPS]
    gt_ref[1] = sums[ROW_GT1 : ROW_GT1 + TAPS]
    ge_ref[...] = sums[ROW_GE : ROW_GE + BASES]


def call(kernel, n_in, out_shape, scratch, limit):
    vmem = pl.BlockSpec(memory_space=pltpu.VMEM)
    return pl.pallas_call(
        kernel,
        out_shape=out_shape,
        in_specs=[pl.BlockSpec(memory_space=pltpu.SMEM)] + [vmem] * n_in,
        out_specs=[vmem] * len(out_shape),
        scratch_shapes=scratch,
        compiler_params=pltpu.CompilerParams(vmem_limit_bytes=limit),
    )


def flip_bits(x, axis, mask):
    return lax.ppermute(x, axis, [(i, i ^ mask) for i in range(lax.axis_size(axis))])


def body(tokens, cotangent, embed, taps, mix, dilations):
    rows, width = cotangent.shape
    n_seq, n_chan = lax.axis_size("seq"), lax.axis_size("chan")
    chans = n_chan * width
    tiles = chans // LANE
    ext = rows + 2 * REACH
    padded = pl.cdiv(ext, LANE) * LANE
    edge = 2 * REACH
    scale = 1.0 / math.sqrt(rows * n_seq)
    scal = jnp.concatenate([lax.axis_index("chan").astype(jnp.int32)[None], dilations])

    pk = jnp.concatenate(
        [embed, taps[0], taps[1], jnp.zeros((TABLE - BASES - 2 * TAPS, width), BF), mix[0]], axis=0
    )
    pks = [pk]
    bits = n_chan.bit_length() - 1
    for bit in reversed(range(bits)):
        moved = [flip_bits(p, "chan", 1 << bit) for p in pks]
        pks = [q for pair in zip(pks, moved) for q in pair]

    shifted = tokens + 1
    before = lax.ppermute(shifted[rows - edge :], "seq", [(i, i + 1) for i in range(n_seq - 1)])
    after = lax.ppermute(shifted[:edge], "seq", [(i + 1, i) for i in range(n_seq - 1)])
    wide = jnp.concatenate([before, shifted, after])
    other = lax.ppermute(wide, "seq", [(i, n_seq - 1 - i) for i in range(n_seq)])[::-1]

    def windows(dilation, margin, count, total):
        out = []
        for strand, source in ((1, wide), (-1, other)):
            for j in range(TAPS):
                first = margin + strand * (j - HALF) * dilation
                out.append(lax.dynamic_slice_in_dim(source, first, count, 0))
        table = jnp.stack(out)
        table = jnp.where(table[HALF : HALF + 1] == 0, 0, table)
        return jnp.pad(table, ((0, 0), (0, total - count)))

    tok0 = windows(dilations[0], REACH, ext, padded)
    tok1 = windows(dilations[1], edge, rows, rows)

    shape = jax.ShapeDtypeStruct
    x2, gm1, s1, x1, gp = call(
        functools.partial(forward_kernel, n_chan, rows, width, scale),
        1 + n_chan + 2,
        [
            shape((rows, width), BF),
            shape((chans, width), BF),
            shape((rows, width), BF),
            shape((2, tiles, ext, LANE), F32),
            shape((2, tiles, ext, LANE), BF),
        ],
        [
            pltpu.VMEM((4 * JB, chans), BF),
            pltpu.VMEM((TABLE, chans), BF),
            pltpu.VMEM((4 * JB, chans), BF),
            pltpu.VMEM((TABLE, chans), BF),
            pltpu.VMEM((padded, 4 * JB), BF),
            pltpu.VMEM((rows, chans), BF),
            pltpu.VMEM((chans, width), BF),
        ],
        32 << 20,
    )(scal, tok0, *pks, mix[1], cotangent)

    (sums,) = call(
        functools.partial(backward_kernel, n_chan, rows, width, scale),
        2 + n_chan + 5,
        [shape((n_chan, SUMS, width), F32)],
        [
            pltpu.VMEM((tiles, rows + 2 * edge, LANE), F32),
            pltpu.VMEM((pl.cdiv(width, LANE), ext, LANE), F32),
            pltpu.VMEM((2, padded, chans), BF),
            pltpu.VMEM((TABLE, chans), BF),
            pltpu.VMEM((TABLE, chans), BF),
            pltpu.VMEM((chans, width), BF),
            pltpu.VMEM((2 * JB, chans), F32),
            pltpu.VMEM((2, 8, chans), F32),
            pltpu.VMEM((8, chans), F32),
            pltpu.VMEM((rows, chans), BF),
        ],
        40 << 20,
    )(scal, tok0, tok1, *pks, mix[1], cotangent, s1, x1, gp)

    g_mine = gm1
    seq_bits = n_seq.bit_length() - 1
    for bit in range(seq_bits):
        g_other = flip_bits(g_mine, "seq", 1 << bit)
        if bit < seq_bits - 1:
            g_mine = lax.optimization_barrier(
                (g_mine.astype(F32) + g_other.astype(F32)).astype(BF)
            )
    pieces = [sums[0]] + [flip_bits(sums[k], "chan", k) for k in range(1, n_chan)]
    s_mine = functools.reduce(jnp.add, pieces)
    for bit in range(seq_bits):
        s_other = flip_bits(s_mine, "seq", 1 << bit)
        if bit < seq_bits - 1:
            s_mine = s_mine + s_other

    grad_mix, grad_taps, grad_embed = call(
        functools.partial(finish_kernel, n_chan, width),
        n_chan + 4,
        [
            shape((BLOCKS, chans, width), F32),
            shape((BLOCKS, TAPS, width), F32),
            shape((BASES, width), F32),
        ],
        [],
        32 << 20,
    )(scal, *[p[:TABLE] for p in pks], s_mine, s_other, g_mine, g_other)
    return x2, grad_mix, grad_taps, grad_embed


def solution(mesh):
    in_specs = (
        P(("groups", "seq")),
        P(("groups", "seq"), "chan"),
        P(None, "chan"),
        P(None, None, "chan"),
        P(None, None, "chan"),
        P(),
    )
    out_specs = (
        P(("groups", "seq"), "chan"),
        P("groups", None, "chan"),
        P("groups", None, "chan"),
        P("groups", "chan"),
    )
    return jax.shard_map(body, mesh=mesh, in_specs=in_specs, out_specs=out_specs, check_vma=False)
```

time: 353 us -> 90.2 us (0.26)
  waiting for transfers between devices: 232 us -> 21.2 us
  Pallas kernels: 0 us -> 32.4 us
  starting transfers between devices: 39.7 us -> 19.9 us
  blocking collectives: 18 us -> 0 us
  other arithmetic: 15.3 us -> 0.41 us
  between operations: 20.6 us -> 7.5 us
  matrix products: 10.7 us -> 0 us
  local copies, waits for them, and re-layouts: 15.9 us -> 8.07 us
    ppermute x24 -> x13, waiting for transfers between devices: 128 us -> 21.2 us  [the longest x10 17.5 us: flip_bits(): lax.ppermute(x, axis, [(i, i ^ mask) for i in range(lax.axis_size(axis))])]
    reduce_scatter x2 -> x0, waiting for transfers between devices: 51.5 us -> none  [body(): lax.psum_scatter(partials.astype(jnp.bfloat16), 'chan', scatter_dimension...]
    all_gather x2 -> x0, waiting for transfers between devices: 36.4 us -> none  [body(): lax.all_gather(mixed_local, 'chan', axis=1, tiled=True)]
    pallas_call x0 -> x3, Pallas kernels: none -> 32.4 us  [the longest x1 19.9 us: body(): call(functools.partial(forward_kernel, n_chan, rows, width, scale), 1 + n...]
    ppermute x24 -> x13, starting transfers between devices: 39.3 us -> 19.9 us  [the longest x10 12.7 us: flip_bits(): lax.ppermute(x, axis, [(i, i ^ mask) for i in range(lax.axis_size(axis))])]
    psum x1 -> x0, blocking collectives: 18 us -> none  [body(): lax.psum((jnp.stack(mix_grads), jnp.stack(taps_grads), embed_grad), 'seq')]
    psum x1 -> x0, waiting for transfers between devices: 16.2 us -> none  [body(): lax.psum((jnp.stack(mix_grads), jnp.stack(taps_grads), embed_grad), 'seq')]
    rev x4 -> x0, local copies, waits for them, and re-layouts: 11.2 us -> none  [mirrored(): result = moved[::-1, ::-1]]
  transfers between devices with their start and end apart: 29 -> 13, of which waited for: 25 -> 6; matrix products, arithmetic and copies ran while one was open for 3% -> 4% of each run, Pallas kernels for 0% -> 12%
where the time goes in v1:
time: 90.2 us; the launch traced here: 89.5 us
  Pallas kernels  32.4 us (36%)
  waiting for transfers between devices  21.2 us (24%)
  starting transfers between devices  19.9 us (22%)
  local copies, waits for them, and re-layouts  8.07 us (9%)
  between operations  7.5 us (8%)
    pallas_call x1, Pallas kernels, body(): call(functools.partial(forward_kernel, n_chan, rows, width, scale), 1 + n...  19.9 us
    ppermute x10, waiting for transfers between devices, flip_bits(): lax.ppermute(x, axis, [(i, i ^ mask) for i in range(lax.axis_size(axis))])  17.5 us
    ppermute x10, starting transfers between devices, flip_bits(): lax.ppermute(x, axis, [(i, i ^ mask) for i in range(lax.axis_size(axis))])  12.7 us
    pallas_call x1, Pallas kernels, body(): call(functools.partial(backward_kernel, n_chan, rows, width, scale), 2 +...  10.7 us
    ppermute x1, starting transfers between devices, body(): lax.ppermute(shifted[rows - edge:], 'seq', [(i, i + 1) for i in range(n_s...  4.55 us
    unnamed x18, local copies, waits for them, and re-layouts  3.79 us
    ppermute x1, waiting for transfers between devices, body(): lax.ppermute(wide, 'seq', [(i, n_seq - 1 - i) for i in range(n_seq)])[::-1]  3.66 us
    pallas_call x1, Pallas kernels, body(): call(functools.partial(finish_kernel, n_chan, width), n_chan + 4, [shape(...  1.82 us
  transfers between devices with their start and end apart: 13, of which 6 were waited for; matrix products, arithmetic and copies ran while one was open for 4% of the time, Pallas kernels for 12%

profile of v1, /device:TPU:0, one launch (start us, length us, event | category | flops | bytes accessed | tf_op | source)
XLA Modules:
  0.0 89.5 jit_solution(17287117251974756784)
XLA Ops:
  0.7 0.8 fusion.4
  1.4 1.1 %fusion.3 = (bf16[1,768,192]{1,2,0:T(8,128)(2,1)S(1)}, bf16[1,768,192]{1,2,0:T(8,128)(2,1)S(1)}) fusion(bf16[2,768,192]{1,2,0:T(8,128)(2,1)} %param.10), kind=kLoop, calls=%fused_computation.18 | loop fusion | bytes 1179648 | tf_op jit(solution)/shard_map/slice | solution.py:418
  2.5 0.2 copy.21
  2.7 0.9 concatenate.14.refs_0_
  3.6 0.5 collective-permute-start.3
  4.2 2.6 %collective-permute-start.4 = (bf16[784,192]{1,0:T(8,128)(2,1)S(1)}, bf16[784,192]{1,0:T(8,128)(2,1)S(1)}, u32[]{:S(2)}, u32[]{:S(2)}) collective-permute-start(bf16[784,192]{1,0:T(8,128)(2,1)S(1)} %concatenate.14.refs_0_), channel_id=1, source_target_pairs={{0,2},{1,3},{2,0},{3,1},{4,6},{5,7},{6,4},{7,5},{8,10},{9,11},{10,... | collective-permute-start | bytes 903176 | tf_op jit(solution)/shard_map/ppermute | solution.py:355
  6.8 1.3 %collective-permute-start.1 = (s32[32]{0:T(128)S(1)}, s32[32]{0:T(128)S(1)}, u32[]{:S(2)}, u32[]{:S(2)}) collective-permute-start(s32[32]{0:T(128)S(1)} %get-tuple-element.49), channel_id=1, source_target_pairs={{4,0},{8,4},{12,8},{5,1},{9,5},{13,9},{6,2},{10,6},{14,10},{7,3},{... | collective-permute-start | bytes 392 | tf_op jit(solution)/shard_map/ppermute | solution.py:380
  8.1 4.5 %collective-permute-start = (s32[32]{0:T(128)S(1)}, s32[32]{0:T(128)S(1)}, u32[]{:S(2)}, u32[]{:S(2)}) collective-permute-start(s32[32]{0:T(128)S(1)} %get-tuple-element.48), channel_id=1, source_target_pairs={{0,4},{4,8},{8,12},{1,5},{5,9},{9,13},{2,6},{6,10},{10,14},{3,7},{... | collective-permute-start | bytes 392 | tf_op jit(solution)/shard_map/ppermute | solution.py:379
  12.7 0.6 fusion.10
  19.8 0.2 copy.22
  20.0 0.2 copy.14.refs_5_
  20.3 1.4 %collective-permute-start.2 = (s32[832]{0:T(1024)S(1)}, s32[832]{0:T(1024)S(1)}, u32[]{:S(2)}, u32[]{:S(2)}) collective-permute-start(s32[832]{0:T(1024)S(1)} %pad_add_fusion), channel_id=1, source_target_pairs={{0,12},{4,8},{8,4},{12,0},{1,13},{5,9},{9,5},{13,1},{2,14},{6,10},... | collective-permute-start | bytes 9992 | tf_op jit(solution)/shard_map/ppermute | solution.py:382
  22.1 3.7 %collective-permute-done.2 = s32[832]{0:T(1024)S(1)} collective-permute-done((s32[832]{0:T(1024)S(1)}, s32[832]{0:T(1024)S(1)}, u32[]{:S(2)}, u32[]{:S(2)}) %collective-permute-start.2) | collective-permute-done | bytes 3360 | tf_op jit(solution)/shard_map/ppermute | solution.py:382
  26.5 0.1 fusion.5
  26.6 0.1 dynamic_slice.79
  26.8 1.3 %collective-permute-done.5.refs_3_ = bf16[784,192]{1,0:T(8,128)(2,1)S(1)} collective-permute-done((bf16[784,192]{1,0:T(8,128)(2,1)S(1)}, bf16[784,192]{1,0:T(8,128)(2,1)S(1)}, u32[]{:S(2)}, u32[]{:S(2)}) %collective-permute-start.5) | collective-permute-done | bytes 301088 | tf_op jit(solution)/shard_map/ppermute | solution.py:355
  28.1 19.9 %shard_map.93 = (bf16[768,192]{1,0:T(8,128)(2,1)S(1)}, bf16[768,192]{1,0:T(8,128)(2,1)S(1)}, bf16[768,192]{1,0:T(8,128)(2,1)S(1)}, f32[2,6,800,128]{3,2,1,0:T(8,128)S(1)}, bf16[2,6,800,128]{3,2,1,0:T(8,128)(2,1)S(1)}) custom-call(s32[3]{0:T(128)S(1)} %pad_add_fusion.1.scal, s32[10,896]{1,0:T(8,128)S(1)} %pad.4.tok, ...), custom_call_target="tpu_custom_call" | custom-call | tf_op jit(solution)/shard_map/pallas_call | solution.py:398
  48.2 10.7 %shard_map.94 = f32[4,88,192]{2,1,0:T(8,128)S(1)} custom-call(s32[3]{0:T(128)S(1)} %pad_add_fusion.1.scal, s32[10,896]{1,0:T(8,128)S(1)} %pad.4.tok, s32[10,768]{1,0:T(8,128)S(1)} %broadcast_select_fusion.1.tok1, bf16[784,192]{1,0:T(8,128)(2,1)S(1)} %concatenate.14.refs_0_, bf16[784,192]{1,0:T(8,128)(2,1)S(1)} %collective-permute-done.3.refs_1_, ...), custom_call_target="tpu_custom_call" | custom-call | tf_op jit(solution)/shard_map/pallas_call | solution.py:420
  59.0 1.7 %collective-permute-start.7 = (f32[88,192]{1,0:T(8,128)S(1)}, f32[88,192]{1,0:T(8,128)S(1)}, u32[]{:S(2)}, u32[]{:S(2)}) collective-permute-start(f32[88,192]{1,0:T(8,128)S(1)} %get-tuple-element.28), channel_id=1, source_target_pairs={{0,2},{1,3},{2,0},{3,1},{4,6},{5,7},{6,4},{7,5},{8,10},{9,11},{10,... | collective-permute-start | bytes 202760 | tf_op jit(solution)/shard_map/ppermute | solution.py:355
  60.7 0.1 collective-permute-start.6
  60.9 0.1 add_convert_fusion.refs_6_
  61.0 1.9 %collective-permute-start.12 = (bf16[768,192]{1,0:T(8,128)(2,1)S(1)}, bf16[768,192]{1,0:T(8,128)(2,1)S(1)}, u32[]{:S(2)}, u32[]{:S(2)}) collective-permute-start(bf16[768,192]{1,0:T(8,128)(2,1)S(1)} %add_convert_fusion.refs_6_), channel_id=1, source_target_pairs={{0,8},{4,12},{8,0},{12,4},{1,9},{5,13},{9,1},{13,5},{2,10},{6,14},... | collective-permute-start | bytes 884744 | tf_op jit(solution)/shard_map/ppermute | solution.py:355
  62.9 0.7 collective-permute-done.8
  63.6 2.2 %collective-permute-done.7 = f32[88,192]{1,0:T(8,128)S(1)} collective-permute-done((f32[88,192]{1,0:T(8,128)S(1)}, f32[88,192]{1,0:T(8,128)S(1)}, u32[]{:S(2)}, u32[]{:S(2)}) %collective-permute-start.7) | collective-permute-done | bytes 67616 | tf_op jit(solution)/shard_map/ppermute | solution.py:355
  65.9 2.0 %collective-permute-start.9 = (f32[88,192]{1,0:T(8,128)S(1)}, f32[88,192]{1,0:T(8,128)S(1)}, u32[]{:S(2)}, u32[]{:S(2)}) collective-permute-start(f32[88,192]{1,0:T(8,128)S(1)} %fusion.2), channel_id=1, source_target_pairs={{0,4},{4,0},{8,12},{12,8},{1,5},{5,1},{9,13},{13,9},{2,6},{6,2},{1... | collective-permute-start | bytes 202760 | tf_op jit(solution)/shard_map/ppermute | solution.py:355
  67.9 5.7 %collective-permute-done.9 = f32[88,192]{1,0:T(8,128)S(1)} collective-permute-done((f32[88,192]{1,0:T(8,128)S(1)}, f32[88,192]{1,0:T(8,128)S(1)}, u32[]{:S(2)}, u32[]{:S(2)}) %collective-permute-start.9) | collective-permute-done | bytes 67616 | tf_op jit(solution)/shard_map/ppermute | solution.py:355
  73.6 3.5 %collective-permute-start.10 = (f32[88,192]{1,0:T(8,128)S(1)}, f32[88,192]{1,0:T(8,128)S(1)}, u32[]{:S(2)}, u32[]{:S(2)}) collective-permute-start(f32[88,192]{1,0:T(8,128)S(1)} %add.188.refs_4_), channel_id=1, source_target_pairs={{0,8},{4,12},{8,0},{12,4},{1,9},{5,13},{9,1},{13,5},{2,10},{6,14},... | collective-permute-start | bytes 202760 | tf_op jit(solution)/shard_map/ppermute | solution.py:355
  77.1 0.9 copy.16
  78.0 7.6 %collective-permute-done.10.refs_5_ = f32[88,192]{1,0:T(8,128)S(1)} collective-permute-done((f32[88,192]{1,0:T(8,128)S(1)}, f32[88,192]{1,0:T(8,128)S(1)}, u32[]{:S(2)}, u32[]{:S(2)}) %collective-permute-start.10) | collective-permute-done | bytes 67616 | tf_op jit(solution)/shard_map/ppermute | solution.py:355
  85.6 1.8 %shard_map.95 = (f32[2,768,192]{2,1,0:T(8,128)S(1)}, f32[2,5,192]{2,1,0:T(8,128)S(1)}, f32[4,192]{1,0:T(4,128)}) custom-call(s32[3]{0:T(128)S(1)} %pad_add_fusion.1.scal, bf16[16,192]{1,0:T(8,128)(2,1)S(1)} %pad_maximum_fusion.refs_0_, bf16[16,192]{1,0:T(8,128)(2,1)S(1)} %slice.65.refs_1_, bf16[16,192]{1,0:T(8,128)(2,1)S(1)} %slice.66.refs_2_, ...), custom_call_target="tpu_custom_call" | custom-call | tf_op jit(solution)/shard_map/pallas_call | solution.py:454
  87.5 1.5 %copy.17 = f32[2,768,192]{1,2,0:T(8,128)} copy(f32[2,768,192]{2,1,0:T(8,128)S(1)} %get-tuple-element.21) | data formatting | bytes 2359296
  88.9 0.6 copy.18
  (67 shorter events, 1.6 us)
Async XLA Ops:
  0.6 6.1 %copy-start.1 = (s32[768]{0:T(1024)S(1)}, s32[768]{0:T(1024)}, u32[]{:S(2)}) copy-start(s32[768]{0:T(1024)} %param.6) | copy-start | bytes 9220
  0.6 12.0 %copy-start.3 = (s32[2]{0:T(128)S(1)}, s32[2]{0:T(128)}, u32[]{:S(2)}) copy-start(s32[2]{0:T(128)} %param.11) | copy-start | bytes 28
  0.7 19.3 %copy-start = (bf16[768,192]{0,1:T(8,128)(2,1)S(1)}, bf16[768,192]{0,1:T(8,128)(2,1)}, u32[]{:S(2)}) copy-start(bf16[768,192]{0,1:T(8,128)(2,1)} %param.7) | copy-start | bytes 884740
  3.6 23.2 %collective-permute-start.3 = (bf16[784,192]{1,0:T(8,128)(2,1)S(1)}, bf16[784,192]{1,0:T(8,128)(2,1)S(1)}, u32[]{:S(2)}, u32[]{:S(2)}) collective-permute-start(bf16[784,192]{1,0:T(8,128)(2,1)S(1)} %concatenate.14.refs_0_), channel_id=1, source_target_pairs={{0,1},{1,0},{2,3},{3,2},{4,5},{5,4},{6,7},{7,6},{8,9},{9,8},{10,11... | collective-permute-start | bytes 903176 | tf_op jit(solution)/shard_map/ppermute | solution.py:355
  4.2 22.2 %collective-permute-start.4 = (bf16[784,192]{1,0:T(8,128)(2,1)S(1)}, bf16[784,192]{1,0:T(8,128)(2,1)S(1)}, u32[]{:S(2)}, u32[]{:S(2)}) collective-permute-start(bf16[784,192]{1,0:T(8,128)(2,1)S(1)} %concatenate.14.refs_0_), channel_id=1, source_target_pairs={{0,2},{1,3},{2,0},{3,1},{4,6},{5,7},{6,4},{7,5},{8,10},{9,11},{10,... | collective-permute-start | bytes 903176 | tf_op jit(solution)/shard_map/ppermute | solution.py:355
  6.8 13.4 %collective-permute-start.1 = (s32[32]{0:T(128)S(1)}, s32[32]{0:T(128)S(1)}, u32[]{:S(2)}, u32[]{:S(2)}) collective-permute-start(s32[32]{0:T(128)S(1)} %get-tuple-element.49), channel_id=1, source_target_pairs={{4,0},{8,4},{12,8},{5,1},{9,5},{13,9},{6,2},{10,6},{14,10},{7,3},{... | collective-permute-start | bytes 392 | tf_op jit(solution)/shard_map/ppermute | solution.py:380
  8.1 12.2 %collective-permute-start = (s32[32]{0:T(128)S(1)}, s32[32]{0:T(128)S(1)}, u32[]{:S(2)}, u32[]{:S(2)}) collective-permute-start(s32[32]{0:T(128)S(1)} %get-tuple-element.48), channel_id=1, source_target_pairs={{0,4},{4,8},{8,12},{1,5},{5,9},{9,13},{2,6},{6,10},{10,14},{3,7},{... | collective-permute-start | bytes 392 | tf_op jit(solution)/shard_map/ppermute | solution.py:379
  20.3 5.4 %collective-permute-start.2 = (s32[832]{0:T(1024)S(1)}, s32[832]{0:T(1024)S(1)}, u32[]{:S(2)}, u32[]{:S(2)}) collective-permute-start(s32[832]{0:T(1024)S(1)} %pad_add_fusion), channel_id=1, source_target_pairs={{0,12},{4,8},{8,4},{12,0},{1,13},{5,9},{9,5},{13,1},{2,14},{6,10},... | collective-permute-start | bytes 9992 | tf_op jit(solution)/shard_map/ppermute | solution.py:382
  26.3 1.8 %collective-permute-start.5 = (bf16[784,192]{1,0:T(8,128)(2,1)S(1)}, bf16[784,192]{1,0:T(8,128)(2,1)S(1)}, u32[]{:S(2)}, u32[]{:S(2)}) collective-permute-start(bf16[784,192]{1,0:T(8,128)(2,1)S(1)} %collective-permute-done.4.refs_2_), channel_id=1, source_target_pairs={{0,1},{1,0},{2,3},{3,2},{4,5},{5,4},{6,7},{7,6},{8,9},{9,8},{10,11... | collective-permute-start | bytes 903176 | tf_op jit(solution)/shard_map/ppermute | solution.py:355
  48.1 12.8 %collective-permute-start.11 = (bf16[768,192]{1,0:T(8,128)(2,1)S(1)}, bf16[768,192]{1,0:T(8,128)(2,1)S(1)}, u32[]{:S(2)}, u32[]{:S(2)}) collective-permute-start(bf16[768,192]{1,0:T(8,128)(2,1)S(1)} %get-tuple-element.16), channel_id=1, source_target_pairs={{0,4},{4,0},{8,12},{12,8},{1,5},{5,1},{9,13},{13,9},{2,6},{6,2},{1... | collective-permute-start | bytes 884744 | tf_op jit(solution)/shard_map/ppermute | solution.py:355
  48.2 29.0 %copy-start.2 = (bf16[4,192]{1,0:T(4,128)(2,1)S(1)}, bf16[4,192]{1,0:T(4,128)(2,1)}, u32[]{:S(2)}) copy-start(bf16[4,192]{1,0:T(4,128)(2,1)} %param.8) | copy-start | bytes 4612
  58.9 4.7 %collective-permute-start.8 = (f32[88,192]{1,0:T(8,128)S(1)}, f32[88,192]{1,0:T(8,128)S(1)}, u32[]{:S(2)}, u32[]{:S(2)}) collective-permute-start(f32[88,192]{1,0:T(8,128)S(1)} %get-tuple-element.27), channel_id=1, source_target_pairs={{0,3},{1,2},{2,1},{3,0},{4,7},{5,6},{6,5},{7,4},{8,11},{9,10},{10,... | collective-permute-start | bytes 202760 | tf_op jit(solution)/shard_map/ppermute | solution.py:355
  59.0 6.9 %collective-permute-start.7 = (f32[88,192]{1,0:T(8,128)S(1)}, f32[88,192]{1,0:T(8,128)S(1)}, u32[]{:S(2)}, u32[]{:S(2)}) collective-permute-start(f32[88,192]{1,0:T(8,128)S(1)} %get-tuple-element.28), channel_id=1, source_target_pairs={{0,2},{1,3},{2,0},{3,1},{4,6},{5,7},{6,4},{7,5},{8,10},{9,11},{10,... | collective-permute-start | bytes 202760 | tf_op jit(solution)/shard_map/ppermute | solution.py:355
  60.7 5.1 %collective-permute-start.6 = (f32[88,192]{1,0:T(8,128)S(1)}, f32[88,192]{1,0:T(8,128)S(1)}, u32[]{:S(2)}, u32[]{:S(2)}) collective-permute-start(f32[88,192]{1,0:T(8,128)S(1)} %get-tuple-element.26), channel_id=1, source_target_pairs={{0,1},{1,0},{2,3},{3,2},{4,5},{5,4},{6,7},{7,6},{8,9},{9,8},{10,11... | collective-permute-start | bytes 202760 | tf_op jit(solution)/shard_map/ppermute | solution.py:355
  61.0 24.6 %collective-permute-start.12 = (bf16[768,192]{1,0:T(8,128)(2,1)S(1)}, bf16[768,192]{1,0:T(8,128)(2,1)S(1)}, u32[]{:S(2)}, u32[]{:S(2)}) collective-permute-start(bf16[768,192]{1,0:T(8,128)(2,1)S(1)} %add_convert_fusion.refs_6_), channel_id=1, source_target_pairs={{0,8},{4,12},{8,0},{12,4},{1,9},{5,13},{9,1},{13,5},{2,10},{6,14},... | collective-permute-start | bytes 884744 | tf_op jit(solution)/shard_map/ppermute | solution.py:355
  65.9 7.7 %collective-permute-start.9 = (f32[88,192]{1,0:T(8,128)S(1)}, f32[88,192]{1,0:T(8,128)S(1)}, u32[]{:S(2)}, u32[]{:S(2)}) collective-permute-start(f32[88,192]{1,0:T(8,128)S(1)} %fusion.2), channel_id=1, source_target_pairs={{0,4},{4,0},{8,12},{12,8},{1,5},{5,1},{9,13},{13,9},{2,6},{6,2},{1... | collective-permute-start | bytes 202760 | tf_op jit(solution)/shard_map/ppermute | solution.py:355
  73.6 12.0 %collective-permute-start.10 = (f32[88,192]{1,0:T(8,128)S(1)}, f32[88,192]{1,0:T(8,128)S(1)}, u32[]{:S(2)}, u32[]{:S(2)}) collective-permute-start(f32[88,192]{1,0:T(8,128)S(1)} %add.188.refs_4_), channel_id=1, source_target_pairs={{0,8},{4,12},{8,0},{12,4},{1,9},{5,13},{9,1},{13,5},{2,10},{6,14},... | collective-permute-start | bytes 202760 | tf_op jit(solution)/shard_map/ppermute | solution.py:355

commit v2 on v1

v2 whole, which is shorter than its diff:
```python
import functools
import math

import jax
import jax.numpy as jnp
from jax import lax
from jax.experimental import pallas as pl
from jax.experimental.pallas import tpu as pltpu
from jax.sharding import PartitionSpec as P

TAPS = 5
BASES = 4
BLOCKS = 2
DMAX = 8
HALF = TAPS // 2
REACH = HALF * DMAX
LANE = 128
JB = 32
GELU_SCALE = math.sqrt(2.0 / math.pi)
CUBIC = 0.044715
BF = jnp.bfloat16
F32 = jnp.float32
ROW_EMBED, ROW_TAPS0, ROW_TAPS1, TABLE = 0, BASES, BASES + TAPS, 16
ROW_GT0, ROW_GT1, ROW_GE, SUMS = 2 * JB, 2 * JB + 8, 2 * JB + 16, 2 * JB + 24


def dot(a, b, **kw):
    return jnp.dot(a, b, preferred_element_type=F32, **kw)


def dot_t(a, b):
    return lax.dot_general(a, b, (((1,), (1,)), ((), ())), preferred_element_type=F32)


def t_dot(a, b):
    return lax.dot_general(a, b, (((0,), (0,)), ((), ())), preferred_element_type=F32)


def iotas(shape):
    return lax.broadcasted_iota(jnp.int32, shape, 0), lax.broadcasted_iota(jnp.int32, shape, 1)


def as_bf(mask):
    return mask.astype(F32).astype(BF)


def reversal(size):
    row, col = iotas((size, size))
    return as_bf(row + col == size - 1)


def split_bf(x):
    high = x.astype(BF)
    return high, (x - high.astype(F32)).astype(BF)


def flip_exact(x, rev):
    high, rest = split_bf(x)
    mid, low = split_bf(x - high.astype(F32))
    del rest
    return dot(high, rev) + dot(mid, rev) + dot(low, rev)


def xor_blocks(blocks, me):
    for bit in range(len(blocks).bit_length() - 1):
        swap = lax.bitwise_and(lax.shift_right_logical(me, bit), 1) == 1
        blocks = [jnp.where(swap, blocks[k ^ (1 << bit)], blocks[k]) for k in range(len(blocks))]
    return blocks


def gelu_parts(v):
    square = v * v
    tangent = jnp.tanh(v * (GELU_SCALE + (GELU_SCALE * CUBIC) * square))
    half = 0.5 + 0.5 * tangent
    value = v * half
    slope = half + (v * (1.0 - tangent * tangent)) * (
        0.5 * GELU_SCALE + (1.5 * GELU_SCALE * CUBIC) * square
    )
    return value, slope


def select_rows(kind, rows):
    row, col = iotas((rows, TABLE))
    local = row % JB
    used = local < TAPS * BASES
    tap, letter = local // BASES, local % BASES
    want = {"tap0": ROW_TAPS0 + tap, "tap1": ROW_TAPS1 + tap, "letter": ROW_EMBED + letter}[kind]
    return as_bf(used & (col == want))


def one_hot_t(tokens):
    n = tokens[0].shape[1]
    inside = tokens[HALF] != 0
    row = lax.broadcasted_iota(jnp.int32, (2 * JB, n), 0)
    local = row % JB
    group = jnp.where(local < TAPS * BASES, local // BASES + TAPS * (row // JB), -1)
    seen = jnp.zeros((2 * JB, n), jnp.int32)
    for g, line in enumerate(tokens):
        line = jnp.where(inside, line, 0)
        seen = jnp.where(group == g, jnp.broadcast_to(line, (2 * JB, n)), seen)
    return (seen == local % BASES + 1).astype(F32)


def pair_table(tables, rev_w):
    sel_t, sel_e = select_rows("tap0", JB), select_rows("letter", JB)
    plain = [dot(sel_t, t) * dot(sel_e, t) for t in tables]
    n = len(tables)
    out = []
    for k in range(n):
        high, low = split_bf(plain[k])
        fhigh, flow = split_bf(plain[n - 1 - k])
        out.append((high, dot(fhigh, rev_w).astype(BF), low, dot(flow, rev_w).astype(BF)))
    return out


def pack_kernel(width, mix_ref, embed_ref, taps_ref, out_ref, sem):
    copy = pltpu.make_async_copy(mix_ref.at[0], out_ref.at[pl.ds(0, width)], sem)
    copy.start()
    taps = taps_ref[...].astype(F32)
    lines = [embed_ref[...].astype(F32)]
    lines += [taps[j, block : block + 1, :] for block in range(BLOCKS) for j in range(TAPS)]
    lines.append(jnp.zeros((TABLE - BASES - 2 * TAPS, width), F32))
    table = jnp.concatenate(lines, axis=0).astype(BF)
    out_ref[width:, :] = jnp.zeros((TABLE, out_ref.shape[1]), BF)
    out_ref[width:, :width] = table
    copy.wait()


def prep_kernel(n_chan, n_seq, rows, width, scal, tok_ref, mix_ref, a_ref, hot_ref, hot1_ref, mixl_ref):
    me, place = scal[0], scal[1]
    blocks = [mix_ref[0, :, k * width : (k + 1) * width] for k in range(n_chan)]
    for k, block in enumerate(xor_blocks(blocks, me)):
        mixl_ref[:, k * width : (k + 1) * width] = block

    def line(block):
        inside = jnp.logical_and(block >= 0, block < n_seq)
        safe = jnp.clip(block, 0, n_seq - 1)
        letters = tok_ref[pl.ds(lax.bitwise_xor(safe, place), 1), :] + 1
        return jnp.where(inside, letters, 0)

    def around(block):
        lines = [line(block - 1)[:, rows - LANE :], line(block), line(block + 1)[:, :LANE]]
        return jnp.concatenate(lines, axis=1)

    total = rows + 2 * LANE
    this = jnp.broadcast_to(around(place), (8, total))
    mirror = jnp.broadcast_to(around(n_seq - 1 - place), (8, total)).astype(F32).astype(BF)
    rev, n_tiles = reversal(LANE), total // LANE
    other = jnp.concatenate(
        [dot(mirror[:, t * LANE : (t + 1) * LANE], rev) for t in reversed(range(n_tiles))], axis=1
    ).astype(jnp.int32)

    def windows(dilation, margin, count):
        out = []
        for strand, source in ((1, this), (-1, other)):
            for j in range(TAPS):
                first = LANE - margin + strand * (j - HALF) * dilation
                out.append(pltpu.roll(source, total - first, 1)[:1, :count])
        return out

    hot = one_hot_t(windows(scal[2], REACH, a_ref.shape[0]))
    a_ref[...] = jnp.concatenate([hot, hot], axis=0).T.astype(BF)
    hot_ref[...] = hot.astype(BF)
    hot1_ref[...] = one_hot_t(windows(scal[3], 0, rows)).astype(BF)


def forward_kernel(n_chan, rows, width, scale, scal, *refs):
    pks = refs[:n_chan]
    a_ref, mixl_ref, cot_ref = refs[n_chan : n_chan + 3]
    x2_ref, gm_ref, s_ref, x1_ref, gp_ref, st_ref = refs[n_chan + 3 : n_chan + 9]
    w_ref, e_ref, wt_ref, et_ref, m_ref = refs[n_chan + 9 :]
    tiles = n_chan * width // LANE
    ext = rows + 2 * REACH
    me, dil = scal[0], scal[3]
    rev, rev_w = reversal(LANE), reversal(width)

    tables = [pk[width:, :width] for pk in pks]
    stacks = [jnp.concatenate(p, axis=0) for p in pair_table(tables, rev_w)]
    for k, stack in enumerate(xor_blocks(stacks, me)):
        st_ref[:, k * width : (k + 1) * width] = stack
    for k in range(n_chan):
        total = dot_t(st_ref[...], pks[k][:width, :])
        high, low = split_bf(total[: 2 * JB] + total[2 * JB :])
        w_ref[:, k * width : (k + 1) * width] = jnp.concatenate([high, low], axis=0)
        e_ref[:, k * width : (k + 1) * width] = tables[k]

    for t in range(tiles):
        src = slice((tiles - 1 - t) * LANE, (tiles - t) * LANE)
        dst = slice(t * LANE, (t + 1) * LANE)
        flipped = dot(w_ref[:, src], rev).astype(BF)
        wt_ref[:, dst] = jnp.concatenate(
            [flipped[JB : 2 * JB], flipped[:JB], flipped[3 * JB :], flipped[2 * JB : 3 * JB]], axis=0
        )
        et_ref[:, dst] = dot(e_ref[:, src], rev).astype(BF)

    row, col = iotas((4 * JB, TABLE))
    centre = HALF * BASES
    pick_f = as_bf((row - centre == col) & (col < BASES))
    pick_r = as_bf((row - centre - JB == col) & (col < BASES))
    chunk = ext // 5
    for t in range(tiles):
        dst = slice(t * LANE, (t + 1) * LANE)
        for strand, (wr, er, pick) in enumerate(((w_ref, e_ref, pick_f), (wt_ref, et_ref, pick_r))):
            rhs = jnp.concatenate([wr[:, dst], dot(pick, er[:, dst]).astype(BF)], axis=1)

            for i in range(5):
                where = pl.ds(i * chunk, chunk)
                both = dot(a_ref[where, :], rhs)
                value, slope = gelu_parts(both[:, :LANE])
                x1 = (both[:, LANE:] + value).astype(BF).astype(F32)
                x1_ref[strand, t, where, :] = x1
                gp_ref[strand, t, where, :] = slope.astype(BF)

    mchunk = rows // 6
    for t in range(tiles):
        dst = slice(t * LANE, (t + 1) * LANE)
        taps_f = e_ref[:, dst].astype(F32)
        taps_r = et_ref[:, dst].astype(F32)

        for i in range(6):
            first = i * mchunk
            u = jnp.zeros((mchunk, LANE), F32)
            v = jnp.zeros((mchunk, LANE), F32)
            for j in range(TAPS):
                shift = (j - HALF) * dil
                u += taps_f[ROW_TAPS1 + j : ROW_TAPS1 + j + 1, :] * x1_ref[0, t, pl.ds(first + REACH + shift, mchunk), :]
                v += taps_r[ROW_TAPS1 + j : ROW_TAPS1 + j + 1, :] * x1_ref[1, t, pl.ds(first + REACH - shift, mchunk), :]
            total = u.astype(BF).astype(F32) + v.astype(BF).astype(F32)
            m_ref[first : first + mchunk, dst] = total.astype(BF)

    half = rows // 2
    for i in range(2):
        where = pl.ds(i * half, half)
        value, slope = gelu_parts(dot_t(m_ref[where, :], mixl_ref[...]))
        inner = pl.ds(REACH + i * half, half)
        n_own = pl.cdiv(width, LANE)
        own = jnp.concatenate([x1_ref[0, t, inner, :] for t in range(n_own)], axis=1)[:, :width]
        x2_ref[where, :] = (own + value).astype(BF)
        s_ref[where, :] = ((cot_ref[where, :].astype(F32) * scale) * slope).astype(BF)

    gm_ref[...] = t_dot(s_ref[...], m_ref[...]).astype(BF)


def backward_kernel(n_chan, rows, width, scale, scal, *refs):
    pks = refs[:n_chan]
    hot_ref, hot1_ref, mixl_ref, cot_ref, s_ref, x1_ref, gp_ref = refs[n_chan : n_chan + 7]
    out_ref = refs[n_chan + 7]
    p_ref, g2_ref, s0_ref, e_ref, et_ref, dw_ref, gt_ref, g1_ref, pb_ref, st_ref = refs[n_chan + 8 :]
    chans = n_chan * width
    tiles = chans // LANE
    ext = rows + 2 * REACH
    padded = hot_ref.shape[1]
    me, dil = scal[0], scal[3]
    rev, rev_w = reversal(LANE), reversal(width)
    tables = [pk[width:, :width] for pk in pks]
    for k in range(n_chan):
        e_ref[:, k * width : (k + 1) * width] = tables[k]
    for t in range(tiles):
        src = slice((tiles - 1 - t) * LANE, (tiles - t) * LANE)
        et_ref[:, t * LANE : (t + 1) * LANE] = dot(e_ref[:, src], rev).astype(BF)

    edge = 2 * REACH
    n_own = pl.cdiv(width, LANE)
    g2 = cot_ref[...].astype(F32) * scale
    g2_ref[:, :REACH, :] = jnp.zeros((n_own, REACH, LANE), F32)
    g2_ref[:, rows + REACH :, :] = jnp.zeros((n_own, REACH, LANE), F32)
    g2 = jnp.concatenate([g2, jnp.zeros((rows, n_own * LANE - width), F32)], axis=1)
    for t in range(n_own):
        g2_ref[t, REACH : rows + REACH, :] = g2[:, t * LANE : (t + 1) * LANE]
    s0_ref[:, ext:, :] = jnp.zeros((2, padded - ext, chans), BF)
    for t in range(tiles):
        p_ref[t, :edge, :] = jnp.zeros((edge, LANE), F32)
        p_ref[t, rows + edge :, :] = jnp.zeros((edge, LANE), F32)
        part = dot(s_ref[...], mixl_ref[:, t * LANE : (t + 1) * LANE])
        p_ref[t, edge : rows + edge, :] = part
        pb_ref[:, t * LANE : (t + 1) * LANE] = part.astype(BF)

    mchunk, chunk = rows // 6, ext // 5
    for t in range(tiles):
        dst = slice(t * LANE, (t + 1) * LANE)
        taps_f = e_ref[:, dst].astype(F32)
        taps_r = et_ref[:, dst].astype(F32)

        for i in range(5):
            first = i * chunk
            where = pl.ds(first, chunk)
            f = jnp.zeros((chunk, LANE), F32)
            r = jnp.zeros((chunk, LANE), F32)
            for j in range(TAPS):
                shift = (j - HALF) * dil
                tap_f = taps_f[ROW_TAPS1 + j : ROW_TAPS1 + j + 1, :]
                tap_r = taps_r[ROW_TAPS1 + j : ROW_TAPS1 + j + 1, :]
                f += tap_f * p_ref[t, pl.ds(first + REACH - shift, chunk), :]
                r += tap_r * p_ref[t, pl.ds(first + REACH + shift, chunk), :]
            if t < n_own:
                f += g2_ref[t, where, :]
            s0_ref[0, where, dst] = (f * gp_ref[0, t, where, :].astype(F32)).astype(BF)
            s0_ref[1, where, dst] = (r * gp_ref[1, t, where, :].astype(F32)).astype(BF)

        def taps_step(i, carry, t=t):
            first = i * mchunk
            here = p_ref[t, pl.ds(edge + first, mchunk), :]
            out = []
            for strand in range(2):
                for j in range(TAPS):
                    shift = (j - HALF) * dil * (1 - 2 * strand)
                    prod = here * x1_ref[strand, t, pl.ds(first + REACH + shift, mchunk), :]
                    out.append(carry[strand * TAPS + j] + prod.reshape(mchunk // 8, 8, LANE).sum(0))
            return tuple(out)

        sums = tuple(jnp.zeros((8, LANE), F32) for _ in range(2 * TAPS))
        for i in range(6):
            sums = taps_step(i, sums)
        for strand in range(2):
            rows_t = [jnp.sum(sums[strand * TAPS + j], axis=0, keepdims=True) for j in range(TAPS)]
            gt_ref[strand, :, dst] = jnp.concatenate(rows_t + [jnp.zeros((8 - TAPS, LANE), F32)], axis=0)

    hot, hot1 = hot_ref[...], hot1_ref[...]
    dw_ref[...] = dot(hot, s0_ref[0])
    other = dot(hot, s0_ref[1])
    by_tap = dot(hot1, pb_ref[...])
    own_letters = dot(hot1[: 16, :], cot_ref[...]) * scale
    srow, scol = iotas((8, JB))
    sum_letter = as_bf((scol % BASES == srow) & (scol < TAPS * BASES))
    sum_tap = as_bf((scol // BASES == srow) & (scol < TAPS * BASES))

    def sums_of(sel, x):
        high, rest = split_bf(x)
        return dot(sel, high) + dot(sel, rest)

    sel1 = select_rows("tap1", JB)
    g1_other = []
    for t in range(tiles):
        dst = slice(t * LANE, (t + 1) * LANE)
        g1_ref[:, dst] = sums_of(sum_letter, by_tap[:JB, dst] * dot(sel1, e_ref[:, dst]))
        g1_other.append(sums_of(sum_letter, by_tap[JB:, dst] * dot(sel1, et_ref[:, dst])))
    for t in range(tiles):
        dst = slice(t * LANE, (t + 1) * LANE)
        src = slice((tiles - 1 - t) * LANE, (tiles - t) * LANE)
        flipped = flip_exact(other[:, src], rev)
        dw_ref[:, dst] += jnp.concatenate([flipped[JB:], flipped[:JB]], axis=0)
        g1_ref[:, dst] += flip_exact(g1_other[tiles - 1 - t], rev)
        gt_ref[0, :, dst] += flip_exact(gt_ref[1, :, src], rev)

    sel_t, sel_e = select_rows("tap0", JB), select_rows("letter", JB)
    total = jnp.zeros((2 * JB, chans), F32)
    for k in range(n_chan):
        part = dw_ref[:, k * width : (k + 1) * width].astype(BF)
        total = total + dot(part, pks[k][:width, :])
    st_ref[...] = total
    grads = xor_blocks([st_ref[:, k * width : (k + 1) * width] for k in range(n_chan)], me)
    for kk in range(n_chan):
        both = grads[kk][:JB] + flip_exact(grads[n_chan - 1 - kk][JB:], rev_w)
        table = tables[kk]
        lanes = slice(kk * width, (kk + 1) * width)
        out_ref[kk, : 2 * JB, :] = dw_ref[:, lanes]
        out_ref[kk, ROW_GT0 : ROW_GT0 + 8, :] = sums_of(sum_tap, both * dot(sel_e, table))
        out_ref[kk, ROW_GT1 : ROW_GT1 + 8, :] = gt_ref[0, :, lanes]
        letters = sums_of(sum_letter, both * dot(sel_t, table)) + g1_ref[:, lanes]
        if kk == 0:
            zeros = jnp.zeros((BASES, width), F32)
            own = own_letters[HALF * BASES : (HALF + 1) * BASES, :]
            letters = letters + jnp.concatenate([own, zeros], axis=0)
        out_ref[kk, ROW_GE : ROW_GE + 8, :] = letters


def mix1_kernel(n_chan, width, scal, a_ref, b_ref, out_ref, held, sem):
    def block(k):
        lanes = slice(k * width, (k + 1) * width)
        return a_ref[:, lanes].astype(F32) + b_ref[:, lanes].astype(F32)

    for k, part in enumerate(xor_blocks([block(k) for k in range(n_chan)], scal[0])):
        held[:, k * width : (k + 1) * width] = part
    copy = pltpu.make_async_copy(held, out_ref.at[1], sem)
    copy.start()
    copy.wait()


def finish_kernel(n_chan, width, scal, st_ref, sa_ref, sb_ref, _, gm_ref, gt_ref, ge_ref, held, sem):
    sums = sa_ref[...] + sb_ref[...]
    dw = sums[: 2 * JB].astype(BF)
    held[...] = t_dot(dw, st_ref[: 2 * JB, :])
    copy = pltpu.make_async_copy(held, gm_ref.at[0], sem)
    copy.start()
    for j in range(TAPS):
        gt_ref[j, 0:1, :] = sums[ROW_GT0 + j : ROW_GT0 + j + 1]
        gt_ref[j, 1:2, :] = sums[ROW_GT1 + j : ROW_GT1 + j + 1]
    ge_ref[...] = sums[ROW_GE : ROW_GE + BASES]
    copy.wait()


VMEM = pl.BlockSpec(memory_space=pltpu.VMEM)
SMEM = pl.BlockSpec(memory_space=pltpu.SMEM)
HBM = pl.BlockSpec(memory_space=pltpu.HBM)


def call(kernel, in_specs, out_shape, out_specs, scratch, limit, cost, aliases=None):
    flops, moved = cost
    return pl.pallas_call(
        kernel,
        out_shape=out_shape,
        in_specs=in_specs,
        out_specs=out_specs,
        scratch_shapes=scratch,
        input_output_aliases=aliases or {},
        compiler_params=pltpu.CompilerParams(vmem_limit_bytes=limit << 20),
        cost_estimate=pl.CostEstimate(flops=flops, bytes_accessed=moved, transcendentals=0),
    )


def flip_bits(x, axis, mask):
    return lax.ppermute(x, axis, [(i, i ^ mask) for i in range(lax.axis_size(axis))])


def body(tokens, cotangent, embed, taps, mix, dilations):
    rows, width = cotangent.shape
    n_seq, n_chan = lax.axis_size("seq"), lax.axis_size("chan")
    chans = n_chan * width
    tiles = chans // LANE
    ext = rows + 2 * REACH
    padded = pl.cdiv(ext, LANE) * LANE
    edge = 2 * REACH
    own_tiles = pl.cdiv(width, LANE)
    scale = 1.0 / math.sqrt(rows * n_seq)
    shape = jax.ShapeDtypeStruct
    place = jnp.stack([lax.axis_index("chan"), lax.axis_index("seq")]).astype(jnp.int32)
    scal = jnp.concatenate([place, dilations])
    mix_t = jnp.swapaxes(mix, 1, 2)

    (pk,) = call(
        functools.partial(pack_kernel, width),
        [HBM, VMEM, VMEM],
        [shape((width + TABLE, chans), BF)],
        [VMEM],
        [pltpu.SemaphoreType.DMA],
        8,
        (0, width * chans * 4),
    )(mix_t, embed, jnp.swapaxes(taps, 0, 1))
    pks = [pk]
    for bit in reversed(range(n_chan.bit_length() - 1)):
        moved = [flip_bits(p, "chan", 1 << bit) for p in pks]
        pks = [q for pair in zip(pks, moved) for q in pair]

    letters = tokens.reshape(1, rows)
    seq_bits = n_seq.bit_length() - 1
    for bit in range(seq_bits):
        letters = jnp.concatenate([letters, flip_bits(letters, "seq", 1 << bit)], axis=0)

    hot_t, hot, hot1, mixl = call(
        functools.partial(prep_kernel, n_chan, n_seq, rows, width),
        [SMEM, VMEM, VMEM],
        [
            shape((padded, 4 * JB), BF),
            shape((2 * JB, padded), BF),
            shape((2 * JB, rows), BF),
            shape((width, chans), BF),
        ],
        [VMEM] * 4,
        [],
        16,
        (1 << 20, 1 << 20),
    )(scal, letters, mix_t[1:])

    x2, gm1, s1, x1, gp, stack = call(
        functools.partial(forward_kernel, n_chan, rows, width, scale),
        [SMEM] + [VMEM] * (n_chan + 3),
        [
            shape((rows, width), BF),
            shape((width, chans), BF),
            shape((rows, width), BF),
            shape((2, tiles, ext, LANE), F32),
            shape((2, tiles, ext, LANE), BF),
            shape((4 * JB, chans), BF),
        ],
        [VMEM] * 6,
        [
            pltpu.VMEM((4 * JB, chans), BF),
            pltpu.VMEM((TABLE, chans), BF),
            pltpu.VMEM((4 * JB, chans), BF),
            pltpu.VMEM((TABLE, chans), BF),
            pltpu.VMEM((rows, chans), BF),
        ],
        32,
        (3 << 30, 8 << 20),
    )(scal, *pks, hot_t, mixl, cotangent)

    (sums,) = call(
        functools.partial(backward_kernel, n_chan, rows, width, scale),
        [SMEM] + [VMEM] * (n_chan + 7),
        [shape((n_chan, SUMS, width), F32)],
        [VMEM],
        [
            pltpu.VMEM((tiles, rows + 2 * edge, LANE), F32),
            pltpu.VMEM((own_tiles, ext, LANE), F32),
            pltpu.VMEM((2, padded, chans), BF),
            pltpu.VMEM((TABLE, chans), BF),
            pltpu.VMEM((TABLE, chans), BF),
            pltpu.VMEM((2 * JB, chans), F32),
            pltpu.VMEM((2, 8, chans), F32),
            pltpu.VMEM((8, chans), F32),
            pltpu.VMEM((rows, chans), BF),
            pltpu.VMEM((2 * JB, chans), F32),
        ],
        40,
        (3 << 30, 8 << 20),
    )(scal, *pks, hot, hot1, mixl, cotangent, s1, x1, gp)

    g_mine = gm1
    for bit in range(seq_bits):
        g_other = flip_bits(g_mine, "seq", 1 << bit)
        if bit < seq_bits - 1:
            g_mine = lax.optimization_barrier(
                (g_mine.astype(F32) + g_other.astype(F32)).astype(BF)
            )
    pieces = [sums[0]] + [flip_bits(sums[k], "chan", k) for k in range(1, n_chan)]
    s_mine = functools.reduce(jnp.add, pieces)
    for bit in range(seq_bits):
        s_other = flip_bits(s_mine, "seq", 1 << bit)
        if bit < seq_bits - 1:
            s_mine = s_mine + s_other

    big = pltpu.VMEM((width, chans), F32)
    (grad_mix,) = call(
        functools.partial(mix1_kernel, n_chan, width),
        [SMEM, VMEM, VMEM],
        [shape((BLOCKS, width, chans), F32)],
        [HBM],
        [big, pltpu.SemaphoreType.DMA],
        16,
        (1 << 20, 1 << 21),
    )(scal, g_mine, g_other)
    grad_mix, grad_taps, grad_embed = call(
        functools.partial(finish_kernel, n_chan, width),
        [SMEM, VMEM, VMEM, VMEM, HBM],
        [
            shape((BLOCKS, width, chans), F32),
            shape((TAPS, BLOCKS, width), F32),
            shape((BASES, width), F32),
        ],
        [HBM, VMEM, VMEM],
        [big, pltpu.SemaphoreType.DMA],
        16,
        (1 << 24, 1 << 21),
        {4: 0},
    )(scal, stack, s_mine, s_other, grad_mix)
    return x2, jnp.swapaxes(grad_mix, 1, 2), jnp.swapaxes(grad_taps, 0, 1), grad_embed


def solution(mesh):
    in_specs = (
        P(("groups", "seq")),
        P(("groups", "seq"), "chan"),
        P(None, "chan"),
        P(None, None, "chan"),
        P(None, None, "chan"),
        P(),
    )
    out_specs = (
        P(("groups", "seq"), "chan"),
        P("groups", None, "chan"),
        P("groups", None, "chan"),
        P("groups", "chan"),
    )
    return jax.shard_map(body, mesh=mesh, in_specs=in_specs, out_specs=out_specs, check_vma=False)
```

time: 90.2 us -> 66.7 us (0.74)
  Pallas kernels: 32.4 us -> 24.8 us
  between operations: 7.5 us -> 0.91 us
  starting transfers between devices: 19.9 us -> 15.5 us
  waiting for transfers between devices: 21.2 us -> 18.2 us
  local copies, waits for them, and re-layouts: 8.07 us -> 6.13 us
    pallas_call x3 -> x6, Pallas kernels: 32.4 us -> 24.8 us  [the longest x1 10.1 us: body(): call(functools.partial(backward_kernel, n_chan, rows, width, scale), [SME...]
    ppermute x3 -> x0, starting transfers between devices: 7.24 us -> none  [the longest x1 4.55 us: body(): lax.ppermute(shifted[rows - edge:], 'seq', [(i, i + 1) for i in range(n_s...]
    ppermute x3 -> x0, waiting for transfers between devices: 3.67 us -> none  [the longest x1 3.66 us: body(): lax.ppermute(wide, 'seq', [(i, n_seq - 1 - i) for i in range(n_seq)])[::-1]]
    ppermute x10 -> x12, starting transfers between devices: 12.7 us -> 15.5 us  [flip_bits(): lax.ppermute(x, axis, [(i, i ^ mask) for i in range(lax.axis_size(axis))])]
    slice x7 -> x1, local copies, waits for them, and re-layouts: 2.54 us -> 0.98 us  [body(): mix_t[1:]]
    ppermute x10 -> x12, waiting for transfers between devices: 17.5 us -> 18.2 us  [flip_bits(): lax.ppermute(x, axis, [(i, i ^ mask) for i in range(lax.axis_size(axis))])]
    unnamed x18 -> x8, local copies, waits for them, and re-layouts: 3.79 us -> 4.43 us
  transfers between devices with their start and end apart: 13 -> 12, of which waited for: 6 -> 5; matrix products, arithmetic and copies ran while one was open for 4% -> 7% of each run, Pallas kernels for 12% -> 20%
where the time goes in v2:
time: 66.7 us; the launch traced here: 66.4 us
  Pallas kernels  24.8 us (37%)
  waiting for transfers between devices  18.2 us (27%)
  starting transfers between devices  15.5 us (23%)
  local copies, waits for them, and re-layouts  6.13 us (9%)
  between operations  0.91 us (1%)
  other arithmetic  0.86 us (1%)
    ppermute x12, waiting for transfers between devices, flip_bits(): lax.ppermute(x, axis, [(i, i ^ mask) for i in range(lax.axis_size(axis))])  18.2 us
    ppermute x12, starting transfers between devices, flip_bits(): lax.ppermute(x, axis, [(i, i ^ mask) for i in range(lax.axis_size(axis))])  15.5 us
    pallas_call x1, Pallas kernels, body(): call(functools.partial(backward_kernel, n_chan, rows, width, scale), [SME...  10.1 us
    pallas_call x1, Pallas kernels, body(): call(functools.partial(forward_kernel, n_chan, rows, width, scale), [SMEM...  9.22 us
    unnamed x8, local copies, waits for them, and re-layouts  4.43 us
    pallas_call x1, Pallas kernels, body(): call(functools.partial(finish_kernel, n_chan, width), [SMEM, VMEM, VMEM,...  2.23 us
    pallas_call x1, Pallas kernels, body(): call(functools.partial(mix1_kernel, n_chan, width), [SMEM, VMEM, VMEM], [...  1.84 us
    pallas_call x1, Pallas kernels, body(): call(functools.partial(prep_kernel, n_chan, n_seq, rows, width), [SMEM, V...  1.34 us
  transfers between devices with their start and end apart: 12, of which 5 were waited for; matrix products, arithmetic and copies ran while one was open for 7% of the time, Pallas kernels for 20%

profile of v2, /device:TPU:0, one launch (start us, length us, event | category | flops | bytes accessed | tf_op | source)
XLA Modules:
  0.0 66.4 jit_solution(1222370112542761083)
XLA Ops:
  0.6 0.0 copy-start
  0.6 1.1 %copy-done = bf16[2,768,192]{1,2,0:T(8,128)(2,1)S(1)} copy-done((bf16[2,768,192]{1,2,0:T(8,128)(2,1)S(1)}, bf16[2,768,192]{1,2,0:T(8,128)(2,1)}, u32[]{:S(2)}) %copy-start) | copy-done | bytes 589848
  1.7 0.7 %copy-done.1 = bf16[2,5,192]{2,0,1:T(2,128)(2,1)S(1)} copy-done((bf16[2,5,192]{2,0,1:T(2,128)(2,1)S(1)}, bf16[2,5,192]{2,0,1:T(2,128)(2,1)}, u32[]{:S(2)}) %copy-start.1) | copy-done | bytes 3864
  2.4 0.7 %copy-done.2 = bf16[4,192]{1,0:T(4,128)(2,1)S(1)} copy-done((bf16[4,192]{1,0:T(4,128)(2,1)S(1)}, bf16[4,192]{1,0:T(4,128)(2,1)}, u32[]{:S(2)}) %copy-start.2) | copy-done | bytes 1560
  3.1 0.1 shard_map.93.refs_0_
  3.2 3.0 %collective-permute-start.1 = (bf16[208,768]{1,0:T(8,128)(2,1)S(1)}, bf16[208,768]{1,0:T(8,128)(2,1)S(1)}, u32[]{:S(2)}, u32[]{:S(2)}) collective-permute-start(bf16[208,768]{1,0:T(8,128)(2,1)S(1)} %shard_map.93.refs_0_), channel_id=1, source_target_pairs={{0,2},{1,3},{2,0},{3,1},{4,6},{5,7},{6,4},{7,5},{8,10},{9,11},{10,... | collective-permute-start | bytes 958472 | tf_op jit(solution)/shard_map/ppermute | solution.py:412
  6.2 0.7 %reshape.11 = s32[1,768]{1,0:T(1,128)S(1)} reshape(s32[768]{0:T(1024)} %param.6) | data formatting | bytes 6144 | tf_op jit(solution)/shard_map/reshape | solution.py:444
  6.8 1.6 %collective-permute-start.3 = (s32[1,768]{1,0:T(1,128)S(1)}, s32[1,768]{1,0:T(1,128)S(1)}, u32[]{:S(2)}, u32[]{:S(2)}) collective-permute-start(s32[1,768]{1,0:T(1,128)S(1)} %reshape.11), channel_id=1, source_target_pairs={{0,4},{4,0},{8,12},{12,8},{1,5},{5,1},{9,13},{13,9},{2,6},{6,2},{1... | collective-permute-start | bytes 9224 | tf_op jit(solution)/shard_map/ppermute | solution.py:412
  8.4 5.3 %collective-permute-done.1.refs_2_ = bf16[208,768]{1,0:T(8,128)(2,1)S(1)} collective-permute-done((bf16[208,768]{1,0:T(8,128)(2,1)S(1)}, bf16[208,768]{1,0:T(8,128)(2,1)S(1)}, u32[]{:S(2)}, u32[]{:S(2)}) %collective-permute-start.1) | collective-permute-done | bytes 319520 | tf_op jit(solution)/shard_map/ppermute | solution.py:412
  13.7 2.9 %collective-permute-start.4 = (s32[2,768]{1,0:T(2,128)S(1)}, s32[2,768]{1,0:T(2,128)S(1)}, u32[]{:S(2)}, u32[]{:S(2)}) collective-permute-start(s32[2,768]{1,0:T(2,128)S(1)} %pad_add_fusion.1), channel_id=1, source_target_pairs={{0,8},{4,12},{8,0},{12,4},{1,9},{5,13},{9,1},{13,5},{2,10},{6,14},... | collective-permute-start | bytes 18440 | tf_op jit(solution)/shard_map/ppermute | solution.py:412
  16.6 0.7 %pad_add_fusion.2.scal = s32[4]{0:T(128)S(1)} fusion(s32[2]{0:T(128)} %param.11, s32[1]{0:T(128)} %bitcast.1, s32[1]{0:T(128)} %bitcast), kind=kLoop, calls=%fused_computation.10 | loop fusion | flops 8 | bytes 32 | tf_op jit(solution)/shard_map/concatenate | solution.py:427
  17.3 1.0 %slice.20.mix_ref = bf16[1,192,768]{2,1,0:T(8,128)(2,1)S(1)} slice(bf16[2,192,768]{2,1,0:T(8,128)(2,1)} %bitcast.20), slice={[1:2], [0:192], [0:768]} | slice | bytes 589824 | tf_op jit(solution)/shard_map/slice | solution.py:462
  18.3 1.1 %copy.11.refs_6_.refs_7_ = bf16[768,192]{1,0:T(8,128)(2,1)S(1)} copy(bf16[768,192]{0,1:T(8,128)(2,1)} %param.7) | data formatting | bytes 589824 | tf_op args[1]
  19.5 1.3 %shard_map.94 = (bf16[896,128]{1,0:T(8,128)(2,1)S(1)}, bf16[64,896]{1,0:T(8,128)(2,1)S(1)}, bf16[64,768]{1,0:T(8,128)(2,1)S(1)}, bf16[192,768]{1,0:T(8,128)(2,1)S(1)}) custom-call(s32[4]{0:T(128)S(1)} %pad_add_fusion.2.scal, s32[4,768]{1,0:T(4,128)S(1)} %pad_add_fusion.tok_ref, bf16[1,192,768]{2,1,0:T(8,128)(2,1)S(1)} %slice.20.mix_ref), custom_call_target="tpu_custom_call" | custom-call | flops 1048576 | bytes 1048576 | tf_op jit(solution)/shard_map/pallas_call | solution.py:449
  20.9 9.2 %shard_map.95 = (bf16[768,192]{1,0:T(8,128)(2,1)S(1)}, bf16[192,768]{1,0:T(8,128)(2,1)S(1)}, bf16[768,192]{1,0:T(8,128)(2,1)S(1)}, f32[2,6,800,128]{3,2,1,0:T(8,...) custom-call(s32[4]{0:T(128)S(1)} %pad_add_fusion.2.scal, ...), custom_call_target="tpu_custom_call" | custom-call | flops 3221225472 | bytes 8388608 | tf_op jit(solution)/shard_map/pallas_call | solution.py:464
  30.1 1.6 %collective-permute-start.10 = (bf16[192,768]{1,0:T(8,128)(2,1)S(1)}, bf16[192,768]{1,0:T(8,128)(2,1)S(1)}, u32[]{:S(2)}, u32[]{:S(2)}) collective-permute-start(bf16[192,768]{1,0:T(8,128)(2,1)S(1)} %get-tuple-element.26), channel_id=1, source_target_pairs={{0,4},{4,0},{8,12},{12,8},{1,5},{5,1},{9,13},{13,9},{2,6},{6,2},{1... | collective-permute-start | bytes 884744 | tf_op jit(solution)/shard_map/ppermute | solution.py:412
  31.7 10.1 %shard_map.96 = f32[4,88,192]{2,1,0:T(8,128)S(1)} custom-call(s32[4]{0:T(128)S(1)} %pad_add_fusion.2.scal, bf16[208,768]{1,0:T(8,128)(2,1)S(1)} %shard_map.93.refs_0_, bf16[208,768]{1,0:T(8,128)(2,1)S(1)} %collective-permute-done.refs_1_, bf16[208,768]{1,0:T(8,128)(2,1)S(1)} %collective-permute-done.1.refs_2_, ...), custom_call_target="tpu_custom_call" | custom-call | flops 3221225472 | bytes 8388608 | tf_op jit(solution)/shard_map/pallas_call | solution.py:487
  41.8 1.1 %collective-permute-start.7 = (f32[88,192]{1,0:T(8,128)S(1)}, f32[88,192]{1,0:T(8,128)S(1)}, u32[]{:S(2)}, u32[]{:S(2)}) collective-permute-start(f32[88,192]{1,0:T(8,128)S(1)} %get-tuple-element.35), channel_id=1, source_target_pairs={{0,3},{1,2},{2,1},{3,0},{4,7},{5,6},{6,5},{7,4},{8,11},{9,10},{10,... | collective-permute-start | bytes 202760 | tf_op jit(solution)/shard_map/ppermute | solution.py:412
  42.9 0.5 collective-permute-start.6
  43.5 0.3 collective-permute-start.5
  43.8 0.1 add_convert_fusion.a_ref
  43.8 1.7 %collective-permute-start.11 = (bf16[192,768]{1,0:T(8,128)(2,1)S(1)}, bf16[192,768]{1,0:T(8,128)(2,1)S(1)}, u32[]{:S(2)}, u32[]{:S(2)}) collective-permute-start(bf16[192,768]{1,0:T(8,128)(2,1)S(1)} %add_convert_fusion.a_ref), channel_id=1, source_target_pairs={{0,8},{4,12},{8,0},{12,4},{1,9},{5,13},{9,1},{13,5},{2,10},{6,14},... | collective-permute-start | bytes 884744 | tf_op jit(solution)/shard_map/ppermute | solution.py:412
  45.6 1.1 %collective-permute-done.7 = f32[88,192]{1,0:T(8,128)S(1)} collective-permute-done((f32[88,192]{1,0:T(8,128)S(1)}, f32[88,192]{1,0:T(8,128)S(1)}, u32[]{:S(2)}, u32[]{:S(2)}) %collective-permute-start.7) | collective-permute-done | bytes 67616 | tf_op jit(solution)/shard_map/ppermute | solution.py:412
  46.7 2.1 %collective-permute-done.6 = f32[88,192]{1,0:T(8,128)S(1)} collective-permute-done((f32[88,192]{1,0:T(8,128)S(1)}, f32[88,192]{1,0:T(8,128)S(1)}, u32[]{:S(2)}, u32[]{:S(2)}) %collective-permute-start.6) | collective-permute-done | bytes 67616 | tf_op jit(solution)/shard_map/ppermute | solution.py:412
  48.8 0.5 collective-permute-start.8
  49.3 4.9 %collective-permute-done.8 = f32[88,192]{1,0:T(8,128)S(1)} collective-permute-done((f32[88,192]{1,0:T(8,128)S(1)}, f32[88,192]{1,0:T(8,128)S(1)}, u32[]{:S(2)}, u32[]{:S(2)}) %collective-permute-start.8) | collective-permute-done | bytes 67616 | tf_op jit(solution)/shard_map/ppermute | solution.py:412
  54.2 2.2 %collective-permute-start.9 = (f32[88,192]{1,0:T(8,128)S(1)}, f32[88,192]{1,0:T(8,128)S(1)}, u32[]{:S(2)}, u32[]{:S(2)}) collective-permute-start(f32[88,192]{1,0:T(8,128)S(1)} %add.18.sa_ref), channel_id=1, source_target_pairs={{0,8},{4,12},{8,0},{12,4},{1,9},{5,13},{9,1},{13,5},{2,10},{6,14},... | collective-permute-start | bytes 202760 | tf_op jit(solution)/shard_map/ppermute | solution.py:412
  56.5 0.9 %copy.13 = bf16[768,192]{0,1:T(8,128)(2,1)} copy(bf16[768,192]{1,0:T(8,128)(2,1)S(1)} %get-tuple-element.30) | data formatting | bytes 589824
  57.3 4.8 %collective-permute-done.11.b_ref = bf16[192,768]{1,0:T(8,128)(2,1)S(1)} collective-permute-done((bf16[192,768]{1,0:T(8,128)(2,1)S(1)}, bf16[192,768]{1,0:T(8,128)(2,1)S(1)}, u32[]{:S(2)}, u32[]{:S(2)}) %collective-permute-start.11) | collective-permute-done | bytes 294944 | tf_op jit(solution)/shard_map/ppermute | solution.py:412
  62.2 1.8 %shard_map.97._ = f32[2,192,768]{2,1,0:T(8,128)} custom-call(s32[4]{0:T(128)S(1)} %pad_add_fusion.2.scal, bf16[192,768]{1,0:T(8,128)(2,1)S(1)} %add_convert_fusion.a_ref, bf16[192,768]{1,0:T(8,128)(2,1)S(1)} %collective-permute-done.11.b_ref), custom_call_target="tpu_custom_call" | custom-call | flops 1048576 | bytes 2097152 | tf_op jit(solution)/shard_map/pallas_call | solution.py:523
  64.0 0.0 collective-permute-done.9.sb_ref
  64.0 2.2 %shard_map.98 = (f32[2,192,768]{2,1,0:T(8,128)}, f32[5,2,192]{2,1,0:T(2,128)}, f32[4,192]{1,0:T(4,128)}) custom-call(s32[4]{0:T(128)S(1)} %pad_add_fusion.2.scal, bf16[128,768]{1,0:T(8,128)(2,1)S(1)} %get-tuple-element.20.st_ref, f32[88,192]{1,0:T(8,128)S(1)} %add.18.sa_ref, ...), custom_call_target="tpu_custom_call", output_to_operand_aliasing={{0}: (4, {})} | custom-call | flops 16777216 | bytes 2097152 | tf_op jit(solution)/shard_map/pallas_call | solution.py:532
  (15 shorter events, 0.1 us)
Async XLA Ops:
  0.6 1.1 %copy-start = (bf16[2,768,192]{1,2,0:T(8,128)(2,1)S(1)}, bf16[2,768,192]{1,2,0:T(8,128)(2,1)}, u32[]{:S(2)}) copy-start(bf16[2,768,192]{1,2,0:T(8,128)(2,1)} %param.10) | copy-start | bytes 1769476
  1.7 0.7 %copy-start.1 = (bf16[2,5,192]{2,0,1:T(2,128)(2,1)S(1)}, bf16[2,5,192]{2,0,1:T(2,128)(2,1)}, u32[]{:S(2)}) copy-start(bf16[2,5,192]{2,0,1:T(2,128)(2,1)} %param.9) | copy-start | bytes 11524
  2.4 0.7 %copy-start.2 = (bf16[4,192]{1,0:T(4,128)(2,1)S(1)}, bf16[4,192]{1,0:T(4,128)(2,1)}, u32[]{:S(2)}) copy-start(bf16[4,192]{1,0:T(4,128)(2,1)} %embed_ref.1) | copy-start | bytes 4612
  3.2 10.5 %collective-permute-start.1 = (bf16[208,768]{1,0:T(8,128)(2,1)S(1)}, bf16[208,768]{1,0:T(8,128)(2,1)S(1)}, u32[]{:S(2)}, u32[]{:S(2)}) collective-permute-start(bf16[208,768]{1,0:T(8,128)(2,1)S(1)} %shard_map.93.refs_0_), channel_id=1, source_target_pairs={{0,2},{1,3},{2,0},{3,1},{4,6},{5,7},{6,4},{7,5},{8,10},{9,11},{10,... | collective-permute-start | bytes 958472 | tf_op jit(solution)/shard_map/ppermute | solution.py:412
  6.8 6.9 %collective-permute-start.3 = (s32[1,768]{1,0:T(1,128)S(1)}, s32[1,768]{1,0:T(1,128)S(1)}, u32[]{:S(2)}, u32[]{:S(2)}) collective-permute-start(s32[1,768]{1,0:T(1,128)S(1)} %reshape.11), channel_id=1, source_target_pairs={{0,4},{4,0},{8,12},{12,8},{1,5},{5,1},{9,13},{13,9},{2,6},{6,2},{1... | collective-permute-start | bytes 9224 | tf_op jit(solution)/shard_map/ppermute | solution.py:412
  8.4 12.4 %collective-permute-start = (bf16[208,768]{1,0:T(8,128)(2,1)S(1)}, bf16[208,768]{1,0:T(8,128)(2,1)S(1)}, u32[]{:S(2)}, u32[]{:S(2)}) collective-permute-start(bf16[208,768]{1,0:T(8,128)(2,1)S(1)} %shard_map.93.refs_0_), channel_id=1, source_target_pairs={{0,1},{1,0},{2,3},{3,2},{4,5},{5,4},{6,7},{7,6},{8,9},{9,8},{10,11... | collective-permute-start | bytes 958472 | tf_op jit(solution)/shard_map/ppermute | solution.py:412
  13.7 7.2 %collective-permute-start.2 = (bf16[208,768]{1,0:T(8,128)(2,1)S(1)}, bf16[208,768]{1,0:T(8,128)(2,1)S(1)}, u32[]{:S(2)}, u32[]{:S(2)}) collective-permute-start(bf16[208,768]{1,0:T(8,128)(2,1)S(1)} %collective-permute-done.1.refs_2_), channel_id=1, source_target_pairs={{0,1},{1,0},{2,3},{3,2},{4,5},{5,4},{6,7},{7,6},{8,9},{9,8},{10,11... | collective-permute-start | bytes 958472 | tf_op jit(solution)/shard_map/ppermute | solution.py:412
  13.7 5.8 %collective-permute-start.4 = (s32[2,768]{1,0:T(2,128)S(1)}, s32[2,768]{1,0:T(2,128)S(1)}, u32[]{:S(2)}, u32[]{:S(2)}) collective-permute-start(s32[2,768]{1,0:T(2,128)S(1)} %pad_add_fusion.1), channel_id=1, source_target_pairs={{0,8},{4,12},{8,0},{12,4},{1,9},{5,13},{9,1},{13,5},{2,10},{6,14},... | collective-permute-start | bytes 18440 | tf_op jit(solution)/shard_map/ppermute | solution.py:412
  30.1 13.7 %collective-permute-start.10 = (bf16[192,768]{1,0:T(8,128)(2,1)S(1)}, bf16[192,768]{1,0:T(8,128)(2,1)S(1)}, u32[]{:S(2)}, u32[]{:S(2)}) collective-permute-start(bf16[192,768]{1,0:T(8,128)(2,1)S(1)} %get-tuple-element.26), channel_id=1, source_target_pairs={{0,4},{4,0},{8,12},{12,8},{1,5},{5,1},{9,13},{13,9},{2,6},{6,2},{1... | collective-permute-start | bytes 884744 | tf_op jit(solution)/shard_map/ppermute | solution.py:412
  41.8 4.8 %collective-permute-start.7 = (f32[88,192]{1,0:T(8,128)S(1)}, f32[88,192]{1,0:T(8,128)S(1)}, u32[]{:S(2)}, u32[]{:S(2)}) collective-permute-start(f32[88,192]{1,0:T(8,128)S(1)} %get-tuple-element.35), channel_id=1, source_target_pairs={{0,3},{1,2},{2,1},{3,0},{4,7},{5,6},{6,5},{7,4},{8,11},{9,10},{10,... | collective-permute-start | bytes 202760 | tf_op jit(solution)/shard_map/ppermute | solution.py:412
  42.9 5.8 %collective-permute-start.6 = (f32[88,192]{1,0:T(8,128)S(1)}, f32[88,192]{1,0:T(8,128)S(1)}, u32[]{:S(2)}, u32[]{:S(2)}) collective-permute-start(f32[88,192]{1,0:T(8,128)S(1)} %get-tuple-element.36), channel_id=1, source_target_pairs={{0,2},{1,3},{2,0},{3,1},{4,6},{5,7},{6,4},{7,5},{8,10},{9,11},{10,... | collective-permute-start | bytes 202760 | tf_op jit(solution)/shard_map/ppermute | solution.py:412
  43.5 5.3 %collective-permute-start.5 = (f32[88,192]{1,0:T(8,128)S(1)}, f32[88,192]{1,0:T(8,128)S(1)}, u32[]{:S(2)}, u32[]{:S(2)}) collective-permute-start(f32[88,192]{1,0:T(8,128)S(1)} %get-tuple-element.34), channel_id=1, source_target_pairs={{0,1},{1,0},{2,3},{3,2},{4,5},{5,4},{6,7},{7,6},{8,9},{9,8},{10,11... | collective-permute-start | bytes 202760 | tf_op jit(solution)/shard_map/ppermute | solution.py:412
  43.8 18.3 %collective-permute-start.11 = (bf16[192,768]{1,0:T(8,128)(2,1)S(1)}, bf16[192,768]{1,0:T(8,128)(2,1)S(1)}, u32[]{:S(2)}, u32[]{:S(2)}) collective-permute-start(bf16[192,768]{1,0:T(8,128)(2,1)S(1)} %add_convert_fusion.a_ref), channel_id=1, source_target_pairs={{0,8},{4,12},{8,0},{12,4},{1,9},{5,13},{9,1},{13,5},{2,10},{6,14},... | collective-permute-start | bytes 884744 | tf_op jit(solution)/shard_map/ppermute | solution.py:412
  48.8 5.4 %collective-permute-start.8 = (f32[88,192]{1,0:T(8,128)S(1)}, f32[88,192]{1,0:T(8,128)S(1)}, u32[]{:S(2)}, u32[]{:S(2)}) collective-permute-start(f32[88,192]{1,0:T(8,128)S(1)} %fusion.2), channel_id=1, source_target_pairs={{0,4},{4,0},{8,12},{12,8},{1,5},{5,1},{9,13},{13,9},{2,6},{6,2},{1... | collective-permute-start | bytes 202760 | tf_op jit(solution)/shard_map/ppermute | solution.py:412
  54.2 9.8 %collective-permute-start.9 = (f32[88,192]{1,0:T(8,128)S(1)}, f32[88,192]{1,0:T(8,128)S(1)}, u32[]{:S(2)}, u32[]{:S(2)}) collective-permute-start(f32[88,192]{1,0:T(8,128)S(1)} %add.18.sa_ref), channel_id=1, source_target_pairs={{0,8},{4,12},{8,0},{12,4},{1,9},{5,13},{9,1},{13,5},{2,10},{6,14},... | collective-permute-start | bytes 202760 | tf_op jit(solution)/shard_map/ppermute | solution.py:412

commit v3 on v2

--- a/solution.py
+++ b/solution.py
@@ -21,7 +21,7 @@
 BF = jnp.bfloat16
 F32 = jnp.float32
 ROW_EMBED, ROW_TAPS0, ROW_TAPS1, TABLE = 0, BASES, BASES + TAPS, 16
-ROW_GT0, ROW_GT1, ROW_GE, SUMS = 2 * JB, 2 * JB + 8, 2 * JB + 16, 2 * JB + 24
+ROW_GE, ROW_R, ROW_GT0, ROW_GT1, SUMS = 20, 24, 48, 56, 64
 
 
 def dot(a, b, **kw):
@@ -113,24 +113,40 @@
     return out
 
 
-def pack_kernel(width, mix_ref, embed_ref, taps_ref, out_ref, sem):
-    copy = pltpu.make_async_copy(mix_ref.at[0], out_ref.at[pl.ds(0, width)], sem)
-    copy.start()
-    taps = taps_ref[...].astype(F32)
-    lines = [embed_ref[...].astype(F32)]
+def pack_kernel(width, mix_ref, embed_ref, taps_ref, out_ref, e_ref, t_ref, sems):
+    big = pltpu.make_async_copy(mix_ref.at[0], out_ref.at[pl.ds(0, width)], sems.at[0])
+    small = [
+        pltpu.make_async_copy(embed_ref, e_ref, sems.at[1]),
+        pltpu.make_async_copy(taps_ref, t_ref, sems.at[2]),
+    ]
+    for copy in small + [big]:
+        copy.start()
+    out_ref[width:, :] = jnp.zeros((TABLE, out_ref.shape[1]), BF)
+    for copy in small:
+        copy.wait()
+    taps = t_ref[...].astype(F32)
+    lines = [e_ref[...].astype(F32)]
     lines += [taps[j, block : block + 1, :] for block in range(BLOCKS) for j in range(TAPS)]
     lines.append(jnp.zeros((TABLE - BASES - 2 * TAPS, width), F32))
-    table = jnp.concatenate(lines, axis=0).astype(BF)
-    out_ref[width:, :] = jnp.zeros((TABLE, out_ref.shape[1]), BF)
-    out_ref[width:, :width] = table
-    copy.wait()
-
-
-def prep_kernel(n_chan, n_seq, rows, width, scal, tok_ref, mix_ref, a_ref, hot_ref, hot1_ref, mixl_ref):
-    me, place = scal[0], scal[1]
-    blocks = [mix_ref[0, :, k * width : (k + 1) * width] for k in range(n_chan)]
-    for k, block in enumerate(xor_blocks(blocks, me)):
+    out_ref[width:, :width] = jnp.concatenate(lines, axis=0).astype(BF)
+    big.wait()
+
+
+def local_kernel(n_chan, width, scal, mix_ref, cot_ref, mixl_ref, cotl_ref, m_ref, c_ref, sems):
+    first = pltpu.make_async_copy(mix_ref.at[1], m_ref, sems.at[0])
+    second = pltpu.make_async_copy(cot_ref, c_ref, sems.at[1])
+    first.start()
+    second.start()
+    first.wait()
+    blocks = [m_ref[:, k * width : (k + 1) * width] for k in range(n_chan)]
+    for k, block in enumerate(xor_blocks(blocks, scal[0])):
         mixl_ref[:, k * width : (k + 1) * width] = block
+    second.wait()
+    cotl_ref[...] = c_ref[...].astype(F32).T.astype(BF)
+
+
+def prep_kernel(n_seq, rows, scal, tok_ref, a_ref, hot_ref, hot1_ref):
+    place = scal[1]
 
     def line(block):
         inside = jnp.logical_and(block >= 0, block < n_seq)
@@ -244,8 +260,8 @@
 def backward_kernel(n_chan, rows, width, scale, scal, *refs):
     pks = refs[:n_chan]
     hot_ref, hot1_ref, mixl_ref, cot_ref, s_ref, x1_ref, gp_ref = refs[n_chan : n_chan + 7]
-    out_ref = refs[n_chan + 7]
-    p_ref, g2_ref, s0_ref, e_ref, et_ref, dw_ref, gt_ref, g1_ref, pb_ref, st_ref = refs[n_chan + 8 :]
+    keep_ref, send_ref = refs[n_chan + 7 : n_chan + 9]
+    p_ref, g2_ref, s0_ref, e_ref, et_ref, dw_ref, gt_ref, g1_ref, pb_ref, st_ref = refs[n_chan + 9 :]
     chans = n_chan * width
     tiles = chans // LANE
     ext = rows + 2 * REACH
@@ -353,15 +369,16 @@
         both = grads[kk][:JB] + flip_exact(grads[n_chan - 1 - kk][JB:], rev_w)
         table = tables[kk]
         lanes = slice(kk * width, (kk + 1) * width)
-        out_ref[kk, : 2 * JB, :] = dw_ref[:, lanes]
-        out_ref[kk, ROW_GT0 : ROW_GT0 + 8, :] = sums_of(sum_tap, both * dot(sel_e, table))
-        out_ref[kk, ROW_GT1 : ROW_GT1 + 8, :] = gt_ref[0, :, lanes]
         letters = sums_of(sum_letter, both * dot(sel_t, table)) + g1_ref[:, lanes]
         if kk == 0:
             zeros = jnp.zeros((BASES, width), F32)
             own = own_letters[HALF * BASES : (HALF + 1) * BASES, :]
             letters = letters + jnp.concatenate([own, zeros], axis=0)
-        out_ref[kk, ROW_GE : ROW_GE + 8, :] = letters
+        place = (keep_ref, send_ref)[kk % 2]
+        place[kk // 2, :ROW_R, :] = jnp.concatenate([dw_ref[:ROW_GE, lanes], letters[:BASES]], axis=0)
+        place[kk // 2, ROW_R : 2 * ROW_R, :] = dw_ref[JB : JB + ROW_R, lanes]
+        place[kk // 2, ROW_GT0 : ROW_GT0 + 8, :] = sums_of(sum_tap, both * dot(sel_e, table))
+        place[kk // 2, ROW_GT1 : ROW_GT1 + 8, :] = gt_ref[0, :, lanes]
 
 
 def mix1_kernel(n_chan, width, scal, a_ref, b_ref, out_ref, held, sem):
@@ -376,22 +393,32 @@
     copy.wait()
 
 
-def finish_kernel(n_chan, width, scal, st_ref, sa_ref, sb_ref, _, gm_ref, gt_ref, ge_ref, held, sem):
+def finish_kernel(n_chan, width, scal, st_ref, sa_ref, sb_ref, _, gm_ref, gt_ref, ge_ref, held, sems):
     sums = sa_ref[...] + sb_ref[...]
-    dw = sums[: 2 * JB].astype(BF)
-    held[...] = t_dot(dw, st_ref[: 2 * JB, :])
-    copy = pltpu.make_async_copy(held, gm_ref.at[0], sem)
-    copy.start()
+    fill = jnp.zeros((JB - ROW_GE, width), F32)
+    dw = jnp.concatenate([sums[:ROW_GE], fill, sums[ROW_R : ROW_R + ROW_GE], fill], axis=0).astype(BF)
+    copies = []
+    step = 2 * LANE
+    for i in range(n_chan * width // step):
+        lanes = pl.ds(i * step, step)
+        held[:, lanes] = t_dot(dw, st_ref[: 2 * JB, lanes])
+        copies.append(pltpu.make_async_copy(held.at[:, lanes], gm_ref.at[0, :, lanes], sems.at[i]))
+        copies[-1].start()
     for j in range(TAPS):
         gt_ref[j, 0:1, :] = sums[ROW_GT0 + j : ROW_GT0 + j + 1]
         gt_ref[j, 1:2, :] = sums[ROW_GT1 + j : ROW_GT1 + j + 1]
     ge_ref[...] = sums[ROW_GE : ROW_GE + BASES]
-    copy.wait()
+    for copy in copies:
+        copy.wait()
 
 
 VMEM = pl.BlockSpec(memory_space=pltpu.VMEM)
 SMEM = pl.BlockSpec(memory_space=pltpu.SMEM)
 HBM = pl.BlockSpec(memory_space=pltpu.HBM)
+
+
+def in_hbm(x):
+    return pltpu.with_memory_space_constraint(x, pltpu.HBM)
 
 
 def call(kernel, in_specs, out_shape, out_specs, scratch, limit, cost, aliases=None):
@@ -429,37 +456,52 @@
 
     (pk,) = call(
         functools.partial(pack_kernel, width),
-        [HBM, VMEM, VMEM],
+        [HBM, HBM, HBM],
         [shape((width + TABLE, chans), BF)],
         [VMEM],
-        [pltpu.SemaphoreType.DMA],
+        [
+            pltpu.VMEM((BASES, width), BF),
+            pltpu.VMEM((TAPS, BLOCKS, width), BF),
+            pltpu.SemaphoreType.DMA((3,)),
+        ],
         8,
         (0, width * chans * 4),
-    )(mix_t, embed, jnp.swapaxes(taps, 0, 1))
-    pks = [pk]
-    for bit in reversed(range(n_chan.bit_length() - 1)):
-        moved = [flip_bits(p, "chan", 1 << bit) for p in pks]
-        pks = [q for pair in zip(pks, moved) for q in pair]
+    )(in_hbm(mix_t), in_hbm(embed), in_hbm(jnp.swapaxes(taps, 0, 1)))
 
     letters = tokens.reshape(1, rows)
     seq_bits = n_seq.bit_length() - 1
     for bit in range(seq_bits):
         letters = jnp.concatenate([letters, flip_bits(letters, "seq", 1 << bit)], axis=0)
 
-    hot_t, hot, hot1, mixl = call(
-        functools.partial(prep_kernel, n_chan, n_seq, rows, width),
-        [SMEM, VMEM, VMEM],
+    mixl, cot = call(
+        functools.partial(local_kernel, n_chan, width),
+        [SMEM, HBM, HBM],
+        [shape((width, chans), BF), shape((rows, width), BF)],
+        [VMEM] * 2,
         [
-            shape((padded, 4 * JB), BF),
-            shape((2 * JB, padded), BF),
-            shape((2 * JB, rows), BF),
-            shape((width, chans), BF),
+            pltpu.VMEM((width, chans), BF),
+            pltpu.VMEM((width, rows), BF),
+            pltpu.SemaphoreType.DMA((2,)),
         ],
-        [VMEM] * 4,
+        16,
+        (1 << 20, 1 << 20),
+    )(scal, in_hbm(mix_t), in_hbm(cotangent.T))
+
+    pks = [pk]
+    for bit in reversed(range(n_chan.bit_length() - 1)):
+        ready = [pks[0]] + [lax.optimization_barrier((p, letters, mixl, cot))[0] for p in pks[1:]]
+        moved = [flip_bits(p, "chan", 1 << bit) for p in ready]
+        pks = [q for pair in zip(pks, moved) for q in pair]
+
+    hot_t, hot, hot1 = call(
+        functools.partial(prep_kernel, n_seq, rows),
+        [SMEM, VMEM],
+        [shape((padded, 4 * JB), BF), shape((2 * JB, padded), BF), shape((2 * JB, rows), BF)],
+        [VMEM] * 3,
         [],
         16,
         (1 << 20, 1 << 20),
-    )(scal, letters, mix_t[1:])
+    )(scal, letters)
 
     x2, gm1, s1, x1, gp, stack = call(
         functools.partial(forward_kernel, n_chan, rows, width, scale),
@@ -482,13 +524,13 @@
         ],
         32,
         (3 << 30, 8 << 20),
-    )(scal, *pks, hot_t, mixl, cotangent)
-
-    (sums,) = call(
+    )(scal, *pks, hot_t, mixl, cot)
+
+    keep, send = call(
         functools.partial(backward_kernel, n_chan, rows, width, scale),
         [SMEM] + [VMEM] * (n_chan + 7),
-        [shape((n_chan, SUMS, width), F32)],
-        [VMEM],
+        [shape((n_chan // 2, SUMS, width), F32)] * 2,
+        [VMEM] * 2,
         [
             pltpu.VMEM((tiles, rows + 2 * edge, LANE), F32),
             pltpu.VMEM((own_tiles, ext, LANE), F32),
@@ -503,20 +545,22 @@
         ],
         40,
         (3 << 30, 8 << 20),
-    )(scal, *pks, hot, hot1, mixl, cotangent, s1, x1, gp)
+    )(scal, *pks, hot, hot1, mixl, cot, s1, x1, gp)
 
     g_mine = gm1
-    for bit in range(seq_bits):
+    for bit in reversed(range(seq_bits)):
         g_other = flip_bits(g_mine, "seq", 1 << bit)
-        if bit < seq_bits - 1:
+        if bit:
             g_mine = lax.optimization_barrier(
                 (g_mine.astype(F32) + g_other.astype(F32)).astype(BF)
             )
-    pieces = [sums[0]] + [flip_bits(sums[k], "chan", k) for k in range(1, n_chan)]
-    s_mine = functools.reduce(jnp.add, pieces)
-    for bit in range(seq_bits):
+    s_mine = keep + flip_bits(send, "chan", 1)
+    for bit in range(1, n_chan.bit_length() - 1):
+        s_mine = s_mine[0::2] + flip_bits(s_mine[1::2], "chan", 1 << bit)
+    s_mine = s_mine[0]
+    for bit in reversed(range(seq_bits)):
         s_other = flip_bits(s_mine, "seq", 1 << bit)
-        if bit < seq_bits - 1:
+        if bit:
             s_mine = s_mine + s_other
 
     big = pltpu.VMEM((width, chans), F32)
@@ -538,7 +582,7 @@
             shape((BASES, width), F32),
         ],
         [HBM, VMEM, VMEM],
-        [big, pltpu.SemaphoreType.DMA],
+        [big, pltpu.SemaphoreType.DMA((chans // (2 * LANE),))],
         16,
         (1 << 24, 1 << 21),
         {4: 0},

time: 66.7 us -> 58 us (0.87)
  waiting for transfers between devices: 18.2 us -> 11.3 us
  local copies, waits for them, and re-layouts: 6.13 us -> 1.57 us
  Pallas kernels: 24.8 us -> 26.8 us
  starting transfers between devices: 15.5 us -> 16.2 us
    ppermute x12 -> x11, waiting for transfers between devices: 18.2 us -> 11.3 us  [flip_bits(): lax.ppermute(x, axis, [(i, i ^ mask) for i in range(lax.axis_size(axis))])]
    unnamed x8 -> x1, local copies, waits for them, and re-layouts: 4.43 us -> 0.87 us
    pallas_call x2 -> x3, Pallas kernels: 1.41 us -> 4.16 us  [the longest x1 1.98 us: body(): call(functools.partial(local_kernel, n_chan, width), [SMEM, HBM, HBM], [s...]
    slice x1, local copies, waits for them, and re-layouts: 0.98 us -> 0.01 us  [body(): s_mine = s_mine[0::2] + flip_bits(s_mine[1::2], 'chan', 1 << bit)]
    ppermute x12 -> x11, starting transfers between devices: 15.5 us -> 16.2 us  [flip_bits(): lax.ppermute(x, axis, [(i, i ^ mask) for i in range(lax.axis_size(axis))])]
  transfers between devices with their start and end apart: 12 -> 11, of which waited for: 5 -> 6; matrix products, arithmetic and copies ran while one was open for 7% -> 3% of each run, Pallas kernels for 20% -> 27%
where the time goes in v3:
time: 58 us; the launch traced here: 57.7 us
  Pallas kernels  26.8 us (46%)
  starting transfers between devices  16.2 us (28%)
  waiting for transfers between devices  11.3 us (19%)
  local copies, waits for them, and re-layouts  1.57 us (3%)
  between operations  0.91 us (2%)
  other arithmetic  0.88 us (2%)
    ppermute x11, starting transfers between devices, flip_bits(): lax.ppermute(x, axis, [(i, i ^ mask) for i in range(lax.axis_size(axis))])  16.2 us
    ppermute x11, waiting for transfers between devices, flip_bits(): lax.ppermute(x, axis, [(i, i ^ mask) for i in range(lax.axis_size(axis))])  11.3 us
    pallas_call x1, Pallas kernels, body(): call(functools.partial(backward_kernel, n_chan, rows, width, scale), [SME...  9.58 us
    pallas_call x1, Pallas kernels, body(): call(functools.partial(forward_kernel, n_chan, rows, width, scale), [SMEM...  9.05 us
    pallas_call x1, Pallas kernels, body(): call(functools.partial(finish_kernel, n_chan, width), [SMEM, VMEM, VMEM,...  2.19 us
    pallas_call x1, Pallas kernels, body(): call(functools.partial(local_kernel, n_chan, width), [SMEM, HBM, HBM], [s...  1.98 us
    pallas_call x1, Pallas kernels, body(): call(functools.partial(mix1_kernel, n_chan, width), [SMEM, VMEM, VMEM], [...  1.84 us
  transfers between devices with their start and end apart: 11, of which 6 were waited for; matrix products, arithmetic and copies ran while one was open for 3% of the time, Pallas kernels for 27%

profile of v3, /device:TPU:0, one launch (start us, length us, event | category | flops | bytes accessed | tf_op | source)
XLA Modules:
  0.0 57.7 jit_solution(1860288212427060745)
XLA Ops:
  0.6 0.7 %reshape.11 = s32[1,768]{1,0:T(1,128)S(1)} reshape(s32[768]{0:T(1024)} %param.6) | data formatting | bytes 6144 | tf_op jit(solution)/shard_map/reshape | solution.py:471
  1.3 3.0 %collective-permute-start.2 = (s32[1,768]{1,0:T(1,128)S(1)}, s32[1,768]{1,0:T(1,128)S(1)}, u32[]{:S(2)}, u32[]{:S(2)}) collective-permute-start(s32[1,768]{1,0:T(1,128)S(1)} %reshape.11), channel_id=1, source_target_pairs={{0,4},{4,0},{8,12},{12,8},{1,5},{5,1},{9,13},{13,9},{2,6},{6,2},{1... | collective-permute-start | bytes 9224 | tf_op jit(solution)/shard_map/ppermute | solution.py:439
  4.3 1.0 %shard_map.93.refs_0_ = bf16[208,768]{1,0:T(8,128)(2,1)S(1)} custom-call(bf16[2,192,768]{2,1,0:T(8,128)(2,1)} %bitcast.10, bf16[4,192]{1,0:T(4,128)(2,1)} %embed_ref.1, bf16[5,2,192]{2,1,0:T(2,128)(2,1)} %bitcast.13), custom_call_target="tpu_custom_call" | custom-call | bytes 589824 | tf_op jit(solution)/shard_map/pallas_call | solution.py:457
  5.4 1.6 %collective-permute-start.1 = (bf16[208,768]{1,0:T(8,128)(2,1)S(1)}, bf16[208,768]{1,0:T(8,128)(2,1)S(1)}, u32[]{:S(2)}, u32[]{:S(2)}) collective-permute-start(bf16[208,768]{1,0:T(8,128)(2,1)S(1)} %shard_map.93.refs_0_), channel_id=1, source_target_pairs={{0,2},{1,3},{2,0},{3,1},{4,6},{5,7},{6,4},{7,5},{8,10},{9,11},{10,... | collective-permute-start | bytes 958472 | tf_op jit(solution)/shard_map/ppermute | solution.py:439
  6.9 0.0 collective-permute-start
  6.9 0.0 collective-permute-done.2
  6.9 2.7 %collective-permute-start.3 = (s32[2,768]{1,0:T(2,128)S(1)}, s32[2,768]{1,0:T(2,128)S(1)}, u32[]{:S(2)}, u32[]{:S(2)}) collective-permute-start(s32[2,768]{1,0:T(2,128)S(1)} %pad_add_fusion.1), channel_id=1, source_target_pairs={{0,8},{4,12},{8,0},{12,4},{1,9},{5,13},{9,1},{13,5},{2,10},{6,14},... | collective-permute-start | bytes 18440 | tf_op jit(solution)/shard_map/ppermute | solution.py:439
  9.6 0.7 %pad_add_fusion.2.scal = s32[4]{0:T(128)S(1)} fusion(s32[2]{0:T(128)} %param.11, s32[1]{0:T(128)} %bitcast.1, s32[1]{0:T(128)} %bitcast), kind=kLoop, calls=%fused_computation.5 | loop fusion | flops 8 | bytes 32 | tf_op jit(solution)/shard_map/concatenate | solution.py:454
  10.3 2.0 %shard_map.94 = (bf16[192,768]{1,0:T(8,128)(2,1)S(1)}, bf16[768,192]{1,0:T(8,128)(2,1)S(1)}) custom-call(s32[4]{0:T(128)S(1)} %pad_add_fusion.2.scal, bf16[2,192,768]{2,1,0:T(8,128)(2,1)} %bitcast.11, bf16[192,768]{1,0:T(8,128)(2,1)} %bitcast.12), custom_call_target="tpu_custom_call" | custom-call | flops 1048576 | bytes 1048576 | tf_op jit(solution)/shard_map/pallas_call | solution.py:476
  12.3 0.0 collective-permute-done.3
  12.4 2.1 %collective-permute-done.1.refs_2_ = bf16[208,768]{1,0:T(8,128)(2,1)S(1)} collective-permute-done((bf16[208,768]{1,0:T(8,128)(2,1)S(1)}, bf16[208,768]{1,0:T(8,128)(2,1)S(1)}, u32[]{:S(2)}, u32[]{:S(2)}) %collective-permute-start.1) | collective-permute-done | bytes 319520 | tf_op jit(solution)/shard_map/ppermute | solution.py:439
  14.4 0.0 collective-permute-start.4
  14.4 1.2 %shard_map.95 = (bf16[896,128]{1,0:T(8,128)(2,1)S(1)}, bf16[64,896]{1,0:T(8,128)(2,1)S(1)}, bf16[64,768]{1,0:T(8,128)(2,1)S(1)}) custom-call(s32[4]{0:T(128)S(1)} %pad_add_fusion.2.scal, s32[4,768]{1,0:T(4,128)S(1)} %pad_add_fusion.tok_ref), custom_call_target="tpu_custom_call" | custom-call | flops 1048576 | bytes 1048576 | tf_op jit(solution)/shard_map/pallas_call | solution.py:496
  15.6 0.4 collective-permute-done.4.refs_3_
  16.1 9.1 %shard_map.96 = (bf16[768,192]{1,0:T(8,128)(2,1)S(1)}, bf16[192,768]{1,0:T(8,128)(2,1)S(1)}, bf16[768,192]{1,0:T(8,128)(2,1)S(1)}, f32[2,6,800,128]{3,2,1,0:T(8,...) custom-call(s32[4]{0:T(128)S(1)} %pad_add_fusion.2.scal, ...), custom_call_target="tpu_custom_call" | custom-call | flops 3221225472 | bytes 8388608 | tf_op jit(solution)/shard_map/pallas_call | solution.py:506
  25.1 2.7 %collective-permute-start.9 = (bf16[192,768]{1,0:T(8,128)(2,1)S(1)}, bf16[192,768]{1,0:T(8,128)(2,1)S(1)}, u32[]{:S(2)}, u32[]{:S(2)}) collective-permute-start(bf16[192,768]{1,0:T(8,128)(2,1)S(1)} %get-tuple-element.34), channel_id=1, source_target_pairs={{0,8},{4,12},{8,0},{12,4},{1,9},{5,13},{9,1},{13,5},{2,10},{6,14},... | collective-permute-start | bytes 884744 | tf_op jit(solution)/shard_map/ppermute | solution.py:439
  27.8 9.6 %shard_map.97 = (f32[2,64,192]{2,1,0:T(8,128)S(1)}, f32[2,64,192]{2,1,0:T(8,128)S(1)}) custom-call(s32[4]{0:T(128)S(1)} %pad_add_fusion.2.scal, bf16[208,768]{1,0:T(8,128)(2,1)S(1)} %shard_map.93.refs_0_, bf16[208,768]{1,0:T(8,128)(2,1)S(1)} %collective-permute-done.refs_1_, bf16[208,768]{1,0:T(8,128)(2,1)S(1)} %collective-permute-done.1.refs_2_, ...), custom_call_target="tpu_custom_call" | custom-call | flops 3221225472 | bytes 8388608 | tf_op jit(solution)/shard_map/pallas_call | solution.py:529
  37.4 0.0 collective-permute-start.5
  37.4 1.3 %collective-permute-done.5 = f32[2,64,192]{2,1,0:T(8,128)S(1)} collective-permute-done((f32[2,64,192]{2,1,0:T(8,128)S(1)}, f32[2,64,192]{2,1,0:T(8,128)S(1)}, u32[]{:S(2)}, u32[]{:S(2)}) %collective-permute-start.5) | collective-permute-done | bytes 98336 | tf_op jit(solution)/shard_map/ppermute | solution.py:439
  38.8 1.5 %collective-permute-start.6 = (f32[1,64,192]{2,1,0:T(8,128)S(1)}, f32[1,64,192]{2,1,0:T(8,128)S(1)}, u32[]{:S(2)}, u32[]{:S(2)}) collective-permute-start(f32[1,64,192]{2,1,0:T(8,128)S(1)} %slice.11), channel_id=1, source_target_pairs={{0,2},{1,3},{2,0},{3,1},{4,6},{5,7},{6,4},{7,5},{8,10},{9,11},{10,... | collective-permute-start | bytes 147464 | tf_op jit(solution)/shard_map/ppermute | solution.py:439
  40.3 1.0 %collective-permute-done.9 = bf16[192,768]{1,0:T(8,128)(2,1)S(1)} collective-permute-done((bf16[192,768]{1,0:T(8,128)(2,1)S(1)}, bf16[192,768]{1,0:T(8,128)(2,1)S(1)}, u32[]{:S(2)}, u32[]{:S(2)}) %collective-permute-start.9) | collective-permute-done | bytes 294944 | tf_op jit(solution)/shard_map/ppermute | solution.py:439
  41.3 0.1 add_convert_fusion.a_ref
  41.4 0.1 collective-permute-start.10
  41.4 1.7 %collective-permute-done.6 = f32[1,64,192]{2,1,0:T(8,128)S(1)} collective-permute-done((f32[1,64,192]{2,1,0:T(8,128)S(1)}, f32[1,64,192]{2,1,0:T(8,128)S(1)}, u32[]{:S(2)}, u32[]{:S(2)}) %collective-permute-start.6) | collective-permute-done | bytes 49184 | tf_op jit(solution)/shard_map/ppermute | solution.py:439
  43.1 1.6 %collective-permute-start.7 = (f32[64,192]{1,0:T(8,128)S(1)}, f32[64,192]{1,0:T(8,128)S(1)}, u32[]{:S(2)}, u32[]{:S(2)}) collective-permute-start(f32[64,192]{1,0:T(8,128)S(1)} %fusion), channel_id=1, source_target_pairs={{0,8},{4,12},{8,0},{12,4},{1,9},{5,13},{9,1},{13,5},{2,10},{6,14},... | collective-permute-start | bytes 147464 | tf_op jit(solution)/shard_map/ppermute | solution.py:439
  44.7 4.9 %collective-permute-done.7 = f32[64,192]{1,0:T(8,128)S(1)} collective-permute-done((f32[64,192]{1,0:T(8,128)S(1)}, f32[64,192]{1,0:T(8,128)S(1)}, u32[]{:S(2)}, u32[]{:S(2)}) %collective-permute-start.7) | collective-permute-done | bytes 49184 | tf_op jit(solution)/shard_map/ppermute | solution.py:439
  49.6 3.0 %collective-permute-start.8 = (f32[64,192]{1,0:T(8,128)S(1)}, f32[64,192]{1,0:T(8,128)S(1)}, u32[]{:S(2)}, u32[]{:S(2)}) collective-permute-start(f32[64,192]{1,0:T(8,128)S(1)} %add.14.sa_ref), channel_id=1, source_target_pairs={{0,4},{4,0},{8,12},{12,8},{1,5},{5,1},{9,13},{13,9},{2,6},{6,2},{1... | collective-permute-start | bytes 147464 | tf_op jit(solution)/shard_map/ppermute | solution.py:439
  52.6 0.9 %copy.11 = bf16[768,192]{0,1:T(8,128)(2,1)} copy(bf16[768,192]{1,0:T(8,128)(2,1)S(1)} %get-tuple-element.38) | data formatting | bytes 589824
  53.5 0.0 collective-permute-done.10.b_ref
  53.5 1.8 %shard_map.98._ = f32[2,192,768]{2,1,0:T(8,128)} custom-call(s32[4]{0:T(128)S(1)} %pad_add_fusion.2.scal, bf16[192,768]{1,0:T(8,128)(2,1)S(1)} %add_convert_fusion.a_ref, bf16[192,768]{1,0:T(8,128)(2,1)S(1)} %collective-permute-done.10.b_ref), custom_call_target="tpu_custom_call" | custom-call | flops 1048576 | bytes 2097152 | tf_op jit(solution)/shard_map/pallas_call | solution.py:567
  55.3 0.0 collective-permute-done.8.sb_ref
  55.3 2.2 %shard_map.99 = (f32[2,192,768]{2,1,0:T(8,128)}, f32[5,2,192]{2,1,0:T(2,128)}, f32[4,192]{1,0:T(4,128)}) custom-call(s32[4]{0:T(128)S(1)} %pad_add_fusion.2.scal, bf16[128,768]{1,0:T(8,128)(2,1)S(1)} %get-tuple-element.26.st_ref, f32[64,192]{1,0:T(8,128)S(1)} %add.14.sa_ref, ...), custom_call_target="tpu_custom_call", output_to_operand_aliasing={{0}: (4, {})} | custom-call | flops 16777216 | bytes 2097152 | tf_op jit(solution)/shard_map/pallas_call | solution.py:576
  (7 shorter events, 0.1 us)
Async XLA Ops:
  1.3 5.6 %collective-permute-start.2 = (s32[1,768]{1,0:T(1,128)S(1)}, s32[1,768]{1,0:T(1,128)S(1)}, u32[]{:S(2)}, u32[]{:S(2)}) collective-permute-start(s32[1,768]{1,0:T(1,128)S(1)} %reshape.11), channel_id=1, source_target_pairs={{0,4},{4,0},{8,12},{12,8},{1,5},{5,1},{9,13},{13,9},{2,6},{6,2},{1... | collective-permute-start | bytes 9224 | tf_op jit(solution)/shard_map/ppermute | solution.py:439
  5.4 9.1 %collective-permute-start.1 = (bf16[208,768]{1,0:T(8,128)(2,1)S(1)}, bf16[208,768]{1,0:T(8,128)(2,1)S(1)}, u32[]{:S(2)}, u32[]{:S(2)}) collective-permute-start(bf16[208,768]{1,0:T(8,128)(2,1)S(1)} %shard_map.93.refs_0_), channel_id=1, source_target_pairs={{0,2},{1,3},{2,0},{3,1},{4,6},{5,7},{6,4},{7,5},{8,10},{9,11},{10,... | collective-permute-start | bytes 958472 | tf_op jit(solution)/shard_map/ppermute | solution.py:439
  6.9 8.7 %collective-permute-start = (bf16[208,768]{1,0:T(8,128)(2,1)S(1)}, bf16[208,768]{1,0:T(8,128)(2,1)S(1)}, u32[]{:S(2)}, u32[]{:S(2)}) collective-permute-start(bf16[208,768]{1,0:T(8,128)(2,1)S(1)} %shard_map.93.refs_0_), channel_id=1, source_target_pairs={{0,1},{1,0},{2,3},{3,2},{4,5},{5,4},{6,7},{7,6},{8,9},{9,8},{10,11... | collective-permute-start | bytes 958472 | tf_op jit(solution)/shard_map/ppermute | solution.py:439
  6.9 5.4 %collective-permute-start.3 = (s32[2,768]{1,0:T(2,128)S(1)}, s32[2,768]{1,0:T(2,128)S(1)}, u32[]{:S(2)}, u32[]{:S(2)}) collective-permute-start(s32[2,768]{1,0:T(2,128)S(1)} %pad_add_fusion.1), channel_id=1, source_target_pairs={{0,8},{4,12},{8,0},{12,4},{1,9},{5,13},{9,1},{13,5},{2,10},{6,14},... | collective-permute-start | bytes 18440 | tf_op jit(solution)/shard_map/ppermute | solution.py:439
  14.4 1.6 %collective-permute-start.4 = (bf16[208,768]{1,0:T(8,128)(2,1)S(1)}, bf16[208,768]{1,0:T(8,128)(2,1)S(1)}, u32[]{:S(2)}, u32[]{:S(2)}) collective-permute-start(bf16[208,768]{1,0:T(8,128)(2,1)S(1)} %collective-permute-done.1.refs_2_), channel_id=1, source_target_pairs={{0,1},{1,0},{2,3},{3,2},{4,5},{5,4},{6,7},{7,6},{8,9},{9,8},{10,11... | collective-permute-start | bytes 958472 | tf_op jit(solution)/shard_map/ppermute | solution.py:439
  25.1 16.2 %collective-permute-start.9 = (bf16[192,768]{1,0:T(8,128)(2,1)S(1)}, bf16[192,768]{1,0:T(8,128)(2,1)S(1)}, u32[]{:S(2)}, u32[]{:S(2)}) collective-permute-start(bf16[192,768]{1,0:T(8,128)(2,1)S(1)} %get-tuple-element.34), channel_id=1, source_target_pairs={{0,8},{4,12},{8,0},{12,4},{1,9},{5,13},{9,1},{13,5},{2,10},{6,14},... | collective-permute-start | bytes 884744 | tf_op jit(solution)/shard_map/ppermute | solution.py:439
  37.4 1.4 %collective-permute-start.5 = (f32[2,64,192]{2,1,0:T(8,128)S(1)}, f32[2,64,192]{2,1,0:T(8,128)S(1)}, u32[]{:S(2)}, u32[]{:S(2)}) collective-permute-start(f32[2,64,192]{2,1,0:T(8,128)S(1)} %get-tuple-element.33), channel_id=1, source_target_pairs={{0,1},{1,0},{2,3},{3,2},{4,5},{5,4},{6,7},{7,6},{8,9},{9,8},{10,11... | collective-permute-start | bytes 294920 | tf_op jit(solution)/shard_map/ppermute | solution.py:439
  38.8 4.3 %collective-permute-start.6 = (f32[1,64,192]{2,1,0:T(8,128)S(1)}, f32[1,64,192]{2,1,0:T(8,128)S(1)}, u32[]{:S(2)}, u32[]{:S(2)}) collective-permute-start(f32[1,64,192]{2,1,0:T(8,128)S(1)} %slice.11), channel_id=1, source_target_pairs={{0,2},{1,3},{2,0},{3,1},{4,6},{5,7},{6,4},{7,5},{8,10},{9,11},{10,... | collective-permute-start | bytes 147464 | tf_op jit(solution)/shard_map/ppermute | solution.py:439
  41.4 12.1 %collective-permute-start.10 = (bf16[192,768]{1,0:T(8,128)(2,1)S(1)}, bf16[192,768]{1,0:T(8,128)(2,1)S(1)}, u32[]{:S(2)}, u32[]{:S(2)}) collective-permute-start(bf16[192,768]{1,0:T(8,128)(2,1)S(1)} %add_convert_fusion.a_ref), channel_id=1, source_target_pairs={{0,4},{4,0},{8,12},{12,8},{1,5},{5,1},{9,13},{13,9},{2,6},{6,2},{1... | collective-permute-start | bytes 884744 | tf_op jit(solution)/shard_map/ppermute | solution.py:439
  43.1 6.5 %collective-permute-start.7 = (f32[64,192]{1,0:T(8,128)S(1)}, f32[64,192]{1,0:T(8,128)S(1)}, u32[]{:S(2)}, u32[]{:S(2)}) collective-permute-start(f32[64,192]{1,0:T(8,128)S(1)} %fusion), channel_id=1, source_target_pairs={{0,8},{4,12},{8,0},{12,4},{1,9},{5,13},{9,1},{13,5},{2,10},{6,14},... | collective-permute-start | bytes 147464 | tf_op jit(solution)/shard_map/ppermute | solution.py:439
  49.6 5.7 %collective-permute-start.8 = (f32[64,192]{1,0:T(8,128)S(1)}, f32[64,192]{1,0:T(8,128)S(1)}, u32[]{:S(2)}, u32[]{:S(2)}) collective-permute-start(f32[64,192]{1,0:T(8,128)S(1)} %add.14.sa_ref), channel_id=1, source_target_pairs={{0,4},{4,0},{8,12},{12,8},{1,5},{5,1},{9,13},{13,9},{2,6},{6,2},{1... | collective-permute-start | bytes 147464 | tf_op jit(solution)/shard_map/ppermute | solution.py:439

commit v4 on v3

--- a/solution.py
+++ b/solution.py
@@ -132,21 +132,21 @@
     big.wait()
 
 
-def local_kernel(n_chan, width, scal, mix_ref, cot_ref, mixl_ref, cotl_ref, m_ref, c_ref, sems):
+def local_kernel(n_chan, width, mix_ref, cot_ref, mixl_ref, cotl_ref, m_ref, c_ref, sems):
     first = pltpu.make_async_copy(mix_ref.at[1], m_ref, sems.at[0])
     second = pltpu.make_async_copy(cot_ref, c_ref, sems.at[1])
     first.start()
     second.start()
     first.wait()
     blocks = [m_ref[:, k * width : (k + 1) * width] for k in range(n_chan)]
-    for k, block in enumerate(xor_blocks(blocks, scal[0])):
+    for k, block in enumerate(xor_blocks(blocks, lax.axis_index("chan"))):
         mixl_ref[:, k * width : (k + 1) * width] = block
     second.wait()
     cotl_ref[...] = c_ref[...].astype(F32).T.astype(BF)
 
 
-def prep_kernel(n_seq, rows, scal, tok_ref, a_ref, hot_ref, hot1_ref):
-    place = scal[1]
+def prep_kernel(n_seq, rows, dils, tok_ref, a_ref, hot_ref, hot1_ref):
+    place = lax.axis_index("seq")
 
     def line(block):
         inside = jnp.logical_and(block >= 0, block < n_seq)
@@ -174,20 +174,22 @@
                 out.append(pltpu.roll(source, total - first, 1)[:1, :count])
         return out
 
-    hot = one_hot_t(windows(scal[2], REACH, a_ref.shape[0]))
+    hot = one_hot_t(windows(dils[0], REACH, a_ref.shape[0]))
     a_ref[...] = jnp.concatenate([hot, hot], axis=0).T.astype(BF)
     hot_ref[...] = hot.astype(BF)
-    hot1_ref[...] = one_hot_t(windows(scal[3], 0, rows)).astype(BF)
-
-
-def forward_kernel(n_chan, rows, width, scale, scal, *refs):
-    pks = refs[:n_chan]
-    a_ref, mixl_ref, cot_ref = refs[n_chan : n_chan + 3]
-    x2_ref, gm_ref, s_ref, x1_ref, gp_ref, st_ref = refs[n_chan + 3 : n_chan + 9]
-    w_ref, e_ref, wt_ref, et_ref, m_ref = refs[n_chan + 9 :]
+    hot1_ref[...] = one_hot_t(windows(dils[1], 0, rows)).astype(BF)
+
+
+def forward_kernel(n_chan, rows, width, scale, dils, *refs):
     tiles = n_chan * width // LANE
+    pks, refs = refs[:n_chan], refs[n_chan:]
+    (a_ref, mixl_ref, cot_ref), refs = refs[:3], refs[3:]
+    (x2_ref, gm_ref, s_ref, st_ref, e_ref, et_ref), refs = refs[:6], refs[6:]
+    x1_refs, refs = (refs[:tiles], refs[tiles : 2 * tiles]), refs[2 * tiles :]
+    gp_refs, refs = (refs[:tiles], refs[tiles : 2 * tiles]), refs[2 * tiles :]
+    w_ref, wt_ref, m_ref, held, sem = refs
     ext = rows + 2 * REACH
-    me, dil = scal[0], scal[3]
+    me, dil = lax.axis_index("chan"), dils[1]
     rev, rev_w = reversal(LANE), reversal(width)
 
     tables = [pk[width:, :width] for pk in pks]
@@ -213,67 +215,61 @@
     centre = HALF * BASES
     pick_f = as_bf((row - centre == col) & (col < BASES))
     pick_r = as_bf((row - centre - JB == col) & (col < BASES))
-    chunk = ext // 5
+    chunk, mchunk = ext // 5, rows // 6
     for t in range(tiles):
         dst = slice(t * LANE, (t + 1) * LANE)
         for strand, (wr, er, pick) in enumerate(((w_ref, e_ref, pick_f), (wt_ref, et_ref, pick_r))):
             rhs = jnp.concatenate([wr[:, dst], dot(pick, er[:, dst]).astype(BF)], axis=1)
-
             for i in range(5):
                 where = pl.ds(i * chunk, chunk)
                 both = dot(a_ref[where, :], rhs)
                 value, slope = gelu_parts(both[:, :LANE])
-                x1 = (both[:, LANE:] + value).astype(BF).astype(F32)
-                x1_ref[strand, t, where, :] = x1
-                gp_ref[strand, t, where, :] = slope.astype(BF)
-
-    mchunk = rows // 6
-    for t in range(tiles):
-        dst = slice(t * LANE, (t + 1) * LANE)
+                x1_refs[strand][t][where, :] = both[:, LANE:] + value
+                gp_refs[strand][t][where, :] = slope.astype(BF)
+
         taps_f = e_ref[:, dst].astype(F32)
         taps_r = et_ref[:, dst].astype(F32)
-
         for i in range(6):
             first = i * mchunk
-            u = jnp.zeros((mchunk, LANE), F32)
-            v = jnp.zeros((mchunk, LANE), F32)
+            total = jnp.zeros((mchunk, LANE), F32)
             for j in range(TAPS):
                 shift = (j - HALF) * dil
-                u += taps_f[ROW_TAPS1 + j : ROW_TAPS1 + j + 1, :] * x1_ref[0, t, pl.ds(first + REACH + shift, mchunk), :]
-                v += taps_r[ROW_TAPS1 + j : ROW_TAPS1 + j + 1, :] * x1_ref[1, t, pl.ds(first + REACH - shift, mchunk), :]
-            total = u.astype(BF).astype(F32) + v.astype(BF).astype(F32)
+                line = slice(ROW_TAPS1 + j, ROW_TAPS1 + j + 1)
+                total += taps_f[line, :] * x1_refs[0][t][pl.ds(first + REACH + shift, mchunk), :]
+                total += taps_r[line, :] * x1_refs[1][t][pl.ds(first + REACH - shift, mchunk), :]
             m_ref[first : first + mchunk, dst] = total.astype(BF)
 
     half = rows // 2
+    n_own = pl.cdiv(width, LANE)
     for i in range(2):
         where = pl.ds(i * half, half)
         value, slope = gelu_parts(dot_t(m_ref[where, :], mixl_ref[...]))
         inner = pl.ds(REACH + i * half, half)
-        n_own = pl.cdiv(width, LANE)
-        own = jnp.concatenate([x1_ref[0, t, inner, :] for t in range(n_own)], axis=1)[:, :width]
-        x2_ref[where, :] = (own + value).astype(BF)
+        own = jnp.concatenate([x1_refs[0][t][inner, :] for t in range(n_own)], axis=1)[:, :width]
+        held[:, where] = (own + value).T.astype(BF)
         s_ref[where, :] = ((cot_ref[where, :].astype(F32) * scale) * slope).astype(BF)
+    copy = pltpu.make_async_copy(held, x2_ref, sem)
+    copy.start()
 
     gm_ref[...] = t_dot(s_ref[...], m_ref[...]).astype(BF)
-
-
-def backward_kernel(n_chan, rows, width, scale, scal, *refs):
-    pks = refs[:n_chan]
-    hot_ref, hot1_ref, mixl_ref, cot_ref, s_ref, x1_ref, gp_ref = refs[n_chan : n_chan + 7]
-    keep_ref, send_ref = refs[n_chan + 7 : n_chan + 9]
-    p_ref, g2_ref, s0_ref, e_ref, et_ref, dw_ref, gt_ref, g1_ref, pb_ref, st_ref = refs[n_chan + 9 :]
+    copy.wait()
+
+
+def backward_kernel(n_chan, rows, width, scale, dils, *refs):
     chans = n_chan * width
     tiles = chans // LANE
+    pks, refs = refs[:n_chan], refs[n_chan:]
+    (hot_ref, hot1_ref, mixl_ref, cot_ref, s_ref, e_ref, et_ref), refs = refs[:7], refs[7:]
+    x1_refs, refs = (refs[:tiles], refs[tiles : 2 * tiles]), refs[2 * tiles :]
+    gp_refs, refs = (refs[:tiles], refs[tiles : 2 * tiles]), refs[2 * tiles :]
+    (keep_ref, send_ref), refs = refs[:2], refs[2:]
+    p_refs, s0_refs, refs = refs[:tiles], refs[tiles : 2 * tiles], refs[2 * tiles :]
+    g2_ref, dw_ref, gt_ref, g1_ref, pb_ref, st_ref = refs
     ext = rows + 2 * REACH
     padded = hot_ref.shape[1]
-    me, dil = scal[0], scal[3]
+    me, dil = lax.axis_index("chan"), dils[1]
     rev, rev_w = reversal(LANE), reversal(width)
     tables = [pk[width:, :width] for pk in pks]
-    for k in range(n_chan):
-        e_ref[:, k * width : (k + 1) * width] = tables[k]
-    for t in range(tiles):
-        src = slice((tiles - 1 - t) * LANE, (tiles - t) * LANE)
-        et_ref[:, t * LANE : (t + 1) * LANE] = dot(e_ref[:, src], rev).astype(BF)
 
     edge = 2 * REACH
     n_own = pl.cdiv(width, LANE)
@@ -283,20 +279,21 @@
     g2 = jnp.concatenate([g2, jnp.zeros((rows, n_own * LANE - width), F32)], axis=1)
     for t in range(n_own):
         g2_ref[t, REACH : rows + REACH, :] = g2[:, t * LANE : (t + 1) * LANE]
-    s0_ref[:, ext:, :] = jnp.zeros((2, padded - ext, chans), BF)
-    for t in range(tiles):
-        p_ref[t, :edge, :] = jnp.zeros((edge, LANE), F32)
-        p_ref[t, rows + edge :, :] = jnp.zeros((edge, LANE), F32)
-        part = dot(s_ref[...], mixl_ref[:, t * LANE : (t + 1) * LANE])
-        p_ref[t, edge : rows + edge, :] = part
-        pb_ref[:, t * LANE : (t + 1) * LANE] = part.astype(BF)
 
     mchunk, chunk = rows // 6, ext // 5
+    others = [None] * tiles
     for t in range(tiles):
         dst = slice(t * LANE, (t + 1) * LANE)
+        p_ref, s0_ref = p_refs[t], s0_refs[t]
+        if t % 2 == 0:
+            pair = dot(s_ref[...], mixl_ref[:, t * LANE : (t + 2) * LANE])
+            pb_ref[:, t * LANE : (t + 2) * LANE] = pair.astype(BF)
+        p_ref[:edge, :] = jnp.zeros((edge, LANE), F32)
+        p_ref[rows + edge :, :] = jnp.zeros((edge, LANE), F32)
+        p_ref[edge : rows + edge, :] = pair[:, (t % 2) * LANE : (t % 2 + 1) * LANE]
+        s0_ref[ext:, :] = jnp.zeros((padded - ext, 2 * LANE), BF)
         taps_f = e_ref[:, dst].astype(F32)
         taps_r = et_ref[:, dst].astype(F32)
-
         for i in range(5):
             first = i * chunk
             where = pl.ds(first, chunk)
@@ -304,36 +301,31 @@
             r = jnp.zeros((chunk, LANE), F32)
             for j in range(TAPS):
                 shift = (j - HALF) * dil
-                tap_f = taps_f[ROW_TAPS1 + j : ROW_TAPS1 + j + 1, :]
-                tap_r = taps_r[ROW_TAPS1 + j : ROW_TAPS1 + j + 1, :]
-                f += tap_f * p_ref[t, pl.ds(first + REACH - shift, chunk), :]
-                r += tap_r * p_ref[t, pl.ds(first + REACH + shift, chunk), :]
+                line = slice(ROW_TAPS1 + j, ROW_TAPS1 + j + 1)
+                f += taps_f[line, :] * p_ref[pl.ds(first + REACH - shift, chunk), :]
+                r += taps_r[line, :] * p_ref[pl.ds(first + REACH + shift, chunk), :]
             if t < n_own:
                 f += g2_ref[t, where, :]
-            s0_ref[0, where, dst] = (f * gp_ref[0, t, where, :].astype(F32)).astype(BF)
-            s0_ref[1, where, dst] = (r * gp_ref[1, t, where, :].astype(F32)).astype(BF)
-
-        def taps_step(i, carry, t=t):
+            s0_ref[where, :LANE] = (f * gp_refs[0][t][where, :].astype(F32)).astype(BF)
+            s0_ref[where, LANE:] = (r * gp_refs[1][t][where, :].astype(F32)).astype(BF)
+        both = dot(hot_ref[...], s0_ref[...])
+        dw_ref[:, dst] = both[:, :LANE]
+        others[t] = both[:, LANE:]
+
+        sums = [jnp.zeros((8, LANE), F32) for _ in range(2 * TAPS)]
+        for i in range(6):
             first = i * mchunk
-            here = p_ref[t, pl.ds(edge + first, mchunk), :]
-            out = []
+            here = p_ref[pl.ds(edge + first, mchunk), :]
             for strand in range(2):
                 for j in range(TAPS):
                     shift = (j - HALF) * dil * (1 - 2 * strand)
-                    prod = here * x1_ref[strand, t, pl.ds(first + REACH + shift, mchunk), :]
-                    out.append(carry[strand * TAPS + j] + prod.reshape(mchunk // 8, 8, LANE).sum(0))
-            return tuple(out)
-
-        sums = tuple(jnp.zeros((8, LANE), F32) for _ in range(2 * TAPS))
-        for i in range(6):
-            sums = taps_step(i, sums)
+                    prod = here * x1_refs[strand][t][pl.ds(first + REACH + shift, mchunk), :]
+                    sums[strand * TAPS + j] += prod.reshape(mchunk // 8, 8, LANE).sum(0)
         for strand in range(2):
-            rows_t = [jnp.sum(sums[strand * TAPS + j], axis=0, keepdims=True) for j in range(TAPS)]
-            gt_ref[strand, :, dst] = jnp.concatenate(rows_t + [jnp.zeros((8 - TAPS, LANE), F32)], axis=0)
-
-    hot, hot1 = hot_ref[...], hot1_ref[...]
-    dw_ref[...] = dot(hot, s0_ref[0])
-    other = dot(hot, s0_ref[1])
+            lines = [jnp.sum(sums[strand * TAPS + j], axis=0, keepdims=True) for j in range(TAPS)]
+            gt_ref[strand, :, dst] = jnp.concatenate(lines + [jnp.zeros((8 - TAPS, LANE), F32)], axis=0)
+
+    hot1 = hot1_ref[...]
     by_tap = dot(hot1, pb_ref[...])
     own_letters = dot(hot1[: 16, :], cot_ref[...]) * scale
     srow, scol = iotas((8, JB))
@@ -353,7 +345,7 @@
     for t in range(tiles):
         dst = slice(t * LANE, (t + 1) * LANE)
         src = slice((tiles - 1 - t) * LANE, (tiles - t) * LANE)
-        flipped = flip_exact(other[:, src], rev)
+        flipped = flip_exact(others[tiles - 1 - t], rev)
         dw_ref[:, dst] += jnp.concatenate([flipped[JB:], flipped[:JB]], axis=0)
         g1_ref[:, dst] += flip_exact(g1_other[tiles - 1 - t], rev)
         gt_ref[0, :, dst] += flip_exact(gt_ref[1, :, src], rev)
@@ -381,19 +373,19 @@
         place[kk // 2, ROW_GT1 : ROW_GT1 + 8, :] = gt_ref[0, :, lanes]
 
 
-def mix1_kernel(n_chan, width, scal, a_ref, b_ref, out_ref, held, sem):
+def mix1_kernel(n_chan, width, a_ref, b_ref, out_ref, held, sem):
     def block(k):
         lanes = slice(k * width, (k + 1) * width)
         return a_ref[:, lanes].astype(F32) + b_ref[:, lanes].astype(F32)
 
-    for k, part in enumerate(xor_blocks([block(k) for k in range(n_chan)], scal[0])):
+    for k, part in enumerate(xor_blocks([block(k) for k in range(n_chan)], lax.axis_index("chan"))):
         held[:, k * width : (k + 1) * width] = part
     copy = pltpu.make_async_copy(held, out_ref.at[1], sem)
     copy.start()
     copy.wait()
 
 
-def finish_kernel(n_chan, width, scal, st_ref, sa_ref, sb_ref, _, gm_ref, gt_ref, ge_ref, held, sems):
+def finish_kernel(n_chan, width, st_ref, sa_ref, sb_ref, _, gm_ref, gt_ref, ge_ref, held, sems):
     sums = sa_ref[...] + sb_ref[...]
     fill = jnp.zeros((JB - ROW_GE, width), F32)
     dw = jnp.concatenate([sums[:ROW_GE], fill, sums[ROW_R : ROW_R + ROW_GE], fill], axis=0).astype(BF)
@@ -450,8 +442,6 @@
     own_tiles = pl.cdiv(width, LANE)
     scale = 1.0 / math.sqrt(rows * n_seq)
     shape = jax.ShapeDtypeStruct
-    place = jnp.stack([lax.axis_index("chan"), lax.axis_index("seq")]).astype(jnp.int32)
-    scal = jnp.concatenate([place, dilations])
     mix_t = jnp.swapaxes(mix, 1, 2)
 
     (pk,) = call(
@@ -468,14 +458,14 @@
         (0, width * chans * 4),
     )(in_hbm(mix_t), in_hbm(embed), in_hbm(jnp.swapaxes(taps, 0, 1)))
 
-    letters = tokens.reshape(1, rows)
+    letters = lax.optimization_barrier((tokens.reshape(1, rows), pk))[0]
     seq_bits = n_seq.bit_length() - 1
     for bit in range(seq_bits):
         letters = jnp.concatenate([letters, flip_bits(letters, "seq", 1 << bit)], axis=0)
 
     mixl, cot = call(
         functools.partial(local_kernel, n_chan, width),
-        [SMEM, HBM, HBM],
+        [HBM, HBM],
         [shape((width, chans), BF), shape((rows, width), BF)],
         [VMEM] * 2,
         [
@@ -485,7 +475,7 @@
         ],
         16,
         (1 << 20, 1 << 20),
-    )(scal, in_hbm(mix_t), in_hbm(cotangent.T))
+    )(in_hbm(mix_t), in_hbm(cotangent.T))
 
     pks = [pk]
     for bit in reversed(range(n_chan.bit_length() - 1)):
@@ -501,42 +491,43 @@
         [],
         16,
         (1 << 20, 1 << 20),
-    )(scal, letters)
-
-    x2, gm1, s1, x1, gp, stack = call(
+    )(dilations, letters)
+
+    rows_ext, slopes = shape((ext, LANE), F32), shape((ext, LANE), BF)
+    x2, gm1, s1, stack, table, table_r, *strands = call(
         functools.partial(forward_kernel, n_chan, rows, width, scale),
         [SMEM] + [VMEM] * (n_chan + 3),
         [
-            shape((rows, width), BF),
+            shape((width, rows), BF),
             shape((width, chans), BF),
             shape((rows, width), BF),
-            shape((2, tiles, ext, LANE), F32),
-            shape((2, tiles, ext, LANE), BF),
             shape((4 * JB, chans), BF),
-        ],
-        [VMEM] * 6,
+            shape((TABLE, chans), BF),
+            shape((TABLE, chans), BF),
+        ]
+        + [rows_ext] * (2 * tiles)
+        + [slopes] * (2 * tiles),
+        [HBM] + [VMEM] * (5 + 4 * tiles),
         [
             pltpu.VMEM((4 * JB, chans), BF),
-            pltpu.VMEM((TABLE, chans), BF),
             pltpu.VMEM((4 * JB, chans), BF),
-            pltpu.VMEM((TABLE, chans), BF),
             pltpu.VMEM((rows, chans), BF),
+            pltpu.VMEM((width, rows), BF),
+            pltpu.SemaphoreType.DMA,
         ],
         32,
         (3 << 30, 8 << 20),
-    )(scal, *pks, hot_t, mixl, cot)
+    )(dilations, *pks, hot_t, mixl, cot)
 
     keep, send = call(
         functools.partial(backward_kernel, n_chan, rows, width, scale),
-        [SMEM] + [VMEM] * (n_chan + 7),
+        [SMEM] + [VMEM] * (n_chan + 7 + 4 * tiles),
         [shape((n_chan // 2, SUMS, width), F32)] * 2,
         [VMEM] * 2,
-        [
-            pltpu.VMEM((tiles, rows + 2 * edge, LANE), F32),
+        [pltpu.VMEM((rows + 2 * edge, LANE), F32)] * tiles
+        + [pltpu.VMEM((padded, 2 * LANE), BF)] * tiles
+        + [
             pltpu.VMEM((own_tiles, ext, LANE), F32),
-            pltpu.VMEM((2, padded, chans), BF),
-            pltpu.VMEM((TABLE, chans), BF),
-            pltpu.VMEM((TABLE, chans), BF),
             pltpu.VMEM((2 * JB, chans), F32),
             pltpu.VMEM((2, 8, chans), F32),
             pltpu.VMEM((8, chans), F32),
@@ -545,7 +536,7 @@
         ],
         40,
         (3 << 30, 8 << 20),
-    )(scal, *pks, hot, hot1, mixl, cot, s1, x1, gp)
+    )(dilations, *pks, hot, hot1, mixl, cot, s1, table, table_r, *strands)
 
     g_mine = gm1
     for bit in reversed(range(seq_bits)):
@@ -566,16 +557,16 @@
     big = pltpu.VMEM((width, chans), F32)
     (grad_mix,) = call(
         functools.partial(mix1_kernel, n_chan, width),
-        [SMEM, VMEM, VMEM],
+        [VMEM, VMEM],
         [shape((BLOCKS, width, chans), F32)],
         [HBM],
         [big, pltpu.SemaphoreType.DMA],
         16,
         (1 << 20, 1 << 21),
-    )(scal, g_mine, g_other)
+    )(g_mine, g_other)
     grad_mix, grad_taps, grad_embed = call(
         functools.partial(finish_kernel, n_chan, width),
-        [SMEM, VMEM, VMEM, VMEM, HBM],
+        [VMEM, VMEM, VMEM, HBM],
         [
             shape((BLOCKS, width, chans), F32),
             shape((TAPS, BLOCKS, width), F32),
@@ -585,9 +576,9 @@
         [big, pltpu.SemaphoreType.DMA((chans // (2 * LANE),))],
         16,
         (1 << 24, 1 << 21),
-        {4: 0},
-    )(scal, stack, s_mine, s_other, grad_mix)
-    return x2, jnp.swapaxes(grad_mix, 1, 2), jnp.swapaxes(grad_taps, 0, 1), grad_embed
+        {3: 0},
+    )(stack, s_mine, s_other, grad_mix)
+    return x2.T, jnp.swapaxes(grad_mix, 1, 2), jnp.swapaxes(grad_taps, 0, 1), grad_embed
 
 
 def solution(mesh):

time: 58 us -> 58 us (level)
  starting transfers between devices: 16.2 us -> 18.3 us
  Pallas kernels: 26.8 us -> 25.1 us
  waiting for transfers between devices: 11.3 us -> 12.6 us
  local copies, waits for them, and re-layouts: 1.57 us -> 0.7 us
  other arithmetic: 0.88 us -> 0.13 us
    ppermute x11, starting transfers between devices: 16.2 us -> 18.3 us  [flip_bits(): lax.ppermute(x, axis, [(i, i ^ mask) for i in range(lax.axis_size(axis))])]
    pallas_call x3, Pallas kernels: 6.01 us -> 4.38 us  [the longest x1 1.64 us: body(): call(functools.partial(finish_kernel, n_chan, width), [VMEM, VMEM, VMEM,...]
    ppermute x11, waiting for transfers between devices: 11.3 us -> 12.6 us  [flip_bits(): lax.ppermute(x, axis, [(i, i ^ mask) for i in range(lax.axis_size(axis))])]
    unnamed x1 -> x2, local copies, waits for them, and re-layouts: 0.87 us -> 0.01 us
    concatenate x1 -> x0, other arithmetic: 0.73 us -> none  [body(): scal = jnp.concatenate([place, dilations])]
  transfers between devices with their start and end apart: 11 -> 11, of which waited for: 6 -> 8; matrix products, arithmetic and copies ran while one was open for 3% -> 1% of each run, Pallas kernels for 27% -> 23%
where the time goes in v4:
time: 58 us; the launch traced here: 57.7 us
  Pallas kernels  25.1 us (43%)
  starting transfers between devices  18.3 us (32%)
  waiting for transfers between devices  12.6 us (22%)
  between operations  0.9 us (2%)
  local copies, waits for them, and re-layouts  0.7 us (1%)
    ppermute x11, starting transfers between devices, flip_bits(): lax.ppermute(x, axis, [(i, i ^ mask) for i in range(lax.axis_size(axis))])  18.3 us
    ppermute x11, waiting for transfers between devices, flip_bits(): lax.ppermute(x, axis, [(i, i ^ mask) for i in range(lax.axis_size(axis))])  12.6 us
    pallas_call x1, Pallas kernels, body(): call(functools.partial(backward_kernel, n_chan, rows, width, scale), [SME...  9.42 us
    pallas_call x1, Pallas kernels, body(): call(functools.partial(forward_kernel, n_chan, rows, width, scale), [SMEM...  9.15 us
    pallas_call x1, Pallas kernels, body(): call(functools.partial(finish_kernel, n_chan, width), [VMEM, VMEM, VMEM,...  1.64 us
    pallas_call x1, Pallas kernels, body(): call(functools.partial(local_kernel, n_chan, width), [HBM, HBM], [shape((...  1.44 us
    pallas_call x1, Pallas kernels, body(): call(functools.partial(mix1_kernel, n_chan, width), [VMEM, VMEM], [shape(...  1.3 us
  transfers between devices with their start and end apart: 11, of which 8 were waited for; matrix products, arithmetic and copies ran while one was open for 1% of the time, Pallas kernels for 23%

profile of v4, /device:TPU:0, one launch (start us, length us, event | category | flops | bytes accessed | tf_op | source)
XLA Modules:
  0.0 57.7 jit_solution(794138223674339960)
XLA Ops:
  0.6 0.0 copy-start
  0.6 1.0 %shard_map.93.refs_0_ = bf16[208,768]{1,0:T(8,128)(2,1)S(1)} custom-call(bf16[2,192,768]{2,1,0:T(8,128)(2,1)} %bitcast.9, bf16[4,192]{1,0:T(4,128)(2,1)} %embed_ref.1, bf16[5,2,192]{2,1,0:T(2,128)(2,1)} %bitcast.12), custom_call_target="tpu_custom_call" | custom-call | bytes 589824 | tf_op jit(solution)/shard_map/pallas_call | solution.py:447
  1.7 3.0 %collective-permute-start.1 = (bf16[208,768]{1,0:T(8,128)(2,1)S(1)}, bf16[208,768]{1,0:T(8,128)(2,1)S(1)}, u32[]{:S(2)}, u32[]{:S(2)}) collective-permute-start(bf16[208,768]{1,0:T(8,128)(2,1)S(1)} %shard_map.93.refs_0_), channel_id=1, source_target_pairs={{0,2},{1,3},{2,0},{3,1},{4,6},{5,7},{6,4},{7,5},{8,10},{9,11},{10,... | collective-permute-start | bytes 958472 | tf_op jit(solution)/shard_map/ppermute | solution.py:431
  4.7 0.7 %reshape.11 = s32[1,768]{1,0:T(1,128)S(1)} reshape(s32[768]{0:T(1024)} %param.6) | data formatting | bytes 6144 | tf_op jit(solution)/shard_map/reshape | solution.py:461
  5.4 1.6 %collective-permute-start.2 = (s32[1,768]{1,0:T(1,128)S(1)}, s32[1,768]{1,0:T(1,128)S(1)}, u32[]{:S(2)}, u32[]{:S(2)}) collective-permute-start(s32[1,768]{1,0:T(1,128)S(1)} %reshape.11), channel_id=1, source_target_pairs={{0,4},{4,0},{8,12},{12,8},{1,5},{5,1},{9,13},{13,9},{2,6},{6,2},{1... | collective-permute-start | bytes 9224 | tf_op jit(solution)/shard_map/ppermute | solution.py:431
  6.9 2.0 %collective-permute-done.2 = s32[1,768]{1,0:T(1,128)S(1)} collective-permute-done((s32[1,768]{1,0:T(1,128)S(1)}, s32[1,768]{1,0:T(1,128)S(1)}, u32[]{:S(2)}, u32[]{:S(2)}) %collective-permute-start.2) | collective-permute-done | bytes 3104 | tf_op jit(solution)/shard_map/ppermute | solution.py:431
  9.0 2.7 %collective-permute-start.3 = (s32[2,768]{1,0:T(2,128)S(1)}, s32[2,768]{1,0:T(2,128)S(1)}, u32[]{:S(2)}, u32[]{:S(2)}) collective-permute-start(s32[2,768]{1,0:T(2,128)S(1)} %pad_add_fusion.1), channel_id=1, source_target_pairs={{0,8},{4,12},{8,0},{12,4},{1,9},{5,13},{9,1},{13,5},{2,10},{6,14},... | collective-permute-start | bytes 18440 | tf_op jit(solution)/shard_map/ppermute | solution.py:431
  11.6 0.0 collective-permute-start
  11.6 1.4 %shard_map.94 = (bf16[192,768]{1,0:T(8,128)(2,1)S(1)}, bf16[768,192]{1,0:T(8,128)(2,1)S(1)}) custom-call(bf16[2,192,768]{2,1,0:T(8,128)(2,1)} %bitcast.10, bf16[192,768]{1,0:T(8,128)(2,1)} %bitcast.11), custom_call_target="tpu_custom_call" | custom-call | flops 1048576 | bytes 1048576 | tf_op jit(solution)/shard_map/pallas_call | solution.py:466
  13.1 0.5 collective-permute-done.3
  13.6 0.0 collective-permute-done.1.refs_2_
  13.6 0.1 collective-permute-start.4
  13.7 1.1 %shard_map.95 = (bf16[896,128]{1,0:T(8,128)(2,1)S(1)}, bf16[64,896]{1,0:T(8,128)(2,1)S(1)}, bf16[64,768]{1,0:T(8,128)(2,1)S(1)}) custom-call(s32[2]{0:T(128)S(1)} %copy-done, s32[4,768]{1,0:T(4,128)S(1)} %pad_add_fusion.tok_ref), custom_call_target="tpu_custom_call" | custom-call | flops 1048576 | bytes 1048576 | tf_op jit(solution)/shard_map/pallas_call | solution.py:486
  14.9 0.0 collective-permute-done.refs_1_
  14.9 0.4 collective-permute-done.4.refs_3_
  15.3 9.2 %shard_map.96 = (bf16[192,768]{1,0:T(8,128)(2,1)}, bf16[192,768]{1,0:T(8,128)(2,1)S(1)}, bf16[768,192]{1,0:T(8,128)(2,1)S(1)}, bf16[128,768]{1,0:T(8,128)(2,1)S(...) custom-call(s32[2]{0:T(128)S(1)} %copy-done, ...), custom_call_target="tpu_custom_call" | custom-call | flops 3221225472 | bytes 8388608 | tf_op jit(solution)/shard_map/pallas_call | solution.py:497
  24.4 2.7 %collective-permute-start.9 = (bf16[192,768]{1,0:T(8,128)(2,1)S(1)}, bf16[192,768]{1,0:T(8,128)(2,1)S(1)}, u32[]{:S(2)}, u32[]{:S(2)}) collective-permute-start(bf16[192,768]{1,0:T(8,128)(2,1)S(1)} %get-tuple-element.84), channel_id=1, source_target_pairs={{0,8},{4,12},{8,0},{12,4},{1,9},{5,13},{9,1},{13,5},{2,10},{6,14},... | collective-permute-start | bytes 884744 | tf_op jit(solution)/shard_map/ppermute | solution.py:431
  27.1 9.4 %shard_map.97 = (f32[2,64,192]{2,1,0:T(8,128)S(1)}, f32[2,64,192]{2,1,0:T(8,128)S(1)}) custom-call(s32[2]{0:T(128)S(1)} %copy-done, bf16[208,768]{1,0:T(8,128)(2,1)S(1)} %shard_map.93.refs_0_, bf16[208,768]{1,0:T(8,128)(2,1)S(1)} %collective-permute-done.refs_1_, bf16[208,768]{1,0:T(8,128)(2,1)S(1)} %collective-permute-done.1.refs_2_, ...), custom_call_target="tpu_custom_call" | custom-call | flops 3221225472 | bytes 8388608 | tf_op jit(solution)/shard_map/pallas_call | solution.py:522
  36.5 0.0 collective-permute-start.5
  36.6 1.3 %collective-permute-done.5 = f32[2,64,192]{2,1,0:T(8,128)S(1)} collective-permute-done((f32[2,64,192]{2,1,0:T(8,128)S(1)}, f32[2,64,192]{2,1,0:T(8,128)S(1)}, u32[]{:S(2)}, u32[]{:S(2)}) %collective-permute-start.5) | collective-permute-done | bytes 98336 | tf_op jit(solution)/shard_map/ppermute | solution.py:431
  37.9 0.6 %collective-permute-start.6 = (f32[1,64,192]{2,1,0:T(8,128)S(1)}, f32[1,64,192]{2,1,0:T(8,128)S(1)}, u32[]{:S(2)}, u32[]{:S(2)}) collective-permute-start(f32[1,64,192]{2,1,0:T(8,128)S(1)} %slice.11), channel_id=1, source_target_pairs={{0,2},{1,3},{2,0},{3,1},{4,6},{5,7},{6,4},{7,5},{8,10},{9,11},{10,... | collective-permute-start | bytes 147464 | tf_op jit(solution)/shard_map/ppermute | solution.py:431
  38.5 2.3 %collective-permute-done.9 = bf16[192,768]{1,0:T(8,128)(2,1)S(1)} collective-permute-done((bf16[192,768]{1,0:T(8,128)(2,1)S(1)}, bf16[192,768]{1,0:T(8,128)(2,1)S(1)}, u32[]{:S(2)}, u32[]{:S(2)}) %collective-permute-start.9) | collective-permute-done | bytes 294944 | tf_op jit(solution)/shard_map/ppermute | solution.py:431
  40.8 0.1 add_convert_fusion.a_ref
  40.9 0.7 %collective-permute-start.10 = (bf16[192,768]{1,0:T(8,128)(2,1)S(1)}, bf16[192,768]{1,0:T(8,128)(2,1)S(1)}, u32[]{:S(2)}, u32[]{:S(2)}) collective-permute-start(bf16[192,768]{1,0:T(8,128)(2,1)S(1)} %add_convert_fusion.a_ref), channel_id=1, source_target_pairs={{0,4},{4,0},{8,12},{12,8},{1,5},{5,1},{9,13},{13,9},{2,6},{6,2},{1... | collective-permute-start | bytes 884744 | tf_op jit(solution)/shard_map/ppermute | solution.py:431
  41.6 0.7 %collective-permute-done.6 = f32[1,64,192]{2,1,0:T(8,128)S(1)} collective-permute-done((f32[1,64,192]{2,1,0:T(8,128)S(1)}, f32[1,64,192]{2,1,0:T(8,128)S(1)}, u32[]{:S(2)}, u32[]{:S(2)}) %collective-permute-start.6) | collective-permute-done | bytes 49184 | tf_op jit(solution)/shard_map/ppermute | solution.py:431
  42.3 2.8 %collective-permute-start.7 = (f32[64,192]{1,0:T(8,128)S(1)}, f32[64,192]{1,0:T(8,128)S(1)}, u32[]{:S(2)}, u32[]{:S(2)}) collective-permute-start(f32[64,192]{1,0:T(8,128)S(1)} %fusion), channel_id=1, source_target_pairs={{0,8},{4,12},{8,0},{12,4},{1,9},{5,13},{9,1},{13,5},{2,10},{6,14},... | collective-permute-start | bytes 147464 | tf_op jit(solution)/shard_map/ppermute | solution.py:431
  45.1 4.4 %collective-permute-done.7 = f32[64,192]{1,0:T(8,128)S(1)} collective-permute-done((f32[64,192]{1,0:T(8,128)S(1)}, f32[64,192]{1,0:T(8,128)S(1)}, u32[]{:S(2)}, u32[]{:S(2)}) %collective-permute-start.7) | collective-permute-done | bytes 49184 | tf_op jit(solution)/shard_map/ppermute | solution.py:431
  49.5 4.2 %collective-permute-start.8 = (f32[64,192]{1,0:T(8,128)S(1)}, f32[64,192]{1,0:T(8,128)S(1)}, u32[]{:S(2)}, u32[]{:S(2)}) collective-permute-start(f32[64,192]{1,0:T(8,128)S(1)} %add.14.sa_ref), channel_id=1, source_target_pairs={{0,4},{4,0},{8,12},{12,8},{1,5},{5,1},{9,13},{13,9},{2,6},{6,2},{1... | collective-permute-start | bytes 147464 | tf_op jit(solution)/shard_map/ppermute | solution.py:431
  53.7 0.0 collective-permute-done.10.b_ref
  53.7 1.3 %shard_map.98._ = f32[2,192,768]{2,1,0:T(8,128)} custom-call(bf16[192,768]{1,0:T(8,128)(2,1)S(1)} %add_convert_fusion.a_ref, bf16[192,768]{1,0:T(8,128)(2,1)S(1)} %collective-permute-done.10.b_ref), custom_call_target="tpu_custom_call" | custom-call | flops 1048576 | bytes 2097152 | tf_op jit(solution)/shard_map/pallas_call | solution.py:558
  55.0 0.9 %collective-permute-done.8.sb_ref = f32[64,192]{1,0:T(8,128)S(1)} collective-permute-done((f32[64,192]{1,0:T(8,128)S(1)}, f32[64,192]{1,0:T(8,128)S(1)}, u32[]{:S(2)}, u32[]{:S(2)}) %collective-permute-start.8) | collective-permute-done | bytes 49184 | tf_op jit(solution)/shard_map/ppermute | solution.py:431
  55.9 1.6 %shard_map.99 = (f32[2,192,768]{2,1,0:T(8,128)}, f32[5,2,192]{2,1,0:T(2,128)}, f32[4,192]{1,0:T(4,128)}) custom-call(bf16[128,768]{1,0:T(8,128)(2,1)S(1)} %get-tuple-element.52.st_ref, f32[64,192]{1,0:T(8,128)S(1)} %add.14.sa_ref, f32[64,192]{1,0:T(8,128)S(1)} %collective-permute-done.8.sb_ref, ...), custom_call_target="tpu_custom_call", output_to_operand_aliasing={{0}: (3, {})} | custom-call | flops 16777216 | bytes 2097152 | tf_op jit(solution)/shard_map/pallas_call | solution.py:567
  (7 shorter events, 0.1 us)
Async XLA Ops:
  0.6 13.1 %copy-start = (s32[2]{0:T(128)S(1)}, s32[2]{0:T(128)}, u32[]{:S(2)}) copy-start(s32[2]{0:T(128)} %dils.5) | copy-start | bytes 28
  1.7 11.9 %collective-permute-start.1 = (bf16[208,768]{1,0:T(8,128)(2,1)S(1)}, bf16[208,768]{1,0:T(8,128)(2,1)S(1)}, u32[]{:S(2)}, u32[]{:S(2)}) collective-permute-start(bf16[208,768]{1,0:T(8,128)(2,1)S(1)} %shard_map.93.refs_0_), channel_id=1, source_target_pairs={{0,2},{1,3},{2,0},{3,1},{4,6},{5,7},{6,4},{7,5},{8,10},{9,11},{10,... | collective-permute-start | bytes 958472 | tf_op jit(solution)/shard_map/ppermute | solution.py:431
  5.4 3.6 %collective-permute-start.2 = (s32[1,768]{1,0:T(1,128)S(1)}, s32[1,768]{1,0:T(1,128)S(1)}, u32[]{:S(2)}, u32[]{:S(2)}) collective-permute-start(s32[1,768]{1,0:T(1,128)S(1)} %reshape.11), channel_id=1, source_target_pairs={{0,4},{4,0},{8,12},{12,8},{1,5},{5,1},{9,13},{13,9},{2,6},{6,2},{1... | collective-permute-start | bytes 9224 | tf_op jit(solution)/shard_map/ppermute | solution.py:431
  9.0 4.6 %collective-permute-start.3 = (s32[2,768]{1,0:T(2,128)S(1)}, s32[2,768]{1,0:T(2,128)S(1)}, u32[]{:S(2)}, u32[]{:S(2)}) collective-permute-start(s32[2,768]{1,0:T(2,128)S(1)} %pad_add_fusion.1), channel_id=1, source_target_pairs={{0,8},{4,12},{8,0},{12,4},{1,9},{5,13},{9,1},{13,5},{2,10},{6,14},... | collective-permute-start | bytes 18440 | tf_op jit(solution)/shard_map/ppermute | solution.py:431
  11.6 3.2 %collective-permute-start = (bf16[208,768]{1,0:T(8,128)(2,1)S(1)}, bf16[208,768]{1,0:T(8,128)(2,1)S(1)}, u32[]{:S(2)}, u32[]{:S(2)}) collective-permute-start(bf16[208,768]{1,0:T(8,128)(2,1)S(1)} %shard_map.93.refs_0_), channel_id=1, source_target_pairs={{0,1},{1,0},{2,3},{3,2},{4,5},{5,4},{6,7},{7,6},{8,9},{9,8},{10,11... | collective-permute-start | bytes 958472 | tf_op jit(solution)/shard_map/ppermute | solution.py:431
  13.6 1.7 %collective-permute-start.4 = (bf16[208,768]{1,0:T(8,128)(2,1)S(1)}, bf16[208,768]{1,0:T(8,128)(2,1)S(1)}, u32[]{:S(2)}, u32[]{:S(2)}) collective-permute-start(bf16[208,768]{1,0:T(8,128)(2,1)S(1)} %collective-permute-done.1.refs_2_), channel_id=1, source_target_pairs={{0,1},{1,0},{2,3},{3,2},{4,5},{5,4},{6,7},{7,6},{8,9},{9,8},{10,11... | collective-permute-start | bytes 958472 | tf_op jit(solution)/shard_map/ppermute | solution.py:431
  24.4 16.3 %collective-permute-start.9 = (bf16[192,768]{1,0:T(8,128)(2,1)S(1)}, bf16[192,768]{1,0:T(8,128)(2,1)S(1)}, u32[]{:S(2)}, u32[]{:S(2)}) collective-permute-start(bf16[192,768]{1,0:T(8,128)(2,1)S(1)} %get-tuple-element.84), channel_id=1, source_target_pairs={{0,8},{4,12},{8,0},{12,4},{1,9},{5,13},{9,1},{13,5},{2,10},{6,14},... | collective-permute-start | bytes 884744 | tf_op jit(solution)/shard_map/ppermute | solution.py:431
  36.5 1.4 %collective-permute-start.5 = (f32[2,64,192]{2,1,0:T(8,128)S(1)}, f32[2,64,192]{2,1,0:T(8,128)S(1)}, u32[]{:S(2)}, u32[]{:S(2)}) collective-permute-start(f32[2,64,192]{2,1,0:T(8,128)S(1)} %get-tuple-element.83), channel_id=1, source_target_pairs={{0,1},{1,0},{2,3},{3,2},{4,5},{5,4},{6,7},{7,6},{8,9},{9,8},{10,11... | collective-permute-start | bytes 294920 | tf_op jit(solution)/shard_map/ppermute | solution.py:431
  37.9 4.3 %collective-permute-start.6 = (f32[1,64,192]{2,1,0:T(8,128)S(1)}, f32[1,64,192]{2,1,0:T(8,128)S(1)}, u32[]{:S(2)}, u32[]{:S(2)}) collective-permute-start(f32[1,64,192]{2,1,0:T(8,128)S(1)} %slice.11), channel_id=1, source_target_pairs={{0,2},{1,3},{2,0},{3,1},{4,6},{5,7},{6,4},{7,5},{8,10},{9,11},{10,... | collective-permute-start | bytes 147464 | tf_op jit(solution)/shard_map/ppermute | solution.py:431
  40.9 12.8 %collective-permute-start.10 = (bf16[192,768]{1,0:T(8,128)(2,1)S(1)}, bf16[192,768]{1,0:T(8,128)(2,1)S(1)}, u32[]{:S(2)}, u32[]{:S(2)}) collective-permute-start(bf16[192,768]{1,0:T(8,128)(2,1)S(1)} %add_convert_fusion.a_ref), channel_id=1, source_target_pairs={{0,4},{4,0},{8,12},{12,8},{1,5},{5,1},{9,13},{13,9},{2,6},{6,2},{1... | collective-permute-start | bytes 884744 | tf_op jit(solution)/shard_map/ppermute | solution.py:431
  42.3 7.2 %collective-permute-start.7 = (f32[64,192]{1,0:T(8,128)S(1)}, f32[64,192]{1,0:T(8,128)S(1)}, u32[]{:S(2)}, u32[]{:S(2)}) collective-permute-start(f32[64,192]{1,0:T(8,128)S(1)} %fusion), channel_id=1, source_target_pairs={{0,8},{4,12},{8,0},{12,4},{1,9},{5,13},{9,1},{13,5},{2,10},{6,14},... | collective-permute-start | bytes 147464 | tf_op jit(solution)/shard_map/ppermute | solution.py:431
  49.5 6.4 %collective-permute-start.8 = (f32[64,192]{1,0:T(8,128)S(1)}, f32[64,192]{1,0:T(8,128)S(1)}, u32[]{:S(2)}, u32[]{:S(2)}) collective-permute-start(f32[64,192]{1,0:T(8,128)S(1)} %add.14.sa_ref), channel_id=1, source_target_pairs={{0,4},{4,0},{8,12},{12,8},{1,5},{5,1},{9,13},{13,9},{2,6},{6,2},{1... | collective-permute-start | bytes 147464 | tf_op jit(solution)/shard_map/ppermute | solution.py:431

commit v5 on v4

--- a/solution.py
+++ b/solution.py
@@ -54,11 +54,23 @@
     return high, (x - high.astype(F32)).astype(BF)
 
 
-def flip_exact(x, rev):
-    high, rest = split_bf(x)
-    mid, low = split_bf(x - high.astype(F32))
-    del rest
-    return dot(high, rev) + dot(mid, rev) + dot(low, rev)
+def reverse_lanes(parts, rev):
+    n = parts[0].shape[1] // LANE
+    rows = [p.shape[0] for p in parts]
+    pile = [p[:, t * LANE : (t + 1) * LANE] for p in parts for t in range(n)]
+    turned = dot(jnp.concatenate(pile, axis=0), rev)
+    out, first = [], 0
+    for count in rows:
+        tiles = [turned[first + t * count : first + (t + 1) * count] for t in range(n)]
+        out.append(jnp.concatenate(tiles[::-1], axis=1))
+        first += n * count
+    return out
+
+
+def reverse_wide(parts, rev):
+    split = [split_bf(p) for p in parts]
+    turned = reverse_lanes([q for pair in split for q in pair], rev)
+    return [turned[2 * i] + turned[2 * i + 1] for i in range(len(parts))]
 
 
 def xor_blocks(blocks, me):
@@ -76,6 +88,15 @@
     slope = half + (v * (1.0 - tangent * tangent)) * (
         0.5 * GELU_SCALE + (1.5 * GELU_SCALE * CUBIC) * square
     )
+    return value, slope
+
+
+def gelu_doubled(half):
+    square = half * half
+    cubic = (8.0 * GELU_SCALE * CUBIC) * square
+    above = 1.0 + jnp.tanh(half * (2.0 * GELU_SCALE + cubic))
+    value = half * above
+    slope = above + value * ((2.0 - above) * (2.0 * GELU_SCALE + 3.0 * cubic))
     return value, slope
 
 
@@ -101,23 +122,12 @@
     return (seen == local % BASES + 1).astype(F32)
 
 
-def pair_table(tables, rev_w):
-    sel_t, sel_e = select_rows("tap0", JB), select_rows("letter", JB)
-    plain = [dot(sel_t, t) * dot(sel_e, t) for t in tables]
-    n = len(tables)
-    out = []
-    for k in range(n):
-        high, low = split_bf(plain[k])
-        fhigh, flow = split_bf(plain[n - 1 - k])
-        out.append((high, dot(fhigh, rev_w).astype(BF), low, dot(flow, rev_w).astype(BF)))
-    return out
-
-
-def pack_kernel(width, mix_ref, embed_ref, taps_ref, out_ref, e_ref, t_ref, sems):
+def pack_kernel(width, mix_ref, embed_ref, taps_ref, tok_ref, out_ref, letters_ref, e_ref, t_ref, sems):
     big = pltpu.make_async_copy(mix_ref.at[0], out_ref.at[pl.ds(0, width)], sems.at[0])
     small = [
         pltpu.make_async_copy(embed_ref, e_ref, sems.at[1]),
         pltpu.make_async_copy(taps_ref, t_ref, sems.at[2]),
+        pltpu.make_async_copy(tok_ref, letters_ref.at[0], sems.at[3]),
     ]
     for copy in small + [big]:
         copy.start()
@@ -187,57 +197,63 @@
     (x2_ref, gm_ref, s_ref, st_ref, e_ref, et_ref), refs = refs[:6], refs[6:]
     x1_refs, refs = (refs[:tiles], refs[tiles : 2 * tiles]), refs[2 * tiles :]
     gp_refs, refs = (refs[:tiles], refs[tiles : 2 * tiles]), refs[2 * tiles :]
-    w_ref, wt_ref, m_ref, held, sem = refs
+    w_ref, b_ref, m_ref, held, sem = refs
+    chans = n_chan * width
     ext = rows + 2 * REACH
     me, dil = lax.axis_index("chan"), dils[1]
-    rev, rev_w = reversal(LANE), reversal(width)
-
-    tables = [pk[width:, :width] for pk in pks]
-    stacks = [jnp.concatenate(p, axis=0) for p in pair_table(tables, rev_w)]
-    for k, stack in enumerate(xor_blocks(stacks, me)):
-        st_ref[:, k * width : (k + 1) * width] = stack
+    rev = reversal(LANE)
+    blocks = [slice(k * width, (k + 1) * width) for k in range(n_chan)]
+
     for k in range(n_chan):
-        total = dot_t(st_ref[...], pks[k][:width, :])
+        e_ref[:, blocks[k]] = pks[k][width:, :width]
+    table = e_ref[...]
+    plain = dot(select_rows("tap0", JB), table) * dot(select_rows("letter", JB), table)
+    high, low = split_bf(plain)
+    turned, turned_low, table_r = reverse_lanes([high, low, table], rev)
+    et_ref[...] = table_r.astype(BF)
+    b_ref[...] = jnp.concatenate([high, turned.astype(BF), low, turned_low.astype(BF)], axis=0)
+    for k, block in enumerate(xor_blocks([b_ref[:, lanes] for lanes in blocks], me)):
+        st_ref[:, blocks[k]] = block
+    for k in range(n_chan):
+        total = 0.5 * dot_t(st_ref[...], pks[k][:width, :])
         high, low = split_bf(total[: 2 * JB] + total[2 * JB :])
-        w_ref[:, k * width : (k + 1) * width] = jnp.concatenate([high, low], axis=0)
-        e_ref[:, k * width : (k + 1) * width] = tables[k]
-
-    for t in range(tiles):
-        src = slice((tiles - 1 - t) * LANE, (tiles - t) * LANE)
-        dst = slice(t * LANE, (t + 1) * LANE)
-        flipped = dot(w_ref[:, src], rev).astype(BF)
-        wt_ref[:, dst] = jnp.concatenate(
-            [flipped[JB : 2 * JB], flipped[:JB], flipped[3 * JB :], flipped[2 * JB : 3 * JB]], axis=0
-        )
-        et_ref[:, dst] = dot(e_ref[:, src], rev).astype(BF)
-
-    row, col = iotas((4 * JB, TABLE))
+        w_ref[:, blocks[k]] = jnp.concatenate([high, low], axis=0)
+    weights = w_ref[...]
+    (swapped,) = reverse_lanes([weights], rev)
+    order = [swapped[JB : 2 * JB], swapped[:JB], swapped[3 * JB :], swapped[2 * JB : 3 * JB]]
+    weights_r = jnp.concatenate(order, axis=0).astype(BF)
+
+    table, table_r = table.astype(F32), et_ref[...].astype(F32)
     centre = HALF * BASES
-    pick_f = as_bf((row - centre == col) & (col < BASES))
-    pick_r = as_bf((row - centre - JB == col) & (col < BASES))
+    keep = lax.broadcasted_iota(jnp.int32, (8, chans), 0) < BASES
+
+    def lookup(source, first):
+        lines = jnp.where(keep, source[:8], 0.0)
+        above, below = jnp.zeros((first, chans), F32), jnp.zeros((4 * JB - first - 8, chans), F32)
+        return jnp.concatenate([above, lines, below], axis=0).astype(BF)
+
+    look, look_r = lookup(table, centre), lookup(table_r, JB + centre)
     chunk, mchunk = ext // 5, rows // 6
     for t in range(tiles):
         dst = slice(t * LANE, (t + 1) * LANE)
-        for strand, (wr, er, pick) in enumerate(((w_ref, e_ref, pick_f), (wt_ref, et_ref, pick_r))):
-            rhs = jnp.concatenate([wr[:, dst], dot(pick, er[:, dst]).astype(BF)], axis=1)
+        for strand, (wr, er) in enumerate(((weights, look), (weights_r, look_r))):
+            rhs = jnp.concatenate([wr[:, dst], er[:, dst]], axis=1)
             for i in range(5):
                 where = pl.ds(i * chunk, chunk)
                 both = dot(a_ref[where, :], rhs)
-                value, slope = gelu_parts(both[:, :LANE])
+                value, slope = gelu_doubled(both[:, :LANE])
                 x1_refs[strand][t][where, :] = both[:, LANE:] + value
-                gp_refs[strand][t][where, :] = slope.astype(BF)
-
-        taps_f = e_ref[:, dst].astype(F32)
-        taps_r = et_ref[:, dst].astype(F32)
+                gp_refs[strand][t][where, :] = slope
+
         for i in range(6):
             first = i * mchunk
-            total = jnp.zeros((mchunk, LANE), F32)
+            terms = []
             for j in range(TAPS):
                 shift = (j - HALF) * dil
                 line = slice(ROW_TAPS1 + j, ROW_TAPS1 + j + 1)
-                total += taps_f[line, :] * x1_refs[0][t][pl.ds(first + REACH + shift, mchunk), :]
-                total += taps_r[line, :] * x1_refs[1][t][pl.ds(first + REACH - shift, mchunk), :]
-            m_ref[first : first + mchunk, dst] = total.astype(BF)
+                terms.append(table[line, dst] * x1_refs[0][t][pl.ds(first + REACH + shift, mchunk), :])
+                terms.append(table_r[line, dst] * x1_refs[1][t][pl.ds(first + REACH - shift, mchunk), :])
+            m_ref[first : first + mchunk, dst] = functools.reduce(jnp.add, terms).astype(BF)
 
     half = rows // 2
     n_own = pl.cdiv(width, LANE)
@@ -264,12 +280,14 @@
     gp_refs, refs = (refs[:tiles], refs[tiles : 2 * tiles]), refs[2 * tiles :]
     (keep_ref, send_ref), refs = refs[:2], refs[2:]
     p_refs, s0_refs, refs = refs[:tiles], refs[tiles : 2 * tiles], refs[2 * tiles :]
-    g2_ref, dw_ref, gt_ref, g1_ref, pb_ref, st_ref = refs
+    g2_ref, gt_ref, pb_ref, dw_ref, st_ref, back_ref, tail_ref = refs
     ext = rows + 2 * REACH
     padded = hot_ref.shape[1]
     me, dil = lax.axis_index("chan"), dils[1]
-    rev, rev_w = reversal(LANE), reversal(width)
-    tables = [pk[width:, :width] for pk in pks]
+    rev = reversal(LANE)
+    blocks = [slice(k * width, (k + 1) * width) for k in range(n_chan)]
+    table, table_r = e_ref[...], et_ref[...]
+    taps_f, taps_r = 0.5 * table.astype(F32), 0.5 * table_r.astype(F32)
 
     edge = 2 * REACH
     n_own = pl.cdiv(width, LANE)
@@ -278,10 +296,10 @@
     g2_ref[:, rows + REACH :, :] = jnp.zeros((n_own, REACH, LANE), F32)
     g2 = jnp.concatenate([g2, jnp.zeros((rows, n_own * LANE - width), F32)], axis=1)
     for t in range(n_own):
-        g2_ref[t, REACH : rows + REACH, :] = g2[:, t * LANE : (t + 1) * LANE]
+        g2_ref[t, REACH : rows + REACH, :] = 0.5 * g2[:, t * LANE : (t + 1) * LANE]
 
     mchunk, chunk = rows // 6, ext // 5
-    others = [None] * tiles
+    plains, others = [None] * tiles, [None] * tiles
     for t in range(tiles):
         dst = slice(t * LANE, (t + 1) * LANE)
         p_ref, s0_ref = p_refs[t], s0_refs[t]
@@ -292,27 +310,24 @@
         p_ref[rows + edge :, :] = jnp.zeros((edge, LANE), F32)
         p_ref[edge : rows + edge, :] = pair[:, (t % 2) * LANE : (t % 2 + 1) * LANE]
         s0_ref[ext:, :] = jnp.zeros((padded - ext, 2 * LANE), BF)
-        taps_f = e_ref[:, dst].astype(F32)
-        taps_r = et_ref[:, dst].astype(F32)
         for i in range(5):
             first = i * chunk
             where = pl.ds(first, chunk)
-            f = jnp.zeros((chunk, LANE), F32)
-            r = jnp.zeros((chunk, LANE), F32)
+            fs, rs = [], []
             for j in range(TAPS):
-                shift = (j - HALF) * dil
-                line = slice(ROW_TAPS1 + j, ROW_TAPS1 + j + 1)
-                f += taps_f[line, :] * p_ref[pl.ds(first + REACH - shift, chunk), :]
-                r += taps_r[line, :] * p_ref[pl.ds(first + REACH + shift, chunk), :]
+                window = p_ref[pl.ds(first + REACH + (j - HALF) * dil, chunk), :]
+                ahead, back = ROW_TAPS1 + j, ROW_TAPS1 + TAPS - 1 - j
+                fs.append(taps_f[back : back + 1, dst] * window)
+                rs.append(taps_r[ahead : ahead + 1, dst] * window)
             if t < n_own:
-                f += g2_ref[t, where, :]
-            s0_ref[where, :LANE] = (f * gp_refs[0][t][where, :].astype(F32)).astype(BF)
-            s0_ref[where, LANE:] = (r * gp_refs[1][t][where, :].astype(F32)).astype(BF)
+                fs.append(g2_ref[t, where, :])
+            f, r = functools.reduce(jnp.add, fs), functools.reduce(jnp.add, rs)
+            s0_ref[where, :LANE] = (f * gp_refs[0][t][where, :]).astype(BF)
+            s0_ref[where, LANE:] = (r * gp_refs[1][t][where, :]).astype(BF)
         both = dot(hot_ref[...], s0_ref[...])
-        dw_ref[:, dst] = both[:, :LANE]
-        others[t] = both[:, LANE:]
-
-        sums = [jnp.zeros((8, LANE), F32) for _ in range(2 * TAPS)]
+        plains[t], others[t] = both[:, :LANE], both[:, LANE:]
+
+        sums = [None] * (2 * TAPS)
         for i in range(6):
             first = i * mchunk
             here = p_ref[pl.ds(edge + first, mchunk), :]
@@ -320,14 +335,15 @@
                 for j in range(TAPS):
                     shift = (j - HALF) * dil * (1 - 2 * strand)
                     prod = here * x1_refs[strand][t][pl.ds(first + REACH + shift, mchunk), :]
-                    sums[strand * TAPS + j] += prod.reshape(mchunk // 8, 8, LANE).sum(0)
+                    part = prod.reshape(mchunk // 8, 8, LANE).sum(0)
+                    slot = strand * TAPS + j
+                    sums[slot] = part if i == 0 else sums[slot] + part
         for strand in range(2):
             lines = [jnp.sum(sums[strand * TAPS + j], axis=0, keepdims=True) for j in range(TAPS)]
             gt_ref[strand, :, dst] = jnp.concatenate(lines + [jnp.zeros((8 - TAPS, LANE), F32)], axis=0)
 
-    hot1 = hot1_ref[...]
-    by_tap = dot(hot1, pb_ref[...])
-    own_letters = dot(hot1[: 16, :], cot_ref[...]) * scale
+    by_tap = dot(hot1_ref[...], pb_ref[...])
+    own_letters = dot(hot1_ref[:16, :], cot_ref[...]) * scale
     srow, scol = iotas((8, JB))
     sum_letter = as_bf((scol % BASES == srow) & (scol < TAPS * BASES))
     sum_tap = as_bf((scol // BASES == srow) & (scol < TAPS * BASES))
@@ -337,40 +353,37 @@
         return dot(sel, high) + dot(sel, rest)
 
     sel1 = select_rows("tap1", JB)
-    g1_other = []
-    for t in range(tiles):
-        dst = slice(t * LANE, (t + 1) * LANE)
-        g1_ref[:, dst] = sums_of(sum_letter, by_tap[:JB, dst] * dot(sel1, e_ref[:, dst]))
-        g1_other.append(sums_of(sum_letter, by_tap[JB:, dst] * dot(sel1, et_ref[:, dst])))
-    for t in range(tiles):
-        dst = slice(t * LANE, (t + 1) * LANE)
-        src = slice((tiles - 1 - t) * LANE, (tiles - t) * LANE)
-        flipped = flip_exact(others[tiles - 1 - t], rev)
-        dw_ref[:, dst] += jnp.concatenate([flipped[JB:], flipped[:JB]], axis=0)
-        g1_ref[:, dst] += flip_exact(g1_other[tiles - 1 - t], rev)
-        gt_ref[0, :, dst] += flip_exact(gt_ref[1, :, src], rev)
-
-    sel_t, sel_e = select_rows("tap0", JB), select_rows("letter", JB)
+    ahead = by_tap[:JB] * dot(sel1, table)
+    other = by_tap[JB:] * dot(sel1, table_r)
+    turned, other, taps_turned = reverse_wide(
+        [jnp.concatenate(others, axis=1), other, gt_ref[1]], rev
+    )
+    sums = jnp.concatenate(plains, axis=1) + jnp.concatenate([turned[JB:], turned[:JB]], axis=0)
+    dw_ref[...] = sums
+    letters = sums_of(sum_letter, ahead + other)
+    tail_ref[8:16, :] = gt_ref[0] + taps_turned
+
     total = jnp.zeros((2 * JB, chans), F32)
     for k in range(n_chan):
-        part = dw_ref[:, k * width : (k + 1) * width].astype(BF)
-        total = total + dot(part, pks[k][:width, :])
+        total = total + dot(dw_ref[:, blocks[k]].astype(BF), pks[k][:width, :])
     st_ref[...] = total
-    grads = xor_blocks([st_ref[:, k * width : (k + 1) * width] for k in range(n_chan)], me)
-    for kk in range(n_chan):
-        both = grads[kk][:JB] + flip_exact(grads[n_chan - 1 - kk][JB:], rev_w)
-        table = tables[kk]
-        lanes = slice(kk * width, (kk + 1) * width)
-        letters = sums_of(sum_letter, both * dot(sel_t, table)) + g1_ref[:, lanes]
+    for k, block in enumerate(xor_blocks([st_ref[:, lanes] for lanes in blocks], me)):
+        back_ref[:, blocks[k]] = block
+    (turned,) = reverse_wide([back_ref[JB:, :]], rev)
+    both = back_ref[:JB, :] + turned
+    tail_ref[0:8, :] = sums_of(sum_tap, both * dot(select_rows("letter", JB), table))
+    letters = letters + sums_of(sum_letter, both * dot(select_rows("tap0", JB), table))
+    tail_ref[16:24, :] = letters
+    zeros = jnp.zeros((BASES, width), F32)
+    own = jnp.concatenate([own_letters[HALF * BASES : (HALF + 1) * BASES, :], zeros], axis=0)
+    for kk, lanes in enumerate(blocks):
+        place, at = (keep_ref, send_ref)[kk % 2], kk // 2
+        letters = tail_ref[16:24, lanes]
         if kk == 0:
-            zeros = jnp.zeros((BASES, width), F32)
-            own = own_letters[HALF * BASES : (HALF + 1) * BASES, :]
-            letters = letters + jnp.concatenate([own, zeros], axis=0)
-        place = (keep_ref, send_ref)[kk % 2]
-        place[kk // 2, :ROW_R, :] = jnp.concatenate([dw_ref[:ROW_GE, lanes], letters[:BASES]], axis=0)
-        place[kk // 2, ROW_R : 2 * ROW_R, :] = dw_ref[JB : JB + ROW_R, lanes]
-        place[kk // 2, ROW_GT0 : ROW_GT0 + 8, :] = sums_of(sum_tap, both * dot(sel_e, table))
-        place[kk // 2, ROW_GT1 : ROW_GT1 + 8, :] = gt_ref[0, :, lanes]
+            letters = letters + own
+        place[at, :ROW_R, :] = jnp.concatenate([dw_ref[:ROW_GE, lanes], letters[:BASES]], axis=0)
+        place[at, ROW_R : 2 * ROW_R, :] = dw_ref[JB : JB + ROW_R, lanes]
+        place[at, ROW_GT0:, :] = tail_ref[0:16, lanes]
 
 
 def mix1_kernel(n_chan, width, a_ref, b_ref, out_ref, held, sem):
@@ -444,21 +457,20 @@
     shape = jax.ShapeDtypeStruct
     mix_t = jnp.swapaxes(mix, 1, 2)
 
-    (pk,) = call(
+    pk, letters = call(
         functools.partial(pack_kernel, width),
-        [HBM, HBM, HBM],
-        [shape((width + TABLE, chans), BF)],
-        [VMEM],
+        [HBM] * 4,
+        [shape((width + TABLE, chans), BF), shape((1, rows), jnp.int32)],
+        [VMEM] * 2,
         [
             pltpu.VMEM((BASES, width), BF),
             pltpu.VMEM((TAPS, BLOCKS, width), BF),
-            pltpu.SemaphoreType.DMA((3,)),
+            pltpu.SemaphoreType.DMA((4,)),
         ],
         8,
         (0, width * chans * 4),
-    )(in_hbm(mix_t), in_hbm(embed), in_hbm(jnp.swapaxes(taps, 0, 1)))
-
-    letters = lax.optimization_barrier((tokens.reshape(1, rows), pk))[0]
+    )(in_hbm(mix_t), in_hbm(embed), in_hbm(jnp.swapaxes(taps, 0, 1)), in_hbm(tokens))
+
     seq_bits = n_seq.bit_length() - 1
     for bit in range(seq_bits):
         letters = jnp.concatenate([letters, flip_bits(letters, "seq", 1 << bit)], axis=0)
@@ -493,7 +505,7 @@
         (1 << 20, 1 << 20),
     )(dilations, letters)
 
-    rows_ext, slopes = shape((ext, LANE), F32), shape((ext, LANE), BF)
+    rows_ext = shape((ext, LANE), F32)
     x2, gm1, s1, stack, table, table_r, *strands = call(
         functools.partial(forward_kernel, n_chan, rows, width, scale),
         [SMEM] + [VMEM] * (n_chan + 3),
@@ -505,8 +517,7 @@
             shape((TABLE, chans), BF),
             shape((TABLE, chans), BF),
         ]
-        + [rows_ext] * (2 * tiles)
-        + [slopes] * (2 * tiles),
+        + [rows_ext] * (4 * tiles),
         [HBM] + [VMEM] * (5 + 4 * tiles),
         [
             pltpu.VMEM((4 * JB, chans), BF),
@@ -528,11 +539,12 @@
         + [pltpu.VMEM((padded, 2 * LANE), BF)] * tiles
         + [
             pltpu.VMEM((own_tiles, ext, LANE), F32),
-            pltpu.VMEM((2 * JB, chans), F32),
             pltpu.VMEM((2, 8, chans), F32),
-            pltpu.VMEM((8, chans), F32),
             pltpu.VMEM((rows, chans), BF),
             pltpu.VMEM((2 * JB, chans), F32),
+            pltpu.VMEM((2 * JB, chans), F32),
+            pltpu.VMEM((2 * JB, chans), F32),
+            pltpu.VMEM((24, chans), F32),
         ],
         40,
         (3 << 30, 8 << 20),

time: 58 us -> 56.1 us (0.967)
  Pallas kernels: 25.1 us -> 22.6 us
  starting transfers between devices: 18.3 us -> 19.4 us
  local copies, waits for them, and re-layouts: 0.7 us -> 0.01 us
    pallas_call x1, Pallas kernels: 9.42 us -> 7.81 us  [body(): call(functools.partial(backward_kernel, n_chan, rows, width, scale), [SME...]
    ppermute x11, starting transfers between devices: 18.3 us -> 19.4 us  [flip_bits(): lax.ppermute(x, axis, [(i, i ^ mask) for i in range(lax.axis_size(axis))])]
    pallas_call x1, Pallas kernels: 9.15 us -> 8.18 us  [body(): call(functools.partial(forward_kernel, n_chan, rows, width, scale), [SMEM...]
    reshape x1 -> x0, local copies, waits for them, and re-layouts: 0.69 us -> none  [body(): letters = lax.optimization_barrier((tokens.reshape(1, rows), pk))[0]]
  transfers between devices with their start and end apart: 11 -> 11, of which waited for: 8 -> 7; matrix products, arithmetic and copies ran while one was open for 1% -> 0% of each run, Pallas kernels for 23% -> 21%
where the time goes in v5:
time: 56.1 us; the launch traced here: 55.9 us
  Pallas kernels  22.6 us (40%)
  starting transfers between devices  19.4 us (35%)
  waiting for transfers between devices  13 us (23%)
  between operations  0.74 us (1%)
    ppermute x11, starting transfers between devices, flip_bits(): lax.ppermute(x, axis, [(i, i ^ mask) for i in range(lax.axis_size(axis))])  19.4 us
    ppermute x11, waiting for transfers between devices, flip_bits(): lax.ppermute(x, axis, [(i, i ^ mask) for i in range(lax.axis_size(axis))])  13 us
    pallas_call x1, Pallas kernels, body(): call(functools.partial(forward_kernel, n_chan, rows, width, scale), [SMEM...  8.18 us
    pallas_call x1, Pallas kernels, body(): call(functools.partial(backward_kernel, n_chan, rows, width, scale), [SME...  7.81 us
    pallas_call x1, Pallas kernels, body(): call(functools.partial(finish_kernel, n_chan, width), [VMEM, VMEM, VMEM,...  1.64 us
    pallas_call x1, Pallas kernels, body(): call(functools.partial(local_kernel, n_chan, width), [HBM, HBM], [shape((...  1.44 us
    pallas_call x1, Pallas kernels, body(): call(functools.partial(mix1_kernel, n_chan, width), [VMEM, VMEM], [shape(...  1.3 us
    pallas_call x1, Pallas kernels, body(): call(functools.partial(prep_kernel, n_seq, rows), [SMEM, VMEM], [shape((p...  1.14 us
  transfers between devices with their start and end apart: 11, of which 7 were waited for; matrix products, arithmetic and copies ran while one was open for 0% of the time, Pallas kernels for 21%

profile of v5, /device:TPU:0, one launch (start us, length us, event | category | flops | bytes accessed | tf_op | source)
XLA Modules:
  0.0 55.9 jit_solution(3588043228755842033)
XLA Ops:
  0.6 0.0 copy-start
  0.6 1.1 %shard_map.93 = (bf16[208,768]{1,0:T(8,128)(2,1)S(1)}, s32[1,768]{1,0:T(1,128)S(1)}) custom-call(bf16[2,192,768]{2,1,0:T(8,128)(2,1)} %bitcast.9, bf16[4,192]{1,0:T(4,128)(2,1)} %embed_ref.1, bf16[5,2,192]{2,1,0:T(2,128)(2,1)} %bitcast.12, s32[768]{0:T(1024)} %tok_ref.1), custom_call_target="tpu_custom_call" | custom-call | bytes 589824 | tf_op jit(solution)/shard_map/pallas_call | solution.py:460
  1.7 3.0 %collective-permute-start.1 = (bf16[208,768]{1,0:T(8,128)(2,1)S(1)}, bf16[208,768]{1,0:T(8,128)(2,1)S(1)}, u32[]{:S(2)}, u32[]{:S(2)}) collective-permute-start(bf16[208,768]{1,0:T(8,128)(2,1)S(1)} %get-tuple-element.47.refs_0_), channel_id=1, source_target_pairs={{0,2},{1,3},{2,0},{3,1},{4,6},{5,7},{6,4},{7,5},{8,10},{9,11},{10,... | collective-permute-start | bytes 958472 | tf_op jit(solution)/shard_map/ppermute | solution.py:444
  4.7 1.6 %collective-permute-start.2 = (s32[1,768]{1,0:T(1,128)S(1)}, s32[1,768]{1,0:T(1,128)S(1)}, u32[]{:S(2)}, u32[]{:S(2)}) collective-permute-start(s32[1,768]{1,0:T(1,128)S(1)} %get-tuple-element.48), channel_id=1, source_target_pairs={{0,4},{4,0},{8,12},{12,8},{1,5},{5,1},{9,13},{13,9},{2,6},{6,2},{1... | collective-permute-start | bytes 9224 | tf_op jit(solution)/shard_map/ppermute | solution.py:444
  6.3 2.0 %collective-permute-done.2 = s32[1,768]{1,0:T(1,128)S(1)} collective-permute-done((s32[1,768]{1,0:T(1,128)S(1)}, s32[1,768]{1,0:T(1,128)S(1)}, u32[]{:S(2)}, u32[]{:S(2)}) %collective-permute-start.2) | collective-permute-done | bytes 3104 | tf_op jit(solution)/shard_map/ppermute | solution.py:444
  8.3 2.7 %collective-permute-start.3 = (s32[2,768]{1,0:T(2,128)S(1)}, s32[2,768]{1,0:T(2,128)S(1)}, u32[]{:S(2)}, u32[]{:S(2)}) collective-permute-start(s32[2,768]{1,0:T(2,128)S(1)} %pad_add_fusion.1), channel_id=1, source_target_pairs={{0,8},{4,12},{8,0},{12,4},{1,9},{5,13},{9,1},{13,5},{2,10},{6,14},... | collective-permute-start | bytes 18440 | tf_op jit(solution)/shard_map/ppermute | solution.py:444
  11.0 0.0 collective-permute-start
  11.0 1.4 %shard_map.94 = (bf16[192,768]{1,0:T(8,128)(2,1)S(1)}, bf16[768,192]{1,0:T(8,128)(2,1)S(1)}) custom-call(bf16[2,192,768]{2,1,0:T(8,128)(2,1)} %bitcast.10, bf16[192,768]{1,0:T(8,128)(2,1)} %bitcast.11), custom_call_target="tpu_custom_call" | custom-call | flops 1048576 | bytes 1048576 | tf_op jit(solution)/shard_map/pallas_call | solution.py:478
  12.4 0.5 collective-permute-done.3
  12.9 0.0 collective-permute-done.1.refs_2_
  12.9 0.1 collective-permute-start.4
  13.0 0.0 copy-done
  13.0 1.1 %shard_map.95 = (bf16[896,128]{1,0:T(8,128)(2,1)S(1)}, bf16[64,896]{1,0:T(8,128)(2,1)S(1)}, bf16[64,768]{1,0:T(8,128)(2,1)S(1)}) custom-call(s32[2]{0:T(128)S(1)} %copy-done, s32[4,768]{1,0:T(4,128)S(1)} %pad_add_fusion.tok_ref), custom_call_target="tpu_custom_call" | custom-call | flops 1048576 | bytes 1048576 | tf_op jit(solution)/shard_map/pallas_call | solution.py:498
  14.2 0.0 collective-permute-done.refs_1_
  14.2 0.4 collective-permute-done.4.refs_3_
  14.6 8.2 %shard_map.96 = (bf16[192,768]{1,0:T(8,128)(2,1)}, bf16[192,768]{1,0:T(8,128)(2,1)S(1)}, bf16[768,192]{1,0:T(8,128)(2,1)S(1)}, bf16[128,768]{1,0:T(8,128)(2,1)S(...) custom-call(s32[2]{0:T(128)S(1)} %copy-done, ...), custom_call_target="tpu_custom_call" | custom-call | flops 3221225472 | bytes 8388608 | tf_op jit(solution)/shard_map/pallas_call | solution.py:509
  22.8 2.7 %collective-permute-start.9 = (bf16[192,768]{1,0:T(8,128)(2,1)S(1)}, bf16[192,768]{1,0:T(8,128)(2,1)S(1)}, u32[]{:S(2)}, u32[]{:S(2)}) collective-permute-start(bf16[192,768]{1,0:T(8,128)(2,1)S(1)} %get-tuple-element.86), channel_id=1, source_target_pairs={{0,8},{4,12},{8,0},{12,4},{1,9},{5,13},{9,1},{13,5},{2,10},{6,14},... | collective-permute-start | bytes 884744 | tf_op jit(solution)/shard_map/ppermute | solution.py:444
  25.5 7.8 %shard_map.97 = (f32[2,64,192]{2,1,0:T(8,128)S(1)}, f32[2,64,192]{2,1,0:T(8,128)S(1)}) custom-call(s32[2]{0:T(128)S(1)} %copy-done, bf16[208,768]{1,0:T(8,128)(2,1)S(1)} %get-tuple-element.47.refs_0_, bf16[208,768]{1,0:T(8,128)(2,1)S(1)} %collective-permute-done.refs_1_, bf16[208,768]{1,0:T(8,128)(2,1)S(1)} %collective-permute-done.1.refs_2_, ...), custom_call_target="tpu_custom_call" | custom-call | flops 3221225472 | bytes 8388608 | tf_op jit(solution)/shard_map/pallas_call | solution.py:533
  33.3 0.0 collective-permute-start.5
  33.3 1.3 %collective-permute-done.5 = f32[2,64,192]{2,1,0:T(8,128)S(1)} collective-permute-done((f32[2,64,192]{2,1,0:T(8,128)S(1)}, f32[2,64,192]{2,1,0:T(8,128)S(1)}, u32[]{:S(2)}, u32[]{:S(2)}) %collective-permute-start.5) | collective-permute-done | bytes 98336 | tf_op jit(solution)/shard_map/ppermute | solution.py:444
  34.7 1.0 %collective-permute-start.6 = (f32[1,64,192]{2,1,0:T(8,128)S(1)}, f32[1,64,192]{2,1,0:T(8,128)S(1)}, u32[]{:S(2)}, u32[]{:S(2)}) collective-permute-start(f32[1,64,192]{2,1,0:T(8,128)S(1)} %slice.11), channel_id=1, source_target_pairs={{0,2},{1,3},{2,0},{3,1},{4,6},{5,7},{6,4},{7,5},{8,10},{9,11},{10,... | collective-permute-start | bytes 147464 | tf_op jit(solution)/shard_map/ppermute | solution.py:444
  35.7 3.4 %collective-permute-done.9 = bf16[192,768]{1,0:T(8,128)(2,1)S(1)} collective-permute-done((bf16[192,768]{1,0:T(8,128)(2,1)S(1)}, bf16[192,768]{1,0:T(8,128)(2,1)S(1)}, u32[]{:S(2)}, u32[]{:S(2)}) %collective-permute-start.9) | collective-permute-done | bytes 294944 | tf_op jit(solution)/shard_map/ppermute | solution.py:444
  39.1 0.1 add_convert_fusion.a_ref
  39.2 0.7 %collective-permute-start.10 = (bf16[192,768]{1,0:T(8,128)(2,1)S(1)}, bf16[192,768]{1,0:T(8,128)(2,1)S(1)}, u32[]{:S(2)}, u32[]{:S(2)}) collective-permute-start(bf16[192,768]{1,0:T(8,128)(2,1)S(1)} %add_convert_fusion.a_ref), channel_id=1, source_target_pairs={{0,4},{4,0},{8,12},{12,8},{1,5},{5,1},{9,13},{13,9},{2,6},{6,2},{1... | collective-permute-start | bytes 884744 | tf_op jit(solution)/shard_map/ppermute | solution.py:444
  40.0 0.0 collective-permute-done.6
  40.0 3.4 %collective-permute-start.7 = (f32[64,192]{1,0:T(8,128)S(1)}, f32[64,192]{1,0:T(8,128)S(1)}, u32[]{:S(2)}, u32[]{:S(2)}) collective-permute-start(f32[64,192]{1,0:T(8,128)S(1)} %fusion), channel_id=1, source_target_pairs={{0,8},{4,12},{8,0},{12,4},{1,9},{5,13},{9,1},{13,5},{2,10},{6,14},... | collective-permute-start | bytes 147464 | tf_op jit(solution)/shard_map/ppermute | solution.py:444
  43.4 4.4 %collective-permute-done.7 = f32[64,192]{1,0:T(8,128)S(1)} collective-permute-done((f32[64,192]{1,0:T(8,128)S(1)}, f32[64,192]{1,0:T(8,128)S(1)}, u32[]{:S(2)}, u32[]{:S(2)}) %collective-permute-start.7) | collective-permute-done | bytes 49184 | tf_op jit(solution)/shard_map/ppermute | solution.py:444
  47.8 4.2 %collective-permute-start.8 = (f32[64,192]{1,0:T(8,128)S(1)}, f32[64,192]{1,0:T(8,128)S(1)}, u32[]{:S(2)}, u32[]{:S(2)}) collective-permute-start(f32[64,192]{1,0:T(8,128)S(1)} %add.14.sa_ref), channel_id=1, source_target_pairs={{0,4},{4,0},{8,12},{12,8},{1,5},{5,1},{9,13},{13,9},{2,6},{6,2},{1... | collective-permute-start | bytes 147464 | tf_op jit(solution)/shard_map/ppermute | solution.py:444
  52.0 0.0 collective-permute-done.10.b_ref
  52.0 1.3 %shard_map.98._ = f32[2,192,768]{2,1,0:T(8,128)} custom-call(bf16[192,768]{1,0:T(8,128)(2,1)S(1)} %add_convert_fusion.a_ref, bf16[192,768]{1,0:T(8,128)(2,1)S(1)} %collective-permute-done.10.b_ref), custom_call_target="tpu_custom_call" | custom-call | flops 1048576 | bytes 2097152 | tf_op jit(solution)/shard_map/pallas_call | solution.py:570
  53.3 0.9 %collective-permute-done.8.sb_ref = f32[64,192]{1,0:T(8,128)S(1)} collective-permute-done((f32[64,192]{1,0:T(8,128)S(1)}, f32[64,192]{1,0:T(8,128)S(1)}, u32[]{:S(2)}, u32[]{:S(2)}) %collective-permute-start.8) | collective-permute-done | bytes 49184 | tf_op jit(solution)/shard_map/ppermute | solution.py:444
  54.3 1.6 %shard_map.99 = (f32[2,192,768]{2,1,0:T(8,128)}, f32[5,2,192]{2,1,0:T(2,128)}, f32[4,192]{1,0:T(4,128)}) custom-call(bf16[128,768]{1,0:T(8,128)(2,1)S(1)} %get-tuple-element.54.st_ref, f32[64,192]{1,0:T(8,128)S(1)} %add.14.sa_ref, f32[64,192]{1,0:T(8,128)S(1)} %collective-permute-done.8.sb_ref, ...), custom_call_target="tpu_custom_call", output_to_operand_aliasing={{0}: (3, {})} | custom-call | flops 16777216 | bytes 2097152 | tf_op jit(solution)/shard_map/pallas_call | solution.py:579
  (6 shorter events, 0.1 us)
Async XLA Ops:
  0.6 12.4 %copy-start = (s32[2]{0:T(128)S(1)}, s32[2]{0:T(128)}, u32[]{:S(2)}) copy-start(s32[2]{0:T(128)} %dils.5) | copy-start | bytes 28
  1.7 11.2 %collective-permute-start.1 = (bf16[208,768]{1,0:T(8,128)(2,1)S(1)}, bf16[208,768]{1,0:T(8,128)(2,1)S(1)}, u32[]{:S(2)}, u32[]{:S(2)}) collective-permute-start(bf16[208,768]{1,0:T(8,128)(2,1)S(1)} %get-tuple-element.47.refs_0_), channel_id=1, source_target_pairs={{0,2},{1,3},{2,0},{3,1},{4,6},{5,7},{6,4},{7,5},{8,10},{9,11},{10,... | collective-permute-start | bytes 958472 | tf_op jit(solution)/shard_map/ppermute | solution.py:444
  4.7 3.6 %collective-permute-start.2 = (s32[1,768]{1,0:T(1,128)S(1)}, s32[1,768]{1,0:T(1,128)S(1)}, u32[]{:S(2)}, u32[]{:S(2)}) collective-permute-start(s32[1,768]{1,0:T(1,128)S(1)} %get-tuple-element.48), channel_id=1, source_target_pairs={{0,4},{4,0},{8,12},{12,8},{1,5},{5,1},{9,13},{13,9},{2,6},{6,2},{1... | collective-permute-start | bytes 9224 | tf_op jit(solution)/shard_map/ppermute | solution.py:444
  8.3 4.6 %collective-permute-start.3 = (s32[2,768]{1,0:T(2,128)S(1)}, s32[2,768]{1,0:T(2,128)S(1)}, u32[]{:S(2)}, u32[]{:S(2)}) collective-permute-start(s32[2,768]{1,0:T(2,128)S(1)} %pad_add_fusion.1), channel_id=1, source_target_pairs={{0,8},{4,12},{8,0},{12,4},{1,9},{5,13},{9,1},{13,5},{2,10},{6,14},... | collective-permute-start | bytes 18440 | tf_op jit(solution)/shard_map/ppermute | solution.py:444
  11.0 3.2 %collective-permute-start = (bf16[208,768]{1,0:T(8,128)(2,1)S(1)}, bf16[208,768]{1,0:T(8,128)(2,1)S(1)}, u32[]{:S(2)}, u32[]{:S(2)}) collective-permute-start(bf16[208,768]{1,0:T(8,128)(2,1)S(1)} %get-tuple-element.47.refs_0_), channel_id=1, source_target_pairs={{0,1},{1,0},{2,3},{3,2},{4,5},{5,4},{6,7},{7,6},{8,9},{9,8},{10,11... | collective-permute-start | bytes 958472 | tf_op jit(solution)/shard_map/ppermute | solution.py:444
  12.9 1.7 %collective-permute-start.4 = (bf16[208,768]{1,0:T(8,128)(2,1)S(1)}, bf16[208,768]{1,0:T(8,128)(2,1)S(1)}, u32[]{:S(2)}, u32[]{:S(2)}) collective-permute-start(bf16[208,768]{1,0:T(8,128)(2,1)S(1)} %collective-permute-done.1.refs_2_), channel_id=1, source_target_pairs={{0,1},{1,0},{2,3},{3,2},{4,5},{5,4},{6,7},{7,6},{8,9},{9,8},{10,11... | collective-permute-start | bytes 958472 | tf_op jit(solution)/shard_map/ppermute | solution.py:444
  22.8 16.3 %collective-permute-start.9 = (bf16[192,768]{1,0:T(8,128)(2,1)S(1)}, bf16[192,768]{1,0:T(8,128)(2,1)S(1)}, u32[]{:S(2)}, u32[]{:S(2)}) collective-permute-start(bf16[192,768]{1,0:T(8,128)(2,1)S(1)} %get-tuple-element.86), channel_id=1, source_target_pairs={{0,8},{4,12},{8,0},{12,4},{1,9},{5,13},{9,1},{13,5},{2,10},{6,14},... | collective-permute-start | bytes 884744 | tf_op jit(solution)/shard_map/ppermute | solution.py:444
  33.3 1.4 %collective-permute-start.5 = (f32[2,64,192]{2,1,0:T(8,128)S(1)}, f32[2,64,192]{2,1,0:T(8,128)S(1)}, u32[]{:S(2)}, u32[]{:S(2)}) collective-permute-start(f32[2,64,192]{2,1,0:T(8,128)S(1)} %get-tuple-element.85), channel_id=1, source_target_pairs={{0,1},{1,0},{2,3},{3,2},{4,5},{5,4},{6,7},{7,6},{8,9},{9,8},{10,11... | collective-permute-start | bytes 294920 | tf_op jit(solution)/shard_map/ppermute | solution.py:444
  34.7 5.3 %collective-permute-start.6 = (f32[1,64,192]{2,1,0:T(8,128)S(1)}, f32[1,64,192]{2,1,0:T(8,128)S(1)}, u32[]{:S(2)}, u32[]{:S(2)}) collective-permute-start(f32[1,64,192]{2,1,0:T(8,128)S(1)} %slice.11), channel_id=1, source_target_pairs={{0,2},{1,3},{2,0},{3,1},{4,6},{5,7},{6,4},{7,5},{8,10},{9,11},{10,... | collective-permute-start | bytes 147464 | tf_op jit(solution)/shard_map/ppermute | solution.py:444
  39.2 12.8 %collective-permute-start.10 = (bf16[192,768]{1,0:T(8,128)(2,1)S(1)}, bf16[192,768]{1,0:T(8,128)(2,1)S(1)}, u32[]{:S(2)}, u32[]{:S(2)}) collective-permute-start(bf16[192,768]{1,0:T(8,128)(2,1)S(1)} %add_convert_fusion.a_ref), channel_id=1, source_target_pairs={{0,4},{4,0},{8,12},{12,8},{1,5},{5,1},{9,13},{13,9},{2,6},{6,2},{1... | collective-permute-start | bytes 884744 | tf_op jit(solution)/shard_map/ppermute | solution.py:444
  40.0 7.9 %collective-permute-start.7 = (f32[64,192]{1,0:T(8,128)S(1)}, f32[64,192]{1,0:T(8,128)S(1)}, u32[]{:S(2)}, u32[]{:S(2)}) collective-permute-start(f32[64,192]{1,0:T(8,128)S(1)} %fusion), channel_id=1, source_target_pairs={{0,8},{4,12},{8,0},{12,4},{1,9},{5,13},{9,1},{13,5},{2,10},{6,14},... | collective-permute-start | bytes 147464 | tf_op jit(solution)/shard_map/ppermute | solution.py:444
  47.8 6.4 %collective-permute-start.8 = (f32[64,192]{1,0:T(8,128)S(1)}, f32[64,192]{1,0:T(8,128)S(1)}, u32[]{:S(2)}, u32[]{:S(2)}) collective-permute-start(f32[64,192]{1,0:T(8,128)S(1)} %add.14.sa_ref), channel_id=1, source_target_pairs={{0,4},{4,0},{8,12},{12,8},{1,5},{5,1},{9,13},{13,9},{2,6},{6,2},{1... | collective-permute-start | bytes 147464 | tf_op jit(solution)/shard_map/ppermute | solution.py:444

commit v6 on v5

--- a/solution.py
+++ b/solution.py
@@ -194,7 +194,7 @@
     tiles = n_chan * width // LANE
     pks, refs = refs[:n_chan], refs[n_chan:]
     (a_ref, mixl_ref, cot_ref), refs = refs[:3], refs[3:]
-    (x2_ref, gm_ref, s_ref, st_ref, e_ref, et_ref), refs = refs[:6], refs[6:]
+    (x2_ref, near_ref, far_ref, s_ref, st_ref, e_ref, et_ref), refs = refs[:7], refs[7:]
     x1_refs, refs = (refs[:tiles], refs[tiles : 2 * tiles]), refs[2 * tiles :]
     gp_refs, refs = (refs[:tiles], refs[tiles : 2 * tiles]), refs[2 * tiles :]
     w_ref, b_ref, m_ref, held, sem = refs
@@ -267,7 +267,10 @@
     copy = pltpu.make_async_copy(held, x2_ref, sem)
     copy.start()
 
-    gm_ref[...] = t_dot(s_ref[...], m_ref[...]).astype(BF)
+    part = t_dot(s_ref[...], m_ref[...]).astype(BF)
+    odd = lax.axis_index("seq") % 2 == 1
+    near_ref[...] = jnp.where(odd, part[width // 2 :], part[: width // 2])
+    far_ref[...] = jnp.where(odd, part[: width // 2], part[width // 2 :])
     copy.wait()
 
 
@@ -386,13 +389,13 @@
         place[at, ROW_GT0:, :] = tail_ref[0:16, lanes]
 
 
-def mix1_kernel(n_chan, width, a_ref, b_ref, out_ref, held, sem):
-    def block(k):
-        lanes = slice(k * width, (k + 1) * width)
-        return a_ref[:, lanes].astype(F32) + b_ref[:, lanes].astype(F32)
-
-    for k, part in enumerate(xor_blocks([block(k) for k in range(n_chan)], lax.axis_index("chan"))):
-        held[:, k * width : (k + 1) * width] = part
+def mix1_kernel(n_chan, width, near_ref, far_ref, out_ref, held, sem):
+    me, odd = lax.axis_index("chan"), lax.axis_index("seq") % 2
+    half = width // 2
+    for source, first in ((near_ref, odd * half), (far_ref, (1 - odd) * half)):
+        blocks = [source[:, k * width : (k + 1) * width].astype(F32) for k in range(n_chan)]
+        for k, part in enumerate(xor_blocks(blocks, me)):
+            held[pl.ds(pl.multiple_of(first, half), half), k * width : (k + 1) * width] = part
     copy = pltpu.make_async_copy(held, out_ref.at[1], sem)
     copy.start()
     copy.wait()
@@ -506,19 +509,20 @@
     )(dilations, letters)
 
     rows_ext = shape((ext, LANE), F32)
-    x2, gm1, s1, stack, table, table_r, *strands = call(
+    x2, near, far, s1, stack, table, table_r, *strands = call(
         functools.partial(forward_kernel, n_chan, rows, width, scale),
         [SMEM] + [VMEM] * (n_chan + 3),
         [
             shape((width, rows), BF),
-            shape((width, chans), BF),
+            shape((width // 2, chans), BF),
+            shape((width // 2, chans), BF),
             shape((rows, width), BF),
             shape((4 * JB, chans), BF),
             shape((TABLE, chans), BF),
             shape((TABLE, chans), BF),
         ]
         + [rows_ext] * (4 * tiles),
-        [HBM] + [VMEM] * (5 + 4 * tiles),
+        [HBM] + [VMEM] * (6 + 4 * tiles),
         [
             pltpu.VMEM((4 * JB, chans), BF),
             pltpu.VMEM((4 * JB, chans), BF),
@@ -550,13 +554,14 @@
         (3 << 30, 8 << 20),
     )(dilations, *pks, hot, hot1, mixl, cot, s1, table, table_r, *strands)
 
-    g_mine = gm1
-    for bit in reversed(range(seq_bits)):
-        g_other = flip_bits(g_mine, "seq", 1 << bit)
-        if bit:
-            g_mine = lax.optimization_barrier(
-                (g_mine.astype(F32) + g_other.astype(F32)).astype(BF)
-            )
+    def rounded_sum(a, b):
+        return lax.optimization_barrier((a.astype(F32) + b.astype(F32)).astype(BF))
+
+    arrived = lax.optimization_barrier((flip_bits(far, "seq", 1), keep))[0]
+    g_mine = rounded_sum(near, arrived)
+    for bit in range(1, seq_bits):
+        g_mine = rounded_sum(g_mine, flip_bits(g_mine, "seq", 1 << bit))
+    g_other = flip_bits(g_mine, "seq", 1)
     s_mine = keep + flip_bits(send, "chan", 1)
     for bit in range(1, n_chan.bit_length() - 1):
         s_mine = s_mine[0::2] + flip_bits(s_mine[1::2], "chan", 1 << bit)

time: 56.1 us -> 54.1 us (0.964)
  starting transfers between devices: 19.4 us -> 17.5 us
  Pallas kernels: 22.6 us -> 21.8 us
    ppermute x11 -> x12, starting transfers between devices: 19.4 us -> 17.5 us  [flip_bits(): lax.ppermute(x, axis, [(i, i ^ mask) for i in range(lax.axis_size(axis))])]
    ppermute x11 -> x12, waiting for transfers between devices: 13 us -> 13.3 us  [flip_bits(): lax.ppermute(x, axis, [(i, i ^ mask) for i in range(lax.axis_size(axis))])]
  transfers between devices with their start and end apart: 11 -> 12, of which waited for: 7 -> 7; matrix products, arithmetic and copies ran while one was open for 0% -> 0% of each run, Pallas kernels for 21% -> 21%
where the time goes in v6:
time: 54.1 us; the launch traced here: 53.6 us
  Pallas kernels  21.8 us (40%)
  starting transfers between devices  17.5 us (32%)
  waiting for transfers between devices  13.3 us (25%)
  between operations  0.77 us (1%)
    ppermute x12, starting transfers between devices, flip_bits(): lax.ppermute(x, axis, [(i, i ^ mask) for i in range(lax.axis_size(axis))])  17.5 us
    ppermute x12, waiting for transfers between devices, flip_bits(): lax.ppermute(x, axis, [(i, i ^ mask) for i in range(lax.axis_size(axis))])  13.3 us
    pallas_call x1, Pallas kernels, body(): call(functools.partial(forward_kernel, n_chan, rows, width, scale), [SMEM...  8 us
    pallas_call x1, Pallas kernels, body(): call(functools.partial(backward_kernel, n_chan, rows, width, scale), [SME...  7.35 us
    pallas_call x1, Pallas kernels, body(): call(functools.partial(finish_kernel, n_chan, width), [VMEM, VMEM, VMEM,...  1.64 us
    pallas_call x1, Pallas kernels, body(): call(functools.partial(local_kernel, n_chan, width), [HBM, HBM], [shape((...  1.44 us
    pallas_call x1, Pallas kernels, body(): call(functools.partial(mix1_kernel, n_chan, width), [VMEM, VMEM], [shape(...  1.2 us
    pallas_call x1, Pallas kernels, body(): call(functools.partial(prep_kernel, n_seq, rows), [SMEM, VMEM], [shape((p...  1.14 us
  transfers between devices with their start and end apart: 12, of which 7 were waited for; matrix products, arithmetic and copies ran while one was open for 0% of the time, Pallas kernels for 21%

profile of v6, /device:TPU:0, one launch (start us, length us, event | category | flops | bytes accessed | tf_op | source)
XLA Modules:
  0.0 53.6 jit_solution(2701113747582634219)
XLA Ops:
  0.6 0.0 copy-start
  0.6 1.1 %shard_map.93 = (bf16[208,768]{1,0:T(8,128)(2,1)S(1)}, s32[1,768]{1,0:T(1,128)S(1)}) custom-call(bf16[2,192,768]{2,1,0:T(8,128)(2,1)} %bitcast.9, bf16[4,192]{1,0:T(4,128)(2,1)} %embed_ref.1, bf16[5,2,192]{2,1,0:T(2,128)(2,1)} %bitcast.12, s32[768]{0:T(1024)} %tok_ref.1), custom_call_target="tpu_custom_call" | custom-call | bytes 589824 | tf_op jit(solution)/shard_map/pallas_call | solution.py:463
  1.7 3.0 %collective-permute-start.1 = (bf16[208,768]{1,0:T(8,128)(2,1)S(1)}, bf16[208,768]{1,0:T(8,128)(2,1)S(1)}, u32[]{:S(2)}, u32[]{:S(2)}) collective-permute-start(bf16[208,768]{1,0:T(8,128)(2,1)S(1)} %get-tuple-element.49.refs_0_), channel_id=1, source_target_pairs={{0,2},{1,3},{2,0},{3,1},{4,6},{5,7},{6,4},{7,5},{8,10},{9,11},{10,... | collective-permute-start | bytes 958472 | tf_op jit(solution)/shard_map/ppermute | solution.py:447
  4.7 1.6 %collective-permute-start.2 = (s32[1,768]{1,0:T(1,128)S(1)}, s32[1,768]{1,0:T(1,128)S(1)}, u32[]{:S(2)}, u32[]{:S(2)}) collective-permute-start(s32[1,768]{1,0:T(1,128)S(1)} %get-tuple-element.50), channel_id=1, source_target_pairs={{0,4},{4,0},{8,12},{12,8},{1,5},{5,1},{9,13},{13,9},{2,6},{6,2},{1... | collective-permute-start | bytes 9224 | tf_op jit(solution)/shard_map/ppermute | solution.py:447
  6.3 2.0 %collective-permute-done.2 = s32[1,768]{1,0:T(1,128)S(1)} collective-permute-done((s32[1,768]{1,0:T(1,128)S(1)}, s32[1,768]{1,0:T(1,128)S(1)}, u32[]{:S(2)}, u32[]{:S(2)}) %collective-permute-start.2) | collective-permute-done | bytes 3104 | tf_op jit(solution)/shard_map/ppermute | solution.py:447
  8.3 2.7 %collective-permute-start.3 = (s32[2,768]{1,0:T(2,128)S(1)}, s32[2,768]{1,0:T(2,128)S(1)}, u32[]{:S(2)}, u32[]{:S(2)}) collective-permute-start(s32[2,768]{1,0:T(2,128)S(1)} %pad_add_fusion.1), channel_id=1, source_target_pairs={{0,8},{4,12},{8,0},{12,4},{1,9},{5,13},{9,1},{13,5},{2,10},{6,14},... | collective-permute-start | bytes 18440 | tf_op jit(solution)/shard_map/ppermute | solution.py:447
  11.0 0.0 collective-permute-start
  11.0 1.4 %shard_map.94 = (bf16[192,768]{1,0:T(8,128)(2,1)S(1)}, bf16[768,192]{1,0:T(8,128)(2,1)S(1)}) custom-call(bf16[2,192,768]{2,1,0:T(8,128)(2,1)} %bitcast.10, bf16[192,768]{1,0:T(8,128)(2,1)} %bitcast.11), custom_call_target="tpu_custom_call" | custom-call | flops 1048576 | bytes 1048576 | tf_op jit(solution)/shard_map/pallas_call | solution.py:481
  12.4 0.5 collective-permute-done.3
  12.9 0.0 collective-permute-done.1.refs_2_
  12.9 0.1 collective-permute-start.4
  13.0 1.1 %shard_map.95 = (bf16[896,128]{1,0:T(8,128)(2,1)S(1)}, bf16[64,896]{1,0:T(8,128)(2,1)S(1)}, bf16[64,768]{1,0:T(8,128)(2,1)S(1)}) custom-call(s32[2]{0:T(128)S(1)} %copy-done, s32[4,768]{1,0:T(4,128)S(1)} %pad_add_fusion.tok_ref), custom_call_target="tpu_custom_call" | custom-call | flops 1048576 | bytes 1048576 | tf_op jit(solution)/shard_map/pallas_call | solution.py:501
  14.2 0.0 collective-permute-done.refs_1_
  14.2 0.4 collective-permute-done.4.refs_3_
  14.6 8.0 %shard_map.96 = (bf16[192,768]{1,0:T(8,128)(2,1)}, bf16[96,768]{1,0:T(8,128)(2,1)S(1)}, bf16[96,768]{1,0:T(8,128)(2,1)S(1)}, bf16[768,192]{1,0:T(8,128)(2,1)S(1)...) custom-call(s32[2]{0:T(128)S(1)} %copy-done, ...), custom_call_target="tpu_custom_call" | custom-call | flops 3221225472 | bytes 8388608 | tf_op jit(solution)/shard_map/pallas_call | solution.py:512
  22.6 1.6 %collective-permute-start.9 = (bf16[96,768]{1,0:T(8,128)(2,1)S(1)}, bf16[96,768]{1,0:T(8,128)(2,1)S(1)}, u32[]{:S(2)}, u32[]{:S(2)}) collective-permute-start(bf16[96,768]{1,0:T(8,128)(2,1)S(1)} %get-tuple-element.89), channel_id=1, source_target_pairs={{0,4},{4,0},{8,12},{12,8},{1,5},{5,1},{9,13},{13,9},{2,6},{6,2},{1... | collective-permute-start | bytes 442376 | tf_op jit(solution)/shard_map/ppermute | solution.py:447
  24.3 7.4 %shard_map.97 = (f32[2,64,192]{2,1,0:T(8,128)S(1)}, f32[2,64,192]{2,1,0:T(8,128)S(1)}) custom-call(s32[2]{0:T(128)S(1)} %copy-done, bf16[208,768]{1,0:T(8,128)(2,1)S(1)} %get-tuple-element.49.refs_0_, bf16[208,768]{1,0:T(8,128)(2,1)S(1)} %collective-permute-done.refs_1_, bf16[208,768]{1,0:T(8,128)(2,1)S(1)} %collective-permute-done.1.refs_2_, ...), custom_call_target="tpu_custom_call" | custom-call | flops 3221225472 | bytes 8388608 | tf_op jit(solution)/shard_map/pallas_call | solution.py:537
  31.6 0.0 collective-permute-done.9
  31.7 2.6 %collective-permute-start.10 = (bf16[96,768]{1,0:T(8,128)(2,1)S(1)}, bf16[96,768]{1,0:T(8,128)(2,1)S(1)}, u32[]{:S(2)}, u32[]{:S(2)}) collective-permute-start(bf16[96,768]{1,0:T(8,128)(2,1)S(1)} %add_convert_fusion.1), channel_id=1, source_target_pairs={{0,8},{4,12},{8,0},{12,4},{1,9},{5,13},{9,1},{13,5},{2,10},{6,14},... | collective-permute-start | bytes 442376 | tf_op jit(solution)/shard_map/ppermute | solution.py:447
  34.3 0.0 collective-permute-start.5
  34.3 1.3 %collective-permute-done.5 = f32[2,64,192]{2,1,0:T(8,128)S(1)} collective-permute-done((f32[2,64,192]{2,1,0:T(8,128)S(1)}, f32[2,64,192]{2,1,0:T(8,128)S(1)}, u32[]{:S(2)}, u32[]{:S(2)}) %collective-permute-start.5) | collective-permute-done | bytes 98336 | tf_op jit(solution)/shard_map/ppermute | solution.py:447
  35.7 1.0 %collective-permute-start.6 = (f32[1,64,192]{2,1,0:T(8,128)S(1)}, f32[1,64,192]{2,1,0:T(8,128)S(1)}, u32[]{:S(2)}, u32[]{:S(2)}) collective-permute-start(f32[1,64,192]{2,1,0:T(8,128)S(1)} %slice.11), channel_id=1, source_target_pairs={{0,2},{1,3},{2,0},{3,1},{4,6},{5,7},{6,4},{7,5},{8,10},{9,11},{10,... | collective-permute-start | bytes 147464 | tf_op jit(solution)/shard_map/ppermute | solution.py:447
  36.8 4.5 %collective-permute-done.10 = bf16[96,768]{1,0:T(8,128)(2,1)S(1)} collective-permute-done((bf16[96,768]{1,0:T(8,128)(2,1)S(1)}, bf16[96,768]{1,0:T(8,128)(2,1)S(1)}, u32[]{:S(2)}, u32[]{:S(2)}) %collective-permute-start.10) | collective-permute-done | bytes 147488 | tf_op jit(solution)/shard_map/ppermute | solution.py:447
  41.3 0.1 collective-permute-start.11
  41.4 0.0 collective-permute-done.6
  41.5 3.2 %collective-permute-start.7 = (f32[64,192]{1,0:T(8,128)S(1)}, f32[64,192]{1,0:T(8,128)S(1)}, u32[]{:S(2)}, u32[]{:S(2)}) collective-permute-start(f32[64,192]{1,0:T(8,128)S(1)} %fusion), channel_id=1, source_target_pairs={{0,8},{4,12},{8,0},{12,4},{1,9},{5,13},{9,1},{13,5},{2,10},{6,14},... | collective-permute-start | bytes 147464 | tf_op jit(solution)/shard_map/ppermute | solution.py:447
  44.6 3.0 %collective-permute-done.7 = f32[64,192]{1,0:T(8,128)S(1)} collective-permute-done((f32[64,192]{1,0:T(8,128)S(1)}, f32[64,192]{1,0:T(8,128)S(1)}, u32[]{:S(2)}, u32[]{:S(2)}) %collective-permute-start.7) | collective-permute-done | bytes 49184 | tf_op jit(solution)/shard_map/ppermute | solution.py:447
  47.6 1.6 %collective-permute-start.8 = (f32[64,192]{1,0:T(8,128)S(1)}, f32[64,192]{1,0:T(8,128)S(1)}, u32[]{:S(2)}, u32[]{:S(2)}) collective-permute-start(f32[64,192]{1,0:T(8,128)S(1)} %add.17.sa_ref), channel_id=1, source_target_pairs={{0,4},{4,0},{8,12},{12,8},{1,5},{5,1},{9,13},{13,9},{2,6},{6,2},{1... | collective-permute-start | bytes 147464 | tf_op jit(solution)/shard_map/ppermute | solution.py:447
  49.2 0.0 collective-permute-done.11.far_ref
  49.2 1.2 %shard_map.98._ = f32[2,192,768]{2,1,0:T(8,128)} custom-call(bf16[96,768]{1,0:T(8,128)(2,1)S(1)} %add_convert_fusion.near_ref, bf16[96,768]{1,0:T(8,128)(2,1)S(1)} %collective-permute-done.11.far_ref), custom_call_target="tpu_custom_call" | custom-call | flops 1048576 | bytes 2097152 | tf_op jit(solution)/shard_map/pallas_call | solution.py:575
  50.4 1.6 %collective-permute-done.8.sb_ref = f32[64,192]{1,0:T(8,128)S(1)} collective-permute-done((f32[64,192]{1,0:T(8,128)S(1)}, f32[64,192]{1,0:T(8,128)S(1)}, u32[]{:S(2)}, u32[]{:S(2)}) %collective-permute-start.8) | collective-permute-done | bytes 49184 | tf_op jit(solution)/shard_map/ppermute | solution.py:447
  51.9 1.6 %shard_map.99 = (f32[2,192,768]{2,1,0:T(8,128)}, f32[5,2,192]{2,1,0:T(2,128)}, f32[4,192]{1,0:T(4,128)}) custom-call(bf16[128,768]{1,0:T(8,128)(2,1)S(1)} %get-tuple-element.56.st_ref, f32[64,192]{1,0:T(8,128)S(1)} %add.17.sa_ref, f32[64,192]{1,0:T(8,128)S(1)} %collective-permute-done.8.sb_ref, ...), custom_call_target="tpu_custom_call", output_to_operand_aliasing={{0}: (3, {})} | custom-call | flops 16777216 | bytes 2097152 | tf_op jit(solution)/shard_map/pallas_call | solution.py:584
  (9 shorter events, 0.1 us)
Async XLA Ops:
  0.6 12.4 %copy-start = (s32[2]{0:T(128)S(1)}, s32[2]{0:T(128)}, u32[]{:S(2)}) copy-start(s32[2]{0:T(128)} %dils.5) | copy-start | bytes 28
  1.7 11.2 %collective-permute-start.1 = (bf16[208,768]{1,0:T(8,128)(2,1)S(1)}, bf16[208,768]{1,0:T(8,128)(2,1)S(1)}, u32[]{:S(2)}, u32[]{:S(2)}) collective-permute-start(bf16[208,768]{1,0:T(8,128)(2,1)S(1)} %get-tuple-element.49.refs_0_), channel_id=1, source_target_pairs={{0,2},{1,3},{2,0},{3,1},{4,6},{5,7},{6,4},{7,5},{8,10},{9,11},{10,... | collective-permute-start | bytes 958472 | tf_op jit(solution)/shard_map/ppermute | solution.py:447
  4.7 3.6 %collective-permute-start.2 = (s32[1,768]{1,0:T(1,128)S(1)}, s32[1,768]{1,0:T(1,128)S(1)}, u32[]{:S(2)}, u32[]{:S(2)}) collective-permute-start(s32[1,768]{1,0:T(1,128)S(1)} %get-tuple-element.50), channel_id=1, source_target_pairs={{0,4},{4,0},{8,12},{12,8},{1,5},{5,1},{9,13},{13,9},{2,6},{6,2},{1... | collective-permute-start | bytes 9224 | tf_op jit(solution)/shard_map/ppermute | solution.py:447
  8.3 4.6 %collective-permute-start.3 = (s32[2,768]{1,0:T(2,128)S(1)}, s32[2,768]{1,0:T(2,128)S(1)}, u32[]{:S(2)}, u32[]{:S(2)}) collective-permute-start(s32[2,768]{1,0:T(2,128)S(1)} %pad_add_fusion.1), channel_id=1, source_target_pairs={{0,8},{4,12},{8,0},{12,4},{1,9},{5,13},{9,1},{13,5},{2,10},{6,14},... | collective-permute-start | bytes 18440 | tf_op jit(solution)/shard_map/ppermute | solution.py:447
  11.0 3.2 %collective-permute-start = (bf16[208,768]{1,0:T(8,128)(2,1)S(1)}, bf16[208,768]{1,0:T(8,128)(2,1)S(1)}, u32[]{:S(2)}, u32[]{:S(2)}) collective-permute-start(bf16[208,768]{1,0:T(8,128)(2,1)S(1)} %get-tuple-element.49.refs_0_), channel_id=1, source_target_pairs={{0,1},{1,0},{2,3},{3,2},{4,5},{5,4},{6,7},{7,6},{8,9},{9,8},{10,11... | collective-permute-start | bytes 958472 | tf_op jit(solution)/shard_map/ppermute | solution.py:447
  12.9 1.7 %collective-permute-start.4 = (bf16[208,768]{1,0:T(8,128)(2,1)S(1)}, bf16[208,768]{1,0:T(8,128)(2,1)S(1)}, u32[]{:S(2)}, u32[]{:S(2)}) collective-permute-start(bf16[208,768]{1,0:T(8,128)(2,1)S(1)} %collective-permute-done.1.refs_2_), channel_id=1, source_target_pairs={{0,1},{1,0},{2,3},{3,2},{4,5},{5,4},{6,7},{7,6},{8,9},{9,8},{10,11... | collective-permute-start | bytes 958472 | tf_op jit(solution)/shard_map/ppermute | solution.py:447
  22.6 9.0 %collective-permute-start.9 = (bf16[96,768]{1,0:T(8,128)(2,1)S(1)}, bf16[96,768]{1,0:T(8,128)(2,1)S(1)}, u32[]{:S(2)}, u32[]{:S(2)}) collective-permute-start(bf16[96,768]{1,0:T(8,128)(2,1)S(1)} %get-tuple-element.89), channel_id=1, source_target_pairs={{0,4},{4,0},{8,12},{12,8},{1,5},{5,1},{9,13},{13,9},{2,6},{6,2},{1... | collective-permute-start | bytes 442376 | tf_op jit(solution)/shard_map/ppermute | solution.py:447
  31.7 9.6 %collective-permute-start.10 = (bf16[96,768]{1,0:T(8,128)(2,1)S(1)}, bf16[96,768]{1,0:T(8,128)(2,1)S(1)}, u32[]{:S(2)}, u32[]{:S(2)}) collective-permute-start(bf16[96,768]{1,0:T(8,128)(2,1)S(1)} %add_convert_fusion.1), channel_id=1, source_target_pairs={{0,8},{4,12},{8,0},{12,4},{1,9},{5,13},{9,1},{13,5},{2,10},{6,14},... | collective-permute-start | bytes 442376 | tf_op jit(solution)/shard_map/ppermute | solution.py:447
  34.3 1.3 %collective-permute-start.5 = (f32[2,64,192]{2,1,0:T(8,128)S(1)}, f32[2,64,192]{2,1,0:T(8,128)S(1)}, u32[]{:S(2)}, u32[]{:S(2)}) collective-permute-start(f32[2,64,192]{2,1,0:T(8,128)S(1)} %get-tuple-element.87), channel_id=1, source_target_pairs={{0,1},{1,0},{2,3},{3,2},{4,5},{5,4},{6,7},{7,6},{8,9},{9,8},{10,11... | collective-permute-start | bytes 294920 | tf_op jit(solution)/shard_map/ppermute | solution.py:447
  35.7 5.7 %collective-permute-start.6 = (f32[1,64,192]{2,1,0:T(8,128)S(1)}, f32[1,64,192]{2,1,0:T(8,128)S(1)}, u32[]{:S(2)}, u32[]{:S(2)}) collective-permute-start(f32[1,64,192]{2,1,0:T(8,128)S(1)} %slice.11), channel_id=1, source_target_pairs={{0,2},{1,3},{2,0},{3,1},{4,6},{5,7},{6,4},{7,5},{8,10},{9,11},{10,... | collective-permute-start | bytes 147464 | tf_op jit(solution)/shard_map/ppermute | solution.py:447
  41.3 7.8 %collective-permute-start.11 = (bf16[96,768]{1,0:T(8,128)(2,1)S(1)}, bf16[96,768]{1,0:T(8,128)(2,1)S(1)}, u32[]{:S(2)}, u32[]{:S(2)}) collective-permute-start(bf16[96,768]{1,0:T(8,128)(2,1)S(1)} %add_convert_fusion.near_ref), channel_id=1, source_target_pairs={{0,4},{4,0},{8,12},{12,8},{1,5},{5,1},{9,13},{13,9},{2,6},{6,2},{1... | collective-permute-start | bytes 442376 | tf_op jit(solution)/shard_map/ppermute | solution.py:447
  41.5 6.1 %collective-permute-start.7 = (f32[64,192]{1,0:T(8,128)S(1)}, f32[64,192]{1,0:T(8,128)S(1)}, u32[]{:S(2)}, u32[]{:S(2)}) collective-permute-start(f32[64,192]{1,0:T(8,128)S(1)} %fusion), channel_id=1, source_target_pairs={{0,8},{4,12},{8,0},{12,4},{1,9},{5,13},{9,1},{13,5},{2,10},{6,14},... | collective-permute-start | bytes 147464 | tf_op jit(solution)/shard_map/ppermute | solution.py:447
  47.6 4.3 %collective-permute-start.8 = (f32[64,192]{1,0:T(8,128)S(1)}, f32[64,192]{1,0:T(8,128)S(1)}, u32[]{:S(2)}, u32[]{:S(2)}) collective-permute-start(f32[64,192]{1,0:T(8,128)S(1)} %add.17.sa_ref), channel_id=1, source_target_pairs={{0,4},{4,0},{8,12},{12,8},{1,5},{5,1},{9,13},{13,9},{2,6},{6,2},{1... | collective-permute-start | bytes 147464 | tf_op jit(solution)/shard_map/ppermute | solution.py:447

commit v7 on v6

--- a/solution.py
+++ b/solution.py
@@ -557,19 +557,25 @@
     def rounded_sum(a, b):
         return lax.optimization_barrier((a.astype(F32) + b.astype(F32)).astype(BF))
 
-    arrived = lax.optimization_barrier((flip_bits(far, "seq", 1), keep))[0]
+    def after(value, *others):
+        return lax.optimization_barrier((value, *others))[0]
+
+    arrived = flip_bits(far, "seq", 1)
+    s_mine = keep + flip_bits(send, "chan", 1)
+    arrived = after(arrived, s_mine)
     g_mine = rounded_sum(near, arrived)
-    for bit in range(1, seq_bits):
-        g_mine = rounded_sum(g_mine, flip_bits(g_mine, "seq", 1 << bit))
-    g_other = flip_bits(g_mine, "seq", 1)
-    s_mine = keep + flip_bits(send, "chan", 1)
     for bit in range(1, n_chan.bit_length() - 1):
         s_mine = s_mine[0::2] + flip_bits(s_mine[1::2], "chan", 1 << bit)
     s_mine = s_mine[0]
+    far_sums = [s_mine]
     for bit in reversed(range(seq_bits)):
         s_other = flip_bits(s_mine, "seq", 1 << bit)
         if bit:
             s_mine = s_mine + s_other
+            far_sums.append(s_mine)
+    for bit in range(1, seq_bits):
+        g_mine = rounded_sum(g_mine, after(flip_bits(g_mine, "seq", 1 << bit), far_sums[bit]))
+    g_other = flip_bits(g_mine, "seq", 1)
 
     big = pltpu.VMEM((width, chans), F32)
     (grad_mix,) = call(

time: 54.1 us -> 56.2 us (1.039)
  waiting for transfers between devices: 13.3 us -> 15.8 us
    ppermute x12, waiting for transfers between devices: 13.3 us -> 15.8 us  [flip_bits(): lax.ppermute(x, axis, [(i, i ^ mask) for i in range(lax.axis_size(axis))])]
  transfers between devices with their start and end apart: 12 -> 12, of which waited for: 7 -> 7; matrix products, arithmetic and copies ran while one was open for 0% -> 0% of each run, Pallas kernels for 21% -> 20%
where the time goes in v7:
time: 56.2 us; the launch traced here: 56 us
  Pallas kernels  21.8 us (39%)
  starting transfers between devices  17.4 us (31%)
  waiting for transfers between devices  15.8 us (28%)
  between operations  0.77 us (1%)
    ppermute x12, starting transfers between devices, flip_bits(): lax.ppermute(x, axis, [(i, i ^ mask) for i in range(lax.axis_size(axis))])  17.4 us
    ppermute x12, waiting for transfers between devices, flip_bits(): lax.ppermute(x, axis, [(i, i ^ mask) for i in range(lax.axis_size(axis))])  15.8 us
    pallas_call x1, Pallas kernels, body(): call(functools.partial(forward_kernel, n_chan, rows, width, scale), [SMEM...  8 us
    pallas_call x1, Pallas kernels, body(): call(functools.partial(backward_kernel, n_chan, rows, width, scale), [SME...  7.35 us
    pallas_call x1, Pallas kernels, body(): call(functools.partial(finish_kernel, n_chan, width), [VMEM, VMEM, VMEM,...  1.65 us
    pallas_call x1, Pallas kernels, body(): call(functools.partial(local_kernel, n_chan, width), [HBM, HBM], [shape((...  1.44 us
    pallas_call x1, Pallas kernels, body(): call(functools.partial(mix1_kernel, n_chan, width), [VMEM, VMEM], [shape(...  1.2 us
    pallas_call x1, Pallas kernels, body(): call(functools.partial(prep_kernel, n_seq, rows), [SMEM, VMEM], [shape((p...  1.14 us
  transfers between devices with their start and end apart: 12, of which 7 were waited for; matrix products, arithmetic and copies ran while one was open for 0% of the time, Pallas kernels for 20%

profile of v7, /device:TPU:0, one launch (start us, length us, event | category | flops | bytes accessed | tf_op | source)
XLA Modules:
  0.0 56.0 jit_solution(3731855353528918667)
XLA Ops:
  0.6 0.0 copy-start
  0.6 1.1 %shard_map.93 = (bf16[208,768]{1,0:T(8,128)(2,1)S(1)}, s32[1,768]{1,0:T(1,128)S(1)}) custom-call(bf16[2,192,768]{2,1,0:T(8,128)(2,1)} %bitcast.9, bf16[4,192]{1,0:T(4,128)(2,1)} %embed_ref.1, bf16[5,2,192]{2,1,0:T(2,128)(2,1)} %bitcast.12, s32[768]{0:T(1024)} %tok_ref.1), custom_call_target="tpu_custom_call" | custom-call | bytes 589824 | tf_op jit(solution)/shard_map/pallas_call | solution.py:463
  1.7 3.0 %collective-permute-start.1 = (bf16[208,768]{1,0:T(8,128)(2,1)S(1)}, bf16[208,768]{1,0:T(8,128)(2,1)S(1)}, u32[]{:S(2)}, u32[]{:S(2)}) collective-permute-start(bf16[208,768]{1,0:T(8,128)(2,1)S(1)} %get-tuple-element.50.refs_0_), channel_id=1, source_target_pairs={{0,2},{1,3},{2,0},{3,1},{4,6},{5,7},{6,4},{7,5},{8,10},{9,11},{10,... | collective-permute-start | bytes 958472 | tf_op jit(solution)/shard_map/ppermute | solution.py:447
  4.7 1.6 %collective-permute-start.2 = (s32[1,768]{1,0:T(1,128)S(1)}, s32[1,768]{1,0:T(1,128)S(1)}, u32[]{:S(2)}, u32[]{:S(2)}) collective-permute-start(s32[1,768]{1,0:T(1,128)S(1)} %get-tuple-element.51), channel_id=1, source_target_pairs={{0,4},{4,0},{8,12},{12,8},{1,5},{5,1},{9,13},{13,9},{2,6},{6,2},{1... | collective-permute-start | bytes 9224 | tf_op jit(solution)/shard_map/ppermute | solution.py:447
  6.3 2.0 %collective-permute-done.2 = s32[1,768]{1,0:T(1,128)S(1)} collective-permute-done((s32[1,768]{1,0:T(1,128)S(1)}, s32[1,768]{1,0:T(1,128)S(1)}, u32[]{:S(2)}, u32[]{:S(2)}) %collective-permute-start.2) | collective-permute-done | bytes 3104 | tf_op jit(solution)/shard_map/ppermute | solution.py:447
  8.3 2.7 %collective-permute-start.3 = (s32[2,768]{1,0:T(2,128)S(1)}, s32[2,768]{1,0:T(2,128)S(1)}, u32[]{:S(2)}, u32[]{:S(2)}) collective-permute-start(s32[2,768]{1,0:T(2,128)S(1)} %pad_add_fusion.1), channel_id=1, source_target_pairs={{0,8},{4,12},{8,0},{12,4},{1,9},{5,13},{9,1},{13,5},{2,10},{6,14},... | collective-permute-start | bytes 18440 | tf_op jit(solution)/shard_map/ppermute | solution.py:447
  11.0 0.0 collective-permute-start
  11.0 1.4 %shard_map.94 = (bf16[192,768]{1,0:T(8,128)(2,1)S(1)}, bf16[768,192]{1,0:T(8,128)(2,1)S(1)}) custom-call(bf16[2,192,768]{2,1,0:T(8,128)(2,1)} %bitcast.10, bf16[192,768]{1,0:T(8,128)(2,1)} %bitcast.11), custom_call_target="tpu_custom_call" | custom-call | flops 1048576 | bytes 1048576 | tf_op jit(solution)/shard_map/pallas_call | solution.py:481
  12.4 0.5 collective-permute-done.3
  12.9 0.0 collective-permute-done.1.refs_2_
  12.9 0.1 collective-permute-start.4
  13.0 1.1 %shard_map.95 = (bf16[896,128]{1,0:T(8,128)(2,1)S(1)}, bf16[64,896]{1,0:T(8,128)(2,1)S(1)}, bf16[64,768]{1,0:T(8,128)(2,1)S(1)}) custom-call(s32[2]{0:T(128)S(1)} %copy-done, s32[4,768]{1,0:T(4,128)S(1)} %pad_add_fusion.tok_ref), custom_call_target="tpu_custom_call" | custom-call | flops 1048576 | bytes 1048576 | tf_op jit(solution)/shard_map/pallas_call | solution.py:501
  14.2 0.0 collective-permute-done.refs_1_
  14.2 0.4 collective-permute-done.4.refs_3_
  14.6 8.0 %shard_map.96 = (bf16[192,768]{1,0:T(8,128)(2,1)}, bf16[96,768]{1,0:T(8,128)(2,1)S(1)}, bf16[96,768]{1,0:T(8,128)(2,1)S(1)}, bf16[768,192]{1,0:T(8,128)(2,1)S(1)...) custom-call(s32[2]{0:T(128)S(1)} %copy-done, ...), custom_call_target="tpu_custom_call" | custom-call | flops 3221225472 | bytes 8388608 | tf_op jit(solution)/shard_map/pallas_call | solution.py:512
  22.6 1.6 %collective-permute-start.9 = (bf16[96,768]{1,0:T(8,128)(2,1)S(1)}, bf16[96,768]{1,0:T(8,128)(2,1)S(1)}, u32[]{:S(2)}, u32[]{:S(2)}) collective-permute-start(bf16[96,768]{1,0:T(8,128)(2,1)S(1)} %get-tuple-element.90), channel_id=1, source_target_pairs={{0,4},{4,0},{8,12},{12,8},{1,5},{5,1},{9,13},{13,9},{2,6},{6,2},{1... | collective-permute-start | bytes 442376 | tf_op jit(solution)/shard_map/ppermute | solution.py:447
  24.3 7.4 %shard_map.97 = (f32[2,64,192]{2,1,0:T(8,128)S(1)}, f32[2,64,192]{2,1,0:T(8,128)S(1)}) custom-call(s32[2]{0:T(128)S(1)} %copy-done, bf16[208,768]{1,0:T(8,128)(2,1)S(1)} %get-tuple-element.50.refs_0_, bf16[208,768]{1,0:T(8,128)(2,1)S(1)} %collective-permute-done.refs_1_, bf16[208,768]{1,0:T(8,128)(2,1)S(1)} %collective-permute-done.1.refs_2_, ...), custom_call_target="tpu_custom_call" | custom-call | flops 3221225472 | bytes 8388608 | tf_op jit(solution)/shard_map/pallas_call | solution.py:537
  31.6 0.0 collective-permute-start.5
  31.7 1.3 %collective-permute-done.5 = f32[2,64,192]{2,1,0:T(8,128)S(1)} collective-permute-done((f32[2,64,192]{2,1,0:T(8,128)S(1)}, f32[2,64,192]{2,1,0:T(8,128)S(1)}, u32[]{:S(2)}, u32[]{:S(2)}) %collective-permute-start.5) | collective-permute-done | bytes 98336 | tf_op jit(solution)/shard_map/ppermute | solution.py:447
  33.0 1.0 %collective-permute-start.6 = (f32[1,64,192]{2,1,0:T(8,128)S(1)}, f32[1,64,192]{2,1,0:T(8,128)S(1)}, u32[]{:S(2)}, u32[]{:S(2)}) collective-permute-start(f32[1,64,192]{2,1,0:T(8,128)S(1)} %slice.11), channel_id=1, source_target_pairs={{0,2},{1,3},{2,0},{3,1},{4,6},{5,7},{6,4},{7,5},{8,10},{9,11},{10,... | collective-permute-start | bytes 147464 | tf_op jit(solution)/shard_map/ppermute | solution.py:447
  34.1 0.0 collective-permute-done.9
  34.1 2.7 %collective-permute-start.10 = (bf16[96,768]{1,0:T(8,128)(2,1)S(1)}, bf16[96,768]{1,0:T(8,128)(2,1)S(1)}, u32[]{:S(2)}, u32[]{:S(2)}) collective-permute-start(bf16[96,768]{1,0:T(8,128)(2,1)S(1)} %add_convert_fusion.1), channel_id=1, source_target_pairs={{0,8},{4,12},{8,0},{12,4},{1,9},{5,13},{9,1},{13,5},{2,10},{6,14},... | collective-permute-start | bytes 442376 | tf_op jit(solution)/shard_map/ppermute | solution.py:447
  36.8 0.6 %collective-permute-done.6 = f32[1,64,192]{2,1,0:T(8,128)S(1)} collective-permute-done((f32[1,64,192]{2,1,0:T(8,128)S(1)}, f32[1,64,192]{2,1,0:T(8,128)S(1)}, u32[]{:S(2)}, u32[]{:S(2)}) %collective-permute-start.6) | collective-permute-done | bytes 49184 | tf_op jit(solution)/shard_map/ppermute | solution.py:447
  37.4 2.6 %collective-permute-start.7 = (f32[64,192]{1,0:T(8,128)S(1)}, f32[64,192]{1,0:T(8,128)S(1)}, u32[]{:S(2)}, u32[]{:S(2)}) collective-permute-start(f32[64,192]{1,0:T(8,128)S(1)} %fusion), channel_id=1, source_target_pairs={{0,8},{4,12},{8,0},{12,4},{1,9},{5,13},{9,1},{13,5},{2,10},{6,14},... | collective-permute-start | bytes 147464 | tf_op jit(solution)/shard_map/ppermute | solution.py:447
  40.0 6.5 %collective-permute-done.7 = f32[64,192]{1,0:T(8,128)S(1)} collective-permute-done((f32[64,192]{1,0:T(8,128)S(1)}, f32[64,192]{1,0:T(8,128)S(1)}, u32[]{:S(2)}, u32[]{:S(2)}) %collective-permute-start.7) | collective-permute-done | bytes 49184 | tf_op jit(solution)/shard_map/ppermute | solution.py:447
  46.6 0.0 collective-permute-done.10
  46.6 0.1 collective-permute-start.11
  46.7 2.0 %collective-permute-start.8 = (f32[64,192]{1,0:T(8,128)S(1)}, f32[64,192]{1,0:T(8,128)S(1)}, u32[]{:S(2)}, u32[]{:S(2)}) collective-permute-start(f32[64,192]{1,0:T(8,128)S(1)} %add.17.sa_ref), channel_id=1, source_target_pairs={{0,4},{4,0},{8,12},{12,8},{1,5},{5,1},{9,13},{13,9},{2,6},{6,2},{1... | collective-permute-start | bytes 147464 | tf_op jit(solution)/shard_map/ppermute | solution.py:447
  48.7 4.4 %collective-permute-done.11.far_ref = bf16[96,768]{1,0:T(8,128)(2,1)S(1)} collective-permute-done((bf16[96,768]{1,0:T(8,128)(2,1)S(1)}, bf16[96,768]{1,0:T(8,128)(2,1)S(1)}, u32[]{:S(2)}, u32[]{:S(2)}) %collective-permute-start.11) | collective-permute-done | bytes 147488 | tf_op jit(solution)/shard_map/ppermute | solution.py:447
  53.2 1.2 %shard_map.98._ = f32[2,192,768]{2,1,0:T(8,128)} custom-call(bf16[96,768]{1,0:T(8,128)(2,1)S(1)} %add_convert_fusion.near_ref, bf16[96,768]{1,0:T(8,128)(2,1)S(1)} %collective-permute-done.11.far_ref), custom_call_target="tpu_custom_call" | custom-call | flops 1048576 | bytes 2097152 | tf_op jit(solution)/shard_map/pallas_call | solution.py:581
  54.4 0.0 collective-permute-done.8.sb_ref
  54.4 1.6 %shard_map.99 = (f32[2,192,768]{2,1,0:T(8,128)}, f32[5,2,192]{2,1,0:T(2,128)}, f32[4,192]{1,0:T(4,128)}) custom-call(bf16[128,768]{1,0:T(8,128)(2,1)S(1)} %get-tuple-element.57.st_ref, f32[64,192]{1,0:T(8,128)S(1)} %add.17.sa_ref, f32[64,192]{1,0:T(8,128)S(1)} %collective-permute-done.8.sb_ref, ...), custom_call_target="tpu_custom_call", output_to_operand_aliasing={{0}: (3, {})} | custom-call | flops 16777216 | bytes 2097152 | tf_op jit(solution)/shard_map/pallas_call | solution.py:590
  (9 shorter events, 0.1 us)
Async XLA Ops:
  0.6 12.4 %copy-start = (s32[2]{0:T(128)S(1)}, s32[2]{0:T(128)}, u32[]{:S(2)}) copy-start(s32[2]{0:T(128)} %dils.5) | copy-start | bytes 28
  1.7 11.2 %collective-permute-start.1 = (bf16[208,768]{1,0:T(8,128)(2,1)S(1)}, bf16[208,768]{1,0:T(8,128)(2,1)S(1)}, u32[]{:S(2)}, u32[]{:S(2)}) collective-permute-start(bf16[208,768]{1,0:T(8,128)(2,1)S(1)} %get-tuple-element.50.refs_0_), channel_id=1, source_target_pairs={{0,2},{1,3},{2,0},{3,1},{4,6},{5,7},{6,4},{7,5},{8,10},{9,11},{10,... | collective-permute-start | bytes 958472 | tf_op jit(solution)/shard_map/ppermute | solution.py:447
  4.7 3.6 %collective-permute-start.2 = (s32[1,768]{1,0:T(1,128)S(1)}, s32[1,768]{1,0:T(1,128)S(1)}, u32[]{:S(2)}, u32[]{:S(2)}) collective-permute-start(s32[1,768]{1,0:T(1,128)S(1)} %get-tuple-element.51), channel_id=1, source_target_pairs={{0,4},{4,0},{8,12},{12,8},{1,5},{5,1},{9,13},{13,9},{2,6},{6,2},{1... | collective-permute-start | bytes 9224 | tf_op jit(solution)/shard_map/ppermute | solution.py:447
  8.3 4.6 %collective-permute-start.3 = (s32[2,768]{1,0:T(2,128)S(1)}, s32[2,768]{1,0:T(2,128)S(1)}, u32[]{:S(2)}, u32[]{:S(2)}) collective-permute-start(s32[2,768]{1,0:T(2,128)S(1)} %pad_add_fusion.1), channel_id=1, source_target_pairs={{0,8},{4,12},{8,0},{12,4},{1,9},{5,13},{9,1},{13,5},{2,10},{6,14},... | collective-permute-start | bytes 18440 | tf_op jit(solution)/shard_map/ppermute | solution.py:447
  11.0 3.2 %collective-permute-start = (bf16[208,768]{1,0:T(8,128)(2,1)S(1)}, bf16[208,768]{1,0:T(8,128)(2,1)S(1)}, u32[]{:S(2)}, u32[]{:S(2)}) collective-permute-start(bf16[208,768]{1,0:T(8,128)(2,1)S(1)} %get-tuple-element.50.refs_0_), channel_id=1, source_target_pairs={{0,1},{1,0},{2,3},{3,2},{4,5},{5,4},{6,7},{7,6},{8,9},{9,8},{10,11... | collective-permute-start | bytes 958472 | tf_op jit(solution)/shard_map/ppermute | solution.py:447
  12.9 1.7 %collective-permute-start.4 = (bf16[208,768]{1,0:T(8,128)(2,1)S(1)}, bf16[208,768]{1,0:T(8,128)(2,1)S(1)}, u32[]{:S(2)}, u32[]{:S(2)}) collective-permute-start(bf16[208,768]{1,0:T(8,128)(2,1)S(1)} %collective-permute-done.1.refs_2_), channel_id=1, source_target_pairs={{0,1},{1,0},{2,3},{3,2},{4,5},{5,4},{6,7},{7,6},{8,9},{9,8},{10,11... | collective-permute-start | bytes 958472 | tf_op jit(solution)/shard_map/ppermute | solution.py:447
  22.6 11.4 %collective-permute-start.9 = (bf16[96,768]{1,0:T(8,128)(2,1)S(1)}, bf16[96,768]{1,0:T(8,128)(2,1)S(1)}, u32[]{:S(2)}, u32[]{:S(2)}) collective-permute-start(bf16[96,768]{1,0:T(8,128)(2,1)S(1)} %get-tuple-element.90), channel_id=1, source_target_pairs={{0,4},{4,0},{8,12},{12,8},{1,5},{5,1},{9,13},{13,9},{2,6},{6,2},{1... | collective-permute-start | bytes 442376 | tf_op jit(solution)/shard_map/ppermute | solution.py:447
  31.6 1.4 %collective-permute-start.5 = (f32[2,64,192]{2,1,0:T(8,128)S(1)}, f32[2,64,192]{2,1,0:T(8,128)S(1)}, u32[]{:S(2)}, u32[]{:S(2)}) collective-permute-start(f32[2,64,192]{2,1,0:T(8,128)S(1)} %get-tuple-element.88), channel_id=1, source_target_pairs={{0,1},{1,0},{2,3},{3,2},{4,5},{5,4},{6,7},{7,6},{8,9},{9,8},{10,11... | collective-permute-start | bytes 294920 | tf_op jit(solution)/shard_map/ppermute | solution.py:447
  33.0 4.3 %collective-permute-start.6 = (f32[1,64,192]{2,1,0:T(8,128)S(1)}, f32[1,64,192]{2,1,0:T(8,128)S(1)}, u32[]{:S(2)}, u32[]{:S(2)}) collective-permute-start(f32[1,64,192]{2,1,0:T(8,128)S(1)} %slice.11), channel_id=1, source_target_pairs={{0,2},{1,3},{2,0},{3,1},{4,6},{5,7},{6,4},{7,5},{8,10},{9,11},{10,... | collective-permute-start | bytes 147464 | tf_op jit(solution)/shard_map/ppermute | solution.py:447
  34.1 12.5 %collective-permute-start.10 = (bf16[96,768]{1,0:T(8,128)(2,1)S(1)}, bf16[96,768]{1,0:T(8,128)(2,1)S(1)}, u32[]{:S(2)}, u32[]{:S(2)}) collective-permute-start(bf16[96,768]{1,0:T(8,128)(2,1)S(1)} %add_convert_fusion.1), channel_id=1, source_target_pairs={{0,8},{4,12},{8,0},{12,4},{1,9},{5,13},{9,1},{13,5},{2,10},{6,14},... | collective-permute-start | bytes 442376 | tf_op jit(solution)/shard_map/ppermute | solution.py:447
  37.4 9.2 %collective-permute-start.7 = (f32[64,192]{1,0:T(8,128)S(1)}, f32[64,192]{1,0:T(8,128)S(1)}, u32[]{:S(2)}, u32[]{:S(2)}) collective-permute-start(f32[64,192]{1,0:T(8,128)S(1)} %fusion), channel_id=1, source_target_pairs={{0,8},{4,12},{8,0},{12,4},{1,9},{5,13},{9,1},{13,5},{2,10},{6,14},... | collective-permute-start | bytes 147464 | tf_op jit(solution)/shard_map/ppermute | solution.py:447
  46.6 6.5 %collective-permute-start.11 = (bf16[96,768]{1,0:T(8,128)(2,1)S(1)}, bf16[96,768]{1,0:T(8,128)(2,1)S(1)}, u32[]{:S(2)}, u32[]{:S(2)}) collective-permute-start(bf16[96,768]{1,0:T(8,128)(2,1)S(1)} %add_convert_fusion.near_ref), channel_id=1, source_target_pairs={{0,4},{4,0},{8,12},{12,8},{1,5},{5,1},{9,13},{13,9},{2,6},{6,2},{1... | collective-permute-start | bytes 442376 | tf_op jit(solution)/shard_map/ppermute | solution.py:447
  46.7 7.7 %collective-permute-start.8 = (f32[64,192]{1,0:T(8,128)S(1)}, f32[64,192]{1,0:T(8,128)S(1)}, u32[]{:S(2)}, u32[]{:S(2)}) collective-permute-start(f32[64,192]{1,0:T(8,128)S(1)} %add.17.sa_ref), channel_id=1, source_target_pairs={{0,4},{4,0},{8,12},{12,8},{1,5},{5,1},{9,13},{13,9},{2,6},{6,2},{1... | collective-permute-start | bytes 147464 | tf_op jit(solution)/shard_map/ppermute | solution.py:447

commit v8 on v6

--- a/solution.py
+++ b/solution.py
@@ -275,22 +275,16 @@
 
 
 def backward_kernel(n_chan, rows, width, scale, dils, *refs):
-    chans = n_chan * width
-    tiles = chans // LANE
-    pks, refs = refs[:n_chan], refs[n_chan:]
-    (hot_ref, hot1_ref, mixl_ref, cot_ref, s_ref, e_ref, et_ref), refs = refs[:7], refs[7:]
+    tiles = n_chan * width // LANE
+    (hot_ref, mixl_ref, cot_ref, s_ref, e_ref, et_ref), refs = refs[:6], refs[6:]
     x1_refs, refs = (refs[:tiles], refs[tiles : 2 * tiles]), refs[2 * tiles :]
     gp_refs, refs = (refs[:tiles], refs[tiles : 2 * tiles]), refs[2 * tiles :]
-    (keep_ref, send_ref), refs = refs[:2], refs[2:]
-    p_refs, s0_refs, refs = refs[:tiles], refs[tiles : 2 * tiles], refs[2 * tiles :]
-    g2_ref, gt_ref, pb_ref, dw_ref, st_ref, back_ref, tail_ref = refs
+    (pb_ref, gt_ref, plain_ref, other_ref), refs = refs[:4], refs[4:]
+    p_refs, s0_refs, (g2_ref,) = refs[:tiles], refs[tiles : 2 * tiles], refs[2 * tiles :]
     ext = rows + 2 * REACH
     padded = hot_ref.shape[1]
-    me, dil = lax.axis_index("chan"), dils[1]
-    rev = reversal(LANE)
-    blocks = [slice(k * width, (k + 1) * width) for k in range(n_chan)]
-    table, table_r = e_ref[...], et_ref[...]
-    taps_f, taps_r = 0.5 * table.astype(F32), 0.5 * table_r.astype(F32)
+    dil = dils[1]
+    taps_f, taps_r = 0.5 * e_ref[...].astype(F32), 0.5 * et_ref[...].astype(F32)
 
     edge = 2 * REACH
     n_own = pl.cdiv(width, LANE)
@@ -302,7 +296,6 @@
         g2_ref[t, REACH : rows + REACH, :] = 0.5 * g2[:, t * LANE : (t + 1) * LANE]
 
     mchunk, chunk = rows // 6, ext // 5
-    plains, others = [None] * tiles, [None] * tiles
     for t in range(tiles):
         dst = slice(t * LANE, (t + 1) * LANE)
         p_ref, s0_ref = p_refs[t], s0_refs[t]
@@ -328,7 +321,7 @@
             s0_ref[where, :LANE] = (f * gp_refs[0][t][where, :]).astype(BF)
             s0_ref[where, LANE:] = (r * gp_refs[1][t][where, :]).astype(BF)
         both = dot(hot_ref[...], s0_ref[...])
-        plains[t], others[t] = both[:, :LANE], both[:, LANE:]
+        plain_ref[:, dst], other_ref[:, dst] = both[:, :LANE], both[:, LANE:]
 
         sums = [None] * (2 * TAPS)
         for i in range(6):
@@ -345,6 +338,16 @@
             lines = [jnp.sum(sums[strand * TAPS + j], axis=0, keepdims=True) for j in range(TAPS)]
             gt_ref[strand, :, dst] = jnp.concatenate(lines + [jnp.zeros((8 - TAPS, LANE), F32)], axis=0)
 
+
+def collect_kernel(n_chan, width, scale, *refs):
+    pks, refs = refs[:n_chan], refs[n_chan:]
+    hot1_ref, cot_ref, e_ref, et_ref, pb_ref, gt_ref, plain_ref, other_ref = refs[:8]
+    keep_ref, send_ref, dw_ref, st_ref, back_ref, tail_ref = refs[8:]
+    chans = n_chan * width
+    me, rev = lax.axis_index("chan"), reversal(LANE)
+    blocks = [slice(k * width, (k + 1) * width) for k in range(n_chan)]
+    table, table_r = e_ref[...], et_ref[...]
+
     by_tap = dot(hot1_ref[...], pb_ref[...])
     own_letters = dot(hot1_ref[:16, :], cot_ref[...]) * scale
     srow, scol = iotas((8, JB))
@@ -358,10 +361,8 @@
     sel1 = select_rows("tap1", JB)
     ahead = by_tap[:JB] * dot(sel1, table)
     other = by_tap[JB:] * dot(sel1, table_r)
-    turned, other, taps_turned = reverse_wide(
-        [jnp.concatenate(others, axis=1), other, gt_ref[1]], rev
-    )
-    sums = jnp.concatenate(plains, axis=1) + jnp.concatenate([turned[JB:], turned[:JB]], axis=0)
+    turned, other, taps_turned = reverse_wide([other_ref[...], other, gt_ref[1]], rev)
+    sums = plain_ref[...] + jnp.concatenate([turned[JB:], turned[:JB]], axis=0)
     dw_ref[...] = sums
     letters = sums_of(sum_letter, ahead + other)
     tail_ref[8:16, :] = gt_ref[0] + taps_turned
@@ -534,31 +535,44 @@
         (3 << 30, 8 << 20),
     )(dilations, *pks, hot_t, mixl, cot)
 
+    arrived = flip_bits(far, "seq", 1)
+    pb, gt, plain, other = call(
+        functools.partial(backward_kernel, n_chan, rows, width, scale),
+        [SMEM] + [VMEM] * (6 + 4 * tiles),
+        [
+            shape((rows, chans), BF),
+            shape((2, 8, chans), F32),
+            shape((2 * JB, chans), F32),
+            shape((2 * JB, chans), F32),
+        ],
+        [VMEM] * 4,
+        [pltpu.VMEM((rows + 2 * edge, LANE), F32)] * tiles
+        + [pltpu.VMEM((padded, 2 * LANE), BF)] * tiles
+        + [pltpu.VMEM((own_tiles, ext, LANE), F32)],
+        40,
+        (3 << 30, 8 << 20),
+    )(dilations, hot, mixl, cot, s1, table, table_r, *strands)
+
+    def rounded_sum(a, b):
+        return lax.optimization_barrier((a.astype(F32) + b.astype(F32)).astype(BF))
+
+    g_mine = rounded_sum(near, lax.optimization_barrier((arrived, plain))[0])
+    gt = lax.optimization_barrier((gt, g_mine))[0]
     keep, send = call(
-        functools.partial(backward_kernel, n_chan, rows, width, scale),
-        [SMEM] + [VMEM] * (n_chan + 7 + 4 * tiles),
+        functools.partial(collect_kernel, n_chan, width, scale),
+        [VMEM] * (n_chan + 8),
         [shape((n_chan // 2, SUMS, width), F32)] * 2,
         [VMEM] * 2,
-        [pltpu.VMEM((rows + 2 * edge, LANE), F32)] * tiles
-        + [pltpu.VMEM((padded, 2 * LANE), BF)] * tiles
-        + [
-            pltpu.VMEM((own_tiles, ext, LANE), F32),
-            pltpu.VMEM((2, 8, chans), F32),
-            pltpu.VMEM((rows, chans), BF),
+        [
             pltpu.VMEM((2 * JB, chans), F32),
             pltpu.VMEM((2 * JB, chans), F32),
             pltpu.VMEM((2 * JB, chans), F32),
             pltpu.VMEM((24, chans), F32),
         ],
-        40,
-        (3 << 30, 8 << 20),
-    )(dilations, *pks, hot, hot1, mixl, cot, s1, table, table_r, *strands)
-
-    def rounded_sum(a, b):
-        return lax.optimization_barrier((a.astype(F32) + b.astype(F32)).astype(BF))
-
-    arrived = lax.optimization_barrier((flip_bits(far, "seq", 1), keep))[0]
-    g_mine = rounded_sum(near, arrived)
+        24,
+        (1 << 30, 8 << 20),
+    )(*pks, hot1, cot, table, table_r, pb, gt, plain, other)
+
     for bit in range(1, seq_bits):
         g_mine = rounded_sum(g_mine, flip_bits(g_mine, "seq", 1 << bit))
     g_other = flip_bits(g_mine, "seq", 1)

time: 54.1 us -> 52.8 us (0.976)
  waiting for transfers between devices: 13.3 us -> 12.3 us
    pallas_call x0 -> x1, Pallas kernels: none -> 1.73 us  [body(): call(functools.partial(collect_kernel, n_chan, width, scale), [VMEM] * (n...]
    pallas_call x1, Pallas kernels: 7.35 us -> 5.95 us  [body(): call(functools.partial(backward_kernel, n_chan, rows, width, scale), [SME...]
    ppermute x12, waiting for transfers between devices: 13.3 us -> 12.3 us  [flip_bits(): lax.ppermute(x, axis, [(i, i ^ mask) for i in range(lax.axis_size(axis))])]
  transfers between devices with their start and end apart: 12 -> 12, of which waited for: 7 -> 8; matrix products, arithmetic and copies ran while one was open for 0% -> 0% of each run, Pallas kernels for 21% -> 22%
where the time goes in v8:
time: 52.8 us; the launch traced here: 52.3 us
  Pallas kernels  22.1 us (42%)
  starting transfers between devices  17 us (32%)
  waiting for transfers between devices  12.3 us (23%)
  between operations  0.77 us (1%)
    ppermute x12, starting transfers between devices, flip_bits(): lax.ppermute(x, axis, [(i, i ^ mask) for i in range(lax.axis_size(axis))])  17 us
    ppermute x12, waiting for transfers between devices, flip_bits(): lax.ppermute(x, axis, [(i, i ^ mask) for i in range(lax.axis_size(axis))])  12.3 us
    pallas_call x1, Pallas kernels, body(): call(functools.partial(forward_kernel, n_chan, rows, width, scale), [SMEM...  7.94 us
    pallas_call x1, Pallas kernels, body(): call(functools.partial(backward_kernel, n_chan, rows, width, scale), [SME...  5.95 us
    pallas_call x1, Pallas kernels, body(): call(functools.partial(collect_kernel, n_chan, width, scale), [VMEM] * (n...  1.73 us
    pallas_call x1, Pallas kernels, body(): call(functools.partial(finish_kernel, n_chan, width), [VMEM, VMEM, VMEM,...  1.64 us
    pallas_call x1, Pallas kernels, body(): call(functools.partial(local_kernel, n_chan, width), [HBM, HBM], [shape((...  1.44 us
    pallas_call x1, Pallas kernels, body(): call(functools.partial(mix1_kernel, n_chan, width), [VMEM, VMEM], [shape(...  1.2 us
  transfers between devices with their start and end apart: 12, of which 8 were waited for; matrix products, arithmetic and copies ran while one was open for 0% of the time, Pallas kernels for 22%

profile of v8, /device:TPU:0, one launch (start us, length us, event | category | flops | bytes accessed | tf_op | source)
XLA Modules:
  0.0 52.3 jit_solution(48316324439406153)
XLA Ops:
  0.6 1.1 %shard_map.93 = (bf16[208,768]{1,0:T(8,128)(2,1)S(1)}, s32[1,768]{1,0:T(1,128)S(1)}) custom-call(bf16[2,192,768]{2,1,0:T(8,128)(2,1)} %bitcast.9, bf16[4,192]{1,0:T(4,128)(2,1)} %embed_ref.1, bf16[5,2,192]{2,1,0:T(2,128)(2,1)} %bitcast.12, s32[768]{0:T(1024)} %tok_ref.1), custom_call_target="tpu_custom_call" | custom-call | bytes 589824 | tf_op jit(solution)/shard_map/pallas_call | solution.py:464
  1.7 3.0 %collective-permute-start.1 = (bf16[208,768]{1,0:T(8,128)(2,1)S(1)}, bf16[208,768]{1,0:T(8,128)(2,1)S(1)}, u32[]{:S(2)}, u32[]{:S(2)}) collective-permute-start(bf16[208,768]{1,0:T(8,128)(2,1)S(1)} %get-tuple-element.54.refs_0_), channel_id=1, source_target_pairs={{0,2},{1,3},{2,0},{3,1},{4,6},{5,7},{6,4},{7,5},{8,10},{9,11},{10,... | collective-permute-start | bytes 958472 | tf_op jit(solution)/shard_map/ppermute | solution.py:448
  4.7 1.6 %collective-permute-start.2 = (s32[1,768]{1,0:T(1,128)S(1)}, s32[1,768]{1,0:T(1,128)S(1)}, u32[]{:S(2)}, u32[]{:S(2)}) collective-permute-start(s32[1,768]{1,0:T(1,128)S(1)} %get-tuple-element.55), channel_id=1, source_target_pairs={{0,4},{4,0},{8,12},{12,8},{1,5},{5,1},{9,13},{13,9},{2,6},{6,2},{1... | collective-permute-start | bytes 9224 | tf_op jit(solution)/shard_map/ppermute | solution.py:448
  6.3 2.0 %collective-permute-done.2 = s32[1,768]{1,0:T(1,128)S(1)} collective-permute-done((s32[1,768]{1,0:T(1,128)S(1)}, s32[1,768]{1,0:T(1,128)S(1)}, u32[]{:S(2)}, u32[]{:S(2)}) %collective-permute-start.2) | collective-permute-done | bytes 3104 | tf_op jit(solution)/shard_map/ppermute | solution.py:448
  8.3 2.7 %collective-permute-start.3 = (s32[2,768]{1,0:T(2,128)S(1)}, s32[2,768]{1,0:T(2,128)S(1)}, u32[]{:S(2)}, u32[]{:S(2)}) collective-permute-start(s32[2,768]{1,0:T(2,128)S(1)} %pad_add_fusion.1), channel_id=1, source_target_pairs={{0,8},{4,12},{8,0},{12,4},{1,9},{5,13},{9,1},{13,5},{2,10},{6,14},... | collective-permute-start | bytes 18440 | tf_op jit(solution)/shard_map/ppermute | solution.py:448
  11.0 0.0 collective-permute-start
  11.0 1.4 %shard_map.94 = (bf16[192,768]{1,0:T(8,128)(2,1)S(1)}, bf16[768,192]{1,0:T(8,128)(2,1)S(1)}) custom-call(bf16[2,192,768]{2,1,0:T(8,128)(2,1)} %bitcast.10, bf16[192,768]{1,0:T(8,128)(2,1)} %bitcast.11), custom_call_target="tpu_custom_call" | custom-call | flops 1048576 | bytes 1048576 | tf_op jit(solution)/shard_map/pallas_call | solution.py:482
  12.4 0.5 collective-permute-done.3
  12.9 0.0 collective-permute-done.1.refs_2_
  12.9 0.1 collective-permute-start.4
  13.0 1.1 %shard_map.95 = (bf16[896,128]{1,0:T(8,128)(2,1)S(1)}, bf16[64,896]{1,0:T(8,128)(2,1)S(1)}, bf16[64,768]{1,0:T(8,128)(2,1)S(1)}) custom-call(s32[2]{0:T(128)S(1)} %copy-done, s32[4,768]{1,0:T(4,128)S(1)} %pad_add_fusion.tok_ref), custom_call_target="tpu_custom_call" | custom-call | flops 1048576 | bytes 1048576 | tf_op jit(solution)/shard_map/pallas_call | solution.py:502
  14.2 0.0 collective-permute-done.refs_1_
  14.2 0.4 collective-permute-done.4.refs_3_
  14.6 7.9 %shard_map.96 = (bf16[192,768]{1,0:T(8,128)(2,1)}, bf16[96,768]{1,0:T(8,128)(2,1)S(1)}, bf16[96,768]{1,0:T(8,128)(2,1)S(1)}, bf16[768,192]{1,0:T(8,128)(2,1)S(1)...) custom-call(s32[2]{0:T(128)S(1)} %copy-done, ...), custom_call_target="tpu_custom_call" | custom-call | flops 3221225472 | bytes 8388608 | tf_op jit(solution)/shard_map/pallas_call | solution.py:513
  22.6 1.6 %collective-permute-start.5 = (bf16[96,768]{1,0:T(8,128)(2,1)S(1)}, bf16[96,768]{1,0:T(8,128)(2,1)S(1)}, u32[]{:S(2)}, u32[]{:S(2)}) collective-permute-start(bf16[96,768]{1,0:T(8,128)(2,1)S(1)} %get-tuple-element.94), channel_id=1, source_target_pairs={{0,4},{4,0},{8,12},{12,8},{1,5},{5,1},{9,13},{13,9},{2,6},{6,2},{1... | collective-permute-start | bytes 442376 | tf_op jit(solution)/shard_map/ppermute | solution.py:448
  24.2 5.9 %shard_map.97 = (bf16[768,768]{1,0:T(8,128)(2,1)S(1)}, f32[2,8,768]{2,1,0:T(8,128)S(1)}, f32[64,768]{1,0:T(8,128)S(1)}, f32[64,768]{1,0:T(8,128)S(1)}) custom-call(s32[2]{0:T(128)S(1)} %copy-done, bf16[64,896]{1,0:T(8,128)(2,1)S(1)} %get-tuple-element.65.refs_0_, bf16[192,768]{1,0:T(8,128)(2,1)S(1)} %get-tuple-element.56.refs_5_.refs_1_, ...), custom_call_target="tpu_custom_call" | custom-call | flops 3221225472 | bytes 8388608 | tf_op jit(solution)/shard_map/pallas_call | solution.py:539
  30.2 0.0 collective-permute-done.5
  30.2 2.7 %collective-permute-start.10 = (bf16[96,768]{1,0:T(8,128)(2,1)S(1)}, bf16[96,768]{1,0:T(8,128)(2,1)S(1)}, u32[]{:S(2)}, u32[]{:S(2)}) collective-permute-start(bf16[96,768]{1,0:T(8,128)(2,1)S(1)} %add_convert_fusion.1), channel_id=1, source_target_pairs={{0,8},{4,12},{8,0},{12,4},{1,9},{5,13},{9,1},{13,5},{2,10},{6,14},... | collective-permute-start | bytes 442376 | tf_op jit(solution)/shard_map/ppermute | solution.py:448
  32.9 1.7 %shard_map.98 = (f32[2,64,192]{2,1,0:T(8,128)S(1)}, f32[2,64,192]{2,1,0:T(8,128)S(1)}) custom-call(bf16[208,768]{1,0:T(8,128)(2,1)S(1)} %get-tuple-element.54.refs_0_, bf16[208,768]{1,0:T(8,128)(2,1)S(1)} %collective-permute-done.refs_1_, bf16[208,768]{1,0:T(8,128)(2,1)S(1)} %collective-permute-done.1.refs_2_, ...), custom_call_target="tpu_custom_call" | custom-call | flops 1073741824 | bytes 8388608 | tf_op jit(solution)/shard_map/pallas_call | solution.py:561
  34.6 0.0 collective-permute-start.6
  34.7 1.3 %collective-permute-done.6 = f32[2,64,192]{2,1,0:T(8,128)S(1)} collective-permute-done((f32[2,64,192]{2,1,0:T(8,128)S(1)}, f32[2,64,192]{2,1,0:T(8,128)S(1)}, u32[]{:S(2)}, u32[]{:S(2)}) %collective-permute-start.6) | collective-permute-done | bytes 98336 | tf_op jit(solution)/shard_map/ppermute | solution.py:448
  36.0 1.0 %collective-permute-start.7 = (f32[1,64,192]{2,1,0:T(8,128)S(1)}, f32[1,64,192]{2,1,0:T(8,128)S(1)}, u32[]{:S(2)}, u32[]{:S(2)}) collective-permute-start(f32[1,64,192]{2,1,0:T(8,128)S(1)} %slice.11), channel_id=1, source_target_pairs={{0,2},{1,3},{2,0},{3,1},{4,6},{5,7},{6,4},{7,5},{8,10},{9,11},{10,... | collective-permute-start | bytes 147464 | tf_op jit(solution)/shard_map/ppermute | solution.py:448
  37.1 2.8 %collective-permute-done.10 = bf16[96,768]{1,0:T(8,128)(2,1)S(1)} collective-permute-done((bf16[96,768]{1,0:T(8,128)(2,1)S(1)}, bf16[96,768]{1,0:T(8,128)(2,1)S(1)}, u32[]{:S(2)}, u32[]{:S(2)}) %collective-permute-start.10) | collective-permute-done | bytes 147488 | tf_op jit(solution)/shard_map/ppermute | solution.py:448
  39.9 0.1 collective-permute-start.11
  40.0 0.4 collective-permute-done.7
  40.4 2.8 %collective-permute-start.8 = (f32[64,192]{1,0:T(8,128)S(1)}, f32[64,192]{1,0:T(8,128)S(1)}, u32[]{:S(2)}, u32[]{:S(2)}) collective-permute-start(f32[64,192]{1,0:T(8,128)S(1)} %fusion), channel_id=1, source_target_pairs={{0,8},{4,12},{8,0},{12,4},{1,9},{5,13},{9,1},{13,5},{2,10},{6,14},... | collective-permute-start | bytes 147464 | tf_op jit(solution)/shard_map/ppermute | solution.py:448
  43.2 3.1 %collective-permute-done.8 = f32[64,192]{1,0:T(8,128)S(1)} collective-permute-done((f32[64,192]{1,0:T(8,128)S(1)}, f32[64,192]{1,0:T(8,128)S(1)}, u32[]{:S(2)}, u32[]{:S(2)}) %collective-permute-start.8) | collective-permute-done | bytes 49184 | tf_op jit(solution)/shard_map/ppermute | solution.py:448
  46.3 1.4 %collective-permute-start.9 = (f32[64,192]{1,0:T(8,128)S(1)}, f32[64,192]{1,0:T(8,128)S(1)}, u32[]{:S(2)}, u32[]{:S(2)}) collective-permute-start(f32[64,192]{1,0:T(8,128)S(1)} %add.18.sa_ref), channel_id=1, source_target_pairs={{0,4},{4,0},{8,12},{12,8},{1,5},{5,1},{9,13},{13,9},{2,6},{6,2},{1... | collective-permute-start | bytes 147464 | tf_op jit(solution)/shard_map/ppermute | solution.py:448
  47.7 0.0 collective-permute-done.11.far_ref
  47.7 1.2 %shard_map.99._ = f32[2,192,768]{2,1,0:T(8,128)} custom-call(bf16[96,768]{1,0:T(8,128)(2,1)S(1)} %add_convert_fusion.near_ref, bf16[96,768]{1,0:T(8,128)(2,1)S(1)} %collective-permute-done.11.far_ref), custom_call_target="tpu_custom_call" | custom-call | flops 1048576 | bytes 2097152 | tf_op jit(solution)/shard_map/pallas_call | solution.py:589
  48.9 1.7 %collective-permute-done.9.sb_ref = f32[64,192]{1,0:T(8,128)S(1)} collective-permute-done((f32[64,192]{1,0:T(8,128)S(1)}, f32[64,192]{1,0:T(8,128)S(1)}, u32[]{:S(2)}, u32[]{:S(2)}) %collective-permute-start.9) | collective-permute-done | bytes 49184 | tf_op jit(solution)/shard_map/ppermute | solution.py:448
  50.6 1.6 %shard_map.100 = (f32[2,192,768]{2,1,0:T(8,128)}, f32[5,2,192]{2,1,0:T(2,128)}, f32[4,192]{1,0:T(4,128)}) custom-call(bf16[128,768]{1,0:T(8,128)(2,1)S(1)} %get-tuple-element.61.st_ref, f32[64,192]{1,0:T(8,128)S(1)} %add.18.sa_ref, f32[64,192]{1,0:T(8,128)S(1)} %collective-permute-done.9.sb_ref, ...), custom_call_target="tpu_custom_call", output_to_operand_aliasing={{0}: (3, {})} | custom-call | flops 16777216 | bytes 2097152 | tf_op jit(solution)/shard_map/pallas_call | solution.py:598
  (10 shorter events, 0.1 us)
Async XLA Ops:
  0.6 12.4 %copy-start = (s32[2]{0:T(128)S(1)}, s32[2]{0:T(128)}, u32[]{:S(2)}) copy-start(s32[2]{0:T(128)} %dils.5) | copy-start | bytes 28
  1.7 11.2 %collective-permute-start.1 = (bf16[208,768]{1,0:T(8,128)(2,1)S(1)}, bf16[208,768]{1,0:T(8,128)(2,1)S(1)}, u32[]{:S(2)}, u32[]{:S(2)}) collective-permute-start(bf16[208,768]{1,0:T(8,128)(2,1)S(1)} %get-tuple-element.54.refs_0_), channel_id=1, source_target_pairs={{0,2},{1,3},{2,0},{3,1},{4,6},{5,7},{6,4},{7,5},{8,10},{9,11},{10,... | collective-permute-start | bytes 958472 | tf_op jit(solution)/shard_map/ppermute | solution.py:448
  4.7 3.6 %collective-permute-start.2 = (s32[1,768]{1,0:T(1,128)S(1)}, s32[1,768]{1,0:T(1,128)S(1)}, u32[]{:S(2)}, u32[]{:S(2)}) collective-permute-start(s32[1,768]{1,0:T(1,128)S(1)} %get-tuple-element.55), channel_id=1, source_target_pairs={{0,4},{4,0},{8,12},{12,8},{1,5},{5,1},{9,13},{13,9},{2,6},{6,2},{1... | collective-permute-start | bytes 9224 | tf_op jit(solution)/shard_map/ppermute | solution.py:448
  8.3 4.6 %collective-permute-start.3 = (s32[2,768]{1,0:T(2,128)S(1)}, s32[2,768]{1,0:T(2,128)S(1)}, u32[]{:S(2)}, u32[]{:S(2)}) collective-permute-start(s32[2,768]{1,0:T(2,128)S(1)} %pad_add_fusion.1), channel_id=1, source_target_pairs={{0,8},{4,12},{8,0},{12,4},{1,9},{5,13},{9,1},{13,5},{2,10},{6,14},... | collective-permute-start | bytes 18440 | tf_op jit(solution)/shard_map/ppermute | solution.py:448
  11.0 3.2 %collective-permute-start = (bf16[208,768]{1,0:T(8,128)(2,1)S(1)}, bf16[208,768]{1,0:T(8,128)(2,1)S(1)}, u32[]{:S(2)}, u32[]{:S(2)}) collective-permute-start(bf16[208,768]{1,0:T(8,128)(2,1)S(1)} %get-tuple-element.54.refs_0_), channel_id=1, source_target_pairs={{0,1},{1,0},{2,3},{3,2},{4,5},{5,4},{6,7},{7,6},{8,9},{9,8},{10,11... | collective-permute-start | bytes 958472 | tf_op jit(solution)/shard_map/ppermute | solution.py:448
  12.9 1.7 %collective-permute-start.4 = (bf16[208,768]{1,0:T(8,128)(2,1)S(1)}, bf16[208,768]{1,0:T(8,128)(2,1)S(1)}, u32[]{:S(2)}, u32[]{:S(2)}) collective-permute-start(bf16[208,768]{1,0:T(8,128)(2,1)S(1)} %collective-permute-done.1.refs_2_), channel_id=1, source_target_pairs={{0,1},{1,0},{2,3},{3,2},{4,5},{5,4},{6,7},{7,6},{8,9},{9,8},{10,11... | collective-permute-start | bytes 958472 | tf_op jit(solution)/shard_map/ppermute | solution.py:448
  22.6 7.6 %collective-permute-start.5 = (bf16[96,768]{1,0:T(8,128)(2,1)S(1)}, bf16[96,768]{1,0:T(8,128)(2,1)S(1)}, u32[]{:S(2)}, u32[]{:S(2)}) collective-permute-start(bf16[96,768]{1,0:T(8,128)(2,1)S(1)} %get-tuple-element.94), channel_id=1, source_target_pairs={{0,4},{4,0},{8,12},{12,8},{1,5},{5,1},{9,13},{13,9},{2,6},{6,2},{1... | collective-permute-start | bytes 442376 | tf_op jit(solution)/shard_map/ppermute | solution.py:448
  30.2 9.6 %collective-permute-start.10 = (bf16[96,768]{1,0:T(8,128)(2,1)S(1)}, bf16[96,768]{1,0:T(8,128)(2,1)S(1)}, u32[]{:S(2)}, u32[]{:S(2)}) collective-permute-start(bf16[96,768]{1,0:T(8,128)(2,1)S(1)} %add_convert_fusion.1), channel_id=1, source_target_pairs={{0,8},{4,12},{8,0},{12,4},{1,9},{5,13},{9,1},{13,5},{2,10},{6,14},... | collective-permute-start | bytes 442376 | tf_op jit(solution)/shard_map/ppermute | solution.py:448
  34.6 1.4 %collective-permute-start.6 = (f32[2,64,192]{2,1,0:T(8,128)S(1)}, f32[2,64,192]{2,1,0:T(8,128)S(1)}, u32[]{:S(2)}, u32[]{:S(2)}) collective-permute-start(f32[2,64,192]{2,1,0:T(8,128)S(1)} %get-tuple-element.100), channel_id=1, source_target_pairs={{0,1},{1,0},{2,3},{3,2},{4,5},{5,4},{6,7},{7,6},{8,9},{9,8},{10,11... | collective-permute-start | bytes 294920 | tf_op jit(solution)/shard_map/ppermute | solution.py:448
  36.0 4.3 %collective-permute-start.7 = (f32[1,64,192]{2,1,0:T(8,128)S(1)}, f32[1,64,192]{2,1,0:T(8,128)S(1)}, u32[]{:S(2)}, u32[]{:S(2)}) collective-permute-start(f32[1,64,192]{2,1,0:T(8,128)S(1)} %slice.11), channel_id=1, source_target_pairs={{0,2},{1,3},{2,0},{3,1},{4,6},{5,7},{6,4},{7,5},{8,10},{9,11},{10,... | collective-permute-start | bytes 147464 | tf_op jit(solution)/shard_map/ppermute | solution.py:448
  39.9 7.8 %collective-permute-start.11 = (bf16[96,768]{1,0:T(8,128)(2,1)S(1)}, bf16[96,768]{1,0:T(8,128)(2,1)S(1)}, u32[]{:S(2)}, u32[]{:S(2)}) collective-permute-start(bf16[96,768]{1,0:T(8,128)(2,1)S(1)} %add_convert_fusion.near_ref), channel_id=1, source_target_pairs={{0,4},{4,0},{8,12},{12,8},{1,5},{5,1},{9,13},{13,9},{2,6},{6,2},{1... | collective-permute-start | bytes 442376 | tf_op jit(solution)/shard_map/ppermute | solution.py:448
  40.4 5.9 %collective-permute-start.8 = (f32[64,192]{1,0:T(8,128)S(1)}, f32[64,192]{1,0:T(8,128)S(1)}, u32[]{:S(2)}, u32[]{:S(2)}) collective-permute-start(f32[64,192]{1,0:T(8,128)S(1)} %fusion), channel_id=1, source_target_pairs={{0,8},{4,12},{8,0},{12,4},{1,9},{5,13},{9,1},{13,5},{2,10},{6,14},... | collective-permute-start | bytes 147464 | tf_op jit(solution)/shard_map/ppermute | solution.py:448
  46.3 4.3 %collective-permute-start.9 = (f32[64,192]{1,0:T(8,128)S(1)}, f32[64,192]{1,0:T(8,128)S(1)}, u32[]{:S(2)}, u32[]{:S(2)}) collective-permute-start(f32[64,192]{1,0:T(8,128)S(1)} %add.18.sa_ref), channel_id=1, source_target_pairs={{0,4},{4,0},{8,12},{12,8},{1,5},{5,1},{9,13},{13,9},{2,6},{6,2},{1... | collective-permute-start | bytes 147464 | tf_op jit(solution)/shard_map/ppermute | solution.py:448

commit v9 on v8

--- a/solution.py
+++ b/solution.py
@@ -390,6 +390,11 @@
         place[at, ROW_GT0:, :] = tail_ref[0:16, lanes]
 
 
+def add_kernel(a_ref, b_ref, first_ref, second_ref):
+    first_ref[...] = a_ref[0] + b_ref[0]
+    second_ref[...] = a_ref[1] + b_ref[1]
+
+
 def mix1_kernel(n_chan, width, near_ref, far_ref, out_ref, held, sem):
     me, odd = lax.axis_index("chan"), lax.axis_index("seq") % 2
     half = width // 2
@@ -570,19 +575,35 @@
             pltpu.VMEM((24, chans), F32),
         ],
         24,
-        (1 << 30, 8 << 20),
+        (1 << 20, 1 << 16),
     )(*pks, hot1, cot, table, table_r, pb, gt, plain, other)
 
     for bit in range(1, seq_bits):
         g_mine = rounded_sum(g_mine, flip_bits(g_mine, "seq", 1 << bit))
     g_other = flip_bits(g_mine, "seq", 1)
-    s_mine = keep + flip_bits(send, "chan", 1)
-    for bit in range(1, n_chan.bit_length() - 1):
-        s_mine = s_mine[0::2] + flip_bits(s_mine[1::2], "chan", 1 << bit)
-    s_mine = s_mine[0]
-    for bit in reversed(range(seq_bits)):
+    last = n_chan.bit_length() - 2
+    mine, theirs = keep, flip_bits(send, "chan", 1)
+    for bit in range(1, last):
+        mine = mine + theirs
+        mine, theirs = mine[0::2], flip_bits(mine[1::2], "chan", 1 << bit)
+    s_mine = call(
+        add_kernel,
+        [VMEM] * 2,
+        [shape((SUMS, width), F32)] * 2,
+        [VMEM] * 2,
+        [],
+        8,
+        (0, 0),
+    )(mine, theirs)
+    across = flip_bits(s_mine[1], "chan", 1 << last)
+    along = flip_bits(s_mine[0], "seq", 1)
+    places = [(i, j) for i in range(n_seq) for j in range(n_chan)]
+    pairs = [(i * n_chan + j, (i ^ 1) * n_chan + (j ^ (1 << last))) for i, j in places]
+    corner = lax.ppermute(s_mine[1], ("seq", "chan"), pairs)
+    s_mine = (s_mine[0] + across) + (along + corner)
+    for bit in range(1, seq_bits):
         s_other = flip_bits(s_mine, "seq", 1 << bit)
-        if bit:
+        if bit < seq_bits - 1:
             s_mine = s_mine + s_other
 
     big = pltpu.VMEM((width, chans), F32)

time: 52.8 us -> 50.2 us (0.951); the launches traced: 52.3 us -> 50.4 us
  waiting for transfers between devices: 12.3 us -> 10.7 us
  starting transfers between devices: 17 us -> 15.9 us
  Pallas kernels: 22.1 us -> 22.9 us
    ppermute x12, starting transfers between devices: 17 us -> 15 us  [flip_bits(): lax.ppermute(x, axis, [(i, i ^ mask) for i in range(lax.axis_size(axis))])]
    ppermute x12, waiting for transfers between devices: 12.3 us -> 10.7 us  [flip_bits(): lax.ppermute(x, axis, [(i, i ^ mask) for i in range(lax.axis_size(axis))])]
    ppermute x0 -> x1, starting transfers between devices: none -> 0.93 us  [body(): corner = lax.ppermute(s_mine[1], ('seq', 'chan'), pairs)]
  transfers between devices with their start and end apart: 12 -> 13, of which waited for: 8 -> 8; matrix products, arithmetic and copies ran while one was open for 0% -> 0% of each run, Pallas kernels for 22% -> 24%
where the time goes in v9:
time: 50.2 us; the launch traced here: 50.4 us
  Pallas kernels  22.9 us (46%)
  starting transfers between devices  15.9 us (32%)
  waiting for transfers between devices  10.7 us (21%)
  between operations  0.76 us (2%)
    ppermute x12, starting transfers between devices, flip_bits(): lax.ppermute(x, axis, [(i, i ^ mask) for i in range(lax.axis_size(axis))])  15 us
    ppermute x12, waiting for transfers between devices, flip_bits(): lax.ppermute(x, axis, [(i, i ^ mask) for i in range(lax.axis_size(axis))])  10.7 us
    pallas_call x1, Pallas kernels, body(): call(functools.partial(forward_kernel, n_chan, rows, width, scale), [SMEM...  8.19 us
    pallas_call x1, Pallas kernels, body(): call(functools.partial(backward_kernel, n_chan, rows, width, scale), [SME...  6.47 us
    pallas_call x1, Pallas kernels, body(): call(functools.partial(collect_kernel, n_chan, width, scale), [VMEM] * (n...  1.73 us
    pallas_call x1, Pallas kernels, body(): call(functools.partial(finish_kernel, n_chan, width), [VMEM, VMEM, VMEM,...  1.64 us
    pallas_call x1, Pallas kernels, body(): call(functools.partial(local_kernel, n_chan, width), [HBM, HBM], [shape((...  1.44 us
    pallas_call x1, Pallas kernels, body(): call(functools.partial(mix1_kernel, n_chan, width), [VMEM, VMEM], [shape(...  1.2 us
  transfers between devices with their start and end apart: 13, of which 8 were waited for; matrix products, arithmetic and copies ran while one was open for 0% of the time, Pallas kernels for 24%

profile of v9, /device:TPU:0, one launch (start us, length us, event | category | flops | bytes accessed | tf_op | source)
XLA Modules:
  0.0 50.4 jit_solution(21778986892374777)
XLA Ops:
  0.6 1.1 %shard_map.93 = (bf16[208,768]{1,0:T(8,128)(2,1)S(1)}, s32[1,768]{1,0:T(1,128)S(1)}) custom-call(bf16[2,192,768]{2,1,0:T(8,128)(2,1)} %bitcast.7, bf16[4,192]{1,0:T(4,128)(2,1)} %embed_ref.1, bf16[5,2,192]{2,1,0:T(2,128)(2,1)} %bitcast.10, s32[768]{0:T(1024)} %tok_ref.1), custom_call_target="tpu_custom_call" | custom-call | bytes 589824 | tf_op jit(solution)/shard_map/pallas_call | solution.py:469
  1.7 3.0 %collective-permute-start.1 = (bf16[208,768]{1,0:T(8,128)(2,1)S(1)}, bf16[208,768]{1,0:T(8,128)(2,1)S(1)}, u32[]{:S(2)}, u32[]{:S(2)}) collective-permute-start(bf16[208,768]{1,0:T(8,128)(2,1)S(1)} %get-tuple-element.56.refs_0_), channel_id=1, source_target_pairs={{0,2},{1,3},{2,0},{3,1},{4,6},{5,7},{6,4},{7,5},{8,10},{9,11},{10,... | collective-permute-start | bytes 958472 | tf_op jit(solution)/shard_map/ppermute | solution.py:453
  4.7 1.6 %collective-permute-start.2 = (s32[1,768]{1,0:T(1,128)S(1)}, s32[1,768]{1,0:T(1,128)S(1)}, u32[]{:S(2)}, u32[]{:S(2)}) collective-permute-start(s32[1,768]{1,0:T(1,128)S(1)} %get-tuple-element.57), channel_id=1, source_target_pairs={{0,4},{4,0},{8,12},{12,8},{1,5},{5,1},{9,13},{13,9},{2,6},{6,2},{1... | collective-permute-start | bytes 9224 | tf_op jit(solution)/shard_map/ppermute | solution.py:453
  6.3 2.0 %collective-permute-done.2 = s32[1,768]{1,0:T(1,128)S(1)} collective-permute-done((s32[1,768]{1,0:T(1,128)S(1)}, s32[1,768]{1,0:T(1,128)S(1)}, u32[]{:S(2)}, u32[]{:S(2)}) %collective-permute-start.2) | collective-permute-done | bytes 3104 | tf_op jit(solution)/shard_map/ppermute | solution.py:453
  8.3 2.7 %collective-permute-start.3 = (s32[2,768]{1,0:T(2,128)S(1)}, s32[2,768]{1,0:T(2,128)S(1)}, u32[]{:S(2)}, u32[]{:S(2)}) collective-permute-start(s32[2,768]{1,0:T(2,128)S(1)} %pad_add_fusion.1), channel_id=1, source_target_pairs={{0,8},{4,12},{8,0},{12,4},{1,9},{5,13},{9,1},{13,5},{2,10},{6,14},... | collective-permute-start | bytes 18440 | tf_op jit(solution)/shard_map/ppermute | solution.py:453
  11.0 0.0 collective-permute-start
  11.0 1.4 %shard_map.94 = (bf16[192,768]{1,0:T(8,128)(2,1)S(1)}, bf16[768,192]{1,0:T(8,128)(2,1)S(1)}) custom-call(bf16[2,192,768]{2,1,0:T(8,128)(2,1)} %bitcast.8, bf16[192,768]{1,0:T(8,128)(2,1)} %bitcast.9), custom_call_target="tpu_custom_call" | custom-call | flops 1048576 | bytes 1048576 | tf_op jit(solution)/shard_map/pallas_call | solution.py:487
  12.4 0.5 collective-permute-done.3
  12.9 0.0 collective-permute-done.1.refs_2_
  12.9 0.1 collective-permute-start.4
  13.0 1.1 %shard_map.95 = (bf16[896,128]{1,0:T(8,128)(2,1)S(1)}, bf16[64,896]{1,0:T(8,128)(2,1)S(1)}, bf16[64,768]{1,0:T(8,128)(2,1)S(1)}) custom-call(s32[2]{0:T(128)S(1)} %copy-done, s32[4,768]{1,0:T(4,128)S(1)} %pad_add_fusion.tok_ref), custom_call_target="tpu_custom_call" | custom-call | flops 1048576 | bytes 1048576 | tf_op jit(solution)/shard_map/pallas_call | solution.py:507
  14.2 0.0 collective-permute-done.refs_1_
  14.2 0.4 collective-permute-done.4.refs_3_
  14.6 8.2 %shard_map.96 = (bf16[192,768]{1,0:T(8,128)(2,1)}, bf16[96,768]{1,0:T(8,128)(2,1)S(1)}, bf16[96,768]{1,0:T(8,128)(2,1)S(1)}, bf16[768,192]{1,0:T(8,128)(2,1)S(1)...) custom-call(s32[2]{0:T(128)S(1)} %copy-done, ...), custom_call_target="tpu_custom_call" | custom-call | flops 3221225472 | bytes 8388608 | tf_op jit(solution)/shard_map/pallas_call | solution.py:518
  22.8 1.6 %collective-permute-start.5 = (bf16[96,768]{1,0:T(8,128)(2,1)S(1)}, bf16[96,768]{1,0:T(8,128)(2,1)S(1)}, u32[]{:S(2)}, u32[]{:S(2)}) collective-permute-start(bf16[96,768]{1,0:T(8,128)(2,1)S(1)} %get-tuple-element.96), channel_id=1, source_target_pairs={{0,4},{4,0},{8,12},{12,8},{1,5},{5,1},{9,13},{13,9},{2,6},{6,2},{1... | collective-permute-start | bytes 442376 | tf_op jit(solution)/shard_map/ppermute | solution.py:453
  24.5 6.5 %shard_map.97 = (bf16[768,768]{1,0:T(8,128)(2,1)S(1)}, f32[2,8,768]{2,1,0:T(8,128)S(1)}, f32[64,768]{1,0:T(8,128)S(1)}, f32[64,768]{1,0:T(8,128)S(1)}) custom-call(s32[2]{0:T(128)S(1)} %copy-done, bf16[64,896]{1,0:T(8,128)(2,1)S(1)} %get-tuple-element.67.refs_0_, bf16[192,768]{1,0:T(8,128)(2,1)S(1)} %get-tuple-element.58.refs_5_.refs_1_, ...), custom_call_target="tpu_custom_call" | custom-call | flops 3221225472 | bytes 8388608 | tf_op jit(solution)/shard_map/pallas_call | solution.py:544
  30.9 0.0 collective-permute-done.5
  31.0 2.7 %collective-permute-start.11 = (bf16[96,768]{1,0:T(8,128)(2,1)S(1)}, bf16[96,768]{1,0:T(8,128)(2,1)S(1)}, u32[]{:S(2)}, u32[]{:S(2)}) collective-permute-start(bf16[96,768]{1,0:T(8,128)(2,1)S(1)} %add_convert_fusion.1), channel_id=1, source_target_pairs={{0,8},{4,12},{8,0},{12,4},{1,9},{5,13},{9,1},{13,5},{2,10},{6,14},... | collective-permute-start | bytes 442376 | tf_op jit(solution)/shard_map/ppermute | solution.py:453
  33.6 1.7 %shard_map.98 = (f32[2,64,192]{2,1,0:T(8,128)S(1)}, f32[2,64,192]{2,1,0:T(8,128)S(1)}) custom-call(bf16[208,768]{1,0:T(8,128)(2,1)S(1)} %get-tuple-element.56.refs_0_, bf16[208,768]{1,0:T(8,128)(2,1)S(1)} %collective-permute-done.refs_1_, bf16[208,768]{1,0:T(8,128)(2,1)S(1)} %collective-permute-done.1.refs_2_, ...), custom_call_target="tpu_custom_call" | custom-call | flops 1048576 | bytes 65536 | tf_op jit(solution)/shard_map/pallas_call | solution.py:566
  35.4 0.0 collective-permute-start.6
  35.4 1.3 %collective-permute-done.6.b_ref = f32[2,64,192]{2,1,0:T(8,128)S(1)} collective-permute-done((f32[2,64,192]{2,1,0:T(8,128)S(1)}, f32[2,64,192]{2,1,0:T(8,128)S(1)}, u32[]{:S(2)}, u32[]{:S(2)}) %collective-permute-start.6) | collective-permute-done | bytes 98336 | tf_op jit(solution)/shard_map/ppermute | solution.py:453
  36.8 0.9 %collective-permute-start.9 = (f32[64,192]{1,0:T(8,128)S(1)}, f32[64,192]{1,0:T(8,128)S(1)}, u32[]{:S(2)}, u32[]{:S(2)}) collective-permute-start(f32[64,192]{1,0:T(8,128)S(1)} %get-tuple-element.104), channel_id=1, source_target_pairs={{0,6},{1,7},{2,4},{3,5},{4,2},{5,3},{6,0},{7,1},{8,14},{9,15},{10,... | collective-permute-start | bytes 147464 | tf_op jit(solution)/shard_map/ppermute | solution.py:602
  37.7 1.0 %collective-permute-start.7 = (f32[64,192]{1,0:T(8,128)S(1)}, f32[64,192]{1,0:T(8,128)S(1)}, u32[]{:S(2)}, u32[]{:S(2)}) collective-permute-start(f32[64,192]{1,0:T(8,128)S(1)} %get-tuple-element.104), channel_id=1, source_target_pairs={{0,2},{1,3},{2,0},{3,1},{4,6},{5,7},{6,4},{7,5},{8,10},{9,11},{10,... | collective-permute-start | bytes 147464 | tf_op jit(solution)/shard_map/ppermute | solution.py:453
  38.8 1.6 %collective-permute-start.8 = (f32[64,192]{1,0:T(8,128)S(1)}, f32[64,192]{1,0:T(8,128)S(1)}, u32[]{:S(2)}, u32[]{:S(2)}) collective-permute-start(f32[64,192]{1,0:T(8,128)S(1)} %get-tuple-element.103), channel_id=1, source_target_pairs={{0,4},{4,0},{8,12},{12,8},{1,5},{5,1},{9,13},{13,9},{2,6},{6,2},{1... | collective-permute-start | bytes 147464 | tf_op jit(solution)/shard_map/ppermute | solution.py:453
  40.3 0.3 collective-permute-done.11
  40.7 0.2 collective-permute-start.12
  40.9 2.6 %collective-permute-done.8 = f32[64,192]{1,0:T(8,128)S(1)} collective-permute-done((f32[64,192]{1,0:T(8,128)S(1)}, f32[64,192]{1,0:T(8,128)S(1)}, u32[]{:S(2)}, u32[]{:S(2)}) %collective-permute-start.8) | collective-permute-done | bytes 49184 | tf_op jit(solution)/shard_map/ppermute | solution.py:453
  43.5 0.5 %collective-permute-start.10 = (f32[64,192]{1,0:T(8,128)S(1)}, f32[64,192]{1,0:T(8,128)S(1)}, u32[]{:S(2)}, u32[]{:S(2)}) collective-permute-start(f32[64,192]{1,0:T(8,128)S(1)} %add_add_fusion.sa_ref), channel_id=1, source_target_pairs={{0,8},{4,12},{8,0},{12,4},{1,9},{5,13},{9,1},{13,5},{2,10},{6,14},... | collective-permute-start | bytes 147464 | tf_op jit(solution)/shard_map/ppermute | solution.py:453
  44.1 2.5 %collective-permute-done.12.far_ref = bf16[96,768]{1,0:T(8,128)(2,1)S(1)} collective-permute-done((bf16[96,768]{1,0:T(8,128)(2,1)S(1)}, bf16[96,768]{1,0:T(8,128)(2,1)S(1)}, u32[]{:S(2)}, u32[]{:S(2)}) %collective-permute-start.12) | collective-permute-done | bytes 147488 | tf_op jit(solution)/shard_map/ppermute | solution.py:453
  46.6 1.2 %shard_map.100._ = f32[2,192,768]{2,1,0:T(8,128)} custom-call(bf16[96,768]{1,0:T(8,128)(2,1)S(1)} %add_convert_fusion.near_ref, bf16[96,768]{1,0:T(8,128)(2,1)S(1)} %collective-permute-done.12.far_ref), custom_call_target="tpu_custom_call" | custom-call | flops 1048576 | bytes 2097152 | tf_op jit(solution)/shard_map/pallas_call | solution.py:610
  47.8 1.0 %collective-permute-done.10.sb_ref = f32[64,192]{1,0:T(8,128)S(1)} collective-permute-done((f32[64,192]{1,0:T(8,128)S(1)}, f32[64,192]{1,0:T(8,128)S(1)}, u32[]{:S(2)}, u32[]{:S(2)}) %collective-permute-start.10) | collective-permute-done | bytes 49184 | tf_op jit(solution)/shard_map/ppermute | solution.py:453
  48.8 1.6 %shard_map.101 = (f32[2,192,768]{2,1,0:T(8,128)}, f32[5,2,192]{2,1,0:T(2,128)}, f32[4,192]{1,0:T(4,128)}) custom-call(bf16[128,768]{1,0:T(8,128)(2,1)S(1)} %get-tuple-element.63.st_ref, f32[64,192]{1,0:T(8,128)S(1)} %add_add_fusion.sa_ref, f32[64,192]{1,0:T(8,128)S(1)} %collective-permute-done.10.sb_ref, ...), custom_call_target="tpu_custom_call", output_to_operand_aliasing={{0}: (3, {})} | custom-call | flops 16777216 | bytes 2097152 | tf_op jit(solution)/shard_map/pallas_call | solution.py:619
  (10 shorter events, 0.1 us)
Async XLA Ops:
  0.6 12.4 %copy-start = (s32[2]{0:T(128)S(1)}, s32[2]{0:T(128)}, u32[]{:S(2)}) copy-start(s32[2]{0:T(128)} %dils.5) | copy-start | bytes 28
  1.7 11.2 %collective-permute-start.1 = (bf16[208,768]{1,0:T(8,128)(2,1)S(1)}, bf16[208,768]{1,0:T(8,128)(2,1)S(1)}, u32[]{:S(2)}, u32[]{:S(2)}) collective-permute-start(bf16[208,768]{1,0:T(8,128)(2,1)S(1)} %get-tuple-element.56.refs_0_), channel_id=1, source_target_pairs={{0,2},{1,3},{2,0},{3,1},{4,6},{5,7},{6,4},{7,5},{8,10},{9,11},{10,... | collective-permute-start | bytes 958472 | tf_op jit(solution)/shard_map/ppermute | solution.py:453
  4.7 3.6 %collective-permute-start.2 = (s32[1,768]{1,0:T(1,128)S(1)}, s32[1,768]{1,0:T(1,128)S(1)}, u32[]{:S(2)}, u32[]{:S(2)}) collective-permute-start(s32[1,768]{1,0:T(1,128)S(1)} %get-tuple-element.57), channel_id=1, source_target_pairs={{0,4},{4,0},{8,12},{12,8},{1,5},{5,1},{9,13},{13,9},{2,6},{6,2},{1... | collective-permute-start | bytes 9224 | tf_op jit(solution)/shard_map/ppermute | solution.py:453
  8.3 4.6 %collective-permute-start.3 = (s32[2,768]{1,0:T(2,128)S(1)}, s32[2,768]{1,0:T(2,128)S(1)}, u32[]{:S(2)}, u32[]{:S(2)}) collective-permute-start(s32[2,768]{1,0:T(2,128)S(1)} %pad_add_fusion.1), channel_id=1, source_target_pairs={{0,8},{4,12},{8,0},{12,4},{1,9},{5,13},{9,1},{13,5},{2,10},{6,14},... | collective-permute-start | bytes 18440 | tf_op jit(solution)/shard_map/ppermute | solution.py:453
  11.0 3.2 %collective-permute-start = (bf16[208,768]{1,0:T(8,128)(2,1)S(1)}, bf16[208,768]{1,0:T(8,128)(2,1)S(1)}, u32[]{:S(2)}, u32[]{:S(2)}) collective-permute-start(bf16[208,768]{1,0:T(8,128)(2,1)S(1)} %get-tuple-element.56.refs_0_), channel_id=1, source_target_pairs={{0,1},{1,0},{2,3},{3,2},{4,5},{5,4},{6,7},{7,6},{8,9},{9,8},{10,11... | collective-permute-start | bytes 958472 | tf_op jit(solution)/shard_map/ppermute | solution.py:453
  12.9 1.7 %collective-permute-start.4 = (bf16[208,768]{1,0:T(8,128)(2,1)S(1)}, bf16[208,768]{1,0:T(8,128)(2,1)S(1)}, u32[]{:S(2)}, u32[]{:S(2)}) collective-permute-start(bf16[208,768]{1,0:T(8,128)(2,1)S(1)} %collective-permute-done.1.refs_2_), channel_id=1, source_target_pairs={{0,1},{1,0},{2,3},{3,2},{4,5},{5,4},{6,7},{7,6},{8,9},{9,8},{10,11... | collective-permute-start | bytes 958472 | tf_op jit(solution)/shard_map/ppermute | solution.py:453
  22.8 8.1 %collective-permute-start.5 = (bf16[96,768]{1,0:T(8,128)(2,1)S(1)}, bf16[96,768]{1,0:T(8,128)(2,1)S(1)}, u32[]{:S(2)}, u32[]{:S(2)}) collective-permute-start(bf16[96,768]{1,0:T(8,128)(2,1)S(1)} %get-tuple-element.96), channel_id=1, source_target_pairs={{0,4},{4,0},{8,12},{12,8},{1,5},{5,1},{9,13},{13,9},{2,6},{6,2},{1... | collective-permute-start | bytes 442376 | tf_op jit(solution)/shard_map/ppermute | solution.py:453
  31.0 9.7 %collective-permute-start.11 = (bf16[96,768]{1,0:T(8,128)(2,1)S(1)}, bf16[96,768]{1,0:T(8,128)(2,1)S(1)}, u32[]{:S(2)}, u32[]{:S(2)}) collective-permute-start(bf16[96,768]{1,0:T(8,128)(2,1)S(1)} %add_convert_fusion.1), channel_id=1, source_target_pairs={{0,8},{4,12},{8,0},{12,4},{1,9},{5,13},{9,1},{13,5},{2,10},{6,14},... | collective-permute-start | bytes 442376 | tf_op jit(solution)/shard_map/ppermute | solution.py:453
  35.4 1.4 %collective-permute-start.6 = (f32[2,64,192]{2,1,0:T(8,128)S(1)}, f32[2,64,192]{2,1,0:T(8,128)S(1)}, u32[]{:S(2)}, u32[]{:S(2)}) collective-permute-start(f32[2,64,192]{2,1,0:T(8,128)S(1)} %get-tuple-element.102), channel_id=1, source_target_pairs={{0,1},{1,0},{2,3},{3,2},{4,5},{5,4},{6,7},{7,6},{8,9},{9,8},{10,11... | collective-permute-start | bytes 294920 | tf_op jit(solution)/shard_map/ppermute | solution.py:453
  36.8 6.7 %collective-permute-start.9 = (f32[64,192]{1,0:T(8,128)S(1)}, f32[64,192]{1,0:T(8,128)S(1)}, u32[]{:S(2)}, u32[]{:S(2)}) collective-permute-start(f32[64,192]{1,0:T(8,128)S(1)} %get-tuple-element.104), channel_id=1, source_target_pairs={{0,6},{1,7},{2,4},{3,5},{4,2},{5,3},{6,0},{7,1},{8,14},{9,15},{10,... | collective-permute-start | bytes 147464 | tf_op jit(solution)/shard_map/ppermute | solution.py:602
  37.7 5.8 %collective-permute-start.7 = (f32[64,192]{1,0:T(8,128)S(1)}, f32[64,192]{1,0:T(8,128)S(1)}, u32[]{:S(2)}, u32[]{:S(2)}) collective-permute-start(f32[64,192]{1,0:T(8,128)S(1)} %get-tuple-element.104), channel_id=1, source_target_pairs={{0,2},{1,3},{2,0},{3,1},{4,6},{5,7},{6,4},{7,5},{8,10},{9,11},{10,... | collective-permute-start | bytes 147464 | tf_op jit(solution)/shard_map/ppermute | solution.py:453
  38.8 4.8 %collective-permute-start.8 = (f32[64,192]{1,0:T(8,128)S(1)}, f32[64,192]{1,0:T(8,128)S(1)}, u32[]{:S(2)}, u32[]{:S(2)}) collective-permute-start(f32[64,192]{1,0:T(8,128)S(1)} %get-tuple-element.103), channel_id=1, source_target_pairs={{0,4},{4,0},{8,12},{12,8},{1,5},{5,1},{9,13},{13,9},{2,6},{6,2},{1... | collective-permute-start | bytes 147464 | tf_op jit(solution)/shard_map/ppermute | solution.py:453
  40.7 5.9 %collective-permute-start.12 = (bf16[96,768]{1,0:T(8,128)(2,1)S(1)}, bf16[96,768]{1,0:T(8,128)(2,1)S(1)}, u32[]{:S(2)}, u32[]{:S(2)}) collective-permute-start(bf16[96,768]{1,0:T(8,128)(2,1)S(1)} %add_convert_fusion.near_ref), channel_id=1, source_target_pairs={{0,4},{4,0},{8,12},{12,8},{1,5},{5,1},{9,13},{13,9},{2,6},{6,2},{1... | collective-permute-start | bytes 442376 | tf_op jit(solution)/shard_map/ppermute | solution.py:453
  43.5 5.2 %collective-permute-start.10 = (f32[64,192]{1,0:T(8,128)S(1)}, f32[64,192]{1,0:T(8,128)S(1)}, u32[]{:S(2)}, u32[]{:S(2)}) collective-permute-start(f32[64,192]{1,0:T(8,128)S(1)} %add_add_fusion.sa_ref), channel_id=1, source_target_pairs={{0,8},{4,12},{8,0},{12,4},{1,9},{5,13},{9,1},{13,5},{2,10},{6,14},... | collective-permute-start | bytes 147464 | tf_op jit(solution)/shard_map/ppermute | solution.py:453

commit v10 on v9

--- a/solution.py
+++ b/solution.py
@@ -481,8 +481,9 @@
     )(in_hbm(mix_t), in_hbm(embed), in_hbm(jnp.swapaxes(taps, 0, 1)), in_hbm(tokens))
 
     seq_bits = n_seq.bit_length() - 1
-    for bit in range(seq_bits):
-        letters = jnp.concatenate([letters, flip_bits(letters, "seq", 1 << bit)], axis=0)
+    for bit in range(0, seq_bits, 2):
+        masks = [k << bit for k in range(1, 1 << min(2, seq_bits - bit))]
+        letters = jnp.concatenate([letters] + [flip_bits(letters, "seq", m) for m in masks], axis=0)
 
     mixl, cot = call(
         functools.partial(local_kernel, n_chan, width),

time: 50.2 us -> 49.7 us (0.990)
  Pallas kernels: 22.9 us -> 22.1 us
    ppermute x12 -> x13, starting transfers between devices: 15 us -> 13.9 us  [flip_bits(): lax.ppermute(x, axis, [(i, i ^ mask) for i in range(lax.axis_size(axis))])]
    ppermute x1, starting transfers between devices: 0.93 us -> 1.46 us  [body(): corner = lax.ppermute(s_mine[1], ('seq', 'chan'), pairs)]
    pallas_call x1, Pallas kernels: 6.47 us -> 5.96 us  [body(): call(functools.partial(backward_kernel, n_chan, rows, width, scale), [SME...]
    ppermute x12 -> x13, waiting for transfers between devices: 10.7 us -> 11.1 us  [flip_bits(): lax.ppermute(x, axis, [(i, i ^ mask) for i in range(lax.axis_size(axis))])]
  transfers between devices with their start and end apart: 13 -> 14, of which waited for: 8 -> 7; matrix products, arithmetic and copies ran while one was open for 0% -> 0% of each run, Pallas kernels for 24% -> 23%
where the time goes in v10:
time: 49.7 us; the launch traced here: 49.5 us
  Pallas kernels  22.1 us (44%)
  starting transfers between devices  15.4 us (31%)
  waiting for transfers between devices  11.1 us (22%)
  between operations  0.78 us (2%)
    ppermute x13, starting transfers between devices, flip_bits(): lax.ppermute(x, axis, [(i, i ^ mask) for i in range(lax.axis_size(axis))])  13.9 us
    ppermute x13, waiting for transfers between devices, flip_bits(): lax.ppermute(x, axis, [(i, i ^ mask) for i in range(lax.axis_size(axis))])  11.1 us
    pallas_call x1, Pallas kernels, body(): call(functools.partial(forward_kernel, n_chan, rows, width, scale), [SMEM...  7.96 us
    pallas_call x1, Pallas kernels, body(): call(functools.partial(backward_kernel, n_chan, rows, width, scale), [SME...  5.96 us
    pallas_call x1, Pallas kernels, body(): call(functools.partial(collect_kernel, n_chan, width, scale), [VMEM] * (n...  1.73 us
    pallas_call x1, Pallas kernels, body(): call(functools.partial(finish_kernel, n_chan, width), [VMEM, VMEM, VMEM,...  1.64 us
    ppermute x1, starting transfers between devices, body(): corner = lax.ppermute(s_mine[1], ('seq', 'chan'), pairs)  1.46 us
    pallas_call x1, Pallas kernels, body(): call(functools.partial(local_kernel, n_chan, width), [HBM, HBM], [shape((...  1.44 us
  transfers between devices with their start and end apart: 14, of which 7 were waited for; matrix products, arithmetic and copies ran while one was open for 0% of the time, Pallas kernels for 23%

profile of v10, /device:TPU:0, one launch (start us, length us, event | category | flops | bytes accessed | tf_op | source)
XLA Modules:
  0.0 49.5 jit_solution(1546165168022086552)
XLA Ops:
  0.6 1.1 %shard_map.93 = (bf16[208,768]{1,0:T(8,128)(2,1)S(1)}, s32[1,768]{1,0:T(1,128)S(1)}) custom-call(bf16[2,192,768]{2,1,0:T(8,128)(2,1)} %bitcast.7, bf16[4,192]{1,0:T(4,128)(2,1)} %embed_ref.1, bf16[5,2,192]{2,1,0:T(2,128)(2,1)} %bitcast.10, s32[768]{0:T(1024)} %tok_ref.1), custom_call_target="tpu_custom_call" | custom-call | bytes 589824 | tf_op jit(solution)/shard_map/pallas_call | solution.py:469
  1.7 3.0 %collective-permute-start.1 = (bf16[208,768]{1,0:T(8,128)(2,1)S(1)}, bf16[208,768]{1,0:T(8,128)(2,1)S(1)}, u32[]{:S(2)}, u32[]{:S(2)}) collective-permute-start(bf16[208,768]{1,0:T(8,128)(2,1)S(1)} %get-tuple-element.56.refs_0_), channel_id=1, source_target_pairs={{0,2},{1,3},{2,0},{3,1},{4,6},{5,7},{6,4},{7,5},{8,10},{9,11},{10,... | collective-permute-start | bytes 958472 | tf_op jit(solution)/shard_map/ppermute | solution.py:453
  4.7 3.6 %collective-permute-start.4 = (s32[1,768]{1,0:T(1,128)S(1)}, s32[1,768]{1,0:T(1,128)S(1)}, u32[]{:S(2)}, u32[]{:S(2)}) collective-permute-start(s32[1,768]{1,0:T(1,128)S(1)} %get-tuple-element.57), channel_id=1, source_target_pairs={{0,12},{4,8},{8,4},{12,0},{1,13},{5,9},{9,5},{13,1},{2,14},{6,10},... | collective-permute-start | bytes 9224 | tf_op jit(solution)/shard_map/ppermute | solution.py:453
  8.3 0.0 collective-permute-start.3
  8.3 0.8 %collective-permute-start.2 = (s32[1,768]{1,0:T(1,128)S(1)}, s32[1,768]{1,0:T(1,128)S(1)}, u32[]{:S(2)}, u32[]{:S(2)}) collective-permute-start(s32[1,768]{1,0:T(1,128)S(1)} %get-tuple-element.57), channel_id=1, source_target_pairs={{0,4},{4,0},{8,12},{12,8},{1,5},{5,1},{9,13},{13,9},{2,6},{6,2},{1... | collective-permute-start | bytes 9224 | tf_op jit(solution)/shard_map/ppermute | solution.py:453
  9.1 0.0 collective-permute-start
  9.1 1.4 %shard_map.94 = (bf16[192,768]{1,0:T(8,128)(2,1)S(1)}, bf16[768,192]{1,0:T(8,128)(2,1)S(1)}) custom-call(bf16[2,192,768]{2,1,0:T(8,128)(2,1)} %bitcast.8, bf16[192,768]{1,0:T(8,128)(2,1)} %bitcast.9), custom_call_target="tpu_custom_call" | custom-call | flops 1048576 | bytes 1048576 | tf_op jit(solution)/shard_map/pallas_call | solution.py:488
  10.5 0.0 collective-permute-done.4
  10.6 2.2 %collective-permute-done.3 = s32[1,768]{1,0:T(1,128)S(1)} collective-permute-done((s32[1,768]{1,0:T(1,128)S(1)}, s32[1,768]{1,0:T(1,128)S(1)}, u32[]{:S(2)}, u32[]{:S(2)}) %collective-permute-start.3) | collective-permute-done | bytes 3104 | tf_op jit(solution)/shard_map/ppermute | solution.py:453
  12.8 0.0 collective-permute-done.1.refs_2_
  12.8 0.1 collective-permute-start.5
  12.9 1.1 %shard_map.95 = (bf16[896,128]{1,0:T(8,128)(2,1)S(1)}, bf16[64,896]{1,0:T(8,128)(2,1)S(1)}, bf16[64,768]{1,0:T(8,128)(2,1)S(1)}) custom-call(s32[2]{0:T(128)S(1)} %copy-done, s32[4,768]{1,0:T(4,128)S(1)} %pad_add_fusion.tok_ref), custom_call_target="tpu_custom_call" | custom-call | flops 1048576 | bytes 1048576 | tf_op jit(solution)/shard_map/pallas_call | solution.py:508
  14.1 0.0 collective-permute-done.refs_1_
  14.1 0.4 collective-permute-done.5.refs_3_
  14.5 8.0 %shard_map.96 = (bf16[192,768]{1,0:T(8,128)(2,1)}, bf16[96,768]{1,0:T(8,128)(2,1)S(1)}, bf16[96,768]{1,0:T(8,128)(2,1)S(1)}, bf16[768,192]{1,0:T(8,128)(2,1)S(1)...) custom-call(s32[2]{0:T(128)S(1)} %copy-done, ...), custom_call_target="tpu_custom_call" | custom-call | flops 3221225472 | bytes 8388608 | tf_op jit(solution)/shard_map/pallas_call | solution.py:519
  22.5 1.2 %collective-permute-start.6 = (bf16[96,768]{1,0:T(8,128)(2,1)S(1)}, bf16[96,768]{1,0:T(8,128)(2,1)S(1)}, u32[]{:S(2)}, u32[]{:S(2)}) collective-permute-start(bf16[96,768]{1,0:T(8,128)(2,1)S(1)} %get-tuple-element.96), channel_id=1, source_target_pairs={{0,4},{4,0},{8,12},{12,8},{1,5},{5,1},{9,13},{13,9},{2,6},{6,2},{1... | collective-permute-start | bytes 442376 | tf_op jit(solution)/shard_map/ppermute | solution.py:453
  23.7 6.0 %shard_map.97 = (bf16[768,768]{1,0:T(8,128)(2,1)S(1)}, f32[2,8,768]{2,1,0:T(8,128)S(1)}, f32[64,768]{1,0:T(8,128)S(1)}, f32[64,768]{1,0:T(8,128)S(1)}) custom-call(s32[2]{0:T(128)S(1)} %copy-done, bf16[64,896]{1,0:T(8,128)(2,1)S(1)} %get-tuple-element.67.refs_0_, bf16[192,768]{1,0:T(8,128)(2,1)S(1)} %get-tuple-element.58.refs_5_.refs_1_, ...), custom_call_target="tpu_custom_call" | custom-call | flops 3221225472 | bytes 8388608 | tf_op jit(solution)/shard_map/pallas_call | solution.py:545
  29.7 2.6 %collective-permute-start.12 = (bf16[96,768]{1,0:T(8,128)(2,1)S(1)}, bf16[96,768]{1,0:T(8,128)(2,1)S(1)}, u32[]{:S(2)}, u32[]{:S(2)}) collective-permute-start(bf16[96,768]{1,0:T(8,128)(2,1)S(1)} %add_convert_fusion.1), channel_id=1, source_target_pairs={{0,8},{4,12},{8,0},{12,4},{1,9},{5,13},{9,1},{13,5},{2,10},{6,14},... | collective-permute-start | bytes 442376 | tf_op jit(solution)/shard_map/ppermute | solution.py:453
  32.4 1.7 %shard_map.98 = (f32[2,64,192]{2,1,0:T(8,128)S(1)}, f32[2,64,192]{2,1,0:T(8,128)S(1)}) custom-call(bf16[208,768]{1,0:T(8,128)(2,1)S(1)} %get-tuple-element.56.refs_0_, bf16[208,768]{1,0:T(8,128)(2,1)S(1)} %collective-permute-done.refs_1_, bf16[208,768]{1,0:T(8,128)(2,1)S(1)} %collective-permute-done.1.refs_2_, ...), custom_call_target="tpu_custom_call" | custom-call | flops 1048576 | bytes 65536 | tf_op jit(solution)/shard_map/pallas_call | solution.py:567
  34.1 0.0 collective-permute-start.7
  34.2 1.3 %collective-permute-done.7.b_ref = f32[2,64,192]{2,1,0:T(8,128)S(1)} collective-permute-done((f32[2,64,192]{2,1,0:T(8,128)S(1)}, f32[2,64,192]{2,1,0:T(8,128)S(1)}, u32[]{:S(2)}, u32[]{:S(2)}) %collective-permute-start.7) | collective-permute-done | bytes 98336 | tf_op jit(solution)/shard_map/ppermute | solution.py:453
  35.5 1.5 %collective-permute-start.10 = (f32[64,192]{1,0:T(8,128)S(1)}, f32[64,192]{1,0:T(8,128)S(1)}, u32[]{:S(2)}, u32[]{:S(2)}) collective-permute-start(f32[64,192]{1,0:T(8,128)S(1)} %get-tuple-element.104), channel_id=1, source_target_pairs={{0,6},{1,7},{2,4},{3,5},{4,2},{5,3},{6,0},{7,1},{8,14},{9,15},{10,... | collective-permute-start | bytes 147464 | tf_op jit(solution)/shard_map/ppermute | solution.py:603
  37.0 0.5 %collective-permute-start.8 = (f32[64,192]{1,0:T(8,128)S(1)}, f32[64,192]{1,0:T(8,128)S(1)}, u32[]{:S(2)}, u32[]{:S(2)}) collective-permute-start(f32[64,192]{1,0:T(8,128)S(1)} %get-tuple-element.104), channel_id=1, source_target_pairs={{0,2},{1,3},{2,0},{3,1},{4,6},{5,7},{6,4},{7,5},{8,10},{9,11},{10,... | collective-permute-start | bytes 147464 | tf_op jit(solution)/shard_map/ppermute | solution.py:453
  37.5 1.6 %collective-permute-start.9 = (f32[64,192]{1,0:T(8,128)S(1)}, f32[64,192]{1,0:T(8,128)S(1)}, u32[]{:S(2)}, u32[]{:S(2)}) collective-permute-start(f32[64,192]{1,0:T(8,128)S(1)} %get-tuple-element.103), channel_id=1, source_target_pairs={{0,4},{4,0},{8,12},{12,8},{1,5},{5,1},{9,13},{13,9},{2,6},{6,2},{1... | collective-permute-start | bytes 147464 | tf_op jit(solution)/shard_map/ppermute | solution.py:453
  39.1 0.4 collective-permute-done.12
  39.5 0.1 collective-permute-start.13
  39.6 3.0 %collective-permute-done.9 = f32[64,192]{1,0:T(8,128)S(1)} collective-permute-done((f32[64,192]{1,0:T(8,128)S(1)}, f32[64,192]{1,0:T(8,128)S(1)}, u32[]{:S(2)}, u32[]{:S(2)}) %collective-permute-start.9) | collective-permute-done | bytes 49184 | tf_op jit(solution)/shard_map/ppermute | solution.py:453
  42.7 0.3 collective-permute-start.11
  43.0 2.5 %collective-permute-done.13.far_ref = bf16[96,768]{1,0:T(8,128)(2,1)S(1)} collective-permute-done((bf16[96,768]{1,0:T(8,128)(2,1)S(1)}, bf16[96,768]{1,0:T(8,128)(2,1)S(1)}, u32[]{:S(2)}, u32[]{:S(2)}) %collective-permute-start.13) | collective-permute-done | bytes 147488 | tf_op jit(solution)/shard_map/ppermute | solution.py:453
  45.5 1.2 %shard_map.100._ = f32[2,192,768]{2,1,0:T(8,128)} custom-call(bf16[96,768]{1,0:T(8,128)(2,1)S(1)} %add_convert_fusion.near_ref, bf16[96,768]{1,0:T(8,128)(2,1)S(1)} %collective-permute-done.13.far_ref), custom_call_target="tpu_custom_call" | custom-call | flops 1048576 | bytes 2097152 | tf_op jit(solution)/shard_map/pallas_call | solution.py:611
  46.7 1.2 %collective-permute-done.11.sb_ref = f32[64,192]{1,0:T(8,128)S(1)} collective-permute-done((f32[64,192]{1,0:T(8,128)S(1)}, f32[64,192]{1,0:T(8,128)S(1)}, u32[]{:S(2)}, u32[]{:S(2)}) %collective-permute-start.11) | collective-permute-done | bytes 49184 | tf_op jit(solution)/shard_map/ppermute | solution.py:453
  47.9 1.6 %shard_map.101 = (f32[2,192,768]{2,1,0:T(8,128)}, f32[5,2,192]{2,1,0:T(2,128)}, f32[4,192]{1,0:T(4,128)}) custom-call(bf16[128,768]{1,0:T(8,128)(2,1)S(1)} %get-tuple-element.63.st_ref, f32[64,192]{1,0:T(8,128)S(1)} %add_add_fusion.sa_ref, f32[64,192]{1,0:T(8,128)S(1)} %collective-permute-done.11.sb_ref, ...), custom_call_target="tpu_custom_call", output_to_operand_aliasing={{0}: (3, {})} | custom-call | flops 16777216 | bytes 2097152 | tf_op jit(solution)/shard_map/pallas_call | solution.py:620
  (11 shorter events, 0.1 us)
Async XLA Ops:
  0.6 12.3 %copy-start = (s32[2]{0:T(128)S(1)}, s32[2]{0:T(128)}, u32[]{:S(2)}) copy-start(s32[2]{0:T(128)} %dils.5) | copy-start | bytes 28
  1.7 11.1 %collective-permute-start.1 = (bf16[208,768]{1,0:T(8,128)(2,1)S(1)}, bf16[208,768]{1,0:T(8,128)(2,1)S(1)}, u32[]{:S(2)}, u32[]{:S(2)}) collective-permute-start(bf16[208,768]{1,0:T(8,128)(2,1)S(1)} %get-tuple-element.56.refs_0_), channel_id=1, source_target_pairs={{0,2},{1,3},{2,0},{3,1},{4,6},{5,7},{6,4},{7,5},{8,10},{9,11},{10,... | collective-permute-start | bytes 958472 | tf_op jit(solution)/shard_map/ppermute | solution.py:453
  4.7 5.8 %collective-permute-start.4 = (s32[1,768]{1,0:T(1,128)S(1)}, s32[1,768]{1,0:T(1,128)S(1)}, u32[]{:S(2)}, u32[]{:S(2)}) collective-permute-start(s32[1,768]{1,0:T(1,128)S(1)} %get-tuple-element.57), channel_id=1, source_target_pairs={{0,12},{4,8},{8,4},{12,0},{1,13},{5,9},{9,5},{13,1},{2,14},{6,10},... | collective-permute-start | bytes 9224 | tf_op jit(solution)/shard_map/ppermute | solution.py:453
  8.3 4.5 %collective-permute-start.3 = (s32[1,768]{1,0:T(1,128)S(1)}, s32[1,768]{1,0:T(1,128)S(1)}, u32[]{:S(2)}, u32[]{:S(2)}) collective-permute-start(s32[1,768]{1,0:T(1,128)S(1)} %get-tuple-element.57), channel_id=1, source_target_pairs={{0,8},{4,12},{8,0},{12,4},{1,9},{5,13},{9,1},{13,5},{2,10},{6,14},... | collective-permute-start | bytes 9224 | tf_op jit(solution)/shard_map/ppermute | solution.py:453
  8.3 4.5 %collective-permute-start.2 = (s32[1,768]{1,0:T(1,128)S(1)}, s32[1,768]{1,0:T(1,128)S(1)}, u32[]{:S(2)}, u32[]{:S(2)}) collective-permute-start(s32[1,768]{1,0:T(1,128)S(1)} %get-tuple-element.57), channel_id=1, source_target_pairs={{0,4},{4,0},{8,12},{12,8},{1,5},{5,1},{9,13},{13,9},{2,6},{6,2},{1... | collective-permute-start | bytes 9224 | tf_op jit(solution)/shard_map/ppermute | solution.py:453
  9.1 5.0 %collective-permute-start = (bf16[208,768]{1,0:T(8,128)(2,1)S(1)}, bf16[208,768]{1,0:T(8,128)(2,1)S(1)}, u32[]{:S(2)}, u32[]{:S(2)}) collective-permute-start(bf16[208,768]{1,0:T(8,128)(2,1)S(1)} %get-tuple-element.56.refs_0_), channel_id=1, source_target_pairs={{0,1},{1,0},{2,3},{3,2},{4,5},{5,4},{6,7},{7,6},{8,9},{9,8},{10,11... | collective-permute-start | bytes 958472 | tf_op jit(solution)/shard_map/ppermute | solution.py:453
  12.8 1.7 %collective-permute-start.5 = (bf16[208,768]{1,0:T(8,128)(2,1)S(1)}, bf16[208,768]{1,0:T(8,128)(2,1)S(1)}, u32[]{:S(2)}, u32[]{:S(2)}) collective-permute-start(bf16[208,768]{1,0:T(8,128)(2,1)S(1)} %collective-permute-done.1.refs_2_), channel_id=1, source_target_pairs={{0,1},{1,0},{2,3},{3,2},{4,5},{5,4},{6,7},{7,6},{8,9},{9,8},{10,11... | collective-permute-start | bytes 958472 | tf_op jit(solution)/shard_map/ppermute | solution.py:453
  22.5 7.2 %collective-permute-start.6 = (bf16[96,768]{1,0:T(8,128)(2,1)S(1)}, bf16[96,768]{1,0:T(8,128)(2,1)S(1)}, u32[]{:S(2)}, u32[]{:S(2)}) collective-permute-start(bf16[96,768]{1,0:T(8,128)(2,1)S(1)} %get-tuple-element.96), channel_id=1, source_target_pairs={{0,4},{4,0},{8,12},{12,8},{1,5},{5,1},{9,13},{13,9},{2,6},{6,2},{1... | collective-permute-start | bytes 442376 | tf_op jit(solution)/shard_map/ppermute | solution.py:453
  29.7 9.7 %collective-permute-start.12 = (bf16[96,768]{1,0:T(8,128)(2,1)S(1)}, bf16[96,768]{1,0:T(8,128)(2,1)S(1)}, u32[]{:S(2)}, u32[]{:S(2)}) collective-permute-start(bf16[96,768]{1,0:T(8,128)(2,1)S(1)} %add_convert_fusion.1), channel_id=1, source_target_pairs={{0,8},{4,12},{8,0},{12,4},{1,9},{5,13},{9,1},{13,5},{2,10},{6,14},... | collective-permute-start | bytes 442376 | tf_op jit(solution)/shard_map/ppermute | solution.py:453
  34.1 1.4 %collective-permute-start.7 = (f32[2,64,192]{2,1,0:T(8,128)S(1)}, f32[2,64,192]{2,1,0:T(8,128)S(1)}, u32[]{:S(2)}, u32[]{:S(2)}) collective-permute-start(f32[2,64,192]{2,1,0:T(8,128)S(1)} %get-tuple-element.102), channel_id=1, source_target_pairs={{0,1},{1,0},{2,3},{3,2},{4,5},{5,4},{6,7},{7,6},{8,9},{9,8},{10,11... | collective-permute-start | bytes 294920 | tf_op jit(solution)/shard_map/ppermute | solution.py:453
  35.5 7.1 %collective-permute-start.10 = (f32[64,192]{1,0:T(8,128)S(1)}, f32[64,192]{1,0:T(8,128)S(1)}, u32[]{:S(2)}, u32[]{:S(2)}) collective-permute-start(f32[64,192]{1,0:T(8,128)S(1)} %get-tuple-element.104), channel_id=1, source_target_pairs={{0,6},{1,7},{2,4},{3,5},{4,2},{5,3},{6,0},{7,1},{8,14},{9,15},{10,... | collective-permute-start | bytes 147464 | tf_op jit(solution)/shard_map/ppermute | solution.py:603
  37.0 5.7 %collective-permute-start.8 = (f32[64,192]{1,0:T(8,128)S(1)}, f32[64,192]{1,0:T(8,128)S(1)}, u32[]{:S(2)}, u32[]{:S(2)}) collective-permute-start(f32[64,192]{1,0:T(8,128)S(1)} %get-tuple-element.104), channel_id=1, source_target_pairs={{0,2},{1,3},{2,0},{3,1},{4,6},{5,7},{6,4},{7,5},{8,10},{9,11},{10,... | collective-permute-start | bytes 147464 | tf_op jit(solution)/shard_map/ppermute | solution.py:453
  37.5 5.1 %collective-permute-start.9 = (f32[64,192]{1,0:T(8,128)S(1)}, f32[64,192]{1,0:T(8,128)S(1)}, u32[]{:S(2)}, u32[]{:S(2)}) collective-permute-start(f32[64,192]{1,0:T(8,128)S(1)} %get-tuple-element.103), channel_id=1, source_target_pairs={{0,4},{4,0},{8,12},{12,8},{1,5},{5,1},{9,13},{13,9},{2,6},{6,2},{1... | collective-permute-start | bytes 147464 | tf_op jit(solution)/shard_map/ppermute | solution.py:453
  39.5 5.9 %collective-permute-start.13 = (bf16[96,768]{1,0:T(8,128)(2,1)S(1)}, bf16[96,768]{1,0:T(8,128)(2,1)S(1)}, u32[]{:S(2)}, u32[]{:S(2)}) collective-permute-start(bf16[96,768]{1,0:T(8,128)(2,1)S(1)} %add_convert_fusion.near_ref), channel_id=1, source_target_pairs={{0,4},{4,0},{8,12},{12,8},{1,5},{5,1},{9,13},{13,9},{2,6},{6,2},{1... | collective-permute-start | bytes 442376 | tf_op jit(solution)/shard_map/ppermute | solution.py:453
  42.7 5.2 %collective-permute-start.11 = (f32[64,192]{1,0:T(8,128)S(1)}, f32[64,192]{1,0:T(8,128)S(1)}, u32[]{:S(2)}, u32[]{:S(2)}) collective-permute-start(f32[64,192]{1,0:T(8,128)S(1)} %add_add_fusion.sa_ref), channel_id=1, source_target_pairs={{0,8},{4,12},{8,0},{12,4},{1,9},{5,13},{9,1},{13,5},{2,10},{6,14},... | collective-permute-start | bytes 147464 | tf_op jit(solution)/shard_map/ppermute | solution.py:453

commit v11 on v10

--- a/solution.py
+++ b/solution.py
@@ -391,8 +391,8 @@
 
 
 def add_kernel(a_ref, b_ref, first_ref, second_ref):
-    first_ref[...] = a_ref[0] + b_ref[0]
-    second_ref[...] = a_ref[1] + b_ref[1]
+    first_ref[...] = (a_ref[0] + b_ref[0]).astype(BF)
+    second_ref[...] = (a_ref[1] + b_ref[1]).astype(BF)
 
 
 def mix1_kernel(n_chan, width, near_ref, far_ref, out_ref, held, sem):
@@ -408,7 +408,7 @@
 
 
 def finish_kernel(n_chan, width, st_ref, sa_ref, sb_ref, _, gm_ref, gt_ref, ge_ref, held, sems):
-    sums = sa_ref[...] + sb_ref[...]
+    sums = sa_ref[...].astype(F32) + sb_ref[...].astype(F32)
     fill = jnp.zeros((JB - ROW_GE, width), F32)
     dw = jnp.concatenate([sums[:ROW_GE], fill, sums[ROW_R : ROW_R + ROW_GE], fill], axis=0).astype(BF)
     copies = []
@@ -590,7 +590,7 @@
     s_mine = call(
         add_kernel,
         [VMEM] * 2,
-        [shape((SUMS, width), F32)] * 2,
+        [shape((SUMS, width), BF)] * 2,
         [VMEM] * 2,
         [],
         8,
@@ -601,11 +601,12 @@
     places = [(i, j) for i in range(n_seq) for j in range(n_chan)]
     pairs = [(i * n_chan + j, (i ^ 1) * n_chan + (j ^ (1 << last))) for i, j in places]
     corner = lax.ppermute(s_mine[1], ("seq", "chan"), pairs)
-    s_mine = (s_mine[0] + across) + (along + corner)
+    here, there = (s_mine[0], across), (along, corner)
+    s_mine = rounded_sum(*(a.astype(F32) + b.astype(F32) for a, b in (here, there)))
     for bit in range(1, seq_bits):
         s_other = flip_bits(s_mine, "seq", 1 << bit)
         if bit < seq_bits - 1:
-            s_mine = s_mine + s_other
+            s_mine = rounded_sum(s_mine, s_other)
 
     big = pltpu.VMEM((width, chans), F32)
     (grad_mix,) = call(

time: 49.7 us -> 49.1 us (0.988)
  waiting for transfers between devices: 11.1 us -> 8.78 us
  starting transfers between devices: 15.4 us -> 16.4 us
  Pallas kernels: 22.1 us -> 22.9 us
    ppermute x13, waiting for transfers between devices: 11.1 us -> 8.78 us  [flip_bits(): lax.ppermute(x, axis, [(i, i ^ mask) for i in range(lax.axis_size(axis))])]
    ppermute x13, starting transfers between devices: 13.9 us -> 15 us  [flip_bits(): lax.ppermute(x, axis, [(i, i ^ mask) for i in range(lax.axis_size(axis))])]
    pallas_call x1, Pallas kernels: 5.96 us -> 6.47 us  [body(): call(functools.partial(backward_kernel, n_chan, rows, width, scale), [SME...]
  transfers between devices with their start and end apart: 14 -> 14, of which waited for: 7 -> 6; matrix products, arithmetic and copies ran while one was open for 0% -> 0% of each run, Pallas kernels for 23% -> 24%
where the time goes in v11:
time: 49.1 us; the launch traced here: 49 us
  Pallas kernels  22.9 us (47%)
  starting transfers between devices  16.4 us (33%)
  waiting for transfers between devices  8.78 us (18%)
  between operations  0.78 us (2%)
    ppermute x13, starting transfers between devices, flip_bits(): lax.ppermute(x, axis, [(i, i ^ mask) for i in range(lax.axis_size(axis))])  15 us
    ppermute x13, waiting for transfers between devices, flip_bits(): lax.ppermute(x, axis, [(i, i ^ mask) for i in range(lax.axis_size(axis))])  8.78 us
    pallas_call x1, Pallas kernels, body(): call(functools.partial(forward_kernel, n_chan, rows, width, scale), [SMEM...  8.19 us
    pallas_call x1, Pallas kernels, body(): call(functools.partial(backward_kernel, n_chan, rows, width, scale), [SME...  6.47 us
    pallas_call x1, Pallas kernels, body(): call(functools.partial(collect_kernel, n_chan, width, scale), [VMEM] * (n...  1.73 us
    pallas_call x1, Pallas kernels, body(): call(functools.partial(finish_kernel, n_chan, width), [VMEM, VMEM, VMEM,...  1.65 us
    ppermute x1, starting transfers between devices, body(): corner = lax.ppermute(s_mine[1], ('seq', 'chan'), pairs)  1.45 us
    pallas_call x1, Pallas kernels, body(): call(functools.partial(local_kernel, n_chan, width), [HBM, HBM], [shape((...  1.44 us
  transfers between devices with their start and end apart: 14, of which 6 were waited for; matrix products, arithmetic and copies ran while one was open for 0% of the time, Pallas kernels for 24%

profile of v11, /device:TPU:0, one launch (start us, length us, event | category | flops | bytes accessed | tf_op | source)
XLA Modules:
  0.0 49.0 jit_solution(7949206505376836367)
XLA Ops:
  0.6 1.1 %shard_map.93 = (bf16[208,768]{1,0:T(8,128)(2,1)S(1)}, s32[1,768]{1,0:T(1,128)S(1)}) custom-call(bf16[2,192,768]{2,1,0:T(8,128)(2,1)} %bitcast.7, bf16[4,192]{1,0:T(4,128)(2,1)} %embed_ref.1, bf16[5,2,192]{2,1,0:T(2,128)(2,1)} %bitcast.10, s32[768]{0:T(1024)} %tok_ref.1), custom_call_target="tpu_custom_call" | custom-call | bytes 589824 | tf_op jit(solution)/shard_map/pallas_call | solution.py:469
  1.7 3.0 %collective-permute-start.1 = (bf16[208,768]{1,0:T(8,128)(2,1)S(1)}, bf16[208,768]{1,0:T(8,128)(2,1)S(1)}, u32[]{:S(2)}, u32[]{:S(2)}) collective-permute-start(bf16[208,768]{1,0:T(8,128)(2,1)S(1)} %get-tuple-element.56.refs_0_), channel_id=1, source_target_pairs={{0,2},{1,3},{2,0},{3,1},{4,6},{5,7},{6,4},{7,5},{8,10},{9,11},{10,... | collective-permute-start | bytes 958472 | tf_op jit(solution)/shard_map/ppermute | solution.py:453
  4.7 3.6 %collective-permute-start.4 = (s32[1,768]{1,0:T(1,128)S(1)}, s32[1,768]{1,0:T(1,128)S(1)}, u32[]{:S(2)}, u32[]{:S(2)}) collective-permute-start(s32[1,768]{1,0:T(1,128)S(1)} %get-tuple-element.57), channel_id=1, source_target_pairs={{0,12},{4,8},{8,4},{12,0},{1,13},{5,9},{9,5},{13,1},{2,14},{6,10},... | collective-permute-start | bytes 9224 | tf_op jit(solution)/shard_map/ppermute | solution.py:453
  8.3 0.0 collective-permute-start.3
  8.3 0.8 %collective-permute-start.2 = (s32[1,768]{1,0:T(1,128)S(1)}, s32[1,768]{1,0:T(1,128)S(1)}, u32[]{:S(2)}, u32[]{:S(2)}) collective-permute-start(s32[1,768]{1,0:T(1,128)S(1)} %get-tuple-element.57), channel_id=1, source_target_pairs={{0,4},{4,0},{8,12},{12,8},{1,5},{5,1},{9,13},{13,9},{2,6},{6,2},{1... | collective-permute-start | bytes 9224 | tf_op jit(solution)/shard_map/ppermute | solution.py:453
  9.1 0.0 collective-permute-start
  9.1 1.4 %shard_map.94 = (bf16[192,768]{1,0:T(8,128)(2,1)S(1)}, bf16[768,192]{1,0:T(8,128)(2,1)S(1)}) custom-call(bf16[2,192,768]{2,1,0:T(8,128)(2,1)} %bitcast.8, bf16[192,768]{1,0:T(8,128)(2,1)} %bitcast.9), custom_call_target="tpu_custom_call" | custom-call | flops 1048576 | bytes 1048576 | tf_op jit(solution)/shard_map/pallas_call | solution.py:488
  10.5 0.0 collective-permute-done.4
  10.6 2.2 %collective-permute-done.3 = s32[1,768]{1,0:T(1,128)S(1)} collective-permute-done((s32[1,768]{1,0:T(1,128)S(1)}, s32[1,768]{1,0:T(1,128)S(1)}, u32[]{:S(2)}, u32[]{:S(2)}) %collective-permute-start.3) | collective-permute-done | bytes 3104 | tf_op jit(solution)/shard_map/ppermute | solution.py:453
  12.8 0.0 collective-permute-done.1.refs_2_
  12.8 0.1 collective-permute-start.5
  12.9 1.1 %shard_map.95 = (bf16[896,128]{1,0:T(8,128)(2,1)S(1)}, bf16[64,896]{1,0:T(8,128)(2,1)S(1)}, bf16[64,768]{1,0:T(8,128)(2,1)S(1)}) custom-call(s32[2]{0:T(128)S(1)} %copy-done, s32[4,768]{1,0:T(4,128)S(1)} %pad_add_fusion.tok_ref), custom_call_target="tpu_custom_call" | custom-call | flops 1048576 | bytes 1048576 | tf_op jit(solution)/shard_map/pallas_call | solution.py:508
  14.1 0.0 collective-permute-done.refs_1_
  14.1 0.4 collective-permute-done.5.refs_3_
  14.5 8.2 %shard_map.96 = (bf16[192,768]{1,0:T(8,128)(2,1)}, bf16[96,768]{1,0:T(8,128)(2,1)S(1)}, bf16[96,768]{1,0:T(8,128)(2,1)S(1)}, bf16[768,192]{1,0:T(8,128)(2,1)S(1)...) custom-call(s32[2]{0:T(128)S(1)} %copy-done, ...), custom_call_target="tpu_custom_call" | custom-call | flops 3221225472 | bytes 8388608 | tf_op jit(solution)/shard_map/pallas_call | solution.py:519
  22.7 1.2 %collective-permute-start.6 = (bf16[96,768]{1,0:T(8,128)(2,1)S(1)}, bf16[96,768]{1,0:T(8,128)(2,1)S(1)}, u32[]{:S(2)}, u32[]{:S(2)}) collective-permute-start(bf16[96,768]{1,0:T(8,128)(2,1)S(1)} %get-tuple-element.96), channel_id=1, source_target_pairs={{0,4},{4,0},{8,12},{12,8},{1,5},{5,1},{9,13},{13,9},{2,6},{6,2},{1... | collective-permute-start | bytes 442376 | tf_op jit(solution)/shard_map/ppermute | solution.py:453
  24.0 6.5 %shard_map.97 = (bf16[768,768]{1,0:T(8,128)(2,1)S(1)}, f32[2,8,768]{2,1,0:T(8,128)S(1)}, f32[64,768]{1,0:T(8,128)S(1)}, f32[64,768]{1,0:T(8,128)S(1)}) custom-call(s32[2]{0:T(128)S(1)} %copy-done, bf16[64,896]{1,0:T(8,128)(2,1)S(1)} %get-tuple-element.67.refs_0_, bf16[192,768]{1,0:T(8,128)(2,1)S(1)} %get-tuple-element.58.refs_5_.refs_1_, ...), custom_call_target="tpu_custom_call" | custom-call | flops 3221225472 | bytes 8388608 | tf_op jit(solution)/shard_map/pallas_call | solution.py:545
  30.4 0.0 collective-permute-done.6
  30.5 2.6 %collective-permute-start.12 = (bf16[96,768]{1,0:T(8,128)(2,1)S(1)}, bf16[96,768]{1,0:T(8,128)(2,1)S(1)}, u32[]{:S(2)}, u32[]{:S(2)}) collective-permute-start(bf16[96,768]{1,0:T(8,128)(2,1)S(1)} %add_convert_fusion.1), channel_id=1, source_target_pairs={{0,8},{4,12},{8,0},{12,4},{1,9},{5,13},{9,1},{13,5},{2,10},{6,14},... | collective-permute-start | bytes 442376 | tf_op jit(solution)/shard_map/ppermute | solution.py:453
  33.1 1.7 %shard_map.98 = (f32[2,64,192]{2,1,0:T(8,128)S(1)}, f32[2,64,192]{2,1,0:T(8,128)S(1)}) custom-call(bf16[208,768]{1,0:T(8,128)(2,1)S(1)} %get-tuple-element.56.refs_0_, bf16[208,768]{1,0:T(8,128)(2,1)S(1)} %collective-permute-done.refs_1_, bf16[208,768]{1,0:T(8,128)(2,1)S(1)} %collective-permute-done.1.refs_2_, ...), custom_call_target="tpu_custom_call" | custom-call | flops 1048576 | bytes 65536 | tf_op jit(solution)/shard_map/pallas_call | solution.py:567
  34.9 0.0 collective-permute-start.7
  34.9 1.3 %collective-permute-done.7.b_ref = f32[2,64,192]{2,1,0:T(8,128)S(1)} collective-permute-done((f32[2,64,192]{2,1,0:T(8,128)S(1)}, f32[2,64,192]{2,1,0:T(8,128)S(1)}, u32[]{:S(2)}, u32[]{:S(2)}) %collective-permute-start.7) | collective-permute-done | bytes 98336 | tf_op jit(solution)/shard_map/ppermute | solution.py:453
  36.3 1.4 %collective-permute-start.10 = (bf16[64,192]{1,0:T(8,128)(2,1)S(1)}, bf16[64,192]{1,0:T(8,128)(2,1)S(1)}, u32[]{:S(2)}, u32[]{:S(2)}) collective-permute-start(bf16[64,192]{1,0:T(8,128)(2,1)S(1)} %get-tuple-element.104), channel_id=1, source_target_pairs={{0,6},{1,7},{2,4},{3,5},{4,2},{5,3},{6,0},{7,1},{8,14},{9,15},{10,... | collective-permute-start | bytes 73736 | tf_op jit(solution)/shard_map/ppermute | solution.py:603
  37.7 0.5 %collective-permute-start.8 = (bf16[64,192]{1,0:T(8,128)(2,1)S(1)}, bf16[64,192]{1,0:T(8,128)(2,1)S(1)}, u32[]{:S(2)}, u32[]{:S(2)}) collective-permute-start(bf16[64,192]{1,0:T(8,128)(2,1)S(1)} %get-tuple-element.104), channel_id=1, source_target_pairs={{0,2},{1,3},{2,0},{3,1},{4,6},{5,7},{6,4},{7,5},{8,10},{9,11},{10,... | collective-permute-start | bytes 73736 | tf_op jit(solution)/shard_map/ppermute | solution.py:453
  38.2 1.6 %collective-permute-start.9 = (bf16[64,192]{1,0:T(8,128)(2,1)S(1)}, bf16[64,192]{1,0:T(8,128)(2,1)S(1)}, u32[]{:S(2)}, u32[]{:S(2)}) collective-permute-start(bf16[64,192]{1,0:T(8,128)(2,1)S(1)} %get-tuple-element.103), channel_id=1, source_target_pairs={{0,4},{4,0},{8,12},{12,8},{1,5},{5,1},{9,13},{13,9},{2,6},{6,2},{1... | collective-permute-start | bytes 73736 | tf_op jit(solution)/shard_map/ppermute | solution.py:453
  39.8 0.4 collective-permute-done.12
  40.3 0.1 collective-permute-start.13
  40.4 1.8 %collective-permute-done.9 = bf16[64,192]{1,0:T(8,128)(2,1)S(1)} collective-permute-done((bf16[64,192]{1,0:T(8,128)(2,1)S(1)}, bf16[64,192]{1,0:T(8,128)(2,1)S(1)}, u32[]{:S(2)}, u32[]{:S(2)}) %collective-permute-start.9) | collective-permute-done | bytes 24608 | tf_op jit(solution)/shard_map/ppermute | solution.py:453
  42.2 1.4 %collective-permute-start.11 = (bf16[64,192]{1,0:T(8,128)(2,1)S(1)}, bf16[64,192]{1,0:T(8,128)(2,1)S(1)}, u32[]{:S(2)}, u32[]{:S(2)}) collective-permute-start(bf16[64,192]{1,0:T(8,128)(2,1)S(1)} %add_convert_fusion.2.sa_ref), channel_id=1, source_target_pairs={{0,8},{4,12},{8,0},{12,4},{1,9},{5,13},{9,1},{13,5},{2,10},{6,14},... | collective-permute-start | bytes 73736 | tf_op jit(solution)/shard_map/ppermute | solution.py:453
  43.6 2.6 %collective-permute-done.13.far_ref = bf16[96,768]{1,0:T(8,128)(2,1)S(1)} collective-permute-done((bf16[96,768]{1,0:T(8,128)(2,1)S(1)}, bf16[96,768]{1,0:T(8,128)(2,1)S(1)}, u32[]{:S(2)}, u32[]{:S(2)}) %collective-permute-start.13) | collective-permute-done | bytes 147488 | tf_op jit(solution)/shard_map/ppermute | solution.py:453
  46.1 1.2 %shard_map.100._ = f32[2,192,768]{2,1,0:T(8,128)} custom-call(bf16[96,768]{1,0:T(8,128)(2,1)S(1)} %add_convert_fusion.near_ref, bf16[96,768]{1,0:T(8,128)(2,1)S(1)} %collective-permute-done.13.far_ref), custom_call_target="tpu_custom_call" | custom-call | flops 1048576 | bytes 2097152 | tf_op jit(solution)/shard_map/pallas_call | solution.py:612
  47.3 1.6 %shard_map.101 = (f32[2,192,768]{2,1,0:T(8,128)}, f32[5,2,192]{2,1,0:T(2,128)}, f32[4,192]{1,0:T(4,128)}) custom-call(bf16[128,768]{1,0:T(8,128)(2,1)S(1)} %get-tuple-element.63.st_ref, bf16[64,192]{1,0:T(8,128)(2,1)S(1)} %add_convert_fusion.2.sa_ref, bf16[64,192]{1,0:T(8,128)(2,1)S(1)} %collective-permute-done.11.sb_ref, ...), custom_call_target="tpu_custom_call", output_to_operand_aliasing={{0}: (3, {})} | custom-call | flops 16777216 | bytes 2097152 | tf_op jit(solution)/shard_map/pallas_call | solution.py:621
  (11 shorter events, 0.1 us)
Async XLA Ops:
  0.6 12.3 %copy-start = (s32[2]{0:T(128)S(1)}, s32[2]{0:T(128)}, u32[]{:S(2)}) copy-start(s32[2]{0:T(128)} %dils.5) | copy-start | bytes 28
  1.7 11.1 %collective-permute-start.1 = (bf16[208,768]{1,0:T(8,128)(2,1)S(1)}, bf16[208,768]{1,0:T(8,128)(2,1)S(1)}, u32[]{:S(2)}, u32[]{:S(2)}) collective-permute-start(bf16[208,768]{1,0:T(8,128)(2,1)S(1)} %get-tuple-element.56.refs_0_), channel_id=1, source_target_pairs={{0,2},{1,3},{2,0},{3,1},{4,6},{5,7},{6,4},{7,5},{8,10},{9,11},{10,... | collective-permute-start | bytes 958472 | tf_op jit(solution)/shard_map/ppermute | solution.py:453
  4.7 5.8 %collective-permute-start.4 = (s32[1,768]{1,0:T(1,128)S(1)}, s32[1,768]{1,0:T(1,128)S(1)}, u32[]{:S(2)}, u32[]{:S(2)}) collective-permute-start(s32[1,768]{1,0:T(1,128)S(1)} %get-tuple-element.57), channel_id=1, source_target_pairs={{0,12},{4,8},{8,4},{12,0},{1,13},{5,9},{9,5},{13,1},{2,14},{6,10},... | collective-permute-start | bytes 9224 | tf_op jit(solution)/shard_map/ppermute | solution.py:453
  8.3 4.5 %collective-permute-start.3 = (s32[1,768]{1,0:T(1,128)S(1)}, s32[1,768]{1,0:T(1,128)S(1)}, u32[]{:S(2)}, u32[]{:S(2)}) collective-permute-start(s32[1,768]{1,0:T(1,128)S(1)} %get-tuple-element.57), channel_id=1, source_target_pairs={{0,8},{4,12},{8,0},{12,4},{1,9},{5,13},{9,1},{13,5},{2,10},{6,14},... | collective-permute-start | bytes 9224 | tf_op jit(solution)/shard_map/ppermute | solution.py:453
  8.3 4.5 %collective-permute-start.2 = (s32[1,768]{1,0:T(1,128)S(1)}, s32[1,768]{1,0:T(1,128)S(1)}, u32[]{:S(2)}, u32[]{:S(2)}) collective-permute-start(s32[1,768]{1,0:T(1,128)S(1)} %get-tuple-element.57), channel_id=1, source_target_pairs={{0,4},{4,0},{8,12},{12,8},{1,5},{5,1},{9,13},{13,9},{2,6},{6,2},{1... | collective-permute-start | bytes 9224 | tf_op jit(solution)/shard_map/ppermute | solution.py:453
  9.1 5.0 %collective-permute-start = (bf16[208,768]{1,0:T(8,128)(2,1)S(1)}, bf16[208,768]{1,0:T(8,128)(2,1)S(1)}, u32[]{:S(2)}, u32[]{:S(2)}) collective-permute-start(bf16[208,768]{1,0:T(8,128)(2,1)S(1)} %get-tuple-element.56.refs_0_), channel_id=1, source_target_pairs={{0,1},{1,0},{2,3},{3,2},{4,5},{5,4},{6,7},{7,6},{8,9},{9,8},{10,11... | collective-permute-start | bytes 958472 | tf_op jit(solution)/shard_map/ppermute | solution.py:453
  12.8 1.7 %collective-permute-start.5 = (bf16[208,768]{1,0:T(8,128)(2,1)S(1)}, bf16[208,768]{1,0:T(8,128)(2,1)S(1)}, u32[]{:S(2)}, u32[]{:S(2)}) collective-permute-start(bf16[208,768]{1,0:T(8,128)(2,1)S(1)} %collective-permute-done.1.refs_2_), channel_id=1, source_target_pairs={{0,1},{1,0},{2,3},{3,2},{4,5},{5,4},{6,7},{7,6},{8,9},{9,8},{10,11... | collective-permute-start | bytes 958472 | tf_op jit(solution)/shard_map/ppermute | solution.py:453
  22.7 7.7 %collective-permute-start.6 = (bf16[96,768]{1,0:T(8,128)(2,1)S(1)}, bf16[96,768]{1,0:T(8,128)(2,1)S(1)}, u32[]{:S(2)}, u32[]{:S(2)}) collective-permute-start(bf16[96,768]{1,0:T(8,128)(2,1)S(1)} %get-tuple-element.96), channel_id=1, source_target_pairs={{0,4},{4,0},{8,12},{12,8},{1,5},{5,1},{9,13},{13,9},{2,6},{6,2},{1... | collective-permute-start | bytes 442376 | tf_op jit(solution)/shard_map/ppermute | solution.py:453
  30.5 9.8 %collective-permute-start.12 = (bf16[96,768]{1,0:T(8,128)(2,1)S(1)}, bf16[96,768]{1,0:T(8,128)(2,1)S(1)}, u32[]{:S(2)}, u32[]{:S(2)}) collective-permute-start(bf16[96,768]{1,0:T(8,128)(2,1)S(1)} %add_convert_fusion.1), channel_id=1, source_target_pairs={{0,8},{4,12},{8,0},{12,4},{1,9},{5,13},{9,1},{13,5},{2,10},{6,14},... | collective-permute-start | bytes 442376 | tf_op jit(solution)/shard_map/ppermute | solution.py:453
  34.9 1.4 %collective-permute-start.7 = (f32[2,64,192]{2,1,0:T(8,128)S(1)}, f32[2,64,192]{2,1,0:T(8,128)S(1)}, u32[]{:S(2)}, u32[]{:S(2)}) collective-permute-start(f32[2,64,192]{2,1,0:T(8,128)S(1)} %get-tuple-element.102), channel_id=1, source_target_pairs={{0,1},{1,0},{2,3},{3,2},{4,5},{5,4},{6,7},{7,6},{8,9},{9,8},{10,11... | collective-permute-start | bytes 294920 | tf_op jit(solution)/shard_map/ppermute | solution.py:453
  36.3 5.9 %collective-permute-start.10 = (bf16[64,192]{1,0:T(8,128)(2,1)S(1)}, bf16[64,192]{1,0:T(8,128)(2,1)S(1)}, u32[]{:S(2)}, u32[]{:S(2)}) collective-permute-start(bf16[64,192]{1,0:T(8,128)(2,1)S(1)} %get-tuple-element.104), channel_id=1, source_target_pairs={{0,6},{1,7},{2,4},{3,5},{4,2},{5,3},{6,0},{7,1},{8,14},{9,15},{10,... | collective-permute-start | bytes 73736 | tf_op jit(solution)/shard_map/ppermute | solution.py:603
  37.7 4.5 %collective-permute-start.8 = (bf16[64,192]{1,0:T(8,128)(2,1)S(1)}, bf16[64,192]{1,0:T(8,128)(2,1)S(1)}, u32[]{:S(2)}, u32[]{:S(2)}) collective-permute-start(bf16[64,192]{1,0:T(8,128)(2,1)S(1)} %get-tuple-element.104), channel_id=1, source_target_pairs={{0,2},{1,3},{2,0},{3,1},{4,6},{5,7},{6,4},{7,5},{8,10},{9,11},{10,... | collective-permute-start | bytes 73736 | tf_op jit(solution)/shard_map/ppermute | solution.py:453
  38.2 3.9 %collective-permute-start.9 = (bf16[64,192]{1,0:T(8,128)(2,1)S(1)}, bf16[64,192]{1,0:T(8,128)(2,1)S(1)}, u32[]{:S(2)}, u32[]{:S(2)}) collective-permute-start(bf16[64,192]{1,0:T(8,128)(2,1)S(1)} %get-tuple-element.103), channel_id=1, source_target_pairs={{0,4},{4,0},{8,12},{12,8},{1,5},{5,1},{9,13},{13,9},{2,6},{6,2},{1... | collective-permute-start | bytes 73736 | tf_op jit(solution)/shard_map/ppermute | solution.py:453
  40.3 5.8 %collective-permute-start.13 = (bf16[96,768]{1,0:T(8,128)(2,1)S(1)}, bf16[96,768]{1,0:T(8,128)(2,1)S(1)}, u32[]{:S(2)}, u32[]{:S(2)}) collective-permute-start(bf16[96,768]{1,0:T(8,128)(2,1)S(1)} %add_convert_fusion.near_ref), channel_id=1, source_target_pairs={{0,4},{4,0},{8,12},{12,8},{1,5},{5,1},{9,13},{13,9},{2,6},{6,2},{1... | collective-permute-start | bytes 442376 | tf_op jit(solution)/shard_map/ppermute | solution.py:453
  42.2 5.1 %collective-permute-start.11 = (bf16[64,192]{1,0:T(8,128)(2,1)S(1)}, bf16[64,192]{1,0:T(8,128)(2,1)S(1)}, u32[]{:S(2)}, u32[]{:S(2)}) collective-permute-start(bf16[64,192]{1,0:T(8,128)(2,1)S(1)} %add_convert_fusion.2.sa_ref), channel_id=1, source_target_pairs={{0,8},{4,12},{8,0},{12,4},{1,9},{5,13},{9,1},{13,5},{2,10},{6,14},... | collective-permute-start | bytes 73736 | tf_op jit(solution)/shard_map/ppermute | solution.py:453

commit v12 on v11

--- a/solution.py
+++ b/solution.py
@@ -395,29 +395,31 @@
     second_ref[...] = (a_ref[1] + b_ref[1]).astype(BF)
 
 
-def mix1_kernel(n_chan, width, near_ref, far_ref, out_ref, held, sem):
+def finish_kernel(
+    n_chan, width, st_ref, sa_ref, sb_ref, near_ref, far_ref, gm_ref, gt_ref, ge_ref, held, sems
+):
     me, odd = lax.axis_index("chan"), lax.axis_index("seq") % 2
     half = width // 2
-    for source, first in ((near_ref, odd * half), (far_ref, (1 - odd) * half)):
+    copies = []
+
+    def send(block, part):
+        copies.append(pltpu.make_async_copy(held.at[block, part], gm_ref.at[block, part], sems.at[len(copies)]))
+        copies[-1].start()
+
+    for source, turn in ((near_ref, odd), (far_ref, 1 - odd)):
+        lines = pl.ds(pl.multiple_of(turn * half, half), half)
         blocks = [source[:, k * width : (k + 1) * width].astype(F32) for k in range(n_chan)]
         for k, part in enumerate(xor_blocks(blocks, me)):
-            held[pl.ds(pl.multiple_of(first, half), half), k * width : (k + 1) * width] = part
-    copy = pltpu.make_async_copy(held, out_ref.at[1], sem)
-    copy.start()
-    copy.wait()
-
-
-def finish_kernel(n_chan, width, st_ref, sa_ref, sb_ref, _, gm_ref, gt_ref, ge_ref, held, sems):
+            held[1, lines, k * width : (k + 1) * width] = part
+        send(1, lines)
+
     sums = sa_ref[...].astype(F32) + sb_ref[...].astype(F32)
     fill = jnp.zeros((JB - ROW_GE, width), F32)
     dw = jnp.concatenate([sums[:ROW_GE], fill, sums[ROW_R : ROW_R + ROW_GE], fill], axis=0).astype(BF)
-    copies = []
-    step = 2 * LANE
-    for i in range(n_chan * width // step):
-        lanes = pl.ds(i * step, step)
-        held[:, lanes] = t_dot(dw, st_ref[: 2 * JB, lanes])
-        copies.append(pltpu.make_async_copy(held.at[:, lanes], gm_ref.at[0, :, lanes], sems.at[i]))
-        copies[-1].start()
+    for i in range(2):
+        lines = slice(i * half, (i + 1) * half)
+        held[0, lines, :] = t_dot(dw[:, lines], st_ref[: 2 * JB, :])
+        send(0, pl.ds(i * half, half))
     for j in range(TAPS):
         gt_ref[j, 0:1, :] = sums[ROW_GT0 + j : ROW_GT0 + j + 1]
         gt_ref[j, 1:2, :] = sums[ROW_GT1 + j : ROW_GT1 + j + 1]
@@ -435,7 +437,7 @@
     return pltpu.with_memory_space_constraint(x, pltpu.HBM)
 
 
-def call(kernel, in_specs, out_shape, out_specs, scratch, limit, cost, aliases=None):
+def call(kernel, in_specs, out_shape, out_specs, scratch, limit, cost):
     flops, moved = cost
     return pl.pallas_call(
         kernel,
@@ -443,7 +445,6 @@
         in_specs=in_specs,
         out_specs=out_specs,
         scratch_shapes=scratch,
-        input_output_aliases=aliases or {},
         compiler_params=pltpu.CompilerParams(vmem_limit_bytes=limit << 20),
         cost_estimate=pl.CostEstimate(flops=flops, bytes_accessed=moved, transcendentals=0),
     )
@@ -608,30 +609,19 @@
         if bit < seq_bits - 1:
             s_mine = rounded_sum(s_mine, s_other)
 
-    big = pltpu.VMEM((width, chans), F32)
-    (grad_mix,) = call(
-        functools.partial(mix1_kernel, n_chan, width),
-        [VMEM, VMEM],
-        [shape((BLOCKS, width, chans), F32)],
-        [HBM],
-        [big, pltpu.SemaphoreType.DMA],
-        16,
-        (1 << 20, 1 << 21),
-    )(g_mine, g_other)
     grad_mix, grad_taps, grad_embed = call(
         functools.partial(finish_kernel, n_chan, width),
-        [VMEM, VMEM, VMEM, HBM],
+        [VMEM] * 5,
         [
             shape((BLOCKS, width, chans), F32),
             shape((TAPS, BLOCKS, width), F32),
             shape((BASES, width), F32),
         ],
         [HBM, VMEM, VMEM],
-        [big, pltpu.SemaphoreType.DMA((chans // (2 * LANE),))],
+        [pltpu.VMEM((BLOCKS, width, chans), F32), pltpu.SemaphoreType.DMA((4,))],
         16,
         (1 << 24, 1 << 21),
-        {3: 0},
-    )(stack, s_mine, s_other, grad_mix)
+    )(stack, s_mine, s_other, g_mine, g_other)
     return x2.T, jnp.swapaxes(grad_mix, 1, 2), jnp.swapaxes(grad_taps, 0, 1), grad_embed
 
 

time: 49.1 us -> 48.7 us (level)
  Pallas kernels: 22.9 us -> 21.3 us
  waiting for transfers between devices: 8.78 us -> 9.74 us
    ppermute x13, waiting for transfers between devices: 8.78 us -> 9.73 us  [flip_bits(): lax.ppermute(x, axis, [(i, i ^ mask) for i in range(lax.axis_size(axis))])]
    pallas_call x2 -> x1, Pallas kernels: 2.85 us -> 2.03 us  [body(): call(functools.partial(finish_kernel, n_chan, width), [VMEM] * 5, [shape(...]
    pallas_call x1, Pallas kernels: 6.47 us -> 5.96 us  [body(): call(functools.partial(backward_kernel, n_chan, rows, width, scale), [SME...]
  transfers between devices with their start and end apart: 14 -> 14, of which waited for: 6 -> 6; matrix products, arithmetic and copies ran while one was open for 0% -> 0% of each run, Pallas kernels for 24% -> 21%
where the time goes in v12:
time: 48.7 us; the launch traced here: 48.4 us
  Pallas kernels  21.3 us (44%)
  starting transfers between devices  16.4 us (34%)
  waiting for transfers between devices  9.74 us (20%)
  between operations  0.77 us (2%)
    ppermute x13, starting transfers between devices, flip_bits(): lax.ppermute(x, axis, [(i, i ^ mask) for i in range(lax.axis_size(axis))])  15 us
    ppermute x13, waiting for transfers between devices, flip_bits(): lax.ppermute(x, axis, [(i, i ^ mask) for i in range(lax.axis_size(axis))])  9.73 us
    pallas_call x1, Pallas kernels, body(): call(functools.partial(forward_kernel, n_chan, rows, width, scale), [SMEM...  7.96 us
    pallas_call x1, Pallas kernels, body(): call(functools.partial(backward_kernel, n_chan, rows, width, scale), [SME...  5.96 us
    pallas_call x1, Pallas kernels, body(): call(functools.partial(finish_kernel, n_chan, width), [VMEM] * 5, [shape(...  2.03 us
    pallas_call x1, Pallas kernels, body(): call(functools.partial(collect_kernel, n_chan, width, scale), [VMEM] * (n...  1.73 us
    ppermute x1, starting transfers between devices, body(): corner = lax.ppermute(s_mine[1], ('seq', 'chan'), pairs)  1.46 us
    pallas_call x1, Pallas kernels, body(): call(functools.partial(local_kernel, n_chan, width), [HBM, HBM], [shape((...  1.44 us
  transfers between devices with their start and end apart: 14, of which 6 were waited for; matrix products, arithmetic and copies ran while one was open for 0% of the time, Pallas kernels for 21%

profile of v12, /device:TPU:0, one launch (start us, length us, event | category | flops | bytes accessed | tf_op | source)
XLA Modules:
  0.0 48.4 jit_solution(12541275288816383190)
XLA Ops:
  0.6 1.1 %shard_map.93 = (bf16[208,768]{1,0:T(8,128)(2,1)S(1)}, s32[1,768]{1,0:T(1,128)S(1)}) custom-call(bf16[2,192,768]{2,1,0:T(8,128)(2,1)} %bitcast.6, bf16[4,192]{1,0:T(4,128)(2,1)} %embed_ref.1, bf16[5,2,192]{2,1,0:T(2,128)(2,1)} %bitcast.9, s32[768]{0:T(1024)} %tok_ref.1), custom_call_target="tpu_custom_call" | custom-call | bytes 589824 | tf_op jit(solution)/shard_map/pallas_call | solution.py:470
  1.7 3.0 %collective-permute-start.1 = (bf16[208,768]{1,0:T(8,128)(2,1)S(1)}, bf16[208,768]{1,0:T(8,128)(2,1)S(1)}, u32[]{:S(2)}, u32[]{:S(2)}) collective-permute-start(bf16[208,768]{1,0:T(8,128)(2,1)S(1)} %get-tuple-element.56.refs_0_), channel_id=1, source_target_pairs={{0,2},{1,3},{2,0},{3,1},{4,6},{5,7},{6,4},{7,5},{8,10},{9,11},{10,... | collective-permute-start | bytes 958472 | tf_op jit(solution)/shard_map/ppermute | solution.py:454
  4.7 3.6 %collective-permute-start.4 = (s32[1,768]{1,0:T(1,128)S(1)}, s32[1,768]{1,0:T(1,128)S(1)}, u32[]{:S(2)}, u32[]{:S(2)}) collective-permute-start(s32[1,768]{1,0:T(1,128)S(1)} %get-tuple-element.57), channel_id=1, source_target_pairs={{0,12},{4,8},{8,4},{12,0},{1,13},{5,9},{9,5},{13,1},{2,14},{6,10},... | collective-permute-start | bytes 9224 | tf_op jit(solution)/shard_map/ppermute | solution.py:454
  8.3 0.0 collective-permute-start.3
  8.3 0.8 %collective-permute-start.2 = (s32[1,768]{1,0:T(1,128)S(1)}, s32[1,768]{1,0:T(1,128)S(1)}, u32[]{:S(2)}, u32[]{:S(2)}) collective-permute-start(s32[1,768]{1,0:T(1,128)S(1)} %get-tuple-element.57), channel_id=1, source_target_pairs={{0,4},{4,0},{8,12},{12,8},{1,5},{5,1},{9,13},{13,9},{2,6},{6,2},{1... | collective-permute-start | bytes 9224 | tf_op jit(solution)/shard_map/ppermute | solution.py:454
  9.1 0.0 collective-permute-start
  9.1 1.4 %shard_map.94 = (bf16[192,768]{1,0:T(8,128)(2,1)S(1)}, bf16[768,192]{1,0:T(8,128)(2,1)S(1)}) custom-call(bf16[2,192,768]{2,1,0:T(8,128)(2,1)} %bitcast.7, bf16[192,768]{1,0:T(8,128)(2,1)} %bitcast.8), custom_call_target="tpu_custom_call" | custom-call | flops 1048576 | bytes 1048576 | tf_op jit(solution)/shard_map/pallas_call | solution.py:489
  10.5 0.0 collective-permute-done.4
  10.6 2.2 %collective-permute-done.3 = s32[1,768]{1,0:T(1,128)S(1)} collective-permute-done((s32[1,768]{1,0:T(1,128)S(1)}, s32[1,768]{1,0:T(1,128)S(1)}, u32[]{:S(2)}, u32[]{:S(2)}) %collective-permute-start.3) | collective-permute-done | bytes 3104 | tf_op jit(solution)/shard_map/ppermute | solution.py:454
  12.8 0.0 collective-permute-done.2
  12.8 0.0 collective-permute-done.1.refs_2_
  12.8 0.1 collective-permute-start.5
  12.9 1.1 %shard_map.95 = (bf16[896,128]{1,0:T(8,128)(2,1)S(1)}, bf16[64,896]{1,0:T(8,128)(2,1)S(1)}, bf16[64,768]{1,0:T(8,128)(2,1)S(1)}) custom-call(s32[2]{0:T(128)S(1)} %copy-done, s32[4,768]{1,0:T(4,128)S(1)} %pad_add_fusion.tok_ref), custom_call_target="tpu_custom_call" | custom-call | flops 1048576 | bytes 1048576 | tf_op jit(solution)/shard_map/pallas_call | solution.py:509
  14.1 0.0 collective-permute-done.refs_1_
  14.1 0.4 collective-permute-done.5.refs_3_
  14.5 8.0 %shard_map.96 = (bf16[192,768]{1,0:T(8,128)(2,1)}, bf16[96,768]{1,0:T(8,128)(2,1)S(1)}, bf16[96,768]{1,0:T(8,128)(2,1)S(1)}, bf16[768,192]{1,0:T(8,128)(2,1)S(1)...) custom-call(s32[2]{0:T(128)S(1)} %copy-done, ...), custom_call_target="tpu_custom_call" | custom-call | flops 3221225472 | bytes 8388608 | tf_op jit(solution)/shard_map/pallas_call | solution.py:520
  22.5 1.2 %collective-permute-start.6 = (bf16[96,768]{1,0:T(8,128)(2,1)S(1)}, bf16[96,768]{1,0:T(8,128)(2,1)S(1)}, u32[]{:S(2)}, u32[]{:S(2)}) collective-permute-start(bf16[96,768]{1,0:T(8,128)(2,1)S(1)} %get-tuple-element.96), channel_id=1, source_target_pairs={{0,4},{4,0},{8,12},{12,8},{1,5},{5,1},{9,13},{13,9},{2,6},{6,2},{1... | collective-permute-start | bytes 442376 | tf_op jit(solution)/shard_map/ppermute | solution.py:454
  23.7 6.0 %shard_map.97 = (bf16[768,768]{1,0:T(8,128)(2,1)S(1)}, f32[2,8,768]{2,1,0:T(8,128)S(1)}, f32[64,768]{1,0:T(8,128)S(1)}, f32[64,768]{1,0:T(8,128)S(1)}) custom-call(s32[2]{0:T(128)S(1)} %copy-done, bf16[64,896]{1,0:T(8,128)(2,1)S(1)} %get-tuple-element.67.refs_0_, bf16[192,768]{1,0:T(8,128)(2,1)S(1)} %get-tuple-element.58.refs_5_.refs_1_, ...), custom_call_target="tpu_custom_call" | custom-call | flops 3221225472 | bytes 8388608 | tf_op jit(solution)/shard_map/pallas_call | solution.py:546
  29.7 2.6 %collective-permute-start.12 = (bf16[96,768]{1,0:T(8,128)(2,1)S(1)}, bf16[96,768]{1,0:T(8,128)(2,1)S(1)}, u32[]{:S(2)}, u32[]{:S(2)}) collective-permute-start(bf16[96,768]{1,0:T(8,128)(2,1)S(1)} %add_convert_fusion.1), channel_id=1, source_target_pairs={{0,8},{4,12},{8,0},{12,4},{1,9},{5,13},{9,1},{13,5},{2,10},{6,14},... | collective-permute-start | bytes 442376 | tf_op jit(solution)/shard_map/ppermute | solution.py:454
  32.4 1.7 %shard_map.98 = (f32[2,64,192]{2,1,0:T(8,128)S(1)}, f32[2,64,192]{2,1,0:T(8,128)S(1)}) custom-call(bf16[208,768]{1,0:T(8,128)(2,1)S(1)} %get-tuple-element.56.refs_0_, bf16[208,768]{1,0:T(8,128)(2,1)S(1)} %collective-permute-done.refs_1_, bf16[208,768]{1,0:T(8,128)(2,1)S(1)} %collective-permute-done.1.refs_2_, ...), custom_call_target="tpu_custom_call" | custom-call | flops 1048576 | bytes 65536 | tf_op jit(solution)/shard_map/pallas_call | solution.py:568
  34.1 0.0 collective-permute-start.7
  34.2 1.3 %collective-permute-done.7.b_ref = f32[2,64,192]{2,1,0:T(8,128)S(1)} collective-permute-done((f32[2,64,192]{2,1,0:T(8,128)S(1)}, f32[2,64,192]{2,1,0:T(8,128)S(1)}, u32[]{:S(2)}, u32[]{:S(2)}) %collective-permute-start.7) | collective-permute-done | bytes 98336 | tf_op jit(solution)/shard_map/ppermute | solution.py:454
  35.5 1.5 %collective-permute-start.10 = (bf16[64,192]{1,0:T(8,128)(2,1)S(1)}, bf16[64,192]{1,0:T(8,128)(2,1)S(1)}, u32[]{:S(2)}, u32[]{:S(2)}) collective-permute-start(bf16[64,192]{1,0:T(8,128)(2,1)S(1)} %get-tuple-element.104), channel_id=1, source_target_pairs={{0,6},{1,7},{2,4},{3,5},{4,2},{5,3},{6,0},{7,1},{8,14},{9,15},{10,... | collective-permute-start | bytes 73736 | tf_op jit(solution)/shard_map/ppermute | solution.py:604
  37.0 0.5 %collective-permute-start.8 = (bf16[64,192]{1,0:T(8,128)(2,1)S(1)}, bf16[64,192]{1,0:T(8,128)(2,1)S(1)}, u32[]{:S(2)}, u32[]{:S(2)}) collective-permute-start(bf16[64,192]{1,0:T(8,128)(2,1)S(1)} %get-tuple-element.104), channel_id=1, source_target_pairs={{0,2},{1,3},{2,0},{3,1},{4,6},{5,7},{6,4},{7,5},{8,10},{9,11},{10,... | collective-permute-start | bytes 73736 | tf_op jit(solution)/shard_map/ppermute | solution.py:454
  37.5 1.6 %collective-permute-start.9 = (bf16[64,192]{1,0:T(8,128)(2,1)S(1)}, bf16[64,192]{1,0:T(8,128)(2,1)S(1)}, u32[]{:S(2)}, u32[]{:S(2)}) collective-permute-start(bf16[64,192]{1,0:T(8,128)(2,1)S(1)} %get-tuple-element.103), channel_id=1, source_target_pairs={{0,4},{4,0},{8,12},{12,8},{1,5},{5,1},{9,13},{13,9},{2,6},{6,2},{1... | collective-permute-start | bytes 73736 | tf_op jit(solution)/shard_map/ppermute | solution.py:454
  39.1 0.4 collective-permute-done.12
  39.5 0.1 collective-permute-start.13
  39.6 1.8 %collective-permute-done.9 = bf16[64,192]{1,0:T(8,128)(2,1)S(1)} collective-permute-done((bf16[64,192]{1,0:T(8,128)(2,1)S(1)}, bf16[64,192]{1,0:T(8,128)(2,1)S(1)}, u32[]{:S(2)}, u32[]{:S(2)}) %collective-permute-start.9) | collective-permute-done | bytes 24608 | tf_op jit(solution)/shard_map/ppermute | solution.py:454
  41.4 0.0 collective-permute-done.10
  41.5 1.4 %collective-permute-start.11 = (bf16[64,192]{1,0:T(8,128)(2,1)S(1)}, bf16[64,192]{1,0:T(8,128)(2,1)S(1)}, u32[]{:S(2)}, u32[]{:S(2)}) collective-permute-start(bf16[64,192]{1,0:T(8,128)(2,1)S(1)} %add_convert_fusion.2.sa_ref), channel_id=1, source_target_pairs={{0,8},{4,12},{8,0},{12,4},{1,9},{5,13},{9,1},{13,5},{2,10},{6,14},... | collective-permute-start | bytes 73736 | tf_op jit(solution)/shard_map/ppermute | solution.py:454
  42.8 3.5 %collective-permute-done.11.sb_ref = bf16[64,192]{1,0:T(8,128)(2,1)S(1)} collective-permute-done((bf16[64,192]{1,0:T(8,128)(2,1)S(1)}, bf16[64,192]{1,0:T(8,128)(2,1)S(1)}, u32[]{:S(2)}, u32[]{:S(2)}) %collective-permute-start.11) | collective-permute-done | bytes 24608 | tf_op jit(solution)/shard_map/ppermute | solution.py:454
  46.3 2.0 %shard_map.100 = (f32[2,192,768]{2,1,0:T(8,128)}, f32[5,2,192]{2,1,0:T(2,128)}, f32[4,192]{1,0:T(4,128)}) custom-call(bf16[128,768]{1,0:T(8,128)(2,1)S(1)} %get-tuple-element.63.st_ref, bf16[64,192]{1,0:T(8,128)(2,1)S(1)} %add_convert_fusion.2.sa_ref, bf16[64,192]{1,0:T(8,128)(2,1)S(1)} %collective-permute-done.11.sb_ref, ...), custom_call_target="tpu_custom_call" | custom-call | flops 16777216 | bytes 2097152 | tf_op jit(solution)/shard_map/pallas_call | solution.py:612
  (10 shorter events, 0.1 us)
Async XLA Ops:
  0.6 12.3 %copy-start = (s32[2]{0:T(128)S(1)}, s32[2]{0:T(128)}, u32[]{:S(2)}) copy-start(s32[2]{0:T(128)} %dils.5) | copy-start | bytes 28
  1.7 11.1 %collective-permute-start.1 = (bf16[208,768]{1,0:T(8,128)(2,1)S(1)}, bf16[208,768]{1,0:T(8,128)(2,1)S(1)}, u32[]{:S(2)}, u32[]{:S(2)}) collective-permute-start(bf16[208,768]{1,0:T(8,128)(2,1)S(1)} %get-tuple-element.56.refs_0_), channel_id=1, source_target_pairs={{0,2},{1,3},{2,0},{3,1},{4,6},{5,7},{6,4},{7,5},{8,10},{9,11},{10,... | collective-permute-start | bytes 958472 | tf_op jit(solution)/shard_map/ppermute | solution.py:454
  4.7 5.8 %collective-permute-start.4 = (s32[1,768]{1,0:T(1,128)S(1)}, s32[1,768]{1,0:T(1,128)S(1)}, u32[]{:S(2)}, u32[]{:S(2)}) collective-permute-start(s32[1,768]{1,0:T(1,128)S(1)} %get-tuple-element.57), channel_id=1, source_target_pairs={{0,12},{4,8},{8,4},{12,0},{1,13},{5,9},{9,5},{13,1},{2,14},{6,10},... | collective-permute-start | bytes 9224 | tf_op jit(solution)/shard_map/ppermute | solution.py:454
  8.3 4.5 %collective-permute-start.3 = (s32[1,768]{1,0:T(1,128)S(1)}, s32[1,768]{1,0:T(1,128)S(1)}, u32[]{:S(2)}, u32[]{:S(2)}) collective-permute-start(s32[1,768]{1,0:T(1,128)S(1)} %get-tuple-element.57), channel_id=1, source_target_pairs={{0,8},{4,12},{8,0},{12,4},{1,9},{5,13},{9,1},{13,5},{2,10},{6,14},... | collective-permute-start | bytes 9224 | tf_op jit(solution)/shard_map/ppermute | solution.py:454
  8.3 4.5 %collective-permute-start.2 = (s32[1,768]{1,0:T(1,128)S(1)}, s32[1,768]{1,0:T(1,128)S(1)}, u32[]{:S(2)}, u32[]{:S(2)}) collective-permute-start(s32[1,768]{1,0:T(1,128)S(1)} %get-tuple-element.57), channel_id=1, source_target_pairs={{0,4},{4,0},{8,12},{12,8},{1,5},{5,1},{9,13},{13,9},{2,6},{6,2},{1... | collective-permute-start | bytes 9224 | tf_op jit(solution)/shard_map/ppermute | solution.py:454
  9.1 5.0 %collective-permute-start = (bf16[208,768]{1,0:T(8,128)(2,1)S(1)}, bf16[208,768]{1,0:T(8,128)(2,1)S(1)}, u32[]{:S(2)}, u32[]{:S(2)}) collective-permute-start(bf16[208,768]{1,0:T(8,128)(2,1)S(1)} %get-tuple-element.56.refs_0_), channel_id=1, source_target_pairs={{0,1},{1,0},{2,3},{3,2},{4,5},{5,4},{6,7},{7,6},{8,9},{9,8},{10,11... | collective-permute-start | bytes 958472 | tf_op jit(solution)/shard_map/ppermute | solution.py:454
  12.8 1.7 %collective-permute-start.5 = (bf16[208,768]{1,0:T(8,128)(2,1)S(1)}, bf16[208,768]{1,0:T(8,128)(2,1)S(1)}, u32[]{:S(2)}, u32[]{:S(2)}) collective-permute-start(bf16[208,768]{1,0:T(8,128)(2,1)S(1)} %collective-permute-done.1.refs_2_), channel_id=1, source_target_pairs={{0,1},{1,0},{2,3},{3,2},{4,5},{5,4},{6,7},{7,6},{8,9},{9,8},{10,11... | collective-permute-start | bytes 958472 | tf_op jit(solution)/shard_map/ppermute | solution.py:454
  22.5 7.2 %collective-permute-start.6 = (bf16[96,768]{1,0:T(8,128)(2,1)S(1)}, bf16[96,768]{1,0:T(8,128)(2,1)S(1)}, u32[]{:S(2)}, u32[]{:S(2)}) collective-permute-start(bf16[96,768]{1,0:T(8,128)(2,1)S(1)} %get-tuple-element.96), channel_id=1, source_target_pairs={{0,4},{4,0},{8,12},{12,8},{1,5},{5,1},{9,13},{13,9},{2,6},{6,2},{1... | collective-permute-start | bytes 442376 | tf_op jit(solution)/shard_map/ppermute | solution.py:454
  29.7 9.7 %collective-permute-start.12 = (bf16[96,768]{1,0:T(8,128)(2,1)S(1)}, bf16[96,768]{1,0:T(8,128)(2,1)S(1)}, u32[]{:S(2)}, u32[]{:S(2)}) collective-permute-start(bf16[96,768]{1,0:T(8,128)(2,1)S(1)} %add_convert_fusion.1), channel_id=1, source_target_pairs={{0,8},{4,12},{8,0},{12,4},{1,9},{5,13},{9,1},{13,5},{2,10},{6,14},... | collective-permute-start | bytes 442376 | tf_op jit(solution)/shard_map/ppermute | solution.py:454
  34.1 1.4 %collective-permute-start.7 = (f32[2,64,192]{2,1,0:T(8,128)S(1)}, f32[2,64,192]{2,1,0:T(8,128)S(1)}, u32[]{:S(2)}, u32[]{:S(2)}) collective-permute-start(f32[2,64,192]{2,1,0:T(8,128)S(1)} %get-tuple-element.102), channel_id=1, source_target_pairs={{0,1},{1,0},{2,3},{3,2},{4,5},{5,4},{6,7},{7,6},{8,9},{9,8},{10,11... | collective-permute-start | bytes 294920 | tf_op jit(solution)/shard_map/ppermute | solution.py:454
  35.5 5.9 %collective-permute-start.10 = (bf16[64,192]{1,0:T(8,128)(2,1)S(1)}, bf16[64,192]{1,0:T(8,128)(2,1)S(1)}, u32[]{:S(2)}, u32[]{:S(2)}) collective-permute-start(bf16[64,192]{1,0:T(8,128)(2,1)S(1)} %get-tuple-element.104), channel_id=1, source_target_pairs={{0,6},{1,7},{2,4},{3,5},{4,2},{5,3},{6,0},{7,1},{8,14},{9,15},{10,... | collective-permute-start | bytes 73736 | tf_op jit(solution)/shard_map/ppermute | solution.py:604
  37.0 4.5 %collective-permute-start.8 = (bf16[64,192]{1,0:T(8,128)(2,1)S(1)}, bf16[64,192]{1,0:T(8,128)(2,1)S(1)}, u32[]{:S(2)}, u32[]{:S(2)}) collective-permute-start(bf16[64,192]{1,0:T(8,128)(2,1)S(1)} %get-tuple-element.104), channel_id=1, source_target_pairs={{0,2},{1,3},{2,0},{3,1},{4,6},{5,7},{6,4},{7,5},{8,10},{9,11},{10,... | collective-permute-start | bytes 73736 | tf_op jit(solution)/shard_map/ppermute | solution.py:454
  37.5 3.9 %collective-permute-start.9 = (bf16[64,192]{1,0:T(8,128)(2,1)S(1)}, bf16[64,192]{1,0:T(8,128)(2,1)S(1)}, u32[]{:S(2)}, u32[]{:S(2)}) collective-permute-start(bf16[64,192]{1,0:T(8,128)(2,1)S(1)} %get-tuple-element.103), channel_id=1, source_target_pairs={{0,4},{4,0},{8,12},{12,8},{1,5},{5,1},{9,13},{13,9},{2,6},{6,2},{1... | collective-permute-start | bytes 73736 | tf_op jit(solution)/shard_map/ppermute | solution.py:454
  39.5 6.8 %collective-permute-start.13 = (bf16[96,768]{1,0:T(8,128)(2,1)S(1)}, bf16[96,768]{1,0:T(8,128)(2,1)S(1)}, u32[]{:S(2)}, u32[]{:S(2)}) collective-permute-start(bf16[96,768]{1,0:T(8,128)(2,1)S(1)} %add_convert_fusion.near_ref), channel_id=1, source_target_pairs={{0,4},{4,0},{8,12},{12,8},{1,5},{5,1},{9,13},{13,9},{2,6},{6,2},{1... | collective-permute-start | bytes 442376 | tf_op jit(solution)/shard_map/ppermute | solution.py:454
  41.5 4.9 %collective-permute-start.11 = (bf16[64,192]{1,0:T(8,128)(2,1)S(1)}, bf16[64,192]{1,0:T(8,128)(2,1)S(1)}, u32[]{:S(2)}, u32[]{:S(2)}) collective-permute-start(bf16[64,192]{1,0:T(8,128)(2,1)S(1)} %add_convert_fusion.2.sa_ref), channel_id=1, source_target_pairs={{0,8},{4,12},{8,0},{12,4},{1,9},{5,13},{9,1},{13,5},{2,10},{6,14},... | collective-permute-start | bytes 73736 | tf_op jit(solution)/shard_map/ppermute | solution.py:454

commit v13 on v12

--- a/solution.py
+++ b/solution.py
@@ -597,16 +597,18 @@
         8,
         (0, 0),
     )(mine, theirs)
+    order = sorted(range(seq_bits), key=lambda bit: (bit != 1, bit))
+    jump = 1 << order[0]
     across = flip_bits(s_mine[1], "chan", 1 << last)
-    along = flip_bits(s_mine[0], "seq", 1)
+    along = flip_bits(s_mine[0], "seq", jump)
     places = [(i, j) for i in range(n_seq) for j in range(n_chan)]
-    pairs = [(i * n_chan + j, (i ^ 1) * n_chan + (j ^ (1 << last))) for i, j in places]
+    pairs = [(i * n_chan + j, (i ^ jump) * n_chan + (j ^ (1 << last))) for i, j in places]
     corner = lax.ppermute(s_mine[1], ("seq", "chan"), pairs)
     here, there = (s_mine[0], across), (along, corner)
     s_mine = rounded_sum(*(a.astype(F32) + b.astype(F32) for a, b in (here, there)))
-    for bit in range(1, seq_bits):
+    for bit in order[1:]:
         s_other = flip_bits(s_mine, "seq", 1 << bit)
-        if bit < seq_bits - 1:
+        if bit != order[-1]:
             s_mine = rounded_sum(s_mine, s_other)
 
     grad_mix, grad_taps, grad_embed = call(

time: 48.7 us -> 49.4 us (1.014)
  starting transfers between devices: 16.4 us -> 17 us
    ppermute x13, starting transfers between devices: 15 us -> 15.7 us  [flip_bits(): lax.ppermute(x, axis, [(i, i ^ mask) for i in range(lax.axis_size(axis))])]
  transfers between devices with their start and end apart: 14 -> 14, of which waited for: 6 -> 5; matrix products, arithmetic and copies ran while one was open for 0% -> 0% of each run, Pallas kernels for 21% -> 21%
where the time goes in v13:
time: 49.4 us; the launch traced here: 48.9 us
  Pallas kernels  21.3 us (43%)
  starting transfers between devices  17 us (34%)
  waiting for transfers between devices  9.71 us (20%)
  between operations  0.77 us (2%)
    ppermute x13, starting transfers between devices, flip_bits(): lax.ppermute(x, axis, [(i, i ^ mask) for i in range(lax.axis_size(axis))])  15.7 us
    ppermute x13, waiting for transfers between devices, flip_bits(): lax.ppermute(x, axis, [(i, i ^ mask) for i in range(lax.axis_size(axis))])  9.71 us
    pallas_call x1, Pallas kernels, body(): call(functools.partial(forward_kernel, n_chan, rows, width, scale), [SMEM...  7.96 us
    pallas_call x1, Pallas kernels, body(): call(functools.partial(backward_kernel, n_chan, rows, width, scale), [SME...  5.96 us
    pallas_call x1, Pallas kernels, body(): call(functools.partial(finish_kernel, n_chan, width), [VMEM] * 5, [shape(...  2.04 us
    pallas_call x1, Pallas kernels, body(): call(functools.partial(collect_kernel, n_chan, width, scale), [VMEM] * (n...  1.73 us
    pallas_call x1, Pallas kernels, body(): call(functools.partial(local_kernel, n_chan, width), [HBM, HBM], [shape((...  1.44 us
    ppermute x1, starting transfers between devices, body(): corner = lax.ppermute(s_mine[1], ('seq', 'chan'), pairs)  1.33 us
  transfers between devices with their start and end apart: 14, of which 5 were waited for; matrix products, arithmetic and copies ran while one was open for 0% of the time, Pallas kernels for 21%

profile of v13, /device:TPU:0, one launch (start us, length us, event | category | flops | bytes accessed | tf_op | source)
XLA Modules:
  0.0 48.9 jit_solution(6972519803776811417)
XLA Ops:
  0.6 1.1 %shard_map.93 = (bf16[208,768]{1,0:T(8,128)(2,1)S(1)}, s32[1,768]{1,0:T(1,128)S(1)}) custom-call(bf16[2,192,768]{2,1,0:T(8,128)(2,1)} %bitcast.6, bf16[4,192]{1,0:T(4,128)(2,1)} %embed_ref.1, bf16[5,2,192]{2,1,0:T(2,128)(2,1)} %bitcast.9, s32[768]{0:T(1024)} %tok_ref.1), custom_call_target="tpu_custom_call" | custom-call | bytes 589824 | tf_op jit(solution)/shard_map/pallas_call | solution.py:470
  1.7 3.0 %collective-permute-start.1 = (bf16[208,768]{1,0:T(8,128)(2,1)S(1)}, bf16[208,768]{1,0:T(8,128)(2,1)S(1)}, u32[]{:S(2)}, u32[]{:S(2)}) collective-permute-start(bf16[208,768]{1,0:T(8,128)(2,1)S(1)} %get-tuple-element.56.refs_0_), channel_id=1, source_target_pairs={{0,2},{1,3},{2,0},{3,1},{4,6},{5,7},{6,4},{7,5},{8,10},{9,11},{10,... | collective-permute-start | bytes 958472 | tf_op jit(solution)/shard_map/ppermute | solution.py:454
  4.7 3.6 %collective-permute-start.4 = (s32[1,768]{1,0:T(1,128)S(1)}, s32[1,768]{1,0:T(1,128)S(1)}, u32[]{:S(2)}, u32[]{:S(2)}) collective-permute-start(s32[1,768]{1,0:T(1,128)S(1)} %get-tuple-element.57), channel_id=1, source_target_pairs={{0,12},{4,8},{8,4},{12,0},{1,13},{5,9},{9,5},{13,1},{2,14},{6,10},... | collective-permute-start | bytes 9224 | tf_op jit(solution)/shard_map/ppermute | solution.py:454
  8.3 0.0 collective-permute-start.3
  8.3 0.8 %collective-permute-start.2 = (s32[1,768]{1,0:T(1,128)S(1)}, s32[1,768]{1,0:T(1,128)S(1)}, u32[]{:S(2)}, u32[]{:S(2)}) collective-permute-start(s32[1,768]{1,0:T(1,128)S(1)} %get-tuple-element.57), channel_id=1, source_target_pairs={{0,4},{4,0},{8,12},{12,8},{1,5},{5,1},{9,13},{13,9},{2,6},{6,2},{1... | collective-permute-start | bytes 9224 | tf_op jit(solution)/shard_map/ppermute | solution.py:454
  9.1 0.0 collective-permute-start
  9.1 1.4 %shard_map.94 = (bf16[192,768]{1,0:T(8,128)(2,1)S(1)}, bf16[768,192]{1,0:T(8,128)(2,1)S(1)}) custom-call(bf16[2,192,768]{2,1,0:T(8,128)(2,1)} %bitcast.7, bf16[192,768]{1,0:T(8,128)(2,1)} %bitcast.8), custom_call_target="tpu_custom_call" | custom-call | flops 1048576 | bytes 1048576 | tf_op jit(solution)/shard_map/pallas_call | solution.py:489
  10.5 0.0 collective-permute-done.4
  10.6 2.2 %collective-permute-done.3 = s32[1,768]{1,0:T(1,128)S(1)} collective-permute-done((s32[1,768]{1,0:T(1,128)S(1)}, s32[1,768]{1,0:T(1,128)S(1)}, u32[]{:S(2)}, u32[]{:S(2)}) %collective-permute-start.3) | collective-permute-done | bytes 3104 | tf_op jit(solution)/shard_map/ppermute | solution.py:454
  12.8 0.0 collective-permute-done.2
  12.8 0.0 collective-permute-done.1.refs_2_
  12.8 0.1 collective-permute-start.5
  12.9 1.1 %shard_map.95 = (bf16[896,128]{1,0:T(8,128)(2,1)S(1)}, bf16[64,896]{1,0:T(8,128)(2,1)S(1)}, bf16[64,768]{1,0:T(8,128)(2,1)S(1)}) custom-call(s32[2]{0:T(128)S(1)} %copy-done, s32[4,768]{1,0:T(4,128)S(1)} %pad_add_fusion.tok_ref), custom_call_target="tpu_custom_call" | custom-call | flops 1048576 | bytes 1048576 | tf_op jit(solution)/shard_map/pallas_call | solution.py:509
  14.1 0.4 collective-permute-done.5.refs_3_
  14.5 8.0 %shard_map.96 = (bf16[192,768]{1,0:T(8,128)(2,1)}, bf16[96,768]{1,0:T(8,128)(2,1)S(1)}, bf16[96,768]{1,0:T(8,128)(2,1)S(1)}, bf16[768,192]{1,0:T(8,128)(2,1)S(1)...) custom-call(s32[2]{0:T(128)S(1)} %copy-done, ...), custom_call_target="tpu_custom_call" | custom-call | flops 3221225472 | bytes 8388608 | tf_op jit(solution)/shard_map/pallas_call | solution.py:520
  22.5 1.2 %collective-permute-start.6 = (bf16[96,768]{1,0:T(8,128)(2,1)S(1)}, bf16[96,768]{1,0:T(8,128)(2,1)S(1)}, u32[]{:S(2)}, u32[]{:S(2)}) collective-permute-start(bf16[96,768]{1,0:T(8,128)(2,1)S(1)} %get-tuple-element.96), channel_id=1, source_target_pairs={{0,4},{4,0},{8,12},{12,8},{1,5},{5,1},{9,13},{13,9},{2,6},{6,2},{1... | collective-permute-start | bytes 442376 | tf_op jit(solution)/shard_map/ppermute | solution.py:454
  23.7 6.0 %shard_map.97 = (bf16[768,768]{1,0:T(8,128)(2,1)S(1)}, f32[2,8,768]{2,1,0:T(8,128)S(1)}, f32[64,768]{1,0:T(8,128)S(1)}, f32[64,768]{1,0:T(8,128)S(1)}) custom-call(s32[2]{0:T(128)S(1)} %copy-done, bf16[64,896]{1,0:T(8,128)(2,1)S(1)} %get-tuple-element.67.refs_0_, bf16[192,768]{1,0:T(8,128)(2,1)S(1)} %get-tuple-element.58.refs_5_.refs_1_, ...), custom_call_target="tpu_custom_call" | custom-call | flops 3221225472 | bytes 8388608 | tf_op jit(solution)/shard_map/pallas_call | solution.py:546
  29.7 0.0 collective-permute-done.6
  29.7 2.6 %collective-permute-start.12 = (bf16[96,768]{1,0:T(8,128)(2,1)S(1)}, bf16[96,768]{1,0:T(8,128)(2,1)S(1)}, u32[]{:S(2)}, u32[]{:S(2)}) collective-permute-start(bf16[96,768]{1,0:T(8,128)(2,1)S(1)} %add_convert_fusion.1), channel_id=1, source_target_pairs={{0,8},{4,12},{8,0},{12,4},{1,9},{5,13},{9,1},{13,5},{2,10},{6,14},... | collective-permute-start | bytes 442376 | tf_op jit(solution)/shard_map/ppermute | solution.py:454
  32.4 1.7 %shard_map.98 = (f32[2,64,192]{2,1,0:T(8,128)S(1)}, f32[2,64,192]{2,1,0:T(8,128)S(1)}) custom-call(bf16[208,768]{1,0:T(8,128)(2,1)S(1)} %get-tuple-element.56.refs_0_, bf16[208,768]{1,0:T(8,128)(2,1)S(1)} %collective-permute-done.refs_1_, bf16[208,768]{1,0:T(8,128)(2,1)S(1)} %collective-permute-done.1.refs_2_, ...), custom_call_target="tpu_custom_call" | custom-call | flops 1048576 | bytes 65536 | tf_op jit(solution)/shard_map/pallas_call | solution.py:568
  34.1 0.0 collective-permute-start.7
  34.2 1.3 %collective-permute-done.7.b_ref = f32[2,64,192]{2,1,0:T(8,128)S(1)} collective-permute-done((f32[2,64,192]{2,1,0:T(8,128)S(1)}, f32[2,64,192]{2,1,0:T(8,128)S(1)}, u32[]{:S(2)}, u32[]{:S(2)}) %collective-permute-start.7) | collective-permute-done | bytes 98336 | tf_op jit(solution)/shard_map/ppermute | solution.py:454
  35.5 1.3 %collective-permute-start.10 = (bf16[64,192]{1,0:T(8,128)(2,1)S(1)}, bf16[64,192]{1,0:T(8,128)(2,1)S(1)}, u32[]{:S(2)}, u32[]{:S(2)}) collective-permute-start(bf16[64,192]{1,0:T(8,128)(2,1)S(1)} %get-tuple-element.104), channel_id=1, source_target_pairs={{0,10},{1,11},{2,8},{3,9},{4,14},{5,15},{6,12},{7,13},{8,2},{9,3},... | collective-permute-start | bytes 73736 | tf_op jit(solution)/shard_map/ppermute | solution.py:606
  36.9 0.5 %collective-permute-start.8 = (bf16[64,192]{1,0:T(8,128)(2,1)S(1)}, bf16[64,192]{1,0:T(8,128)(2,1)S(1)}, u32[]{:S(2)}, u32[]{:S(2)}) collective-permute-start(bf16[64,192]{1,0:T(8,128)(2,1)S(1)} %get-tuple-element.104), channel_id=1, source_target_pairs={{0,2},{1,3},{2,0},{3,1},{4,6},{5,7},{6,4},{7,5},{8,10},{9,11},{10,... | collective-permute-start | bytes 73736 | tf_op jit(solution)/shard_map/ppermute | solution.py:454
  37.4 2.6 %collective-permute-start.9 = (bf16[64,192]{1,0:T(8,128)(2,1)S(1)}, bf16[64,192]{1,0:T(8,128)(2,1)S(1)}, u32[]{:S(2)}, u32[]{:S(2)}) collective-permute-start(bf16[64,192]{1,0:T(8,128)(2,1)S(1)} %get-tuple-element.103), channel_id=1, source_target_pairs={{0,8},{4,12},{8,0},{12,4},{1,9},{5,13},{9,1},{13,5},{2,10},{6,14},... | collective-permute-start | bytes 73736 | tf_op jit(solution)/shard_map/ppermute | solution.py:454
  40.0 0.0 collective-permute-done.12
  40.0 0.5 %collective-permute-start.13 = (bf16[96,768]{1,0:T(8,128)(2,1)S(1)}, bf16[96,768]{1,0:T(8,128)(2,1)S(1)}, u32[]{:S(2)}, u32[]{:S(2)}) collective-permute-start(bf16[96,768]{1,0:T(8,128)(2,1)S(1)} %add_convert_fusion.near_ref), channel_id=1, source_target_pairs={{0,4},{4,0},{8,12},{12,8},{1,5},{5,1},{9,13},{13,9},{2,6},{6,2},{1... | collective-permute-start | bytes 442376 | tf_op jit(solution)/shard_map/ppermute | solution.py:454
  40.5 2.3 %collective-permute-done.9 = bf16[64,192]{1,0:T(8,128)(2,1)S(1)} collective-permute-done((bf16[64,192]{1,0:T(8,128)(2,1)S(1)}, bf16[64,192]{1,0:T(8,128)(2,1)S(1)}, u32[]{:S(2)}, u32[]{:S(2)}) %collective-permute-start.9) | collective-permute-done | bytes 24608 | tf_op jit(solution)/shard_map/ppermute | solution.py:454
  42.9 0.6 %collective-permute-start.11 = (bf16[64,192]{1,0:T(8,128)(2,1)S(1)}, bf16[64,192]{1,0:T(8,128)(2,1)S(1)}, u32[]{:S(2)}, u32[]{:S(2)}) collective-permute-start(bf16[64,192]{1,0:T(8,128)(2,1)S(1)} %add_convert_fusion.2.sa_ref), channel_id=1, source_target_pairs={{0,4},{4,0},{8,12},{12,8},{1,5},{5,1},{9,13},{13,9},{2,6},{6,2},{1... | collective-permute-start | bytes 73736 | tf_op jit(solution)/shard_map/ppermute | solution.py:454
  43.5 3.4 %collective-permute-done.11.sb_ref = bf16[64,192]{1,0:T(8,128)(2,1)S(1)} collective-permute-done((bf16[64,192]{1,0:T(8,128)(2,1)S(1)}, bf16[64,192]{1,0:T(8,128)(2,1)S(1)}, u32[]{:S(2)}, u32[]{:S(2)}) %collective-permute-start.11) | collective-permute-done | bytes 24608 | tf_op jit(solution)/shard_map/ppermute | solution.py:454
  46.9 0.0 collective-permute-done.13.far_ref
  46.9 2.0 %shard_map.100 = (f32[2,192,768]{2,1,0:T(8,128)}, f32[5,2,192]{2,1,0:T(2,128)}, f32[4,192]{1,0:T(4,128)}) custom-call(bf16[128,768]{1,0:T(8,128)(2,1)S(1)} %get-tuple-element.63.st_ref, bf16[64,192]{1,0:T(8,128)(2,1)S(1)} %add_convert_fusion.2.sa_ref, bf16[64,192]{1,0:T(8,128)(2,1)S(1)} %collective-permute-done.11.sb_ref, ...), custom_call_target="tpu_custom_call" | custom-call | flops 16777216 | bytes 2097152 | tf_op jit(solution)/shard_map/pallas_call | solution.py:614
  (10 shorter events, 0.1 us)
Async XLA Ops:
  0.6 12.3 %copy-start = (s32[2]{0:T(128)S(1)}, s32[2]{0:T(128)}, u32[]{:S(2)}) copy-start(s32[2]{0:T(128)} %dils.5) | copy-start | bytes 28
  1.7 11.1 %collective-permute-start.1 = (bf16[208,768]{1,0:T(8,128)(2,1)S(1)}, bf16[208,768]{1,0:T(8,128)(2,1)S(1)}, u32[]{:S(2)}, u32[]{:S(2)}) collective-permute-start(bf16[208,768]{1,0:T(8,128)(2,1)S(1)} %get-tuple-element.56.refs_0_), channel_id=1, source_target_pairs={{0,2},{1,3},{2,0},{3,1},{4,6},{5,7},{6,4},{7,5},{8,10},{9,11},{10,... | collective-permute-start | bytes 958472 | tf_op jit(solution)/shard_map/ppermute | solution.py:454
  4.7 5.8 %collective-permute-start.4 = (s32[1,768]{1,0:T(1,128)S(1)}, s32[1,768]{1,0:T(1,128)S(1)}, u32[]{:S(2)}, u32[]{:S(2)}) collective-permute-start(s32[1,768]{1,0:T(1,128)S(1)} %get-tuple-element.57), channel_id=1, source_target_pairs={{0,12},{4,8},{8,4},{12,0},{1,13},{5,9},{9,5},{13,1},{2,14},{6,10},... | collective-permute-start | bytes 9224 | tf_op jit(solution)/shard_map/ppermute | solution.py:454
  8.3 4.5 %collective-permute-start.3 = (s32[1,768]{1,0:T(1,128)S(1)}, s32[1,768]{1,0:T(1,128)S(1)}, u32[]{:S(2)}, u32[]{:S(2)}) collective-permute-start(s32[1,768]{1,0:T(1,128)S(1)} %get-tuple-element.57), channel_id=1, source_target_pairs={{0,8},{4,12},{8,0},{12,4},{1,9},{5,13},{9,1},{13,5},{2,10},{6,14},... | collective-permute-start | bytes 9224 | tf_op jit(solution)/shard_map/ppermute | solution.py:454
  8.3 4.5 %collective-permute-start.2 = (s32[1,768]{1,0:T(1,128)S(1)}, s32[1,768]{1,0:T(1,128)S(1)}, u32[]{:S(2)}, u32[]{:S(2)}) collective-permute-start(s32[1,768]{1,0:T(1,128)S(1)} %get-tuple-element.57), channel_id=1, source_target_pairs={{0,4},{4,0},{8,12},{12,8},{1,5},{5,1},{9,13},{13,9},{2,6},{6,2},{1... | collective-permute-start | bytes 9224 | tf_op jit(solution)/shard_map/ppermute | solution.py:454
  9.1 5.0 %collective-permute-start = (bf16[208,768]{1,0:T(8,128)(2,1)S(1)}, bf16[208,768]{1,0:T(8,128)(2,1)S(1)}, u32[]{:S(2)}, u32[]{:S(2)}) collective-permute-start(bf16[208,768]{1,0:T(8,128)(2,1)S(1)} %get-tuple-element.56.refs_0_), channel_id=1, source_target_pairs={{0,1},{1,0},{2,3},{3,2},{4,5},{5,4},{6,7},{7,6},{8,9},{9,8},{10,11... | collective-permute-start | bytes 958472 | tf_op jit(solution)/shard_map/ppermute | solution.py:454
  12.8 1.7 %collective-permute-start.5 = (bf16[208,768]{1,0:T(8,128)(2,1)S(1)}, bf16[208,768]{1,0:T(8,128)(2,1)S(1)}, u32[]{:S(2)}, u32[]{:S(2)}) collective-permute-start(bf16[208,768]{1,0:T(8,128)(2,1)S(1)} %collective-permute-done.1.refs_2_), channel_id=1, source_target_pairs={{0,1},{1,0},{2,3},{3,2},{4,5},{5,4},{6,7},{7,6},{8,9},{9,8},{10,11... | collective-permute-start | bytes 958472 | tf_op jit(solution)/shard_map/ppermute | solution.py:454
  22.5 7.2 %collective-permute-start.6 = (bf16[96,768]{1,0:T(8,128)(2,1)S(1)}, bf16[96,768]{1,0:T(8,128)(2,1)S(1)}, u32[]{:S(2)}, u32[]{:S(2)}) collective-permute-start(bf16[96,768]{1,0:T(8,128)(2,1)S(1)} %get-tuple-element.96), channel_id=1, source_target_pairs={{0,4},{4,0},{8,12},{12,8},{1,5},{5,1},{9,13},{13,9},{2,6},{6,2},{1... | collective-permute-start | bytes 442376 | tf_op jit(solution)/shard_map/ppermute | solution.py:454
  29.7 10.2 %collective-permute-start.12 = (bf16[96,768]{1,0:T(8,128)(2,1)S(1)}, bf16[96,768]{1,0:T(8,128)(2,1)S(1)}, u32[]{:S(2)}, u32[]{:S(2)}) collective-permute-start(bf16[96,768]{1,0:T(8,128)(2,1)S(1)} %add_convert_fusion.1), channel_id=1, source_target_pairs={{0,8},{4,12},{8,0},{12,4},{1,9},{5,13},{9,1},{13,5},{2,10},{6,14},... | collective-permute-start | bytes 442376 | tf_op jit(solution)/shard_map/ppermute | solution.py:454
  34.1 1.4 %collective-permute-start.7 = (f32[2,64,192]{2,1,0:T(8,128)S(1)}, f32[2,64,192]{2,1,0:T(8,128)S(1)}, u32[]{:S(2)}, u32[]{:S(2)}) collective-permute-start(f32[2,64,192]{2,1,0:T(8,128)S(1)} %get-tuple-element.102), channel_id=1, source_target_pairs={{0,1},{1,0},{2,3},{3,2},{4,5},{5,4},{6,7},{7,6},{8,9},{9,8},{10,11... | collective-permute-start | bytes 294920 | tf_op jit(solution)/shard_map/ppermute | solution.py:454
  35.5 7.3 %collective-permute-start.10 = (bf16[64,192]{1,0:T(8,128)(2,1)S(1)}, bf16[64,192]{1,0:T(8,128)(2,1)S(1)}, u32[]{:S(2)}, u32[]{:S(2)}) collective-permute-start(bf16[64,192]{1,0:T(8,128)(2,1)S(1)} %get-tuple-element.104), channel_id=1, source_target_pairs={{0,10},{1,11},{2,8},{3,9},{4,14},{5,15},{6,12},{7,13},{8,2},{9,3},... | collective-permute-start | bytes 73736 | tf_op jit(solution)/shard_map/ppermute | solution.py:606
  36.9 6.0 %collective-permute-start.8 = (bf16[64,192]{1,0:T(8,128)(2,1)S(1)}, bf16[64,192]{1,0:T(8,128)(2,1)S(1)}, u32[]{:S(2)}, u32[]{:S(2)}) collective-permute-start(bf16[64,192]{1,0:T(8,128)(2,1)S(1)} %get-tuple-element.104), channel_id=1, source_target_pairs={{0,2},{1,3},{2,0},{3,1},{4,6},{5,7},{6,4},{7,5},{8,10},{9,11},{10,... | collective-permute-start | bytes 73736 | tf_op jit(solution)/shard_map/ppermute | solution.py:454
  37.4 5.5 %collective-permute-start.9 = (bf16[64,192]{1,0:T(8,128)(2,1)S(1)}, bf16[64,192]{1,0:T(8,128)(2,1)S(1)}, u32[]{:S(2)}, u32[]{:S(2)}) collective-permute-start(bf16[64,192]{1,0:T(8,128)(2,1)S(1)} %get-tuple-element.103), channel_id=1, source_target_pairs={{0,8},{4,12},{8,0},{12,4},{1,9},{5,13},{9,1},{13,5},{2,10},{6,14},... | collective-permute-start | bytes 73736 | tf_op jit(solution)/shard_map/ppermute | solution.py:454
  40.0 6.9 %collective-permute-start.13 = (bf16[96,768]{1,0:T(8,128)(2,1)S(1)}, bf16[96,768]{1,0:T(8,128)(2,1)S(1)}, u32[]{:S(2)}, u32[]{:S(2)}) collective-permute-start(bf16[96,768]{1,0:T(8,128)(2,1)S(1)} %add_convert_fusion.near_ref), channel_id=1, source_target_pairs={{0,4},{4,0},{8,12},{12,8},{1,5},{5,1},{9,13},{13,9},{2,6},{6,2},{1... | collective-permute-start | bytes 442376 | tf_op jit(solution)/shard_map/ppermute | solution.py:454
  42.9 4.0 %collective-permute-start.11 = (bf16[64,192]{1,0:T(8,128)(2,1)S(1)}, bf16[64,192]{1,0:T(8,128)(2,1)S(1)}, u32[]{:S(2)}, u32[]{:S(2)}) collective-permute-start(bf16[64,192]{1,0:T(8,128)(2,1)S(1)} %add_convert_fusion.2.sa_ref), channel_id=1, source_target_pairs={{0,4},{4,0},{8,12},{12,8},{1,5},{5,1},{9,13},{13,9},{2,6},{6,2},{1... | collective-permute-start | bytes 73736 | tf_op jit(solution)/shard_map/ppermute | solution.py:454

commit v14 on v12

--- a/solution.py
+++ b/solution.py
@@ -233,19 +233,19 @@
         return jnp.concatenate([above, lines, below], axis=0).astype(BF)
 
     look, look_r = lookup(table, centre), lookup(table_r, JB + centre)
-    chunk, mchunk = ext // 5, rows // 6
+    chunk, mchunk = ext // 10, rows // 24
     for t in range(tiles):
         dst = slice(t * LANE, (t + 1) * LANE)
         for strand, (wr, er) in enumerate(((weights, look), (weights_r, look_r))):
             rhs = jnp.concatenate([wr[:, dst], er[:, dst]], axis=1)
-            for i in range(5):
+            for i in range(10):
                 where = pl.ds(i * chunk, chunk)
                 both = dot(a_ref[where, :], rhs)
                 value, slope = gelu_doubled(both[:, :LANE])
                 x1_refs[strand][t][where, :] = both[:, LANE:] + value
                 gp_refs[strand][t][where, :] = slope
 
-        for i in range(6):
+        for i in range(24):
             first = i * mchunk
             terms = []
             for j in range(TAPS):
@@ -295,7 +295,7 @@
     for t in range(n_own):
         g2_ref[t, REACH : rows + REACH, :] = 0.5 * g2[:, t * LANE : (t + 1) * LANE]
 
-    mchunk, chunk = rows // 6, ext // 5
+    mchunk, chunk = rows // 12, ext // 10
     for t in range(tiles):
         dst = slice(t * LANE, (t + 1) * LANE)
         p_ref, s0_ref = p_refs[t], s0_refs[t]
@@ -306,7 +306,7 @@
         p_ref[rows + edge :, :] = jnp.zeros((edge, LANE), F32)
         p_ref[edge : rows + edge, :] = pair[:, (t % 2) * LANE : (t % 2 + 1) * LANE]
         s0_ref[ext:, :] = jnp.zeros((padded - ext, 2 * LANE), BF)
-        for i in range(5):
+        for i in range(10):
             first = i * chunk
             where = pl.ds(first, chunk)
             fs, rs = [], []
@@ -324,7 +324,7 @@
         plain_ref[:, dst], other_ref[:, dst] = both[:, :LANE], both[:, LANE:]
 
         sums = [None] * (2 * TAPS)
-        for i in range(6):
+        for i in range(12):
             first = i * mchunk
             here = p_ref[pl.ds(edge + first, mchunk), :]
             for strand in range(2):

time: 48.7 us -> 48.8 us (level); the launches traced: 48.4 us -> 49 us
  Pallas kernels: 21.3 us -> 21.9 us
  transfers between devices with their start and end apart: 14 -> 14, of which waited for: 6 -> 6; matrix products, arithmetic and copies ran while one was open for 0% -> 0% of each run, Pallas kernels for 21% -> 22%
where the time goes in v14:
time: 48.8 us; the launch traced here: 49 us
  Pallas kernels  21.9 us (45%)
  starting transfers between devices  16.4 us (34%)
  waiting for transfers between devices  9.73 us (20%)
  between operations  0.77 us (2%)
    ppermute x13, starting transfers between devices, flip_bits(): lax.ppermute(x, axis, [(i, i ^ mask) for i in range(lax.axis_size(axis))])  15 us
    ppermute x13, waiting for transfers between devices, flip_bits(): lax.ppermute(x, axis, [(i, i ^ mask) for i in range(lax.axis_size(axis))])  9.73 us
    pallas_call x1, Pallas kernels, body(): call(functools.partial(forward_kernel, n_chan, rows, width, scale), [SMEM...  8.27 us
    pallas_call x1, Pallas kernels, body(): call(functools.partial(backward_kernel, n_chan, rows, width, scale), [SME...  6.27 us
    pallas_call x1, Pallas kernels, body(): call(functools.partial(finish_kernel, n_chan, width), [VMEM] * 5, [shape(...  2.03 us
    pallas_call x1, Pallas kernels, body(): call(functools.partial(collect_kernel, n_chan, width, scale), [VMEM] * (n...  1.72 us
    ppermute x1, starting transfers between devices, body(): corner = lax.ppermute(s_mine[1], ('seq', 'chan'), pairs)  1.46 us
    pallas_call x1, Pallas kernels, body(): call(functools.partial(local_kernel, n_chan, width), [HBM, HBM], [shape((...  1.44 us
  transfers between devices with their start and end apart: 14, of which 6 were waited for; matrix products, arithmetic and copies ran while one was open for 0% of the time, Pallas kernels for 22%

profile of v14, /device:TPU:0, one launch (start us, length us, event | category | flops | bytes accessed | tf_op | source)
XLA Modules:
  0.0 49.0 jit_solution(11855365129080066567)
XLA Ops:
  0.6 1.1 %shard_map.93 = (bf16[208,768]{1,0:T(8,128)(2,1)S(1)}, s32[1,768]{1,0:T(1,128)S(1)}) custom-call(bf16[2,192,768]{2,1,0:T(8,128)(2,1)} %bitcast.6, bf16[4,192]{1,0:T(4,128)(2,1)} %embed_ref.1, bf16[5,2,192]{2,1,0:T(2,128)(2,1)} %bitcast.9, s32[768]{0:T(1024)} %tok_ref.1), custom_call_target="tpu_custom_call" | custom-call | bytes 589824 | tf_op jit(solution)/shard_map/pallas_call | solution.py:470
  1.7 3.0 %collective-permute-start.1 = (bf16[208,768]{1,0:T(8,128)(2,1)S(1)}, bf16[208,768]{1,0:T(8,128)(2,1)S(1)}, u32[]{:S(2)}, u32[]{:S(2)}) collective-permute-start(bf16[208,768]{1,0:T(8,128)(2,1)S(1)} %get-tuple-element.56.refs_0_), channel_id=1, source_target_pairs={{0,2},{1,3},{2,0},{3,1},{4,6},{5,7},{6,4},{7,5},{8,10},{9,11},{10,... | collective-permute-start | bytes 958472 | tf_op jit(solution)/shard_map/ppermute | solution.py:454
  4.7 3.6 %collective-permute-start.4 = (s32[1,768]{1,0:T(1,128)S(1)}, s32[1,768]{1,0:T(1,128)S(1)}, u32[]{:S(2)}, u32[]{:S(2)}) collective-permute-start(s32[1,768]{1,0:T(1,128)S(1)} %get-tuple-element.57), channel_id=1, source_target_pairs={{0,12},{4,8},{8,4},{12,0},{1,13},{5,9},{9,5},{13,1},{2,14},{6,10},... | collective-permute-start | bytes 9224 | tf_op jit(solution)/shard_map/ppermute | solution.py:454
  8.3 0.0 collective-permute-start.3
  8.3 0.8 %collective-permute-start.2 = (s32[1,768]{1,0:T(1,128)S(1)}, s32[1,768]{1,0:T(1,128)S(1)}, u32[]{:S(2)}, u32[]{:S(2)}) collective-permute-start(s32[1,768]{1,0:T(1,128)S(1)} %get-tuple-element.57), channel_id=1, source_target_pairs={{0,4},{4,0},{8,12},{12,8},{1,5},{5,1},{9,13},{13,9},{2,6},{6,2},{1... | collective-permute-start | bytes 9224 | tf_op jit(solution)/shard_map/ppermute | solution.py:454
  9.1 0.0 collective-permute-start
  9.1 1.4 %shard_map.94 = (bf16[192,768]{1,0:T(8,128)(2,1)S(1)}, bf16[768,192]{1,0:T(8,128)(2,1)S(1)}) custom-call(bf16[2,192,768]{2,1,0:T(8,128)(2,1)} %bitcast.7, bf16[192,768]{1,0:T(8,128)(2,1)} %bitcast.8), custom_call_target="tpu_custom_call" | custom-call | flops 1048576 | bytes 1048576 | tf_op jit(solution)/shard_map/pallas_call | solution.py:489
  10.5 0.0 collective-permute-done.4
  10.6 2.2 %collective-permute-done.3 = s32[1,768]{1,0:T(1,128)S(1)} collective-permute-done((s32[1,768]{1,0:T(1,128)S(1)}, s32[1,768]{1,0:T(1,128)S(1)}, u32[]{:S(2)}, u32[]{:S(2)}) %collective-permute-start.3) | collective-permute-done | bytes 3104 | tf_op jit(solution)/shard_map/ppermute | solution.py:454
  12.8 0.0 collective-permute-done.2
  12.8 0.1 collective-permute-start.5
  12.9 1.1 %shard_map.95 = (bf16[896,128]{1,0:T(8,128)(2,1)S(1)}, bf16[64,896]{1,0:T(8,128)(2,1)S(1)}, bf16[64,768]{1,0:T(8,128)(2,1)S(1)}) custom-call(s32[2]{0:T(128)S(1)} %copy-done, s32[4,768]{1,0:T(4,128)S(1)} %pad_add_fusion.tok_ref), custom_call_target="tpu_custom_call" | custom-call | flops 1048576 | bytes 1048576 | tf_op jit(solution)/shard_map/pallas_call | solution.py:509
  14.1 0.0 collective-permute-done.refs_1_
  14.1 0.4 collective-permute-done.5.refs_3_
  14.5 8.3 %shard_map.96 = (bf16[192,768]{1,0:T(8,128)(2,1)}, bf16[96,768]{1,0:T(8,128)(2,1)S(1)}, bf16[96,768]{1,0:T(8,128)(2,1)S(1)}, bf16[768,192]{1,0:T(8,128)(2,1)S(1)...) custom-call(s32[2]{0:T(128)S(1)} %copy-done, ...), custom_call_target="tpu_custom_call" | custom-call | flops 3221225472 | bytes 8388608 | tf_op jit(solution)/shard_map/pallas_call | solution.py:520
  22.8 1.2 %collective-permute-start.6 = (bf16[96,768]{1,0:T(8,128)(2,1)S(1)}, bf16[96,768]{1,0:T(8,128)(2,1)S(1)}, u32[]{:S(2)}, u32[]{:S(2)}) collective-permute-start(bf16[96,768]{1,0:T(8,128)(2,1)S(1)} %get-tuple-element.96), channel_id=1, source_target_pairs={{0,4},{4,0},{8,12},{12,8},{1,5},{5,1},{9,13},{13,9},{2,6},{6,2},{1... | collective-permute-start | bytes 442376 | tf_op jit(solution)/shard_map/ppermute | solution.py:454
  24.0 6.3 %shard_map.97 = (bf16[768,768]{1,0:T(8,128)(2,1)S(1)}, f32[2,8,768]{2,1,0:T(8,128)S(1)}, f32[64,768]{1,0:T(8,128)S(1)}, f32[64,768]{1,0:T(8,128)S(1)}) custom-call(s32[2]{0:T(128)S(1)} %copy-done, bf16[64,896]{1,0:T(8,128)(2,1)S(1)} %get-tuple-element.67.refs_0_, bf16[192,768]{1,0:T(8,128)(2,1)S(1)} %get-tuple-element.58.refs_5_.refs_1_, ...), custom_call_target="tpu_custom_call" | custom-call | flops 3221225472 | bytes 8388608 | tf_op jit(solution)/shard_map/pallas_call | solution.py:546
  30.3 0.0 collective-permute-done.6
  30.4 2.6 %collective-permute-start.12 = (bf16[96,768]{1,0:T(8,128)(2,1)S(1)}, bf16[96,768]{1,0:T(8,128)(2,1)S(1)}, u32[]{:S(2)}, u32[]{:S(2)}) collective-permute-start(bf16[96,768]{1,0:T(8,128)(2,1)S(1)} %add_convert_fusion.1), channel_id=1, source_target_pairs={{0,8},{4,12},{8,0},{12,4},{1,9},{5,13},{9,1},{13,5},{2,10},{6,14},... | collective-permute-start | bytes 442376 | tf_op jit(solution)/shard_map/ppermute | solution.py:454
  33.0 1.7 %shard_map.98 = (f32[2,64,192]{2,1,0:T(8,128)S(1)}, f32[2,64,192]{2,1,0:T(8,128)S(1)}) custom-call(bf16[208,768]{1,0:T(8,128)(2,1)S(1)} %get-tuple-element.56.refs_0_, bf16[208,768]{1,0:T(8,128)(2,1)S(1)} %collective-permute-done.refs_1_, bf16[208,768]{1,0:T(8,128)(2,1)S(1)} %collective-permute-done.1.refs_2_, ...), custom_call_target="tpu_custom_call" | custom-call | flops 1048576 | bytes 65536 | tf_op jit(solution)/shard_map/pallas_call | solution.py:568
  34.7 0.0 collective-permute-start.7
  34.8 1.3 %collective-permute-done.7.b_ref = f32[2,64,192]{2,1,0:T(8,128)S(1)} collective-permute-done((f32[2,64,192]{2,1,0:T(8,128)S(1)}, f32[2,64,192]{2,1,0:T(8,128)S(1)}, u32[]{:S(2)}, u32[]{:S(2)}) %collective-permute-start.7) | collective-permute-done | bytes 98336 | tf_op jit(solution)/shard_map/ppermute | solution.py:454
  36.1 1.5 %collective-permute-start.10 = (bf16[64,192]{1,0:T(8,128)(2,1)S(1)}, bf16[64,192]{1,0:T(8,128)(2,1)S(1)}, u32[]{:S(2)}, u32[]{:S(2)}) collective-permute-start(bf16[64,192]{1,0:T(8,128)(2,1)S(1)} %get-tuple-element.104), channel_id=1, source_target_pairs={{0,6},{1,7},{2,4},{3,5},{4,2},{5,3},{6,0},{7,1},{8,14},{9,15},{10,... | collective-permute-start | bytes 73736 | tf_op jit(solution)/shard_map/ppermute | solution.py:604
  37.6 0.5 %collective-permute-start.8 = (bf16[64,192]{1,0:T(8,128)(2,1)S(1)}, bf16[64,192]{1,0:T(8,128)(2,1)S(1)}, u32[]{:S(2)}, u32[]{:S(2)}) collective-permute-start(bf16[64,192]{1,0:T(8,128)(2,1)S(1)} %get-tuple-element.104), channel_id=1, source_target_pairs={{0,2},{1,3},{2,0},{3,1},{4,6},{5,7},{6,4},{7,5},{8,10},{9,11},{10,... | collective-permute-start | bytes 73736 | tf_op jit(solution)/shard_map/ppermute | solution.py:454
  38.1 1.6 %collective-permute-start.9 = (bf16[64,192]{1,0:T(8,128)(2,1)S(1)}, bf16[64,192]{1,0:T(8,128)(2,1)S(1)}, u32[]{:S(2)}, u32[]{:S(2)}) collective-permute-start(bf16[64,192]{1,0:T(8,128)(2,1)S(1)} %get-tuple-element.103), channel_id=1, source_target_pairs={{0,4},{4,0},{8,12},{12,8},{1,5},{5,1},{9,13},{13,9},{2,6},{6,2},{1... | collective-permute-start | bytes 73736 | tf_op jit(solution)/shard_map/ppermute | solution.py:454
  39.7 0.4 collective-permute-done.12
  40.2 0.1 collective-permute-start.13
  40.3 1.8 %collective-permute-done.9 = bf16[64,192]{1,0:T(8,128)(2,1)S(1)} collective-permute-done((bf16[64,192]{1,0:T(8,128)(2,1)S(1)}, bf16[64,192]{1,0:T(8,128)(2,1)S(1)}, u32[]{:S(2)}, u32[]{:S(2)}) %collective-permute-start.9) | collective-permute-done | bytes 24608 | tf_op jit(solution)/shard_map/ppermute | solution.py:454
  42.1 1.4 %collective-permute-start.11 = (bf16[64,192]{1,0:T(8,128)(2,1)S(1)}, bf16[64,192]{1,0:T(8,128)(2,1)S(1)}, u32[]{:S(2)}, u32[]{:S(2)}) collective-permute-start(bf16[64,192]{1,0:T(8,128)(2,1)S(1)} %add_convert_fusion.2.sa_ref), channel_id=1, source_target_pairs={{0,8},{4,12},{8,0},{12,4},{1,9},{5,13},{9,1},{13,5},{2,10},{6,14},... | collective-permute-start | bytes 73736 | tf_op jit(solution)/shard_map/ppermute | solution.py:454
  43.5 3.5 %collective-permute-done.11.sb_ref = bf16[64,192]{1,0:T(8,128)(2,1)S(1)} collective-permute-done((bf16[64,192]{1,0:T(8,128)(2,1)S(1)}, bf16[64,192]{1,0:T(8,128)(2,1)S(1)}, u32[]{:S(2)}, u32[]{:S(2)}) %collective-permute-start.11) | collective-permute-done | bytes 24608 | tf_op jit(solution)/shard_map/ppermute | solution.py:454
  47.0 0.0 collective-permute-done.13.far_ref
  47.0 2.0 %shard_map.100 = (f32[2,192,768]{2,1,0:T(8,128)}, f32[5,2,192]{2,1,0:T(2,128)}, f32[4,192]{1,0:T(4,128)}) custom-call(bf16[128,768]{1,0:T(8,128)(2,1)S(1)} %get-tuple-element.63.st_ref, bf16[64,192]{1,0:T(8,128)(2,1)S(1)} %add_convert_fusion.2.sa_ref, bf16[64,192]{1,0:T(8,128)(2,1)S(1)} %collective-permute-done.11.sb_ref, ...), custom_call_target="tpu_custom_call" | custom-call | flops 16777216 | bytes 2097152 | tf_op jit(solution)/shard_map/pallas_call | solution.py:612
  (10 shorter events, 0.1 us)
Async XLA Ops:
  0.6 12.3 %copy-start = (s32[2]{0:T(128)S(1)}, s32[2]{0:T(128)}, u32[]{:S(2)}) copy-start(s32[2]{0:T(128)} %dils.5) | copy-start | bytes 28
  1.7 11.1 %collective-permute-start.1 = (bf16[208,768]{1,0:T(8,128)(2,1)S(1)}, bf16[208,768]{1,0:T(8,128)(2,1)S(1)}, u32[]{:S(2)}, u32[]{:S(2)}) collective-permute-start(bf16[208,768]{1,0:T(8,128)(2,1)S(1)} %get-tuple-element.56.refs_0_), channel_id=1, source_target_pairs={{0,2},{1,3},{2,0},{3,1},{4,6},{5,7},{6,4},{7,5},{8,10},{9,11},{10,... | collective-permute-start | bytes 958472 | tf_op jit(solution)/shard_map/ppermute | solution.py:454
  4.7 5.8 %collective-permute-start.4 = (s32[1,768]{1,0:T(1,128)S(1)}, s32[1,768]{1,0:T(1,128)S(1)}, u32[]{:S(2)}, u32[]{:S(2)}) collective-permute-start(s32[1,768]{1,0:T(1,128)S(1)} %get-tuple-element.57), channel_id=1, source_target_pairs={{0,12},{4,8},{8,4},{12,0},{1,13},{5,9},{9,5},{13,1},{2,14},{6,10},... | collective-permute-start | bytes 9224 | tf_op jit(solution)/shard_map/ppermute | solution.py:454
  8.3 4.5 %collective-permute-start.3 = (s32[1,768]{1,0:T(1,128)S(1)}, s32[1,768]{1,0:T(1,128)S(1)}, u32[]{:S(2)}, u32[]{:S(2)}) collective-permute-start(s32[1,768]{1,0:T(1,128)S(1)} %get-tuple-element.57), channel_id=1, source_target_pairs={{0,8},{4,12},{8,0},{12,4},{1,9},{5,13},{9,1},{13,5},{2,10},{6,14},... | collective-permute-start | bytes 9224 | tf_op jit(solution)/shard_map/ppermute | solution.py:454
  8.3 4.5 %collective-permute-start.2 = (s32[1,768]{1,0:T(1,128)S(1)}, s32[1,768]{1,0:T(1,128)S(1)}, u32[]{:S(2)}, u32[]{:S(2)}) collective-permute-start(s32[1,768]{1,0:T(1,128)S(1)} %get-tuple-element.57), channel_id=1, source_target_pairs={{0,4},{4,0},{8,12},{12,8},{1,5},{5,1},{9,13},{13,9},{2,6},{6,2},{1... | collective-permute-start | bytes 9224 | tf_op jit(solution)/shard_map/ppermute | solution.py:454
  9.1 5.0 %collective-permute-start = (bf16[208,768]{1,0:T(8,128)(2,1)S(1)}, bf16[208,768]{1,0:T(8,128)(2,1)S(1)}, u32[]{:S(2)}, u32[]{:S(2)}) collective-permute-start(bf16[208,768]{1,0:T(8,128)(2,1)S(1)} %get-tuple-element.56.refs_0_), channel_id=1, source_target_pairs={{0,1},{1,0},{2,3},{3,2},{4,5},{5,4},{6,7},{7,6},{8,9},{9,8},{10,11... | collective-permute-start | bytes 958472 | tf_op jit(solution)/shard_map/ppermute | solution.py:454
  12.8 1.7 %collective-permute-start.5 = (bf16[208,768]{1,0:T(8,128)(2,1)S(1)}, bf16[208,768]{1,0:T(8,128)(2,1)S(1)}, u32[]{:S(2)}, u32[]{:S(2)}) collective-permute-start(bf16[208,768]{1,0:T(8,128)(2,1)S(1)} %collective-permute-done.1.refs_2_), channel_id=1, source_target_pairs={{0,1},{1,0},{2,3},{3,2},{4,5},{5,4},{6,7},{7,6},{8,9},{9,8},{10,11... | collective-permute-start | bytes 958472 | tf_op jit(solution)/shard_map/ppermute | solution.py:454
  22.8 7.5 %collective-permute-start.6 = (bf16[96,768]{1,0:T(8,128)(2,1)S(1)}, bf16[96,768]{1,0:T(8,128)(2,1)S(1)}, u32[]{:S(2)}, u32[]{:S(2)}) collective-permute-start(bf16[96,768]{1,0:T(8,128)(2,1)S(1)} %get-tuple-element.96), channel_id=1, source_target_pairs={{0,4},{4,0},{8,12},{12,8},{1,5},{5,1},{9,13},{13,9},{2,6},{6,2},{1... | collective-permute-start | bytes 442376 | tf_op jit(solution)/shard_map/ppermute | solution.py:454
  30.4 9.8 %collective-permute-start.12 = (bf16[96,768]{1,0:T(8,128)(2,1)S(1)}, bf16[96,768]{1,0:T(8,128)(2,1)S(1)}, u32[]{:S(2)}, u32[]{:S(2)}) collective-permute-start(bf16[96,768]{1,0:T(8,128)(2,1)S(1)} %add_convert_fusion.1), channel_id=1, source_target_pairs={{0,8},{4,12},{8,0},{12,4},{1,9},{5,13},{9,1},{13,5},{2,10},{6,14},... | collective-permute-start | bytes 442376 | tf_op jit(solution)/shard_map/ppermute | solution.py:454
  34.7 1.4 %collective-permute-start.7 = (f32[2,64,192]{2,1,0:T(8,128)S(1)}, f32[2,64,192]{2,1,0:T(8,128)S(1)}, u32[]{:S(2)}, u32[]{:S(2)}) collective-permute-start(f32[2,64,192]{2,1,0:T(8,128)S(1)} %get-tuple-element.102), channel_id=1, source_target_pairs={{0,1},{1,0},{2,3},{3,2},{4,5},{5,4},{6,7},{7,6},{8,9},{9,8},{10,11... | collective-permute-start | bytes 294920 | tf_op jit(solution)/shard_map/ppermute | solution.py:454
  36.1 5.9 %collective-permute-start.10 = (bf16[64,192]{1,0:T(8,128)(2,1)S(1)}, bf16[64,192]{1,0:T(8,128)(2,1)S(1)}, u32[]{:S(2)}, u32[]{:S(2)}) collective-permute-start(bf16[64,192]{1,0:T(8,128)(2,1)S(1)} %get-tuple-element.104), channel_id=1, source_target_pairs={{0,6},{1,7},{2,4},{3,5},{4,2},{5,3},{6,0},{7,1},{8,14},{9,15},{10,... | collective-permute-start | bytes 73736 | tf_op jit(solution)/shard_map/ppermute | solution.py:604
  37.6 4.5 %collective-permute-start.8 = (bf16[64,192]{1,0:T(8,128)(2,1)S(1)}, bf16[64,192]{1,0:T(8,128)(2,1)S(1)}, u32[]{:S(2)}, u32[]{:S(2)}) collective-permute-start(bf16[64,192]{1,0:T(8,128)(2,1)S(1)} %get-tuple-element.104), channel_id=1, source_target_pairs={{0,2},{1,3},{2,0},{3,1},{4,6},{5,7},{6,4},{7,5},{8,10},{9,11},{10,... | collective-permute-start | bytes 73736 | tf_op jit(solution)/shard_map/ppermute | solution.py:454
  38.1 3.9 %collective-permute-start.9 = (bf16[64,192]{1,0:T(8,128)(2,1)S(1)}, bf16[64,192]{1,0:T(8,128)(2,1)S(1)}, u32[]{:S(2)}, u32[]{:S(2)}) collective-permute-start(bf16[64,192]{1,0:T(8,128)(2,1)S(1)} %get-tuple-element.103), channel_id=1, source_target_pairs={{0,4},{4,0},{8,12},{12,8},{1,5},{5,1},{9,13},{13,9},{2,6},{6,2},{1... | collective-permute-start | bytes 73736 | tf_op jit(solution)/shard_map/ppermute | solution.py:454
  40.2 6.8 %collective-permute-start.13 = (bf16[96,768]{1,0:T(8,128)(2,1)S(1)}, bf16[96,768]{1,0:T(8,128)(2,1)S(1)}, u32[]{:S(2)}, u32[]{:S(2)}) collective-permute-start(bf16[96,768]{1,0:T(8,128)(2,1)S(1)} %add_convert_fusion.near_ref), channel_id=1, source_target_pairs={{0,4},{4,0},{8,12},{12,8},{1,5},{5,1},{9,13},{13,9},{2,6},{6,2},{1... | collective-permute-start | bytes 442376 | tf_op jit(solution)/shard_map/ppermute | solution.py:454
  42.1 4.9 %collective-permute-start.11 = (bf16[64,192]{1,0:T(8,128)(2,1)S(1)}, bf16[64,192]{1,0:T(8,128)(2,1)S(1)}, u32[]{:S(2)}, u32[]{:S(2)}) collective-permute-start(bf16[64,192]{1,0:T(8,128)(2,1)S(1)} %add_convert_fusion.2.sa_ref), channel_id=1, source_target_pairs={{0,8},{4,12},{8,0},{12,4},{1,9},{5,13},{9,1},{13,5},{2,10},{6,14},... | collective-permute-start | bytes 73736 | tf_op jit(solution)/shard_map/ppermute | solution.py:454
